TPU v7x, 32 devices: a whole 2x2x4 slice. The times are simulated.
32 devices in a mesh: dp: 8 (over z, y), ctx: 2 (over x), tp: 2 (over core).
Axes of the slice: x: 2, y: 2, z: 4, core: 2. Of those that a mesh axis runs over, the one named last changes fastest.
Arguments:
- hidden_in: bfloat16 [2, 8, 1024, 1152], P(None, 'dp', 'ctx'), may hold values from -6 to 6
- out_grad: bfloat16 [2, 8, 1024, 1152], P(None, 'dp', 'ctx'), may hold values from -6 to 6
- norm1_gain: bfloat16 [1152], P('dp'), may hold values from 0.5 to 1.5
- in_weight: bfloat16 [1152, 2, 2304], P('dp', None, 'tp'), may hold values from -0.1875 to 0.1875
- conv_weight: bfloat16 [4, 2304], P(None, ('tp', 'dp')), may hold values from -3 to 3
- conv_bias: bfloat16 [2304], P(('tp', 'dp')), may hold values from -0.5 to 0.5
- xproj_weight: bfloat16 [2304, 104], P(('tp', 'dp')), may hold values from -0.359375 to 0.359375
- dt_weight: bfloat16 [72, 2304], P(None, ('tp', 'dp')), may hold values from -0.75 to 0.75
- dt_bias: bfloat16 [2304], P(('tp', 'dp')), may hold values from -7 to -3
- decay_log: bfloat16 [16, 2304], P(None, ('tp', 'dp')), may hold values from 0 to 2.796875
- skip_weight: bfloat16 [2304], P(('tp', 'dp')), may hold values from 0.5 to 1.5
- out_weight: bfloat16 [2304, 1152], P('tp', 'dp'), may hold values from -0.375 to 0.375
- norm2_gain: bfloat16 [1152], P('dp'), may hold values from 0.5 to 1.5
- router_weight: bfloat16 [1152, 8], P('dp'), may hold values from -0.119628906 to 0.119628906
- fc1_weight: bfloat16 [8, 1152, 3072], P(None, 'dp', 'tp'), may hold values from -0.1875 to 0.1875
- fc2_weight: bfloat16 [8, 3072, 1152], P(None, 'tp', 'dp'), may hold values from -0.75 to 0.75
- expert_ids: int32 [16384, 1], P(('dp', 'ctx')), may hold values from 0 to 7; in each aligned block of 512 rows (0 to 511, 512 to 1023, ...) at most 128 rows name the same one
- keep_mask: int32 [16384], P(('dp', 'ctx')), may hold values 0 or 1
Outputs:
- output: bfloat16 [2, 8, 1024, 1152], P(None, 'dp', 'ctx')
- input_grad: bfloat16 [2, 8, 1024, 1152], P(None, 'dp', 'ctx')
- norm1_gain_grad: float32 [1152], P('dp')
- in_weight_grad: float32 [1152, 2, 2304], P('dp', None, 'tp')
- conv_weight_grad: float32 [4, 2304], P(None, ('tp', 'dp'))
- conv_bias_grad: float32 [2304], P(('tp', 'dp'))
- xproj_weight_grad: float32 [2304, 104], P(('tp', 'dp'))
- dt_weight_grad: float32 [72, 2304], P(None, ('tp', 'dp'))
- dt_bias_grad: float32 [2304], P(('tp', 'dp'))
- decay_log_grad: float32 [16, 2304], P(None, ('tp', 'dp'))
- skip_weight_grad: float32 [2304], P(('tp', 'dp'))
- out_weight_grad: float32 [2304, 1152], P('tp', 'dp')
- norm2_gain_grad: float32 [1152], P('dp')
- router_weight_grad: float32 [1152, 8], P('dp')
- fc1_weight_grad: float32 [8, 1152, 3072], P(None, 'dp', 'tp')
- fc2_weight_grad: float32 [8, 3072, 1152], P(None, 'tp', 'dp')
Inputs may be any that keep to these rules, and one draw needn't show every extreme that they name: `expert_ids`: in each aligned block of 512 rows (one device's tokens of one micro-batch) no expert is named by more than 128 rows, a bound that some block reaches.
All inputs are finite; a program needn't handle non-finite values. No bound on the sum of `keep_mask` on one device may be relied on, other than what follows from the above.
Results may differ from a plain program's by a relative error of at most 0.014.
The roundings to bfloat16 on the way count: a program that leaves them out, or rounds other values in their place, can miss the bound.
Values may be sent and summed in bfloat16 or wider, within the bound.
A program may use at most 512 MiB of HBM per device.

v0:
```python
from functools import partial
import math

import jax
import jax.numpy as jnp
from jax import lax
from jax.sharding import PartitionSpec as P

EPSILON = 1e-05
HIGHEST = lax.Precision.HIGHEST


def passed_along(value, axis, steps):
    count = lax.axis_size(axis)
    leading, last = (max(0, -steps), min(count, count - steps))
    return lax.ppermute(value, axis, [(source, source + steps) for source in range(leading, last)])


def entering_2(value, axis, join, neutral, backward):
    count, mine = (lax.axis_size(axis), lax.axis_index(axis))
    pieces = jax.tree.map(lambda part: lax.all_gather(part, axis), value)
    if backward:
        pieces = jax.tree.map(lambda part: part[::-1], pieces)
        mine = count - 1 - mine
    running = jax.tree.map(
        lambda part, zero: jnp.full_like(part, 0) + jnp.asarray(zero, part.dtype), value, neutral
    )

    def lap(position, running):
        longer = join(running, jax.tree.map(lambda part: part[position], pieces))
        return jax.tree.map(lambda new, old: jnp.where(position < mine, new, old), longer, running)

    return lax.fori_loop(0, count - 1, lap, running)


def affine_join(first_pair, second_pair):
    return (first_pair[0] * second_pair[0], second_pair[1] + second_pair[0] * first_pair[1])


def contract_rows(left_side, right_side, precision=None):
    return lax.dot_general(
        left_side,
        right_side,
        (((0,), (0,)), ((), ())),
        precision=precision,
        preferred_element_type=jnp.float32,
    )


def contract_cols(left_side, right_side, precision=None):
    return lax.dot_general(
        left_side,
        right_side,
        (((1,), (1,)), ((), ())),
        precision=precision,
        preferred_element_type=jnp.float32,
    )


def rms_forward(values, gain_vec):
    inverse = lax.rsqrt(jnp.mean(values * values, axis=-1, keepdims=True) + EPSILON)
    return (values * inverse * gain_vec, inverse)


def rms_backward(values, inverse, gain_vec, grad_out):
    weighted = grad_out * gain_vec
    inner_mean = jnp.mean(values * weighted, axis=-1, keepdims=True)
    grad_values = inverse * weighted - values * inverse * inverse * inverse * inner_mean
    grad_gain = jnp.sum(grad_out * values * inverse, axis=0)
    return (grad_values, grad_gain)


def time_major(array_in, turns):
    seq_count, length, width = array_in.shape
    return array_in.reshape(seq_count, turns, length // turns, width).transpose(1, 2, 0, 3)


def seq_major(array_in):
    turns, block_len, seq_count = (array_in.shape[0], array_in.shape[1], array_in.shape[2])
    return array_in.transpose(2, 0, 1, *range(3, array_in.ndim)).reshape(
        seq_count, turns * block_len, *array_in.shape[3:]
    )


def forward_sweep(start, inputs, decay_rate, keep_states):

    def block_step(carried, block_in):
        step_block, input_block, mix_in_block, mix_out_block = block_in
        out_list = []
        state_list = []
        for position in range(step_block.shape[0]):
            carried = (
                jnp.exp(step_block[position][:, None, :] * decay_rate) * carried
                + (step_block[position] * input_block[position])[:, None, :]
                * mix_in_block[position][:, :, None]
            )
            if keep_states:
                state_list.append(carried)
                out_list.append(jnp.sum(mix_out_block[position][:, :, None] * carried, axis=1))
        if keep_states:
            return (carried, (jnp.stack(out_list), jnp.stack(state_list)))
        return (carried, None)

    return lax.scan(block_step, start, inputs)


def adjoint_end(start, inputs, decay_rate):

    def block_step(incoming, block_in):
        step_block, mix_out_block, grad_block = block_in
        for position in reversed(range(step_block.shape[0])):
            adjoint = (
                mix_out_block[position][:, :, None] * grad_block[position][:, None, :] + incoming
            )
            incoming = jnp.exp(step_block[position][:, None, :] * decay_rate) * adjoint
        return (incoming, None)

    return lax.scan(block_step, start, inputs, reverse=True)[0]


def adjoint_sweep(start, inputs, decay_rate):

    def block_step(carried, block_in):
        incoming, decay_total = carried
        step_block, input_block, mix_in_block, mix_out_block, grad_block, state_block = block_in
        row_list = [None] * step_block.shape[0]
        for position in reversed(range(step_block.shape[0])):
            driven = step_block[position] * input_block[position]
            adjoint = (
                mix_out_block[position][:, :, None] * grad_block[position][:, None, :] + incoming
            )
            incoming = jnp.exp(step_block[position][:, None, :] * decay_rate) * adjoint
            decay_grad = adjoint * (
                state_block[position] - driven[:, None, :] * mix_in_block[position][:, :, None]
            )
            decay_total = decay_total + jnp.sum(
                decay_grad * step_block[position][:, None, :], axis=0
            )
            row_list[position] = (
                jnp.sum(adjoint * mix_in_block[position][:, :, None], axis=1),
                jnp.sum(decay_grad * decay_rate, axis=1),
                jnp.sum(adjoint * driven[:, None, :], axis=2),
                jnp.sum(grad_block[position][:, None, :] * state_block[position], axis=2),
            )
        stacked = tuple((jnp.stack([entry[member] for entry in row_list]) for member in range(4)))
        return ((incoming, decay_total), stacked)

    return lax.scan(block_step, start, inputs, reverse=True)


def fetch_weights(local_set):
    (
        gain_one,
        input_projection,
        conv_taps,
        conv_shift,
        x_proj,
        dt_proj,
        dt_shift,
        decay_log,
        skip_gain,
        output_projection,
        gain_two,
        router,
        first_layer,
        second_layer,
    ) = local_set
    return (
        lax.all_gather(gain_one, "dp", axis=0, tiled=True),
        lax.all_gather(input_projection, "dp", axis=0, tiled=True),
        lax.all_gather(conv_taps, "dp", axis=1, tiled=True),
        lax.all_gather(conv_shift, "dp", axis=0, tiled=True),
        lax.all_gather(x_proj, "dp", axis=0, tiled=True),
        lax.all_gather(dt_proj, "dp", axis=1, tiled=True),
        lax.all_gather(dt_shift, "dp", axis=0, tiled=True),
        lax.all_gather(decay_log, "dp", axis=1, tiled=True),
        lax.all_gather(skip_gain, "dp", axis=0, tiled=True),
        lax.all_gather(output_projection, "dp", axis=1, tiled=True),
        lax.all_gather(gain_two, "dp", axis=0, tiled=True),
        lax.all_gather(router, "dp", axis=0, tiled=True),
        lax.all_gather(first_layer, "dp", axis=1, tiled=True),
        lax.all_gather(second_layer, "dp", axis=2, tiled=True),
    )


def return_grads(full_set):
    (
        gain_one,
        input_projection,
        conv_taps,
        conv_shift,
        x_proj,
        dt_proj,
        dt_shift,
        decay_log,
        skip_gain,
        output_projection,
        gain_two,
        router,
        first_layer,
        second_layer,
    ) = full_set
    return (
        lax.psum_scatter(gain_one, "dp", scatter_dimension=0, tiled=True),
        lax.psum_scatter(input_projection, "dp", scatter_dimension=0, tiled=True),
        lax.psum_scatter(conv_taps, "dp", scatter_dimension=1, tiled=True),
        lax.psum_scatter(conv_shift, "dp", scatter_dimension=0, tiled=True),
        lax.psum_scatter(x_proj, "dp", scatter_dimension=0, tiled=True),
        lax.psum_scatter(dt_proj, "dp", scatter_dimension=1, tiled=True),
        lax.psum_scatter(dt_shift, "dp", scatter_dimension=0, tiled=True),
        lax.psum_scatter(decay_log, "dp", scatter_dimension=1, tiled=True),
        lax.psum_scatter(skip_gain, "dp", scatter_dimension=0, tiled=True),
        lax.psum_scatter(output_projection, "dp", scatter_dimension=1, tiled=True),
        lax.psum_scatter(gain_two, "dp", scatter_dimension=0, tiled=True),
        lax.psum_scatter(router, "dp", scatter_dimension=0, tiled=True),
        lax.psum_scatter(first_layer, "dp", scatter_dimension=1, tiled=True),
        lax.psum_scatter(second_layer, "dp", scatter_dimension=2, tiled=True),
    )


def pieces_total(shard_set):
    (
        gain_one,
        input_projection,
        conv_taps,
        conv_shift,
        x_proj,
        dt_proj,
        dt_shift,
        decay_log,
        skip_gain,
        output_projection,
        gain_two,
        router,
        first_layer,
        second_layer,
    ) = shard_set
    return lax.psum(
        (
            gain_one,
            input_projection,
            conv_taps,
            conv_shift,
            x_proj,
            dt_proj,
            dt_shift,
            decay_log,
            skip_gain,
            output_projection,
            gain_two,
            router,
            first_layer,
            second_layer,
        ),
        "ctx",
    )


def micro_batch(values_bf, cotan_bf, route_ids, keep_ids, weights):
    (
        gain_one,
        input_projection,
        conv_taps,
        conv_shift,
        x_proj,
        dt_proj,
        dt_shift,
        decay_log,
        skip_gain,
        output_projection,
        gain_two,
        router,
        first_layer,
        second_layer,
    ) = weights
    seq_count, seq_part, model_width = values_bf.shape
    tokens = seq_count * seq_part
    inner_width = input_projection.shape[2]
    tap_count = conv_taps.shape[0]
    low_rank = dt_proj.shape[0]
    state_count = decay_log.shape[0]
    experts = router.shape[1]
    capacity = tokens // 4
    turns = math.gcd(seq_part, 16)
    gain_one_f = gain_one.astype(jnp.float32)
    gain_two_f = gain_two.astype(jnp.float32)
    tap_weights = conv_taps.astype(jnp.float32)
    skip_weight = skip_gain.astype(jnp.float32)
    values = values_bf.reshape(tokens, model_width).astype(jnp.float32)
    normalized_rows, inverse_one = rms_forward(values, gain_one_f)
    normed_bf = normalized_rows.astype(jnp.bfloat16)
    in_flat = input_projection.reshape(model_width, 2 * inner_width)
    mixer_input_rows = jnp.dot(normed_bf, in_flat, preferred_element_type=jnp.float32)
    x_pre = (
        mixer_input_rows[:, :inner_width]
        .astype(jnp.bfloat16)
        .reshape(seq_count, seq_part, inner_width)
    )
    z_gate = mixer_input_rows[:, inner_width:]
    edge_in = passed_along(x_pre[:, seq_part - tap_count + 1 :], "ctx", 1)
    extended = jnp.concatenate([edge_in, x_pre], axis=1).astype(jnp.float32)
    conv_pre = jnp.zeros((seq_count, seq_part, inner_width), jnp.float32) + conv_shift.astype(
        jnp.float32
    )
    for tap_index in range(tap_count):
        conv_pre = conv_pre + tap_weights[tap_index] * extended[:, tap_index : tap_index + seq_part]
    xconv_bf = jax.nn.silu(conv_pre).astype(jnp.bfloat16)
    xconv = xconv_bf.astype(jnp.float32)
    projected = lax.psum(
        jnp.dot(xconv_bf.reshape(tokens, inner_width), x_proj, preferred_element_type=jnp.float32),
        "tp",
    )
    dt_low = projected[:, :low_rank].astype(jnp.bfloat16)
    state_in = projected[:, low_rank : low_rank + state_count].reshape(
        seq_count, seq_part, state_count
    )
    state_out = projected[:, low_rank + state_count :].reshape(seq_count, seq_part, state_count)
    dt_pre = (
        jnp.dot(dt_low, dt_proj, preferred_element_type=jnp.float32) + dt_shift.astype(jnp.float32)
    ).reshape(seq_count, seq_part, inner_width)
    step_size = jax.nn.softplus(dt_pre)
    decay_rate = -jnp.exp(decay_log.astype(jnp.float32))
    step_tm = time_major(step_size, turns)
    xconv_tm = time_major(xconv, turns)
    in_tm = time_major(state_in, turns)
    out_tm = time_major(state_out, turns)
    chain_zero = jnp.zeros((seq_count, state_count, inner_width), jnp.float32)
    chain_unit = jnp.ones_like(chain_zero)
    local_end = forward_sweep(chain_zero, (step_tm, xconv_tm, in_tm, out_tm), decay_rate, False)[0]
    piece_decay = jnp.exp(decay_rate * jnp.sum(step_size, axis=1)[:, None, :])
    entering = entering_2(
        (piece_decay, local_end), "ctx", affine_join, (chain_unit, chain_zero), False
    )[1]
    scanned_tm, states_tm = forward_sweep(
        entering, (step_tm, xconv_tm, in_tm, out_tm), decay_rate, True
    )[1]
    scanned = seq_major(scanned_tm) + skip_weight * xconv
    z_silu = jax.nn.silu(z_gate).reshape(seq_count, seq_part, inner_width)
    gated_bf = (scanned * z_silu).astype(jnp.bfloat16).reshape(tokens, inner_width)
    mixer_output_rows = lax.psum(
        jnp.dot(gated_bf, output_projection, preferred_element_type=jnp.float32), "tp"
    )
    middle = values + mixer_output_rows
    normed_two, inverse_two = rms_forward(middle, gain_two_f)
    normed_two_bf = normed_two.astype(jnp.bfloat16)
    logits = jnp.dot(normed_two_bf, router, preferred_element_type=jnp.float32)
    router_prob = jax.nn.softmax(logits, axis=-1)
    onehot_int = (route_ids[:, None] == jnp.arange(experts, dtype=jnp.int32)[None, :]).astype(
        jnp.int32
    )
    onehot = onehot_int.astype(jnp.float32)
    keep_float = keep_ids.astype(jnp.float32)
    gate_prob = jnp.sum(router_prob * onehot, axis=1) * keep_float
    slot_rank = jnp.sum((jnp.cumsum(onehot_int, axis=0) - 1) * onehot_int, axis=1)
    token_slot = route_ids * capacity + slot_rank
    matches = token_slot[None, :] == jnp.arange(experts * capacity, dtype=jnp.int32)[:, None]
    filled = jnp.any(matches, axis=1)
    slot_ids = jnp.sum(jnp.where(matches, jnp.arange(tokens, dtype=jnp.int32)[None, :], 0), axis=1)
    picked = jnp.take(normed_two_bf, slot_ids, axis=0).reshape(experts, capacity, model_width)
    hidden = jnp.einsum("ecd,edf->ecf", picked, first_layer, preferred_element_type=jnp.float32)
    active_bf = jax.nn.gelu(hidden, approximate=False).astype(jnp.bfloat16)
    slot_out = jnp.einsum(
        "ecf,efd->ecd", active_bf, second_layer, preferred_element_type=jnp.float32
    )
    expert_part = jnp.take(slot_out.reshape(experts * capacity, model_width), token_slot, axis=0)
    expert_out = lax.psum(expert_part, "tp")
    result = (middle + gate_prob[:, None] * expert_out).astype(jnp.bfloat16)
    cotan = cotan_bf.reshape(tokens, model_width).astype(jnp.float32)
    gate_grad = jnp.sum(expert_out * cotan, axis=1)
    expert_grad_bf = (gate_prob[:, None] * cotan).astype(jnp.bfloat16)
    logit_grad = (gate_grad * gate_prob)[:, None] * (onehot - router_prob)
    router_grad = contract_rows(normed_two_bf.astype(jnp.float32), logit_grad, HIGHEST)
    slot_grad = jnp.where(
        filled[:, None], jnp.take(expert_grad_bf, slot_ids, axis=0), jnp.zeros((), jnp.bfloat16)
    ).reshape(experts, capacity, model_width)
    active_grad = jnp.einsum(
        "ecd,efd->ecf", slot_grad, second_layer, preferred_element_type=jnp.float32
    )
    second_grad = jnp.einsum(
        "ecf,ecd->efd", active_bf, slot_grad, preferred_element_type=jnp.float32
    )
    hidden_grad_bf = jax.vjp(partial(jax.nn.gelu, approximate=False), hidden)[1](active_grad)[
        0
    ].astype(jnp.bfloat16)
    first_grad = jnp.einsum(
        "ecd,ecf->edf", picked, hidden_grad_bf, preferred_element_type=jnp.float32
    )
    picked_grad = jnp.einsum(
        "ecf,edf->ecd", hidden_grad_bf, first_layer, preferred_element_type=jnp.float32
    )
    token_grad = lax.psum(
        jnp.take(picked_grad.reshape(experts * capacity, model_width), token_slot, axis=0), "tp"
    )
    normed_two_grad = token_grad + contract_cols(logit_grad, router.astype(jnp.float32), HIGHEST)
    middle_norm_grad, gain_two_grad = rms_backward(middle, inverse_two, gain_two_f, normed_two_grad)
    middle_grad = cotan + middle_norm_grad
    mixer_grad_bf = middle_grad.astype(jnp.bfloat16)
    out_proj_grad = contract_rows(gated_bf, mixer_grad_bf)
    gated_grad = contract_cols(mixer_grad_bf, output_projection).reshape(
        seq_count, seq_part, inner_width
    )
    scan_grad = gated_grad * z_silu
    z_grad = jax.vjp(jax.nn.silu, z_gate)[1]((gated_grad * scanned).reshape(tokens, inner_width))[0]
    grad_tm = time_major(scan_grad, turns)
    local_back = adjoint_end(chain_zero, (step_tm, out_tm, grad_tm), decay_rate)
    leaving = entering_2(
        (piece_decay, local_back), "ctx", affine_join, (chain_unit, chain_zero), True
    )[1]
    decay_zero = jnp.zeros((state_count, inner_width), jnp.float32)
    (ignored, decay_total), (in_sum_tm, step_term_tm, state_in_grad_tm, state_out_grad_tm) = (
        adjoint_sweep(
            (leaving, decay_zero),
            (step_tm, xconv_tm, in_tm, out_tm, grad_tm, states_tm),
            decay_rate,
        )
    )
    in_sum = seq_major(in_sum_tm)
    step_grad = seq_major(step_term_tm) + in_sum * xconv
    decay_log_grad = decay_total * decay_rate
    xconv_grad = in_sum * step_size + skip_weight * scan_grad
    state_in_grad = seq_major(state_in_grad_tm)
    state_out_grad = seq_major(state_out_grad_tm)
    skip_grad = jnp.sum(scan_grad * xconv, axis=(0, 1))
    pre_grad = (step_grad * jax.nn.sigmoid(dt_pre)).reshape(tokens, inner_width)
    dt_shift_grad = jnp.sum(pre_grad, axis=0)
    dt_proj_grad = contract_rows(dt_low.astype(jnp.float32), pre_grad, HIGHEST)
    dt_low_grad = contract_cols(pre_grad, dt_proj.astype(jnp.float32), HIGHEST)
    proj_part = jnp.concatenate(
        [
            dt_low_grad,
            state_in_grad.reshape(tokens, state_count),
            state_out_grad.reshape(tokens, state_count),
        ],
        axis=1,
    )
    proj_grad_bf = lax.psum(proj_part, "tp").astype(jnp.bfloat16)
    x_proj_grad = contract_rows(xconv_bf.reshape(tokens, inner_width), proj_grad_bf)
    xconv_grad = xconv_grad + contract_cols(proj_grad_bf, x_proj).reshape(
        seq_count, seq_part, inner_width
    )
    conv_grad = jax.vjp(jax.nn.silu, conv_pre)[1](xconv_grad)[0]
    taps_grad = jnp.stack(
        [
            jnp.sum(conv_grad * extended[:, tap_index : tap_index + seq_part], axis=(0, 1))
            for tap_index in range(tap_count)
        ]
    )
    shift_grad = jnp.sum(conv_grad, axis=(0, 1))
    ext_grad = jnp.zeros((seq_count, seq_part + tap_count - 1, inner_width), jnp.float32)
    for tap_index in range(tap_count):
        ext_grad = ext_grad + tap_weights[tap_index] * jnp.pad(
            conv_grad, ((0, 0), (tap_index, tap_count - 1 - tap_index), (0, 0))
        )
    edge_grad = passed_along(ext_grad[:, : tap_count - 1].astype(jnp.bfloat16), "ctx", -1).astype(
        jnp.float32
    )
    own_grad = ext_grad[:, tap_count - 1 :]
    x_pre_grad = jnp.concatenate(
        [
            own_grad[:, : seq_part - tap_count + 1],
            own_grad[:, seq_part - tap_count + 1 :] + edge_grad,
        ],
        axis=1,
    )
    mixed_grad_bf = jnp.concatenate(
        [x_pre_grad.reshape(tokens, inner_width), z_grad], axis=1
    ).astype(jnp.bfloat16)
    in_proj_grad = contract_rows(normed_bf, mixed_grad_bf).reshape(model_width, 2, inner_width)
    normed_grad = lax.psum(contract_cols(mixed_grad_bf, in_flat), "tp")
    values_norm_grad, gain_one_grad = rms_backward(values, inverse_one, gain_one_f, normed_grad)
    input_grad = (middle_grad + values_norm_grad).astype(jnp.bfloat16)
    grads = (
        gain_one_grad,
        in_proj_grad,
        taps_grad,
        shift_grad,
        x_proj_grad,
        dt_proj_grad,
        dt_shift_grad,
        decay_log_grad,
        skip_grad,
        out_proj_grad,
        gain_two_grad,
        router_grad,
        first_grad,
        second_grad,
    )
    return (
        result.reshape(seq_count, seq_part, model_width),
        input_grad.reshape(seq_count, seq_part, model_width),
        grads,
    )


def local(
    hidden_in,
    out_grad,
    norm1_gain,
    in_weight,
    conv_weight,
    conv_bias,
    xproj_weight,
    dt_weight,
    dt_bias,
    decay_log,
    skip_weight,
    out_weight,
    norm2_gain,
    router_weight,
    fc1_weight,
    fc2_weight,
    expert_ids,
    keep_mask,
):
    local_set = (
        norm1_gain,
        in_weight,
        conv_weight,
        conv_bias,
        xproj_weight,
        dt_weight,
        dt_bias,
        decay_log,
        skip_weight,
        out_weight,
        norm2_gain,
        router_weight,
        fc1_weight,
        fc2_weight,
    )
    batches = hidden_in.shape[0]
    tokens = hidden_in.shape[1] * hidden_in.shape[2]
    route_all = expert_ids.reshape(batches, tokens)
    keep_all = keep_mask.reshape(batches, tokens)
    results = []
    input_grads = []
    totals = tuple((jnp.zeros(weight.shape, jnp.float32) for weight in local_set))
    for batch_index in range(batches):
        weights = fetch_weights(local_set)
        result, input_grad, grads = micro_batch(
            hidden_in[batch_index],
            out_grad[batch_index],
            route_all[batch_index],
            keep_all[batch_index],
            weights,
        )
        results.append(result)
        input_grads.append(input_grad)
        shards = return_grads(grads)
        totals = tuple((total + shard for total, shard in zip(totals, shards)))
    totals = pieces_total(totals)
    output = jnp.stack(results)
    input_grad_all = jnp.stack(input_grads)
    return (
        output,
        input_grad_all,
        totals[0],
        totals[1],
        totals[2],
        totals[3],
        totals[4],
        totals[5],
        totals[6],
        totals[7],
        totals[8],
        totals[9],
        totals[10],
        totals[11],
        totals[12],
        totals[13],
    )


def solution(mesh):
    placed = (
        P(None, "dp", "ctx", None),
        P(None, "dp", "ctx", None),
        P("dp"),
        P("dp", None, "tp"),
        P(None, ("tp", "dp")),
        P(("tp", "dp")),
        P(("tp", "dp"), None),
        P(None, ("tp", "dp")),
        P(("tp", "dp")),
        P(None, ("tp", "dp")),
        P(("tp", "dp")),
        P("tp", "dp"),
        P("dp"),
        P("dp", None),
        P(None, "dp", "tp"),
        P(None, "tp", "dp"),
        P(("dp", "ctx"), None),
        P(("dp", "ctx")),
    )
    return jax.shard_map(
        local,
        mesh=mesh,
        in_specs=placed,
        out_specs=(
            P(None, "dp", "ctx", None),
            P(None, "dp", "ctx", None),
            P("dp"),
            P("dp", None, "tp"),
            P(None, ("tp", "dp")),
            P(("tp", "dp")),
            P(("tp", "dp"), None),
            P(None, ("tp", "dp")),
            P(("tp", "dp")),
            P(None, ("tp", "dp")),
            P(("tp", "dp")),
            P("tp", "dp"),
            P("dp"),
            P("dp", None),
            P(None, "dp", "tp"),
            P(None, "tp", "dp"),
        ),
        check_vma=False,
    )
```

profile of v0, /device:TPU:0, one launch (start us, length us, event | category | flops | bytes accessed | tf_op | source)
XLA Modules:
  0.0 6554.3 jit_solution(1834719215213257838)
XLA Ops:
  14.2 40.4 all-reduce.26
  54.6 26.7 all-gather.6
  81.4 31.9 all_gather.100
  140.7 30.8 all_gather.101
  171.5 31.4 all-gather.7
  227.8 137.3 %while.152 = (s32[]{:T(128)}, f32[1,16,1152]{2,1,0:T(8,128)}, f32[16,32,1,1152]{3,2,1,0:T(1,128)}, f32[16,1152]{1,0:T(8,128)S(1)}, f32[16,32,1,1152]{3,2,1,0:T(1...) while((s32[]{:T(128)}, f32[1,16,1152]{2,1,0:T(8,128)}, ...), condition=%wide.region_3.4_spmd.clone, body=%wide.region_2.3_spmd.clone.sunk | while | flops 2414626 | bytes 1555551 | solution.py:104
  385.1 185.3 %while.150 = (s32[]{:T(128)}, f32[1,16,1152]{2,1,0:T(8,128)S(1)}, f32[16,32,1,1152]{3,1,2,0:T(8,128)}, f32[16,32,1,16,1152]{4,3,1,2,0:T(8,128)}, f32[16,32,1,115...) while((s32[]{:T(128)}, f32[1,16,1152]{2,1,0:T(8,128)S(1)}, ...), condition=%wide.region_38.39_spmd, body=%wide.region_5.38_spmd.sunk | while | flops 5898272 | bytes 17515772 | solution.py:104
  581.4 114.2 %while.153 = (s32[]{:T(128)}, f32[1,16,1152]{2,1,0:T(8,128)S(1)}, f32[16,32,1,1152]{3,2,1,0:T(1,128)}, f32[16,1152]{1,0:T(8,128)S(1)}, f32[16,32,1,1152]{3,2,1,0...) while((s32[]{:T(128)}, f32[1,16,1152]{2,1,0:T(8,128)S(1)}, ...), condition=%wide.region_52.55_spmd.clone, body=%wide.region_51.54_spmd.clone.sunk | while | flops 2414626 | bytes 1555551 | solution.py:104
  715.2 185.1 %while.151 = (s32[]{:T(128)}, f32[1,16,1152]{2,1,0:T(8,128)S(1)}, f32[16,32,1,1152]{3,1,2,0:T(8,128)}, f32[16,32,1,16,1152]{4,3,1,2,0:T(8,128)}, f32[16,32,1,115...) while((s32[]{:T(128)}, f32[1,16,1152]{2,1,0:T(8,128)S(1)}, ...), condition=%wide.region_87.90_spmd, body=%wide.region_54.89_spmd.sunk | while | flops 5898272 | bytes 17515772 | solution.py:104
  917.6 30.8 all-gather.8
  990.9 493.3 %all-gather.18.cloned.1.call-done = bf16[8,1152,1536]{2,1,0:T(8,128)(2,1)} async-done(((bf16[8,144,1536]{2,1,0:T(8,128)(2,1)}), bf16[8,1152,1536]{2,1,0:T(8,128)(2,1)}) %all-gather.18.cloned.1.call-update) | async-done | bytes 28311568 | tf_op jit(solution)/shard_map/all_gather | solution.py:181
  1503.6 521.4 %all-gather.20.cloned.1.call-done = bf16[8,1536,1152]{1,2,0:T(8,128)(2,1)} async-done(((bf16[8,1536,144]{1,2,0:T(8,128)(2,1)}), bf16[8,1536,1152]{1,2,0:T(8,128)(2,1)}) %all-gather.20.cloned.1.call-update) | async-done | bytes 28311568 | tf_op jit(solution)/shard_map/all_gather | solution.py:182
  2025.0 23.8 add_convert_fusion
  2118.0 23.8 add_convert_fusion.1
  2199.7 41.0 all-reduce.37.cloned.1.call-done
  2265.5 97.2 %while.154 = (s32[]{:T(128)}, f32[1,16,1152]{2,1,0:T(8,128)S(1)}, f32[16,32,1,1152]{3,2,1,0:T(1,128)}, f32[16,1152]{1,0:T(8,128)S(1)}, f32[16,32,1,16]{3,2,1,0:T...) while((s32[]{:T(128)}, f32[1,16,1152]{2,1,0:T(8,128)S(1)}, ...), condition=%wide.region_103.106_spmd.clone, body=%wide.region_102.105_spmd.clone.sunk | while | flops 2377763 | bytes 1113143 | solution.py:118
  2371.2 605.3 %while.155 = (s32[]{:T(128)}, f32[1,16,1152]{2,1,0:T(8,128)S(1)}, f32[16,1152]{1,0:T(8,128)S(1)}, f32[16,32,1,1152]{3,1,2,0:T(8,128)}, f32[16,32,1,1152]{3,1,2,0...) while((s32[]{:T(128)}, f32[1,16,1152]{2,1,0:T(8,128)S(1)}, ...), condition=%wide.region_233.236_spmd.clone, body=%wide.region_104.235_spmd.clone.sunk | while | flops 14062627 | bytes 15263171 | solution.py:148
  2987.8 97.0 %while.156 = (s32[]{:T(128)}, f32[1,16,1152]{2,1,0:T(8,128)S(1)}, f32[16,32,1,1152]{3,2,1,0:T(1,128)}, f32[16,1152]{1,0:T(8,128)S(1)}, f32[16,32,1,16]{3,2,1,0:T...) while((s32[]{:T(128)}, f32[1,16,1152]{2,1,0:T(8,128)S(1)}, ...), condition=%wide.region_242.245_spmd.clone, body=%wide.region_241.244_spmd.clone.sunk | while | flops 2377763 | bytes 1113143 | solution.py:118
  3093.2 604.8 %while.157 = (s32[]{:T(128)}, f32[1,16,1152]{2,1,0:T(8,128)S(1)}, f32[16,1152]{1,0:T(8,128)S(1)}, f32[16,32,1,1152]{3,1,2,0:T(8,128)}, f32[16,32,1,1152]{3,1,2,0...) while((s32[]{:T(128)}, f32[1,16,1152]{2,1,0:T(8,128)S(1)}, ...), condition=%wide.region_372.375_spmd.clone, body=%wide.region_243.374_spmd.clone.sunk | while | flops 14062627 | bytes 15263171 | solution.py:148
  3801.5 39.6 convolution_add_fusion.1
  3866.0 40.4 convolution_add_fusion
  3939.3 55.4 reduce-scatter.18.cloned.1.call-done
  3994.7 886.4 %reduce-scatter.24.cloned.1.call-done = f32[8,144,1536]{2,1,0:T(8,128)} async-done(((f32[8,1152,1536]{2,1,0:T(8,128)}), f32[8,144,1536]{2,1,0:T(8,128)}) %reduce-scatter.24.cloned.1.call-update) | async-done | bytes 7077904 | tf_op jit(solution)/shard_map/reduce_scatter | solution.py:216
  4881.0 886.6 %reduce-scatter.26.cloned.1.call-done = f32[8,1536,144]{1,2,0:T(8,128)} async-done(((f32[8,1536,1152]{1,2,0:T(8,128)}), f32[8,1536,144]{1,2,0:T(8,128)}) %reduce-scatter.26.cloned.1.call-update) | async-done | bytes 7077904 | tf_op jit(solution)/shard_map/reduce_scatter | solution.py:217
  5774.0 58.9 reduce-scatter.28.cloned.1.call-done
  5834.5 62.9 reduce-scatter.34.cloned.1.call-done
  5898.9 63.2 reduce-scatter.32.cloned.1.call-done
  5963.7 62.7 reduce-scatter.30.cloned.1.call-done
  6027.9 30.4 all-reduce.35.cloned.1.call-done
  6061.9 37.9 all-reduce.18
  6127.8 365.9 %all-reduce.45.cloned.1.call-done = (f32[144,2,1152]{2,0,1:T(8,128)}, f32[1152,144]{0,1:T(8,128)}, f32[8,144,1536]{2,1,0:T(8,128)}, f32[8,1536,144]{1,2,0:T(8,128)}) async-done(((f32[144,2,1152]{2,0,1:T(8,128)}, f32[1152,144]{0,1:T(8,128)}, f32[8,144,1536]{2,1,0:T(8,128)}, f32[8,1536,144]{1,2,0:T(8,128)}), (f32[144,2,1152]{2,0,1:T(8,128)}, f32[1152,144]{0,1:T(8,128)}, f32[8,144,1536]{2,1,0:T(8,128)}, ...) | async-done | bytes 16146448 | tf_op jit(solution)/shard_map/psum | solution.py:238
  6496.8 26.4 all-reduce.43.cloned.1.call-done
  (11786 shorter events, 2576.3 us)
Async XLA Ops:
  7.2 108.5 %all-gather.14.cloned.1.call-start = ((), (), s32[]{:S(2)}) async-start(), calls=%async_computation.9 | async-start | bytes 5971968 | tf_op jit(solution)/shard_map/all_gather | solution.py:170
  7.9 201.7 %all-reduce.41.cloned.1.call-start = ((), (), s32[]{:S(2)}) async-start(), calls=%async_computation.25 | async-start | bytes 851968 | tf_op jit(solution)/shard_map/psum | solution.py:309
  122.9 8.1 collective-permute-start
  129.7 2.7 collective-permute-start.1
  137.1 763.1 %copy-start.12 = (bf16[1,512,1152]{2,1,0:T(8,128)(2,1)}, bf16[1,512,1152]{2,1,0:T(8,128)(2,1)S(1)}, u32[]{:S(2)}) copy-start(bf16[1,512,1152]{2,1,0:T(8,128)(2,1)S(1)} %get-tuple-element.2974) | copy-start | bytes 3538948
  137.1 763.1 %copy-start.15 = (bf16[1,512,1152]{2,1,0:T(8,128)(2,1)}, bf16[1,512,1152]{2,1,0:T(8,128)(2,1)S(1)}, u32[]{:S(2)}) copy-start(bf16[1,512,1152]{2,1,0:T(8,128)(2,1)S(1)} %get-tuple-element.3452) | copy-start | bytes 3538948
  139.8 766.2 %all-gather.16.cloned.1.call-start = ((), (), s32[]{:S(2)}) async-start(), calls=%async_computation.10 | async-start | bytes 2985984 | tf_op jit(solution)/shard_map/all_gather | solution.py:178
  140.5 814.2 %all-reduce.39.cloned.1.call-start = ((), (), s32[]{:S(2)}) async-start(), calls=%async_computation.24 | async-start | bytes 9437184 | tf_op jit(solution)/shard_map/psum | solution.py:340
  203.2 697.1 %copy-start.110 = (f32[1152]{0:T(1024)}, f32[1152]{0:T(1024)S(1)}, u32[]{:S(2)}) copy-start(f32[1152]{0:T(1024)S(1)} %convert_element_type.241) | copy-start | bytes 13828
  914.9 569.3 %all-gather.18.cloned.1.call-start = ((), (), s32[]{:S(2)}) async-start(), calls=%async_computation.11 | async-start | bytes 31850496 | tf_op jit(solution)/shard_map/all_gather | solution.py:181
  915.5 1109.5 %all-gather.20.cloned.1.call-start = ((), (), s32[]{:S(2)}) async-start(), calls=%async_computation.12 | async-start | bytes 31850496 | tf_op jit(solution)/shard_map/all_gather | solution.py:182
  916.1 1324.6 %all-reduce.37.cloned.1.call-start = ((), (), s32[]{:S(2)}) async-start(), calls=%async_computation.23 | async-start | bytes 18874368 | tf_op jit(solution)/shard_map/psum | solution.py:366
  1484.1 540.9 %copy-start.50 = (bf16[1024,1152]{1,0:T(8,128)(2,1)S(1)}, bf16[1024,1152]{1,0:T(8,128)(2,1)}, u32[]{:S(2)}) copy-start(bf16[1024,1152]{1,0:T(8,128)(2,1)} %get-tuple-element.3471) | copy-start | bytes 7077892
  2199.6 1739.7 %reduce-scatter.22.cloned.1.call-start = ((), (), s32[]{:S(2)}) async-start(), calls=%async_computation.15 | async-start | bytes 5971968 | tf_op jit(solution)/shard_map/reduce_scatter | solution.py:213
  2371.2 605.4 %copy-start.16 = (bf16[1,512,1152]{2,1,0:T(8,128)(2,1)S(1)}, bf16[1,512,1152]{2,1,0:T(8,128)(2,1)}, u32[]{:S(2)}) copy-start(bf16[1,512,1152]{2,1,0:T(8,128)(2,1)} %copy-done.15) | copy-start | bytes 3538948
  3705.8 288.9 %reduce-scatter.18.cloned.1.call-start = ((), (), s32[]{:S(2)}) async-start(), calls=%async_computation.13 | async-start | bytes 11943936 | tf_op jit(solution)/shard_map/reduce_scatter | solution.py:205
  3744.4 9.0 collective-permute-start.2
  3752.1 5.7 collective-permute-start.3
  3776.9 1104.1 %reduce-scatter.24.cloned.1.call-start = ((), (), s32[]{:S(2)}) async-start(), calls=%async_computation.16 | async-start | bytes 63700992 | tf_op jit(solution)/shard_map/reduce_scatter | solution.py:216
  3841.1 1926.5 %reduce-scatter.26.cloned.1.call-start = ((), (), s32[]{:S(2)}) async-start(), calls=%async_computation.17 | async-start | bytes 63700992 | tf_op jit(solution)/shard_map/reduce_scatter | solution.py:217
  3906.6 1926.3 %reduce-scatter.28.cloned.1.call-start = ((), (), s32[]{:S(2)}) async-start(), calls=%async_computation.18 | async-start | bytes 663552
  3909.0 1988.4 %reduce-scatter.34.cloned.1.call-start = ((), (), s32[]{:S(2)}) async-start(), calls=%async_computation.21 | async-start | bytes 663552
  3910.9 2051.2 %reduce-scatter.32.cloned.1.call-start = ((), (), s32[]{:S(2)}) async-start(), calls=%async_computation.20 | async-start | bytes 663552
  3915.6 2110.7 %reduce-scatter.30.cloned.1.call-start = ((), (), s32[]{:S(2)}) async-start(), calls=%async_computation.19 | async-start | bytes 663552
  3920.9 2137.5 %all-reduce.35.cloned.1.call-start = ((), (), s32[]{:S(2)}) async-start(), calls=%async_computation.22 | async-start | bytes 9437184 | tf_op jit(solution)/shard_map/psum | solution.py:469
  3936.1 2188.8 %reduce-scatter.20.cloned.1.call-start = ((), (), s32[]{:S(2)}) async-start(), calls=%async_computation.14 | async-start | bytes 663552 | tf_op jit(solution)/shard_map/reduce_scatter | solution.py:208
  3939.2 2554.5 %all-reduce.45.cloned.1.call-start = ((), (), s32[]{:S(2)}) async-start(), calls=%async_computation.27 | async-start | bytes 32292864 | tf_op jit(solution)/shard_map/psum | solution.py:238
  5767.7 755.5 %all-reduce.43.cloned.1.call-start = ((), (), s32[]{:S(2)}) async-start(), calls=%async_computation.26 | async-start | bytes 362496 | tf_op jit(solution)/shard_map/psum | solution.py:238
  5770.9 287.4 %copy-start.21 = (bf16[2,1,512,1152]{3,2,1,0:T(8,128)(2,1)S(1)}, bf16[2,1,512,1152]{3,2,1,0:T(8,128)(2,1)}, u32[]{:S(2)}) copy-start(bf16[2,1,512,1152]{3,2,1,0:T(8,128)(2,1)} %param.38) | copy-start | bytes 7077892
  5770.9 287.4 %copy-start.109 = (f32[1152]{0:T(1024)S(1)}, f32[1152]{0:T(1024)}, u32[]{:S(2)}) copy-start(f32[1152]{0:T(1024)} %copy-done.107) | copy-start | bytes 13828
  5770.9 287.4 %copy-start.134 = (f32[512]{0:T(512)S(1)}, f32[512]{0:T(512)}, u32[]{:S(2)}) copy-start(f32[512]{0:T(512)} %copy-done.132) | copy-start | bytes 6148
  5771.0 287.4 %copy-start.161 = (f32[512]{0:T(512)S(1)}, f32[512]{0:T(512)}, u32[]{:S(2)}) copy-start(f32[512]{0:T(512)} %copy-done.159) | copy-start | bytes 6148
  (183 other events, 1774.2 us)
Sparse Core Ops, SparseCore 0:
  10.2 93.5 all-gather.13
  139.9 16.6 all-reduce.40
  158.8 56.5 all-gather.15
  915.0 26.9 all-reduce.38
  943.5 540.6 all-gather.17
  1485.6 539.3 all-gather.19
  2199.7 40.9 all-reduce.36
  3705.9 105.3 reduce-scatter.21
  3814.9 179.7 reduce-scatter.17
  3998.9 882.0 reduce-scatter.23
  4885.0 882.6 reduce-scatter.25
  5771.7 61.2 reduce-scatter.27
  5836.3 61.0 reduce-scatter.33
  5900.9 61.1 reduce-scatter.31
  5965.2 61.0 reduce-scatter.29
  6030.1 28.2 all-reduce.34
  6061.5 63.2 reduce-scatter.19
  6127.6 366.0 all-reduce.44
  6497.7 25.4 all-reduce.42
where the time goes:
time: 6620 us; the launch traced here: 6550 us
  waiting for transfers between devices  3570 us (54%)
  local copies, waits for them, and re-layouts  1140 us (17%)
  other arithmetic  1120 us (17%)
  matrix products  376 us (6%)
  blocking collectives  266 us (4%)
    reduce_scatter x1, waiting for transfers between devices, return_grads(): lax.psum_scatter(second_layer, 'dp', scatter_dimension=2, tiled=True)  887 us
    reduce_scatter x1, waiting for transfers between devices, return_grads(): lax.psum_scatter(first_layer, 'dp', scatter_dimension=1, tiled=True)  886 us
    reduce_sum x480, other arithmetic, block_step(): jnp.sum(decay_grad * decay_rate, axis=1)  609 us
    all_gather x1, waiting for transfers between devices, fetch_weights(): lax.all_gather(second_layer, 'dp', axis=2, tiled=True)  521 us
    all_gather x1, waiting for transfers between devices, fetch_weights(): lax.all_gather(first_layer, 'dp', axis=1, tiled=True)  493 us
    psum x2, waiting for transfers between devices, pieces_total(): lax.psum((gain_one, input_projection, conv_taps, conv_shift, x_proj, dt_p...  392 us
    unnamed x23, waiting for transfers between devices  250 us
    slice x128, local copies, waits for them, and re-layouts, block_step(): incoming = jnp.exp(step_block[position][:, None, :] * decay_rate) * adjoint  150 us

commit v1 on v0

v1 whole, which is shorter than its diff:
```python
from functools import partial
import math

import jax
import jax.numpy as jnp
from jax import lax
from jax.experimental import pallas as pl
from jax.experimental.pallas import tpu as pltpu
from jax.sharding import PartitionSpec as P

EPSILON = 1e-05
HIGHEST = lax.Precision.HIGHEST
SEGMENTS = 8
LANES = 128
VMEM_LIMIT = 56 * 1024 * 1024
LOG2E = math.log2(math.e)
BF16 = jnp.bfloat16
F32 = jnp.float32


def swapped(value, axis):
    return lax.ppermute(value, axis, [(0, 1), (1, 0)])


def passed_along(value, axis, steps):
    count = lax.axis_size(axis)
    leading, last = (max(0, -steps), min(count, count - steps))
    return lax.ppermute(value, axis, [(source, source + steps) for source in range(leading, last)])


def axis_sum(value, axis):
    if lax.axis_size(axis) == 2:
        return value + swapped(value, axis)
    return lax.psum(value, axis)


def entering_pieces(decay, value, axis, backward):
    count = lax.axis_size(axis)
    if count == 2:
        return passed_along(value, axis, -1 if backward else 1)
    mine = lax.axis_index(axis)
    decays = lax.all_gather(decay, axis)
    values = lax.all_gather(value, axis)
    running = jnp.zeros_like(value)
    for position in range(count - 1):
        at = count - 1 - position if backward else position
        longer = values[at] + decays[at] * running
        ahead = at > mine if backward else at < mine
        running = jnp.where(ahead, longer, running)
    return running


def contract_rows(left_side, right_side, precision=None):
    return lax.dot_general(
        left_side,
        right_side,
        (((0,), (0,)), ((), ())),
        precision=precision,
        preferred_element_type=F32,
    )


def contract_cols(left_side, right_side, precision=None):
    return lax.dot_general(
        left_side,
        right_side,
        (((1,), (1,)), ((), ())),
        precision=precision,
        preferred_element_type=F32,
    )


def rms_forward(values, gain_vec):
    inverse = lax.rsqrt(jnp.mean(values * values, axis=-1, keepdims=True) + EPSILON)
    return (values * inverse * gain_vec, inverse)


def rms_backward(values, inverse, gain_vec, grad_out):
    weighted = grad_out * gain_vec
    inner_mean = jnp.mean(values * weighted, axis=-1, keepdims=True)
    grad_values = inverse * weighted - values * inverse * inverse * inverse * inner_mean
    grad_gain = jnp.sum(grad_out * values * inverse, axis=0)
    return (grad_values, grad_gain)


def sublane_rows():
    return lax.broadcasted_iota(jnp.int32, (SEGMENTS, LANES), 0)


def joined_forward(decay, value, row):
    for reach in (1, 2, 4):
        inside = row >= reach
        value = value + jnp.where(inside, decay * pltpu.roll(value, reach, 0), 0.0)
        decay = jnp.where(inside, decay * pltpu.roll(decay, reach, 0), decay)
    return decay, value


def joined_backward(decay, value, row):
    for reach in (1, 2, 4):
        inside = row < SEGMENTS - reach
        value = value + jnp.where(inside, decay * pltpu.roll(value, SEGMENTS - reach, 0), 0.0)
        decay = jnp.where(inside, decay * pltpu.roll(decay, SEGMENTS - reach, 0), decay)
    return decay, value


def ends_kernel(step_ref, input_ref, mix_in_ref, rate_ref, decay_ref, state_ref, last_ref):
    steps, states = step_ref.shape[0], mix_in_ref.shape[1]
    zero = jnp.zeros((SEGMENTS, LANES), F32)

    def body(at, carry):
        held, total = carry
        step = step_ref[at]
        driven = step * input_ref[at]
        held = tuple(
            jnp.exp2(step * rate_ref[n]) * held[n] + mix_in_ref[at, n] * driven
            for n in range(states)
        )
        return held, total + step

    held, total = lax.fori_loop(0, steps, body, ((zero,) * states, zero))
    row = sublane_rows()
    for n in range(states):
        decay, value = joined_forward(jnp.exp2(total * rate_ref[n]), held[n], row)
        decay_ref[n] = decay
        state_ref[n] = value
        last_ref[n : n + 1] = value[SEGMENTS - 1 :]


def states_kernel(
    step_ref, input_ref, mix_in_ref, mix_out_ref, rate_ref, decay_ref, state_ref, enter_ref,
    out_ref, start_ref,
):
    steps, states = step_ref.shape[0], mix_in_ref.shape[1]
    row = sublane_rows()
    held = []
    for n in range(states):
        first = jnp.broadcast_to(enter_ref[n : n + 1], (SEGMENTS, LANES))
        inner = pltpu.roll(state_ref[n], 1, 0) + pltpu.roll(decay_ref[n], 1, 0) * first
        start = jnp.where(row >= 1, inner, first)
        start_ref[n] = start
        held.append(start)

    def body(at, held):
        step = step_ref[at]
        driven = step * input_ref[at]
        held = tuple(
            jnp.exp2(step * rate_ref[n]) * held[n] + mix_in_ref[at, n] * driven
            for n in range(states)
        )
        parts = [mix_out_ref[at, n] * held[n] for n in range(states)]
        while len(parts) > 1:
            parts = [parts[i] + parts[i + 1] for i in range(0, len(parts), 2)]
        out_ref[at] = parts[0]
        return held

    lax.fori_loop(0, steps, body, tuple(held))


def adjoint_ends_kernel(step_ref, mix_out_ref, grad_ref, rate_ref, decay_ref, adjoint_ref, first_ref):
    steps, states = step_ref.shape[0], mix_out_ref.shape[1]
    zero = jnp.zeros((SEGMENTS, LANES), F32)

    def body(back, carry):
        at = steps - 1 - back
        incoming, total = carry
        step = step_ref[at]
        grad = grad_ref[at]
        incoming = tuple(
            jnp.exp2(step * rate_ref[n]) * (mix_out_ref[at, n] * grad + incoming[n])
            for n in range(states)
        )
        return incoming, total + step

    incoming, total = lax.fori_loop(0, steps, body, ((zero,) * states, zero))
    row = sublane_rows()
    for n in range(states):
        decay, value = joined_backward(jnp.exp2(total * rate_ref[n]), incoming[n], row)
        decay_ref[n] = decay
        adjoint_ref[n] = value
        first_ref[n : n + 1] = value[:1]


def adjoint_kernel(
    step_ref, input_ref, mix_in_ref, mix_out_ref, grad_ref, rate_ref, start_ref, decay_ref, adjoint_ref,
    enter_ref,
    in_sum_ref, rate_sum_ref, decay_sum_ref, in_grad_ref, out_grad_ref, states_ref,
):
    steps, states = step_ref.shape[0], mix_in_ref.shape[1]
    row = sublane_rows()
    zero = jnp.zeros((SEGMENTS, LANES), F32)

    @pl.when(pl.program_id(1) == 0)
    def clear():
        in_grad_ref[...] = jnp.zeros_like(in_grad_ref)
        out_grad_ref[...] = jnp.zeros_like(out_grad_ref)

    for n in range(states):
        states_ref[0, n] = start_ref[n]

    def ahead(at, held):
        step = step_ref[at]
        driven = step * input_ref[at]
        held = tuple(
            jnp.exp2(step * rate_ref[n]) * held[n] + mix_in_ref[at, n] * driven
            for n in range(states)
        )
        for n in range(states):
            states_ref[at + 1, n] = held[n]
        return held

    lax.fori_loop(0, steps, ahead, tuple(start_ref[n] for n in range(states)))

    incoming = []
    for n in range(states):
        final = jnp.broadcast_to(enter_ref[n : n + 1], (SEGMENTS, LANES))
        inner = (
            pltpu.roll(adjoint_ref[n], SEGMENTS - 1, 0)
            + pltpu.roll(decay_ref[n], SEGMENTS - 1, 0) * final
        )
        incoming.append(jnp.where(row < SEGMENTS - 1, inner, final))

    def body(back, carry):
        at = steps - 1 - back
        incoming, decay_sums = carry
        step = step_ref[at]
        grad = grad_ref[at]
        driven = step * input_ref[at]
        in_sum, rate_sum = zero, zero
        following, sums = [], []
        for n in range(states):
            rate = rate_ref[n]
            adjoint = mix_out_ref[at, n] * grad + incoming[n]
            onward = jnp.exp2(step * rate) * adjoint
            decay_grad = onward * states_ref[at, n]
            in_sum = in_sum + adjoint * mix_in_ref[at, n]
            rate_sum = rate_sum + decay_grad * rate
            sums.append(decay_sums[n] + decay_grad * step)
            in_grad_ref[at, n] += adjoint * driven
            out_grad_ref[at, n] += grad * states_ref[at + 1, n]
            following.append(onward)
        in_sum_ref[at] = in_sum
        rate_sum_ref[at] = rate_sum
        return tuple(following), tuple(sums)

    _, sums = lax.fori_loop(0, steps, body, (tuple(incoming), (zero,) * states))
    for n in range(states):
        decay_sum_ref[n : n + 1] = jnp.sum(sums[n], axis=0, keepdims=True)


class Scan:
    def __init__(self, steps, chains, states, width):
        self.grid = (chains, width // LANES)
        self.rows_spec = pl.BlockSpec(
            (steps, None, SEGMENTS, LANES), lambda chain, block: (0, chain, 0, block)
        )
        self.mix_spec = pl.BlockSpec(
            (None, steps, states, SEGMENTS, LANES), lambda chain, block: (chain, 0, 0, 0, 0)
        )
        self.rate_spec = pl.BlockSpec((states, SEGMENTS, LANES), lambda chain, block: (0, 0, block))
        self.state_spec = pl.BlockSpec(
            (None, states, SEGMENTS, LANES), lambda chain, block: (chain, 0, 0, block)
        )
        self.edge_spec = pl.BlockSpec((None, states, LANES), lambda chain, block: (chain, 0, block))
        self.rows = jax.ShapeDtypeStruct((steps, chains, SEGMENTS, width), F32)
        self.mix = jax.ShapeDtypeStruct((chains, steps, states, SEGMENTS, LANES), F32)
        self.state = jax.ShapeDtypeStruct((chains, states, SEGMENTS, width), F32)
        self.edge = jax.ShapeDtypeStruct((chains, states, width), F32)
        self.scratch = pltpu.VMEM((steps + 1, states, SEGMENTS, LANES), F32)
        self.work = steps * chains * SEGMENTS * width * states

    def call(self, kernel, ops, args, in_specs, outs, out_specs, scratch=()):
        size = sum(math.prod(a.shape) * a.dtype.itemsize for a in (*args, *outs))
        return pl.pallas_call(
            kernel,
            grid=self.grid,
            in_specs=in_specs,
            out_specs=out_specs,
            out_shape=outs,
            scratch_shapes=list(scratch),
            compiler_params=pltpu.CompilerParams(vmem_limit_bytes=VMEM_LIMIT),
            cost_estimate=pl.CostEstimate(
                flops=ops * self.work, transcendentals=self.work, bytes_accessed=size
            ),
        )(*args)

    def ends(self, step, inputs, mix_in, rate):
        return self.call(
            ends_kernel, 5, (step, inputs, mix_in, rate),
            [self.rows_spec, self.rows_spec, self.mix_spec, self.rate_spec],
            [self.state, self.state, self.edge],
            [self.state_spec, self.state_spec, self.edge_spec],
        )

    def run(self, step, inputs, mix_in, mix_out, rate, decay, state, enter):
        return self.call(
            states_kernel, 7, (step, inputs, mix_in, mix_out, rate, decay, state, enter),
            [self.rows_spec, self.rows_spec, self.mix_spec, self.mix_spec, self.rate_spec,
             self.state_spec, self.state_spec, self.edge_spec],
            [self.rows, self.state],
            [self.rows_spec, self.state_spec],
        )

    def adjoint_ends(self, step, mix_out, grad, rate):
        return self.call(
            adjoint_ends_kernel, 5, (step, mix_out, grad, rate),
            [self.rows_spec, self.mix_spec, self.rows_spec, self.rate_spec],
            [self.state, self.state, self.edge],
            [self.state_spec, self.state_spec, self.edge_spec],
        )

    def adjoint(self, step, inputs, mix_in, mix_out, grad, rate, start, decay, adjoint, enter):
        return self.call(
            adjoint_kernel, 20,
            (step, inputs, mix_in, mix_out, grad, rate, start, decay, adjoint, enter),
            [self.rows_spec, self.rows_spec, self.mix_spec, self.mix_spec, self.rows_spec,
             self.rate_spec, self.state_spec, self.state_spec, self.state_spec, self.edge_spec],
            [self.rows, self.rows, self.edge, self.mix, self.mix],
            [self.rows_spec, self.rows_spec, self.edge_spec, self.mix_spec, self.mix_spec],
            [self.scratch],
        )


def expert_exchange(value, experts):
    count = lax.axis_size("dp")
    groups = None
    if count != experts:
        groups = [
            [base + e for e in range(experts)] for base in range(0, count, experts)
        ]
    return lax.all_to_all(value, "dp", 0, 0, axis_index_groups=groups, tiled=True)


def own_expert(shards):
    experts, rows, columns = shards.shape
    count = lax.axis_size("dp")
    if count != experts:
        shards = jnp.concatenate([shards] * (count // experts), axis=0)
    return lax.all_to_all(shards, "dp", 0, 0, tiled=True).reshape(count * rows, columns)


def halves_sum(value, axis):
    count = lax.axis_size("ctx")
    if count != 2:
        return lax.psum_scatter(value, "ctx", scatter_dimension=axis, tiled=True)
    mine = lax.axis_index("ctx")
    part = value.shape[axis] // 2
    own = lax.dynamic_slice_in_dim(value, mine * part, part, axis)
    other = lax.dynamic_slice_in_dim(value, (1 - mine) * part, part, axis)
    return own + swapped(other.astype(BF16), "ctx").astype(F32)


def halves_joined(value, axis):
    count = lax.axis_size("ctx")
    if count != 2:
        return lax.all_gather(value, "ctx", axis=axis, tiled=True)
    other = swapped(value, "ctx")
    first = lax.axis_index("ctx") == 0
    return jnp.concatenate(
        [jnp.where(first, value, other), jnp.where(first, other, value)], axis=axis
    )


def expert_weight_grad(grad, experts):
    count = lax.axis_size("dp")
    part = halves_sum(grad, 1)
    blocks = part.astype(BF16).reshape(count, part.shape[0] // count, part.shape[1])
    blocks = lax.all_to_all(blocks, "dp", 0, 0, tiled=True)
    if count != experts:
        blocks = jnp.sum(
            blocks.reshape(count // experts, experts, *blocks.shape[1:]).astype(F32), axis=0
        ).astype(BF16)
    return halves_joined(blocks, 2).astype(F32)


def weight_grad(grad, axis):
    count = lax.axis_size("dp")
    blocks = grad.reshape(count, grad.shape[0] // count, grad.shape[1])
    part = halves_sum(blocks, axis)
    part = lax.all_to_all(part.astype(BF16), "dp", 0, 0, tiled=True)
    return halves_joined(jnp.sum(part.astype(F32), axis=0), axis - 1)


def local(
    hidden_in,
    out_grad,
    norm1_gain,
    in_weight,
    conv_weight,
    conv_bias,
    xproj_weight,
    dt_weight,
    dt_bias,
    decay_log,
    skip_weight,
    out_weight,
    norm2_gain,
    router_weight,
    fc1_weight,
    fc2_weight,
    expert_ids,
    keep_mask,
):
    batches, seqs, length, model_width = hidden_in.shape
    chains = batches * seqs
    tokens = chains * length
    steps = length // SEGMENTS
    shard, _, inner = in_weight.shape
    taps = conv_weight.shape[0]
    low_rank = dt_weight.shape[0]
    states = decay_log.shape[0]
    experts = fc1_weight.shape[0]
    dp_count = lax.axis_size("dp")
    tp_count = lax.axis_size("tp")
    capacity = tokens // 4
    part_cap = capacity // tp_count
    slots = experts * part_cap
    tp_index = lax.axis_index("tp")
    scan = Scan(steps, chains, states, inner)

    def to_rows(value):
        value = value.reshape(chains, SEGMENTS, steps, -1).transpose(2, 0, 1, 3)
        return value.reshape(tokens, -1)

    def from_rows(value):
        value = value.reshape(steps, chains, SEGMENTS, -1).transpose(1, 2, 0, 3)
        return value.reshape(batches, seqs, length, -1)

    small = jnp.concatenate(
        [
            norm1_gain[None],
            conv_weight,
            conv_bias[None],
            dt_weight,
            dt_bias[None],
            decay_log,
            skip_weight[None],
            norm2_gain[None],
            router_weight.T,
            xproj_weight.T,
        ],
        axis=0,
    )
    small_all = lax.all_gather(small, "dp", axis=0)
    small_all = small_all.transpose(1, 0, 2).reshape(small.shape[0], dp_count * shard)
    in_flat = lax.all_gather(
        in_weight.reshape(shard, 2 * inner), "dp", axis=0, tiled=True
    )
    bounds = [0]
    for count in (1, taps, 1, low_rank, 1, states, 1, 1, experts, low_rank + 2 * states):
        bounds.append(bounds[-1] + count)
    pieces = [small_all[bounds[i] : bounds[i + 1]] for i in range(len(bounds) - 1)]
    gain_one_f = pieces[0].astype(F32)
    tap_weights = pieces[1].astype(F32)
    conv_shift = pieces[2].astype(F32)
    dt_proj = pieces[3]
    dt_shift = pieces[4].astype(F32)
    decay_rate = -jnp.exp(pieces[5].astype(F32))
    skip_row = pieces[6].astype(F32)
    gain_two_f = pieces[7].astype(F32)
    router_t = pieces[8]
    x_proj_t = pieces[9]
    rate_rows = jnp.broadcast_to((decay_rate * LOG2E)[:, None, :], (states, SEGMENTS, inner))
    out_proj_t = lax.all_gather(out_weight.T, "dp", axis=0, tiled=True)
    first_layer = own_expert(fc1_weight)
    second_layer_t = own_expert(fc2_weight.transpose(0, 2, 1))

    route = to_rows(expert_ids)[:, 0]
    keep = to_rows(keep_mask)[:, 0].astype(F32)
    onehot_int = (route[:, None] == jnp.arange(experts, dtype=jnp.int32)[None, :]).astype(jnp.int32)
    rank = jnp.sum((jnp.cumsum(onehot_int, axis=0) - 1) * onehot_int, axis=1) - tp_index * part_cap
    here = (rank >= 0) & (rank < part_cap)
    token_slot = jnp.where(here, route * part_cap + rank, -1)
    place = (
        token_slot[None, :] == jnp.arange(slots, dtype=jnp.int32)[:, None]
    ).astype(BF16)

    def dispatched(value):
        sent = jnp.dot(place, value, preferred_element_type=F32).astype(BF16)
        got = expert_exchange(sent.reshape(experts, part_cap, -1), experts)
        return got.reshape(slots, -1)

    def returned(value):
        got = expert_exchange(value.reshape(experts, part_cap, -1), experts)
        return axis_sum(contract_rows(place, got.reshape(slots, -1)).astype(BF16), "tp")

    cotan_bf = to_rows(out_grad)
    cotan = cotan_bf.astype(F32)
    slot_cotan = dispatched((cotan * keep[:, None]).astype(BF16))

    values = to_rows(hidden_in).astype(F32)
    normalized_rows, inverse_one = rms_forward(values, gain_one_f)
    normed_bf = normalized_rows.astype(BF16)
    mixed = jnp.dot(normed_bf, in_flat, preferred_element_type=F32)
    x_pre = mixed[:, :inner].astype(BF16).reshape(steps, chains, SEGMENTS, inner)
    z_gate = mixed[:, inner:].reshape(steps, chains, SEGMENTS, inner)
    tail = x_pre[steps - taps + 1 :]
    edge_in = passed_along(tail[:, :, SEGMENTS - 1 :], "ctx", 1)
    halo = jnp.concatenate([edge_in, tail[:, :, : SEGMENTS - 1]], axis=2)
    extended = jnp.concatenate([halo, x_pre], axis=0).astype(F32)
    conv_pre = jnp.broadcast_to(conv_shift[0], x_pre.shape)
    for tap in range(taps):
        conv_pre = conv_pre + tap_weights[tap] * extended[tap : tap + steps]
    xconv_bf = jax.nn.silu(conv_pre).astype(BF16)
    xconv = xconv_bf.astype(F32)
    xconv_rows = xconv_bf.reshape(tokens, inner)
    projected = axis_sum(contract_cols(xconv_rows, x_proj_t), "tp")
    dt_low = projected[:, :low_rank].astype(BF16)

    def mixes(value):
        value = value.reshape(steps, chains, SEGMENTS, states).transpose(1, 0, 3, 2)
        return jnp.broadcast_to(value[..., None], (*value.shape, LANES))

    mix_in = mixes(projected[:, low_rank : low_rank + states])
    mix_out = mixes(projected[:, low_rank + states :])
    dt_pre = (jnp.dot(dt_low, dt_proj, preferred_element_type=F32) + dt_shift).reshape(x_pre.shape)
    step_size = jax.nn.softplus(dt_pre)
    seg_decay, seg_state, last_state = scan.ends(step_size, xconv, mix_in, rate_rows)
    entering = entering_pieces(seg_decay[:, :, SEGMENTS - 1], last_state, "ctx", False)
    scan_out, seg_start = scan.run(
        step_size, xconv, mix_in, mix_out, rate_rows, seg_decay, seg_state, entering
    )
    scanned = scan_out + skip_row[0] * xconv
    z_silu = jax.nn.silu(z_gate)
    gated_bf = (scanned * z_silu).astype(BF16).reshape(tokens, inner)
    middle = values + axis_sum(contract_cols(gated_bf, out_proj_t), "tp")

    normed_two, inverse_two = rms_forward(middle, gain_two_f)
    normed_two_bf = normed_two.astype(BF16)
    own_rows = dispatched(normed_two_bf)
    slot_rows = jnp.concatenate([own_rows, swapped(own_rows, "tp")], axis=0)
    slot_cotan_all = jnp.concatenate([slot_cotan, swapped(slot_cotan, "tp")], axis=0)
    expert_mask = (
        jnp.arange(experts, dtype=jnp.int32) == lax.rem(lax.axis_index("dp"), experts)
    ).astype(F32)[None, :]
    slot_prob = jax.nn.softmax(contract_cols(slot_rows, router_t), axis=-1)
    slot_gate = jnp.sum(slot_prob * expert_mask, axis=1, keepdims=True)
    slot_grad = (slot_gate * slot_cotan_all.astype(F32)).astype(BF16)
    hidden = jnp.dot(slot_rows, first_layer, preferred_element_type=F32)
    active_bf = jax.nn.gelu(hidden, approximate=False).astype(BF16)
    active_grad = jnp.dot(slot_grad, second_layer_t, preferred_element_type=F32)
    hidden_grad_bf = jax.vjp(partial(jax.nn.gelu, approximate=False), hidden)[1](active_grad)[
        0
    ].astype(BF16)

    def own_half(value):
        return value[:slots] + swapped(value[slots:], "tp")

    slot_out = own_half(contract_cols(active_bf, second_layer_t))
    picked_grad = own_half(contract_cols(hidden_grad_bf, first_layer))
    gate_grad = jnp.sum(slot_out * slot_cotan.astype(F32), axis=1, keepdims=True)
    logit_grad = gate_grad * slot_gate[:slots] * (expert_mask - slot_prob[:slots])
    router_grad_t = axis_sum(contract_rows(logit_grad, own_rows.astype(F32), HIGHEST), "tp")
    picked_grad = picked_grad + jnp.dot(
        logit_grad, router_t.astype(F32), precision=HIGHEST, preferred_element_type=F32
    )
    normed_two_grad = returned(picked_grad.astype(BF16)).astype(F32)
    expert_out = returned(slot_out.astype(BF16)).astype(F32)
    first_grad = expert_weight_grad(contract_rows(slot_rows, hidden_grad_bf), experts)
    second_grad = expert_weight_grad(contract_rows(slot_grad, active_bf), experts)
    router_prob = jax.nn.softmax(contract_cols(normed_two_bf, router_t), axis=-1)
    gate_prob = jnp.sum(router_prob * onehot_int.astype(F32), axis=1) * keep
    result = from_rows((middle + gate_prob[:, None] * expert_out).astype(BF16))

    middle_norm_grad, gain_two_grad = rms_backward(middle, inverse_two, gain_two_f, normed_two_grad)
    middle_grad = cotan + middle_norm_grad
    mixer_grad_bf = middle_grad.astype(BF16)
    out_proj_grad = weight_grad(contract_rows(mixer_grad_bf, gated_bf), 1)
    gated_grad = jnp.dot(mixer_grad_bf, out_proj_t, preferred_element_type=F32).reshape(x_pre.shape)
    scan_grad = gated_grad * z_silu
    z_grad = jax.vjp(jax.nn.silu, z_gate)[1](gated_grad * scanned)[0]
    back_decay, back_adjoint, first_adjoint = scan.adjoint_ends(
        step_size, mix_out, scan_grad, rate_rows
    )
    leaving = entering_pieces(back_decay[:, :, 0], first_adjoint, "ctx", True)
    in_sum, rate_sum, decay_sum, in_lanes, out_lanes = scan.adjoint(
        step_size, xconv, mix_in, mix_out, scan_grad, rate_rows, seg_start, back_decay, back_adjoint,
        leaving,
    )
    step_grad = rate_sum * (1.0 / LOG2E) + in_sum * xconv
    decay_log_grad = jnp.sum(decay_sum, axis=0) * decay_rate
    xconv_grad = in_sum * step_size + skip_row[0] * scan_grad

    def unmixed(value):
        return jnp.sum(value, axis=-1).transpose(1, 0, 3, 2).reshape(tokens, states)

    skip_grad = jnp.sum(scan_grad * xconv, axis=(0, 1, 2))
    pre_grad = (step_grad * jax.nn.sigmoid(dt_pre)).reshape(tokens, inner)
    dt_shift_grad = jnp.sum(pre_grad, axis=0)
    dt_proj_grad = contract_rows(dt_low.astype(F32), pre_grad, HIGHEST)
    dt_low_grad = contract_cols(pre_grad, dt_proj.astype(F32), HIGHEST)
    proj_part = jnp.concatenate([dt_low_grad, unmixed(in_lanes), unmixed(out_lanes)], axis=1)
    proj_grad_bf = axis_sum(proj_part, "tp").astype(BF16)
    x_proj_grad_t = contract_rows(proj_grad_bf, xconv_rows)
    xconv_grad = xconv_grad + jnp.dot(
        proj_grad_bf, x_proj_t, preferred_element_type=F32
    ).reshape(x_pre.shape)
    conv_grad = jax.vjp(jax.nn.silu, conv_pre)[1](xconv_grad)[0]
    taps_grad = jnp.stack(
        [
            jnp.sum(conv_grad * extended[tap : tap + steps], axis=(0, 1, 2))
            for tap in range(taps)
        ]
    )
    shift_grad = jnp.sum(conv_grad, axis=(0, 1, 2))
    head = conv_grad[: taps - 1]
    edge_back = passed_along(head[:, :, :1], "ctx", -1)
    later = jnp.concatenate([head[:, :, 1:], edge_back], axis=2)
    reaching = jnp.concatenate([conv_grad, later], axis=0)
    x_pre_grad = tap_weights[taps - 1] * conv_grad
    for tap in range(taps - 1):
        ahead = taps - 1 - tap
        x_pre_grad = x_pre_grad + tap_weights[tap] * reaching[ahead : ahead + steps]
    mixed_grad_bf = jnp.concatenate(
        [
            x_pre_grad.astype(BF16).reshape(tokens, inner),
            z_grad.astype(BF16).reshape(tokens, inner),
        ],
        axis=1,
    )
    in_proj_grad = weight_grad(contract_rows(normed_bf, mixed_grad_bf), 2)
    normed_grad = axis_sum(contract_cols(mixed_grad_bf, in_flat), "tp")
    values_norm_grad, gain_one_grad = rms_backward(values, inverse_one, gain_one_f, normed_grad)
    input_grad = from_rows((middle_grad + values_norm_grad).astype(BF16))

    small_grads = jnp.concatenate(
        [
            gain_one_grad[None],
            taps_grad,
            shift_grad[None],
            dt_proj_grad,
            dt_shift_grad[None],
            decay_log_grad,
            skip_grad[None],
            gain_two_grad[None],
            router_grad_t,
            x_proj_grad_t,
        ],
        axis=0,
    )
    small_grads = small_grads.reshape(small.shape[0], dp_count, shard).transpose(1, 0, 2)
    small_grads = lax.psum_scatter(small_grads, "dp", scatter_dimension=0, tiled=True)[0]
    small_grads = axis_sum(small_grads, "ctx")
    sums = [small_grads[bounds[i] : bounds[i + 1]] for i in range(len(bounds) - 1)]
    return (
        result,
        input_grad,
        sums[0][0],
        in_proj_grad.reshape(shard, 2, inner),
        sums[1],
        sums[2][0],
        sums[9].T,
        sums[3],
        sums[4][0],
        sums[5],
        sums[6][0],
        out_proj_grad.T,
        sums[7][0],
        sums[8].T,
        first_grad,
        second_grad.transpose(0, 2, 1),
    )


def solution(mesh):
    weights = (
        P("dp"),
        P("dp", None, "tp"),
        P(None, ("tp", "dp")),
        P(("tp", "dp")),
        P(("tp", "dp"), None),
        P(None, ("tp", "dp")),
        P(("tp", "dp")),
        P(None, ("tp", "dp")),
        P(("tp", "dp")),
        P("tp", "dp"),
        P("dp"),
        P("dp", None),
        P(None, "dp", "tp"),
        P(None, "tp", "dp"),
    )
    rows = P(None, "dp", "ctx", None)
    return jax.shard_map(
        local,
        mesh=mesh,
        in_specs=(rows, rows, *weights, P(("dp", "ctx"), None), P(("dp", "ctx"))),
        out_specs=(rows, rows, *weights),
        check_vma=False,
    )
```

time: 6620 us -> 1240 us (0.19)
  waiting for transfers between devices: 3570 us -> 398 us
  local copies, waits for them, and re-layouts: 1140 us -> 121 us
  other arithmetic: 1120 us -> 152 us
  Pallas kernels: 0 us -> 183 us
  matrix products: 376 us -> 203 us
  blocking collectives: 266 us -> 93.1 us
    reduce_scatter x5 -> x1, waiting for transfers between devices: 1840 us -> 53.3 us  [local(): lax.psum_scatter(small_grads, 'dp', scatter_dimension=0, tiled=True)[0]]
    all_gather x4 -> x2, waiting for transfers between devices: 1010 us -> 38.5 us  [the longest x1 38.5 us: local(): lax.all_gather(in_weight.reshape(shard, 2 * inner), 'dp', axis=0, tiled=T...]
    reduce_sum x778 -> x14, other arithmetic: 747 us -> 50.2 us  [the longest x1 15.7 us: local(): jnp.sum(conv_grad * extended[tap:tap + steps], axis=(0, 1, 2))]
    slice x555 -> x19, local copies, waits for them, and re-layouts: 613 us -> 10.4 us  [the longest x2 2.92 us: own_half(): return value[:slots] + swapped(value[slots:], 'tp')]
    psum x6 -> x0, waiting for transfers between devices: 464 us -> none  [the longest x2 392 us: pieces_total(): lax.psum((gain_one, input_projection, conv_taps, conv_shift, x_proj, dt_p...]
    unnamed x23 -> x3, waiting for transfers between devices: 250 us -> 0.73 us
    all_to_all x0 -> x9, waiting for transfers between devices: none -> 215 us  [the longest x2 116 us: own_expert(): lax.all_to_all(shards, 'dp', 0, 0, tiled=True)]
    dot_general x22 -> x9, matrix products: 303 us -> 92.7 us  [the longest x1 39.6 us: local(): hidden = jnp.dot(slot_rows, first_layer, preferred_element_type=F32)]
where the time goes in v1:
time: 1240 us; the launch traced here: 1230 us
  waiting for transfers between devices  398 us (32%)
  matrix products  203 us (16%)
  Pallas kernels  183 us (15%)
  other arithmetic  152 us (12%)
  local copies, waits for them, and re-layouts  121 us (10%)
  blocking collectives  93.1 us (8%)
  starting transfers between devices  66.2 us (5%)
  between operations  15.5 us (1%)
    pallas_call x4, Pallas kernels, call(): pl.pallas_call(kernel, grid=self.grid, in_specs=in_specs, out_specs=out_s...  183 us
    all_to_all x2, waiting for transfers between devices, own_expert(): lax.all_to_all(shards, 'dp', 0, 0, tiled=True)  116 us
    all_to_all x3, waiting for transfers between devices, expert_exchange(): lax.all_to_all(value, 'dp', 0, 0, axis_index_groups=groups, tiled=True)  96.3 us
    ppermute x20, waiting for transfers between devices, swapped(): return lax.ppermute(value, axis, [(0, 1), (1, 0)])  90.4 us
    dot_general x9, matrix products, contract_rows(): lax.dot_general(left_side, right_side, (((0,), (0,)), ((), ())), precisio...  59.5 us
    all_to_all x1, blocking collectives, expert_exchange(): lax.all_to_all(value, 'dp', 0, 0, axis_index_groups=groups, tiled=True)  57.6 us
    reduce_scatter x1, waiting for transfers between devices, local(): lax.psum_scatter(small_grads, 'dp', scatter_dimension=0, tiled=True)[0]  53.3 us
    dot_general x8, matrix products, contract_cols(): lax.dot_general(left_side, right_side, (((1,), (1,)), ((), ())), precisio...  50.5 us
  transfers between devices with their start and end apart: 36, of which 16 were waited for; matrix products, arithmetic and copies ran while one was open for 36% of the time, Pallas kernels for 15%

profile of v1, /device:TPU:0, one launch (start us, length us, event | category | flops | bytes accessed | tf_op | source)
XLA Modules:
  0.0 1231.1 jit_solution(899259939117689452)
XLA Ops:
  18.0 35.4 %all-gather.1 = bf16[8,209,144]{1,2,0:T(8,128)(2,1)S(1)} all-gather(bf16[1,209,144]{1,2,0:T(8,128)(2,1)S(1)} %bitcast.263), channel_id=2, replica_groups=mesh['dp'=8,'ctx'=2,'tp'=2] {'dp'}, dimensions={0}, use_global_device_ids=true | all-gather | bytes 541728 | tf_op jit(solution)/shard_map/all_gather | solution.py:443
  67.2 38.5 %all-gather.5.cloned.1.call-done = bf16[1152,2304]{1,0:T(8,128)(2,1)} async-done(((bf16[144,2304]{1,0:T(8,128)(2,1)}), bf16[1152,2304]{1,0:T(8,128)(2,1)}) %all-gather.5.cloned.1.call-update) | async-done | bytes 5308432 | tf_op jit(solution)/shard_map/all_gather | solution.py:445
  105.7 11.4 fusion.92
  150.8 29.1 %shard_map.297 = (f32[2,16,8,1152]{3,2,1,0:T(8,128)}, f32[2,16,8,1152]{3,2,1,0:T(8,128)}, f32[2,16,1152]{2,1,0:T(8,128)}) custom-call(f32[64,2,8,1152]{3,2,1,0:T(8,128)} %compare_select_fusion.step_ref, f32[64,2,8,1152]{3,2,1,0:T(8,128)} %get-tuple-element.142.input_ref, f32[2,64,16,8,128]{4,3,2,1,0:T(8,128)} %broadcast_in_dim.28.mix_in_ref, ...), custom_call_target="tpu_custom_call" | custom-call | flops 94371840 | bytes 20922368 | tf_op jit(solution)/shard_map/pallas_call | solution.py:273
  191.3 36.7 %shard_map.298 = (f32[64,2,8,1152]{3,2,1,0:T(8,128)}, f32[2,16,8,1152]{3,2,1,0:T(8,128)}) custom-call(f32[64,2,8,1152]{3,2,1,0:T(8,128)} %compare_select_fusion.step_ref, f32[64,2,8,1152]{3,2,1,0:T(8,128)} %get-tuple-element.142.input_ref, f32[2,64,16,8,128]{4,3,2,1,0:T(8,128)} %broadcast_in_dim.28.mix_in_ref, ...), custom_call_target="tpu_custom_call" | custom-call | flops 132120576 | bytes 35209216 | tf_op jit(solution)/shard_map/pallas_call | solution.py:273
  233.5 8.3 fusion.96
  272.3 41.6 %all-to-all-done.4 = bf16[8,128,1152]{2,1,0:T(8,128)(2,1)S(1)} async-done(((bf16[8,128,1152]{2,1,0:T(8,128)(2,1)}), bf16[8,128,1152]{2,1,0:T(8,128)(2,1)S(1)}, u32[]{:S(2)}, u32[]{:S(2)}) %all-to-all-start.4) | async-done | bytes 2359328 | tf_op jit(solution)/shard_map/all_to_all | solution.py:330
  315.3 57.6 %all_to_all.50 = bf16[8,128,1152]{2,1,0:T(8,128)(2,1)S(1)} all-to-all(bf16[8,128,1152]{2,1,0:T(8,128)(2,1)} %bitcast.245), channel_id=1, replica_groups=mesh['dp'=8,'ctx'=2,'tp'=2] {'dp'}, dimensions={0} | all-to-all | bytes 4718592 | tf_op jit(solution)/shard_map/all_to_all | solution.py:330
  378.2 77.3 %all-to-all-done.1 = bf16[8,144,1536]{2,1,0:T(8,128)(2,1)} async-done(((bf16[8,144,1536]{2,1,0:T(8,128)(2,1)}), bf16[8,144,1536]{2,1,0:T(8,128)(2,1)}, u32[]{:S(2)}, u32[]{:S(2)}) %all-to-all-start.1) | async-done | bytes 3538976 | tf_op jit(solution)/shard_map/all_to_all | solution.py:338
  460.3 39.6 %multiply_convert_fusion = (bf16[2048,1536]{1,0:T(8,128)(2,1)}, f32[2048,1536]{1,0:T(8,128)}, f32[2048,1536]{1,0:T(8,128)}) fusion(bf16[1152,1536]{1,0:T(8,128)(2,1)} %bitcast.29, bf16[1024,1152]{1,0:T(8,128)(2,1)} %collective-permute-done.4, bf16[1024,1152]{1,0:T(8,128)(2,1)S(1)} %bitcast.207), kind=kOutput, calls=%fused_computation.4 | convolution fusion | flops 7461666816 | bytes 39714816 | tf_op jit(solution)/shard_map/dot_general | solution.py:538
  499.9 39.0 %all-to-all-done.2 = bf16[8,144,1536]{2,1,0:T(8,128)(2,1)} async-done(((bf16[8,144,1536]{2,1,0:T(8,128)(2,1)}), bf16[8,144,1536]{2,1,0:T(8,128)(2,1)}, u32[]{:S(2)}, u32[]{:S(2)}) %all-to-all-start.2) | async-done | bytes 3538976 | tf_op jit(solution)/shard_map/all_to_all | solution.py:338
  538.8 11.5 fusion.97
  558.6 20.1 %add_convert_fusion = bf16[2048,1536]{1,0:T(8,128)(2,1)} fusion(f32[2048,1536]{1,0:T(8,128)} %get-tuple-element.139, f32[2048,1536]{1,0:T(8,128)} %get-tuple-element.161, bf16[1152,1536]{1,0:T(8,128)(2,1)} %bitcast.31, bf16[1024,1152]{1,0:T(8,128)(2,1)} %collective-permute-done.7, bf16[1024,1152]{1,0:T(8,128)(2,1)} %bitcast.214, f32[2048]{0:T(1024)S(1)} %get-tuple-element.136), kind=kOutput, calls=%fused_computation.3 | convolution fusion | flops 7305953280 | bytes 39723008 | tf_op jit(solution)/shard_map/dot_general | solution.py:540
  578.7 11.5 fusion.98
  598.8 6.6 fusion.23
  609.7 54.7 %all-to-all-done.5 = bf16[8,128,1152]{2,1,0:T(8,128)(2,1)} async-done(((bf16[8,128,1152]{2,1,0:T(8,128)(2,1)}), bf16[8,128,1152]{2,1,0:T(8,128)(2,1)}, u32[]{:S(2)}, u32[]{:S(2)}) %all-to-all-start.5) | async-done | bytes 2359328 | tf_op jit(solution)/shard_map/all_to_all | solution.py:330
  668.9 10.9 fusion.45
  682.7 11.2 fusion.53
  701.8 20.4 %collective-permute-done.20 = bf16[1152,768]{1,0:T(8,128)(2,1)S(1)} collective-permute-done((bf16[1152,768]{1,0:T(8,128)(2,1)S(1)}, bf16[1152,768]{1,0:T(8,128)(2,1)S(1)}, u32[]{:S(2)}, u32[]{:S(2)}) %collective-permute-start.20) | collective-permute-done | bytes 1769504 | tf_op jit(solution)/shard_map/ppermute | solution.py:22
  737.4 21.7 %collective-permute-done.22 = bf16[1152,768]{1,0:T(8,128)(2,1)} collective-permute-done((bf16[1152,768]{1,0:T(8,128)(2,1)}, bf16[1152,768]{1,0:T(8,128)(2,1)}, u32[]{:S(2)}, u32[]{:S(2)}) %collective-permute-start.22) | collective-permute-done | bytes 1769504 | tf_op jit(solution)/shard_map/ppermute | solution.py:22
  773.6 8.8 convert_bitcast_fusion.1
  786.9 6.7 multiply_reduce_fusion
  793.6 28.3 %shard_map.299 = (f32[2,16,8,1152]{3,2,1,0:T(8,128)}, f32[2,16,8,1152]{3,2,1,0:T(8,128)}, f32[2,16,1152]{2,1,0:T(8,128)}) custom-call(f32[64,2,8,1152]{3,2,1,0:T(8,128)} %compare_select_fusion.step_ref, f32[2,64,16,8,128]{4,3,2,1,0:T(8,128)} %broadcast_in_dim.29.mix_out_ref, f32[64,2,8,1152]{3,2,1,0:T(8,128)} %get-tuple-element.132.grad_ref, ...), custom_call_target="tpu_custom_call" | custom-call | flops 94371840 | bytes 20922368 | tf_op jit(solution)/shard_map/pallas_call | solution.py:273
  835.6 88.6 %shard_map.300 = (f32[64,2,8,1152]{3,2,1,0:T(8,128)}, f32[64,2,8,1152]{3,2,1,0:T(8,128)}, f32[2,16,1152]{2,1,0:T(8,128)}, f32[2,64,16,8,128]{4,3,2,1,0:T(8,128)}, f32[2,64,16,8,128]{4,3,2,1,0:T(8,128)}) custom-call(f32[64,2,8,1152]{3,2,1,0:T(8,128)} %compare_select_fusion.step_ref, f32[64,2,8,1152]{3,2,1,0:T(8,128)} %get-tuple-element.142.input_ref, ...), custom_call_target="tpu_custom_call" | custom-call | flops 377487360 | bytes 61571072 | tf_op jit(solution)/shard_map/pallas_call | solution.py:273
  952.8 8.0 fusion.101
  961.9 15.7 %multiply_reduce_fusion.1 = (f32[1152]{0:T(1024)}, f32[1152]{0:T(1024)}, f32[1152]{0:T(1024)}, f32[1152]{0:T(1024)}, f32[1152]{0:T(1024)S(1)}, /*index=5*/f32[64,2,8,1152]{3,2,1,0:T(8,128)S(1)}) fusion(f32[67,2,8,1152]{3,2,1,0:T(8,128)} %copy-done, f32[64,2,8,1152]{3,2,1,0:T(8,128)} %get-tuple-element.144, f32[64,2,8,1152]{3,2,1,0:T(8,128)S(1)} %fusion.100, ...), kind=kLoop, calls=%fused_computation.66 | loop fusion | flops 33024384 | bytes 47213568 | tf_op jit(solution)/shard_map/reduce_sum | solution.py:600
  997.7 10.4 fusion.39
  1037.4 32.1 %collective-permute-done.16 = bf16[8,144,1152]{2,1,0:T(8,128)(2,1)} collective-permute-done((bf16[8,144,1152]{2,1,0:T(8,128)(2,1)}, bf16[8,144,1152]{2,1,0:T(8,128)(2,1)}, u32[]{:S(2)}, u32[]{:S(2)}) %collective-permute-start.16) | collective-permute-done | bytes 2654240 | tf_op jit(solution)/shard_map/ppermute | solution.py:22
  1123.2 6.5 fusion.29
  1139.4 7.4 add_convert_fusion.2
  1148.7 53.3 %reduce-scatter.2.cloned.1.call-done = f32[1,209,144]{1,2,0:T(8,128)} async-done(((f32[8,209,144]{1,2,0:T(8,128)}), f32[1,209,144]{1,2,0:T(8,128)}) %reduce-scatter.2.cloned.1.call-update) | async-done | bytes 120400 | tf_op jit(solution)/shard_map/reduce_scatter | solution.py:641
  1214.6 6.7 collective-permute-done.17
  (393 shorter events, 360.2 us)
Async XLA Ops:
  7.2 98.5 %all-gather.5.cloned.1.call-start = ((), (), s32[]{:S(2)}) async-start(), calls=%async_computation.11 | async-start | bytes 5971968 | tf_op jit(solution)/shard_map/all_gather | solution.py:445
  9.2 224.3 %all-gather.7.cloned.1.call-start = ((), (), s32[]{:S(2)}) async-start(), calls=%async_computation.12 | async-start | bytes 2985984 | tf_op jit(solution)/shard_map/all_gather | solution.py:463
  117.2 8.0 collective-permute-start
  241.8 17.7 %collective-permute-start.3 = (f32[1024,1152]{1,0:T(8,128)}, f32[1024,1152]{1,0:T(8,128)}, u32[]{:S(2)}, u32[]{:S(2)}) collective-permute-start(f32[1024,1152]{1,0:T(8,128)} %fusion.96), channel_id=1, source_target_pairs={{0,1},{1,0},{2,3},{3,2},{4,5},{5,4},{6,7},{7,6},{8,9},{9,8},{10,11... | collective-permute-start | bytes 14155784 | tf_op jit(solution)/shard_map/ppermute | solution.py:22
  255.7 58.2 %all-to-all-start.4 = ((bf16[8,128,1152]{2,1,0:T(8,128)(2,1)}), bf16[8,128,1152]{2,1,0:T(8,128)(2,1)S(1)}, u32[]{:S(2)}, u32[]{:S(2)}) async-start(bf16[8,128,1152]{2,1,0:T(8,128)(2,1)} %bitcast.244), calls=%async_computation.4 | async-start | bytes 4718592 | tf_op jit(solution)/shard_map/all_to_all | solution.py:330
  372.9 82.7 %all-to-all-start.1 = ((bf16[8,144,1536]{2,1,0:T(8,128)(2,1)}), bf16[8,144,1536]{2,1,0:T(8,128)(2,1)}, u32[]{:S(2)}, u32[]{:S(2)}) async-start(bf16[8,144,1536]{2,1,0:T(8,128)(2,1)} %param.32), calls=%async_computation.1 | async-start | bytes 7077888 | tf_op jit(solution)/shard_map/all_to_all | solution.py:338
  377.4 82.9 %collective-permute-start.4 = (bf16[1024,1152]{1,0:T(8,128)(2,1)S(1)}, bf16[1024,1152]{1,0:T(8,128)(2,1)}, u32[]{:S(2)}, u32[]{:S(2)}) collective-permute-start(bf16[1024,1152]{1,0:T(8,128)(2,1)S(1)} %bitcast.206), channel_id=1, source_target_pairs={{0,1},{1,0},{2,3},{3,2},{4,5},{5,4},{6,7},{7,6},{8,9},{9,8},{10,11... | collective-permute-start | bytes 7077896 | tf_op jit(solution)/shard_map/ppermute | solution.py:22
  377.7 180.9 %collective-permute-start.7 = (bf16[1024,1152]{1,0:T(8,128)(2,1)}, bf16[1024,1152]{1,0:T(8,128)(2,1)}, u32[]{:S(2)}, u32[]{:S(2)}) collective-permute-start(bf16[1024,1152]{1,0:T(8,128)(2,1)} %bitcast.213), channel_id=1, source_target_pairs={{0,1},{1,0},{2,3},{3,2},{4,5},{5,4},{6,7},{7,6},{8,9},{9,8},{10,11... | collective-permute-start | bytes 7077896 | tf_op jit(solution)/shard_map/ppermute | solution.py:22
  455.6 83.3 %all-to-all-start.2 = ((bf16[8,144,1536]{2,1,0:T(8,128)(2,1)}), bf16[8,144,1536]{2,1,0:T(8,128)(2,1)}, u32[]{:S(2)}, u32[]{:S(2)}) async-start(bf16[8,144,1536]{2,1,0:T(8,128)(2,1)} %bitcast.225), calls=%async_computation.2 | async-start | bytes 7077888 | tf_op jit(solution)/shard_map/all_to_all | solution.py:338
  555.4 35.7 %collective-permute-start.5 = (f32[1024,1152]{1,0:T(8,128)}, f32[1024,1152]{1,0:T(8,128)}, u32[]{:S(2)}, u32[]{:S(2)}) collective-permute-start(f32[1024,1152]{1,0:T(8,128)} %slice.266), channel_id=1, source_target_pairs={{0,1},{1,0},{2,3},{3,2},{4,5},{5,4},{6,7},{7,6},{8,9},{9,8},{10,11... | collective-permute-start | bytes 14155784 | tf_op jit(solution)/shard_map/ppermute | solution.py:22
  590.5 8.2 collective-permute-start.8
  605.3 59.1 %all-to-all-start.5 = ((bf16[8,128,1152]{2,1,0:T(8,128)(2,1)}), bf16[8,128,1152]{2,1,0:T(8,128)(2,1)}, u32[]{:S(2)}, u32[]{:S(2)}) async-start(bf16[8,128,1152]{2,1,0:T(8,128)(2,1)} %bitcast.217), calls=%async_computation.5 | async-start | bytes 4718592 | tf_op jit(solution)/shard_map/all_to_all | solution.py:330
  664.4 59.7 %all-to-all-start.3 = ((bf16[8,128,1152]{2,1,0:T(8,128)(2,1)}), bf16[8,128,1152]{2,1,0:T(8,128)(2,1)}, u32[]{:S(2)}, u32[]{:S(2)}) async-start(bf16[8,128,1152]{2,1,0:T(8,128)(2,1)} %bitcast.216), calls=%async_computation.3 | async-start | bytes 4718592 | tf_op jit(solution)/shard_map/all_to_all | solution.py:330
  680.1 42.1 %collective-permute-start.20 = (bf16[1152,768]{1,0:T(8,128)(2,1)S(1)}, bf16[1152,768]{1,0:T(8,128)(2,1)S(1)}, u32[]{:S(2)}, u32[]{:S(2)}) collective-permute-start(bf16[1152,768]{1,0:T(8,128)(2,1)S(1)} %dynamic-slice_convert_fusion.2), channel_id=1, source_target_pairs={{0,2},{2,0},{1,3},{3,1},{4,6},{6,4},{5,7},{7,5},{8,10},{10,8},{9,1... | collective-permute-start | bytes 5308424 | tf_op jit(solution)/shard_map/ppermute | solution.py:22
  695.5 63.6 %collective-permute-start.22 = (bf16[1152,768]{1,0:T(8,128)(2,1)}, bf16[1152,768]{1,0:T(8,128)(2,1)}, u32[]{:S(2)}, u32[]{:S(2)}) collective-permute-start(bf16[1152,768]{1,0:T(8,128)(2,1)} %dynamic-slice_convert_fusion.1), channel_id=1, source_target_pairs={{0,2},{2,0},{1,3},{3,1},{4,6},{6,4},{5,7},{7,5},{8,10},{10,8},{9,1... | collective-permute-start | bytes 5308424 | tf_op jit(solution)/shard_map/ppermute | solution.py:22
  701.8 61.5 %collective-permute-start.9 = (bf16[1024,1152]{1,0:T(8,128)(2,1)S(1)}, bf16[1024,1152]{1,0:T(8,128)(2,1)}, u32[]{:S(2)}, u32[]{:S(2)}) collective-permute-start(bf16[1024,1152]{1,0:T(8,128)(2,1)S(1)} %fusion.38), channel_id=1, source_target_pairs={{0,1},{1,0},{2,3},{3,2},{4,5},{5,4},{6,7},{7,6},{8,9},{9,8},{10,11... | collective-permute-start | bytes 7077896 | tf_op jit(solution)/shard_map/ppermute | solution.py:22
  724.1 45.2 %all-to-all-start.8 = ((bf16[8,144,768]{2,1,0:T(8,128)(2,1)}), bf16[8,144,768]{2,1,0:T(8,128)(2,1)}, u32[]{:S(2)}, u32[]{:S(2)}) async-start(bf16[8,144,768]{2,1,0:T(8,128)(2,1)} %bitcast.219), calls=%async_computation.9 | async-start | bytes 3538944 | tf_op jit(solution)/shard_map/all_to_all | solution.py:367
  736.4 37.2 %collective-permute-start.6 = (bf16[1024,1152]{1,0:T(8,128)(2,1)}, bf16[1024,1152]{1,0:T(8,128)(2,1)}, u32[]{:S(2)}, u32[]{:S(2)}) collective-permute-start(bf16[1024,1152]{1,0:T(8,128)(2,1)} %fusion.36), channel_id=1, source_target_pairs={{0,1},{1,0},{2,3},{3,2},{4,5},{5,4},{6,7},{7,6},{8,9},{9,8},{10,11... | collective-permute-start | bytes 7077896 | tf_op jit(solution)/shard_map/ppermute | solution.py:22
  769.3 61.3 %all-to-all-start.9 = ((bf16[8,144,768]{2,1,0:T(8,128)(2,1)}), bf16[8,144,768]{2,1,0:T(8,128)(2,1)}, u32[]{:S(2)}, u32[]{:S(2)}) async-start(bf16[8,144,768]{2,1,0:T(8,128)(2,1)} %bitcast.218), calls=%async_computation.10 | async-start | bytes 3538944 | tf_op jit(solution)/shard_map/all_to_all | solution.py:367
  821.9 13.0 %collective-permute-start.10 = (f32[2,16,1152]{2,1,0:T(8,128)}, f32[2,16,1152]{2,1,0:T(8,128)S(1)}, u32[]{:S(2)}, u32[]{:S(2)}) collective-permute-start(f32[2,16,1152]{2,1,0:T(8,128)} %get-tuple-element.36), channel_id=1, source_target_pairs={{2,0},{3,1},{6,4},{7,5},{10,8},{11,9},{14,12},{15,13},{18,16},{19,... | collective-permute-start | bytes 442376 | tf_op jit(solution)/shard_map/ppermute | solution.py:28
  827.9 200.0 %collective-permute-start.21 = (bf16[8,144,768]{2,1,0:T(8,128)(2,1)}, bf16[8,144,768]{2,1,0:T(8,128)(2,1)}, u32[]{:S(2)}, u32[]{:S(2)}) collective-permute-start(bf16[8,144,768]{2,1,0:T(8,128)(2,1)} %all-to-all-done.8), channel_id=1, source_target_pairs={{0,2},{2,0},{1,3},{3,1},{4,6},{6,4},{5,7},{7,5},{8,10},{10,8},{9,1... | collective-permute-start | bytes 5308424 | tf_op jit(solution)/shard_map/ppermute | solution.py:22
  830.6 197.4 %collective-permute-start.23 = (bf16[8,144,768]{2,1,0:T(8,128)(2,1)}, bf16[8,144,768]{2,1,0:T(8,128)(2,1)}, u32[]{:S(2)}, u32[]{:S(2)}) collective-permute-start(bf16[8,144,768]{2,1,0:T(8,128)(2,1)} %all-to-all-done.9), channel_id=1, source_target_pairs={{0,2},{2,0},{1,3},{3,1},{4,6},{6,4},{5,7},{7,5},{8,10},{10,8},{9,1... | collective-permute-start | bytes 5308424 | tf_op jit(solution)/shard_map/ppermute | solution.py:22
  952.7 8.1 collective-permute-start.11
  980.1 32.9 %collective-permute-start.18 = (bf16[8,72,1152]{2,1,0:T(8,128)(2,1)}, bf16[8,72,1152]{2,1,0:T(8,128)(2,1)}, u32[]{:S(2)}, u32[]{:S(2)}) collective-permute-start(bf16[8,72,1152]{2,1,0:T(8,128)(2,1)} %dynamic-slice_convert_fusion.3), channel_id=1, source_target_pairs={{0,2},{2,0},{1,3},{3,1},{4,6},{6,4},{5,7},{7,5},{8,10},{10,8},{9,1... | collective-permute-start | bytes 3981320 | tf_op jit(solution)/shard_map/ppermute | solution.py:22
  997.7 71.8 %collective-permute-start.16 = (bf16[8,144,1152]{2,1,0:T(8,128)(2,1)}, bf16[8,144,1152]{2,1,0:T(8,128)(2,1)}, u32[]{:S(2)}, u32[]{:S(2)}) collective-permute-start(bf16[8,144,1152]{2,1,0:T(8,128)(2,1)} %dynamic-slice_convert_fusion), channel_id=1, source_target_pairs={{0,2},{2,0},{1,3},{3,1},{4,6},{6,4},{5,7},{7,5},{8,10},{10,8},{9,1... | collective-permute-start | bytes 7962632 | tf_op jit(solution)/shard_map/ppermute | solution.py:22
  1008.1 115.1 %collective-permute-start.13 = (f32[1024,1152]{1,0:T(8,128)}, f32[1024,1152]{1,0:T(8,128)}, u32[]{:S(2)}, u32[]{:S(2)}) collective-permute-start(f32[1024,1152]{1,0:T(8,128)} %fusion.39), channel_id=1, source_target_pairs={{0,1},{1,0},{2,3},{3,2},{4,5},{5,4},{6,7},{7,6},{8,9},{9,8},{10,11... | collective-permute-start | bytes 14155784 | tf_op jit(solution)/shard_map/ppermute | solution.py:22
  1015.7 57.8 %all-to-all-start.7 = ((bf16[8,72,1152]{2,1,0:T(8,128)(2,1)}), bf16[8,72,1152]{2,1,0:T(8,128)(2,1)}, u32[]{:S(2)}, u32[]{:S(2)}) async-start(bf16[8,72,1152]{2,1,0:T(8,128)(2,1)} %add_convert_fusion.6), calls=%async_computation.8 | async-start | bytes 2654208 | tf_op jit(solution)/shard_map/all_to_all | solution.py:379
  1073.4 130.1 %all-to-all-start.6 = ((bf16[8,144,1152]{2,1,0:T(8,128)(2,1)}), bf16[8,144,1152]{2,1,0:T(8,128)(2,1)S(1)}, u32[]{:S(2)}, u32[]{:S(2)}) async-start(bf16[8,144,1152]{2,1,0:T(8,128)(2,1)} %add_convert_fusion.1), calls=%async_computation.7 | async-start | bytes 5308416 | tf_op jit(solution)/shard_map/all_to_all | solution.py:379
  1079.4 122.7 %reduce-scatter.2.cloned.1.call-start = ((), (), s32[]{:S(2)}) async-start(), calls=%async_computation.13 | async-start | bytes 1327104 | tf_op jit(solution)/shard_map/reduce_scatter | solution.py:641
  1107.6 13.6 %collective-permute-start.19 = (f32[72,1152]{1,0:T(8,128)}, f32[72,1152]{1,0:T(8,128)}, u32[]{:S(2)}, u32[]{:S(2)}) collective-permute-start(f32[72,1152]{1,0:T(8,128)} %convert_reduce_fusion.1), channel_id=1, source_target_pairs={{0,2},{2,0},{1,3},{3,1},{4,6},{6,4},{5,7},{7,5},{8,10},{10,8},{9,1... | collective-permute-start | bytes 995336 | tf_op jit(solution)/shard_map/ppermute | solution.py:22
  1202.1 6.8 collective-permute-start.15
  1204.7 16.6 %collective-permute-start.17 = (f32[144,1152]{1,0:T(8,128)}, f32[144,1152]{1,0:T(8,128)S(1)}, u32[]{:S(2)}, u32[]{:S(2)}) collective-permute-start(f32[144,1152]{1,0:T(8,128)} %convert_reduce_fusion), channel_id=1, source_target_pairs={{0,2},{2,0},{1,3},{3,1},{4,6},{6,4},{5,7},{7,5},{8,10},{10,8},{9,1... | collective-permute-start | bytes 1990664 | tf_op jit(solution)/shard_map/ppermute | solution.py:22
  (84 other events, 1827.6 us)
Sparse Core Ops, SparseCore 0:
  10.8 94.8 all-gather.4
  107.9 53.2 all-gather.6
  1137.6 64.4 reduce-scatter.1

commit v2 on v1

--- a/solution.py
+++ b/solution.py
@@ -32,6 +32,10 @@
     if lax.axis_size(axis) == 2:
         return value + swapped(value, axis)
     return lax.psum(value, axis)
+
+
+def together(*values):
+    return lax.optimization_barrier(values)
 
 
 def entering_pieces(decay, value, axis, backward):
@@ -320,6 +324,69 @@
         )
 
 
+def expert_kernel(
+    rows_ref, cotan_ref, router_ref, mask_ref, up_a, up_b, down_a, down_b,
+    out_ref, picked_ref, prob_ref, grad_ref, active_a, active_b, hidden_a, hidden_b,
+):
+    rows = rows_ref[...]
+    logits = contract_cols(rows, router_ref[...])
+    shifted = jnp.exp(logits - jnp.max(logits, axis=1, keepdims=True))
+    prob = shifted / jnp.sum(shifted, axis=1, keepdims=True)
+    gate = jnp.sum(prob * mask_ref[...], axis=1, keepdims=True)
+    grad = (gate * cotan_ref[...].astype(F32)).astype(BF16)
+    prob_ref[...] = prob
+    grad_ref[...] = grad
+    out, picked = None, None
+    for up, down, active_ref, hidden_ref in (
+        (up_a, down_a, active_a, hidden_a),
+        (up_b, down_b, active_b, hidden_b),
+    ):
+        hidden = jnp.dot(rows, up[...], preferred_element_type=F32)
+        share = 0.5 + 0.5 * lax.erf(hidden * math.sqrt(0.5))
+        slope = share + hidden * (jnp.exp(-0.5 * hidden * hidden) * (1.0 / math.sqrt(2 * math.pi)))
+        active = (hidden * share).astype(BF16)
+        active_ref[...] = active
+        hidden_grad = (jnp.dot(grad, down[...], preferred_element_type=F32) * slope).astype(BF16)
+        hidden_ref[...] = hidden_grad
+        out_part = contract_cols(active, down[...])
+        picked_part = contract_cols(hidden_grad, up[...])
+        out = out_part if out is None else out + out_part
+        picked = picked_part if picked is None else picked + picked_part
+    out_ref[...] = out
+    picked_ref[...] = picked
+
+
+def expert_call(rows, cotan, router_t, mask, ups, downs):
+    count, width = rows.shape
+    hidden = ups[0].shape[1]
+    block = math.gcd(count, 512)
+    row_spec = pl.BlockSpec((block, width), lambda at: (at, 0))
+    hidden_spec = pl.BlockSpec((block, hidden), lambda at: (at, 0))
+    prob_spec = pl.BlockSpec((block, router_t.shape[0]), lambda at: (at, 0))
+
+    def whole(array):
+        return pl.BlockSpec(array.shape, lambda at: (0, 0), pipeline_mode=pl.Buffered(1))
+
+    fixed = (router_t, mask, *ups, *downs)
+    wide, narrow = jax.ShapeDtypeStruct((count, width), F32), jax.ShapeDtypeStruct((count, width), BF16)
+    inner = jax.ShapeDtypeStruct((count, hidden), BF16)
+    return pl.pallas_call(
+        expert_kernel,
+        grid=(count // block,),
+        in_specs=[row_spec, row_spec, *(whole(array) for array in fixed)],
+        out_specs=[row_spec, row_spec, prob_spec, row_spec, *(hidden_spec,) * 4],
+        out_shape=[
+            wide, wide, jax.ShapeDtypeStruct((count, router_t.shape[0]), F32), narrow, *(inner,) * 4
+        ],
+        compiler_params=pltpu.CompilerParams(vmem_limit_bytes=VMEM_LIMIT),
+        cost_estimate=pl.CostEstimate(
+            flops=16 * count * width * hidden,
+            transcendentals=4 * count * hidden,
+            bytes_accessed=count * (14 * width + 8 * hidden) + 8 * width * hidden,
+        ),
+    )(rows, cotan, *fixed)
+
+
 def expert_exchange(value, experts):
     count = lax.axis_size("dp")
     groups = None
@@ -330,23 +397,73 @@
     return lax.all_to_all(value, "dp", 0, 0, axis_index_groups=groups, tiled=True)
 
 
-def own_expert(shards):
-    experts, rows, columns = shards.shape
+def by_ctx(first, second):
+    lead = lax.axis_index("ctx") == 0
+    return jnp.where(lead, first, second), jnp.where(lead, second, first)
+
+
+def own_expert_blocks(up_shards, down_shards):
+    experts, _, hidden = up_shards.shape
     count = lax.axis_size("dp")
+    half = hidden // 2
+    both = jnp.concatenate([up_shards, down_shards], axis=1)
+    if lax.axis_size("ctx") == 2:
+        both = by_ctx(both[:, :, :half], both[:, :, half:])[0]
     if count != experts:
-        shards = jnp.concatenate([shards] * (count // experts), axis=0)
-    return lax.all_to_all(shards, "dp", 0, 0, tiled=True).reshape(count * rows, columns)
-
-
-def halves_sum(value, axis):
-    count = lax.axis_size("ctx")
-    if count != 2:
-        return lax.psum_scatter(value, "ctx", scatter_dimension=axis, tiled=True)
-    mine = lax.axis_index("ctx")
-    part = value.shape[axis] // 2
-    own = lax.dynamic_slice_in_dim(value, mine * part, part, axis)
-    other = lax.dynamic_slice_in_dim(value, (1 - mine) * part, part, axis)
-    return own + swapped(other.astype(BF16), "ctx").astype(F32)
+        both = jnp.concatenate([both] * (count // experts), axis=0)
+    return lax.all_to_all(both, "dp", 0, 0, tiled=True)
+
+
+def own_expert(both):
+    count, rows = both.shape[0], both.shape[1] // 2
+
+    def layers(value):
+        return tuple(
+            value[:, at : at + rows].reshape(count * rows, value.shape[2]) for at in (0, rows)
+        )
+
+    if lax.axis_size("ctx") == 2:
+        own, other = layers(both), layers(swapped(both, "ctx"))
+    else:
+        half = both.shape[2] // 2
+        own, other = layers(both[:, :, :half]), layers(both[:, :, half:])
+    return (own[0], other[0]), (own[1], other[1])
+
+
+def gathered(*values):
+    bounds = [0]
+    for value in values:
+        bounds.append(bounds[-1] + value.shape[1])
+    got = lax.all_gather(jnp.concatenate(values, axis=1), "dp")
+    return [got[:, :, bounds[i] : bounds[i + 1]] for i in range(len(values))]
+
+
+def half_gathered(*values):
+    if lax.axis_size("ctx") == 2:
+        half = values[0].shape[0] // 2
+        values = [by_ctx(value[:half], value[half:])[0] for value in values]
+    return gathered(*values)
+
+
+def half_joined(*values):
+    joined = []
+    for value in values:
+        if lax.axis_size("ctx") == 2:
+            value = jnp.concatenate(by_ctx(value, swapped(value, "ctx")), axis=1)
+        joined.append(value.reshape(value.shape[0] * value.shape[1], value.shape[2]))
+    return joined
+
+
+def halves_sent(blocks):
+    if lax.axis_size("ctx") != 2:
+        return lax.psum_scatter(blocks, "ctx", scatter_dimension=1, tiled=True), None
+    half = blocks.shape[1] // 2
+    own, other = by_ctx(blocks[:, :half], blocks[:, half:])
+    return own, swapped(other.astype(BF16), "ctx")
+
+
+def halves_added(own, other):
+    return (own if other is None else own + other.astype(F32)).astype(BF16)
 
 
 def halves_joined(value, axis):
@@ -360,24 +477,53 @@
     )
 
 
-def expert_weight_grad(grad, experts):
+def expert_weight_products(rows, hidden_grads, grads, actives):
+    pairs = ((rows, hidden_grads), (grads, actives))
+    far = [contract_rows(left, rights[1]) for left, rights in pairs]
+    if lax.axis_size("ctx") == 2:
+        far = [swapped(value.astype(BF16), "ctx") for value in far]
+    return [contract_rows(left, rights[0]) for left, rights in pairs], far
+
+
+def expert_weight_parts(near, far):
     count = lax.axis_size("dp")
-    part = halves_sum(grad, 1)
-    blocks = part.astype(BF16).reshape(count, part.shape[0] // count, part.shape[1])
-    blocks = lax.all_to_all(blocks, "dp", 0, 0, tiled=True)
+    parts = []
+    for own, other in zip(near, far):
+        if lax.axis_size("ctx") == 2:
+            part = own + other.astype(F32)
+        else:
+            part = lax.psum_scatter(
+                jnp.concatenate([own, other], axis=1), "ctx", scatter_dimension=1, tiled=True
+            )
+        parts.append(part.astype(BF16).reshape(count, part.shape[0] // count, part.shape[1]))
+    return jnp.concatenate(parts, axis=1)
+
+
+def expert_weight_grads(blocks, experts):
+    count = lax.axis_size("dp")
     if count != experts:
         blocks = jnp.sum(
             blocks.reshape(count // experts, experts, *blocks.shape[1:]).astype(F32), axis=0
         ).astype(BF16)
-    return halves_joined(blocks, 2).astype(F32)
-
-
-def weight_grad(grad, axis):
+    if lax.axis_size("ctx") == 2:
+        first, second = by_ctx(blocks, swapped(blocks, "ctx"))
+        joined = jnp.concatenate([first, second], axis=2)
+    else:
+        joined = lax.all_gather(blocks, "ctx", axis=2, tiled=True)
+    shard = joined.shape[1] // 2
+    return joined[:, :shard].astype(F32), joined[:, shard:].astype(F32)
+
+
+def weight_part(grad):
     count = lax.axis_size("dp")
-    blocks = grad.reshape(count, grad.shape[0] // count, grad.shape[1])
-    part = halves_sum(blocks, axis)
-    part = lax.all_to_all(part.astype(BF16), "dp", 0, 0, tiled=True)
-    return halves_joined(jnp.sum(part.astype(F32), axis=0), axis - 1)
+    return halves_sent(grad.reshape(count, grad.shape[0] // count, grad.shape[1]))
+
+
+def weight_shards(blocks, number):
+    sums = jnp.sum(blocks.astype(F32), axis=0)
+    rows = sums.shape[0] // number
+    joined = halves_joined(sums.reshape(number, rows, sums.shape[1]), 1)
+    return [joined[at] for at in range(number)]
 
 
 def local(
@@ -440,10 +586,13 @@
         ],
         axis=0,
     )
-    small_all = lax.all_gather(small, "dp", axis=0)
-    small_all = small_all.transpose(1, 0, 2).reshape(small.shape[0], dp_count * shard)
-    in_flat = lax.all_gather(
-        in_weight.reshape(shard, 2 * inner), "dp", axis=0, tiled=True
+    kinds = small.shape[0]
+    small_wide = jnp.pad(small.T, ((0, 0), (0, -kinds % LANES)))
+    in_x, small_all = gathered(in_weight[:, 0], small_wide)
+    in_x = in_x.reshape(dp_count * shard, inner)
+    small_all = small_all.reshape(dp_count * shard, -1)[:, :kinds].T
+    small_all, out_shard, in_z_shard, up_shards, down_shards = together(
+        small_all, out_weight.T, in_weight[:, 1], fc1_weight, fc2_weight.transpose(0, 2, 1)
     )
     bounds = [0]
     for count in (1, taps, 1, low_rank, 1, states, 1, 1, experts, low_rank + 2 * states):
@@ -460,9 +609,8 @@
     router_t = pieces[8]
     x_proj_t = pieces[9]
     rate_rows = jnp.broadcast_to((decay_rate * LOG2E)[:, None, :], (states, SEGMENTS, inner))
-    out_proj_t = lax.all_gather(out_weight.T, "dp", axis=0, tiled=True)
-    first_layer = own_expert(fc1_weight)
-    second_layer_t = own_expert(fc2_weight.transpose(0, 2, 1))
+    later_halves = half_gathered(out_shard, in_z_shard)
+    expert_blocks = own_expert_blocks(up_shards, down_shards)
 
     route = to_rows(expert_ids)[:, 0]
     keep = to_rows(keep_mask)[:, 0].astype(F32)
@@ -474,25 +622,25 @@
         token_slot[None, :] == jnp.arange(slots, dtype=jnp.int32)[:, None]
     ).astype(BF16)
 
-    def dispatched(value):
+    def slotted(value):
         sent = jnp.dot(place, value, preferred_element_type=F32).astype(BF16)
-        got = expert_exchange(sent.reshape(experts, part_cap, -1), experts)
-        return got.reshape(slots, -1)
-
-    def returned(value):
-        got = expert_exchange(value.reshape(experts, part_cap, -1), experts)
-        return axis_sum(contract_rows(place, got.reshape(slots, -1)).astype(BF16), "tp")
+        return sent.reshape(experts, part_cap, -1)
+
+    def exchanged(value):
+        return expert_exchange(value, experts).reshape(slots, -1)
+
+    def landed(value):
+        return axis_sum(contract_rows(place, value).astype(BF16), "tp").astype(F32)
 
     cotan_bf = to_rows(out_grad)
     cotan = cotan_bf.astype(F32)
-    slot_cotan = dispatched((cotan * keep[:, None]).astype(BF16))
+    sent_cotan = slotted((cotan * keep[:, None]).astype(BF16))
 
     values = to_rows(hidden_in).astype(F32)
     normalized_rows, inverse_one = rms_forward(values, gain_one_f)
     normed_bf = normalized_rows.astype(BF16)
-    mixed = jnp.dot(normed_bf, in_flat, preferred_element_type=F32)
-    x_pre = mixed[:, :inner].astype(BF16).reshape(steps, chains, SEGMENTS, inner)
-    z_gate = mixed[:, inner:].reshape(steps, chains, SEGMENTS, inner)
+    x_pre = jnp.dot(normed_bf, in_x, preferred_element_type=F32).astype(BF16)
+    x_pre = x_pre.reshape(steps, chains, SEGMENTS, inner)
     tail = x_pre[steps - taps + 1 :]
     edge_in = passed_along(tail[:, :, SEGMENTS - 1 :], "ctx", 1)
     halo = jnp.concatenate([edge_in, tail[:, :, : SEGMENTS - 1]], axis=2)
@@ -515,67 +663,84 @@
     dt_pre = (jnp.dot(dt_low, dt_proj, preferred_element_type=F32) + dt_shift).reshape(x_pre.shape)
     step_size = jax.nn.softplus(dt_pre)
     seg_decay, seg_state, last_state = scan.ends(step_size, xconv, mix_in, rate_rows)
+    seg_state, sent_cotan, expert_blocks = together(seg_state, sent_cotan, expert_blocks)
+    ups, downs = own_expert(expert_blocks)
+    slot_cotan = exchanged(sent_cotan)
     entering = entering_pieces(seg_decay[:, :, SEGMENTS - 1], last_state, "ctx", False)
+    entering, later_halves = together(entering, later_halves)
+    out_proj_t, in_z = half_joined(*later_halves)
     scan_out, seg_start = scan.run(
         step_size, xconv, mix_in, mix_out, rate_rows, seg_decay, seg_state, entering
     )
+    z_gate = jnp.dot(normed_bf, in_z, preferred_element_type=F32).reshape(x_pre.shape)
     scanned = scan_out + skip_row[0] * xconv
     z_silu = jax.nn.silu(z_gate)
     gated_bf = (scanned * z_silu).astype(BF16).reshape(tokens, inner)
+    gated_bf, slot_cotan, ups, downs = together(gated_bf, slot_cotan, ups, downs)
     middle = values + axis_sum(contract_cols(gated_bf, out_proj_t), "tp")
 
     normed_two, inverse_two = rms_forward(middle, gain_two_f)
     normed_two_bf = normed_two.astype(BF16)
-    own_rows = dispatched(normed_two_bf)
-    slot_rows = jnp.concatenate([own_rows, swapped(own_rows, "tp")], axis=0)
-    slot_cotan_all = jnp.concatenate([slot_cotan, swapped(slot_cotan, "tp")], axis=0)
+    own_rows = exchanged(slotted(normed_two_bf))
     expert_mask = (
         jnp.arange(experts, dtype=jnp.int32) == lax.rem(lax.axis_index("dp"), experts)
     ).astype(F32)[None, :]
-    slot_prob = jax.nn.softmax(contract_cols(slot_rows, router_t), axis=-1)
+    far_rows, far_cotan = swapped(own_rows, "tp"), swapped(slot_cotan, "tp")
+    far = expert_call(far_rows, far_cotan, router_t, expert_mask, ups, downs)
+    near = expert_call(own_rows, slot_cotan, router_t, expert_mask, ups, downs)
+    slot_out = near[0] + swapped(far[0], "tp")
+    picked_grad = near[1] + swapped(far[1], "tp")
+    slot_prob = near[2]
     slot_gate = jnp.sum(slot_prob * expert_mask, axis=1, keepdims=True)
-    slot_grad = (slot_gate * slot_cotan_all.astype(F32)).astype(BF16)
-    hidden = jnp.dot(slot_rows, first_layer, preferred_element_type=F32)
-    active_bf = jax.nn.gelu(hidden, approximate=False).astype(BF16)
-    active_grad = jnp.dot(slot_grad, second_layer_t, preferred_element_type=F32)
-    hidden_grad_bf = jax.vjp(partial(jax.nn.gelu, approximate=False), hidden)[1](active_grad)[
-        0
-    ].astype(BF16)
-
-    def own_half(value):
-        return value[:slots] + swapped(value[slots:], "tp")
-
-    slot_out = own_half(contract_cols(active_bf, second_layer_t))
-    picked_grad = own_half(contract_cols(hidden_grad_bf, first_layer))
     gate_grad = jnp.sum(slot_out * slot_cotan.astype(F32), axis=1, keepdims=True)
-    logit_grad = gate_grad * slot_gate[:slots] * (expert_mask - slot_prob[:slots])
+    logit_grad = gate_grad * slot_gate * (expert_mask - slot_prob)
     router_grad_t = axis_sum(contract_rows(logit_grad, own_rows.astype(F32), HIGHEST), "tp")
     picked_grad = picked_grad + jnp.dot(
         logit_grad, router_t.astype(F32), precision=HIGHEST, preferred_element_type=F32
     )
-    normed_two_grad = returned(picked_grad.astype(BF16)).astype(F32)
-    expert_out = returned(slot_out.astype(BF16)).astype(F32)
-    first_grad = expert_weight_grad(contract_rows(slot_rows, hidden_grad_bf), experts)
-    second_grad = expert_weight_grad(contract_rows(slot_grad, active_bf), experts)
-    router_prob = jax.nn.softmax(contract_cols(normed_two_bf, router_t), axis=-1)
-    gate_prob = jnp.sum(router_prob * onehot_int.astype(F32), axis=1) * keep
-    result = from_rows((middle + gate_prob[:, None] * expert_out).astype(BF16))
-
+    got_grad = exchanged(picked_grad.astype(BF16).reshape(experts, part_cap, -1))
+
+    def both_rows(at):
+        return jnp.concatenate([far[at], near[at]], axis=0)
+
+    near_parts, far_parts = expert_weight_products(
+        jnp.concatenate([far_rows, own_rows], axis=0),
+        (both_rows(6), both_rows(7)),
+        both_rows(3),
+        (both_rows(4), both_rows(5)),
+    )
+    got_grad, slot_out, near_parts = together(got_grad, slot_out, near_parts)
+    normed_two_grad = landed(got_grad)
+    got_out = exchanged(slot_out.astype(BF16).reshape(experts, part_cap, -1))
     middle_norm_grad, gain_two_grad = rms_backward(middle, inverse_two, gain_two_f, normed_two_grad)
     middle_grad = cotan + middle_norm_grad
     mixer_grad_bf = middle_grad.astype(BF16)
-    out_proj_grad = weight_grad(contract_rows(mixer_grad_bf, gated_bf), 1)
+    out_part = weight_part(contract_rows(mixer_grad_bf, gated_bf))
     gated_grad = jnp.dot(mixer_grad_bf, out_proj_t, preferred_element_type=F32).reshape(x_pre.shape)
     scan_grad = gated_grad * z_silu
     z_grad = jax.vjp(jax.nn.silu, z_gate)[1](gated_grad * scanned)[0]
+    z_grad_bf = z_grad.astype(BF16).reshape(tokens, inner)
+    in_z_part = weight_part(contract_rows(normed_bf, z_grad_bf))
     back_decay, back_adjoint, first_adjoint = scan.adjoint_ends(
         step_size, mix_out, scan_grad, rate_rows
+    )
+    first_adjoint, got_out, far_parts = together(first_adjoint, got_out, far_parts)
+    weight_blocks = lax.all_to_all(
+        expert_weight_parts(near_parts, far_parts), "dp", 0, 0, tiled=True
     )
     leaving = entering_pieces(back_decay[:, :, 0], first_adjoint, "ctx", True)
     in_sum, rate_sum, decay_sum, in_lanes, out_lanes = scan.adjoint(
         step_size, xconv, mix_in, mix_out, scan_grad, rate_rows, seg_start, back_decay, back_adjoint,
         leaving,
     )
+    in_sum, weight_blocks, out_part, in_z_part = together(in_sum, weight_blocks, out_part, in_z_part)
+    out_blocks = lax.all_to_all(
+        jnp.concatenate([halves_added(*out_part), halves_added(*in_z_part)], axis=1),
+        "dp", 0, 0, tiled=True,
+    )
+    router_prob = jax.nn.softmax(contract_cols(normed_two_bf, router_t), axis=-1)
+    gate_prob = jnp.sum(router_prob * onehot_int.astype(F32), axis=1) * keep
+    result = from_rows((middle + gate_prob[:, None] * landed(got_out)).astype(BF16))
     step_grad = rate_sum * (1.0 / LOG2E) + in_sum * xconv
     decay_log_grad = jnp.sum(decay_sum, axis=0) * decay_rate
     xconv_grad = in_sum * step_size + skip_row[0] * scan_grad
@@ -610,42 +775,48 @@
     for tap in range(taps - 1):
         ahead = taps - 1 - tap
         x_pre_grad = x_pre_grad + tap_weights[tap] * reaching[ahead : ahead + steps]
-    mixed_grad_bf = jnp.concatenate(
-        [
-            x_pre_grad.astype(BF16).reshape(tokens, inner),
-            z_grad.astype(BF16).reshape(tokens, inner),
-        ],
-        axis=1,
-    )
-    in_proj_grad = weight_grad(contract_rows(normed_bf, mixed_grad_bf), 2)
-    normed_grad = axis_sum(contract_cols(mixed_grad_bf, in_flat), "tp")
+    x_grad_bf = x_pre_grad.astype(BF16).reshape(tokens, inner)
+    in_x_part = weight_part(contract_rows(normed_bf, x_grad_bf))
+    in_x_part, out_blocks, weight_blocks = together(in_x_part, out_blocks, weight_blocks)
+    first_grad, second_grad = expert_weight_grads(weight_blocks, experts)
+    in_x_blocks = lax.all_to_all(halves_added(*in_x_part), "dp", 0, 0, tiled=True)
+    out_proj_grad, in_z_grad = weight_shards(out_blocks, 2)
+    normed_grad = axis_sum(
+        contract_cols(x_grad_bf, in_x) + contract_cols(z_grad_bf, in_z), "tp"
+    )
     values_norm_grad, gain_one_grad = rms_backward(values, inverse_one, gain_one_f, normed_grad)
     input_grad = from_rows((middle_grad + values_norm_grad).astype(BF16))
 
-    small_grads = jnp.concatenate(
-        [
-            gain_one_grad[None],
-            taps_grad,
-            shift_grad[None],
-            dt_proj_grad,
-            dt_shift_grad[None],
-            decay_log_grad,
-            skip_grad[None],
-            gain_two_grad[None],
-            router_grad_t,
-            x_proj_grad_t,
-        ],
-        axis=0,
-    )
-    small_grads = small_grads.reshape(small.shape[0], dp_count, shard).transpose(1, 0, 2)
-    small_grads = lax.psum_scatter(small_grads, "dp", scatter_dimension=0, tiled=True)[0]
-    small_grads = axis_sum(small_grads, "ctx")
+    in_x_grad = weight_shards(in_x_blocks, 1)[0]
+
+    def scattered(value):
+        value = value.reshape(value.shape[0], dp_count, shard).transpose(1, 0, 2)
+        return lax.psum_scatter(value, "dp", scatter_dimension=0, tiled=True)[0]
+
+    small_grads = scattered(
+        jnp.concatenate(
+            [
+                taps_grad,
+                shift_grad[None],
+                dt_proj_grad,
+                dt_shift_grad[None],
+                decay_log_grad,
+                skip_grad[None],
+                gain_two_grad[None],
+                router_grad_t,
+                x_proj_grad_t,
+            ],
+            axis=0,
+        )
+    )
+    small_grads, gain_one_part = together(small_grads, scattered(gain_one_grad[None]))
+    small_grads = axis_sum(jnp.concatenate([gain_one_part, small_grads], axis=0), "ctx")
     sums = [small_grads[bounds[i] : bounds[i + 1]] for i in range(len(bounds) - 1)]
     return (
         result,
         input_grad,
         sums[0][0],
-        in_proj_grad.reshape(shard, 2, inner),
+        jnp.stack([in_x_grad, in_z_grad], axis=1),
         sums[1],
         sums[2][0],
         sums[9].T,

time: 1240 us -> 1110 us (0.90)
  matrix products: 203 us -> 126 us
  blocking collectives: 93.1 us -> 30.7 us
  Pallas kernels: 183 us -> 230 us
  waiting for transfers between devices: 398 us -> 353 us
  other arithmetic: 152 us -> 166 us
    all_to_all x6 -> x4, waiting for transfers between devices: 118 us -> 0.01 us  [the longest x1 0.01 us: local(): lax.all_to_all(jnp.concatenate([halves_added(*out_part), halves_added(*in...]
    dot_general x5 -> x4, matrix products: 80 us -> 20 us  [the longest x2 8.97 us: slotted(): sent = jnp.dot(place, value, preferred_element_type=F32).astype(BF16)]
    all_to_all x1 -> x0, blocking collectives: 57.6 us -> none  [expert_exchange(): lax.all_to_all(value, 'dp', 0, 0, axis_index_groups=groups, tiled=True)]
    all_gather x2, waiting for transfers between devices: 38.5 us -> 91.6 us  [gathered(): got = lax.all_gather(jnp.concatenate(values, axis=1), 'dp')]
    pallas_call x0 -> x2, Pallas kernels: none -> 47.2 us  [expert_call(): pl.pallas_call(expert_kernel, grid=(count // block,), in_specs=[row_spec,...]
    reduce_scatter x1, waiting for transfers between devices: 53.3 us -> 14.9 us  [scattered(): return lax.psum_scatter(value, 'dp', scatter_dimension=0, tiled=True)[0]]
    all_gather x1 -> x0, blocking collectives: 35.4 us -> none  [local(): small_all = lax.all_gather(small, 'dp', axis=0)]
    ppermute x4, waiting for transfers between devices: 0.56 us -> 35.2 us  [passed_along(): lax.ppermute(value, axis, [(source, source + steps) for source in range(l...]
  transfers between devices with their start and end apart: 36 -> 38, of which waited for: 16 -> 16; matrix products, arithmetic and copies ran while one was open for 36% -> 30% of each run, Pallas kernels for 15% -> 19%
where the time goes in v2:
time: 1110 us; the launch traced here: 1100 us
  waiting for transfers between devices  353 us (32%)
  Pallas kernels  230 us (21%)
  other arithmetic  166 us (15%)
  matrix products  126 us (11%)
  local copies, waits for them, and re-layouts  117 us (11%)
  starting transfers between devices  64.6 us (6%)
  blocking collectives  30.7 us (3%)
  between operations  15.8 us (1%)
    pallas_call x4, Pallas kernels, call(): pl.pallas_call(kernel, grid=self.grid, in_specs=in_specs, out_specs=out_s...  183 us
    ppermute x23, waiting for transfers between devices, swapped(): return lax.ppermute(value, axis, [(0, 1), (1, 0)])  121 us
    all_gather x2, waiting for transfers between devices, gathered(): got = lax.all_gather(jnp.concatenate(values, axis=1), 'dp')  91.6 us
    all_to_all x4, waiting for transfers between devices, expert_exchange(): lax.all_to_all(value, 'dp', 0, 0, axis_index_groups=groups, tiled=True)  90.2 us
    dot_general x12, matrix products, contract_rows(): lax.dot_general(left_side, right_side, (((0,), (0,)), ((), ())), precisio...  64.9 us
    pallas_call x2, Pallas kernels, expert_call(): pl.pallas_call(expert_kernel, grid=(count // block,), in_specs=[row_spec,...  47.2 us
    ppermute x4, waiting for transfers between devices, passed_along(): lax.ppermute(value, axis, [(source, source + steps) for source in range(l...  35.2 us
    unnamed x1, blocking collectives  30.7 us
  transfers between devices with their start and end apart: 38, of which 16 were waited for; matrix products, arithmetic and copies ran while one was open for 30% of the time, Pallas kernels for 19%

profile of v2, /device:TPU:0, one launch (start us, length us, event | category | flops | bytes accessed | tf_op | source)
XLA Modules:
  0.0 1102.9 jit_solution(10182311171179926223)
XLA Ops:
  40.8 46.1 %all-gather.5.cloned.1.call-done = bf16[1152,1408]{1,0:T(8,128)(2,1)} async-done(((bf16[144,1408]{1,0:T(8,128)(2,1)}), bf16[1152,1408]{1,0:T(8,128)(2,1)}) %all-gather.5.cloned.1.call-update) | async-done | bytes 3244048 | tf_op jit(solution)/shard_map/all_gather | solution.py:437
  143.6 29.1 %shard_map.297 = (f32[2,16,8,1152]{3,2,1,0:T(8,128)}, f32[2,16,8,1152]{3,2,1,0:T(8,128)}, f32[2,16,1152]{2,1,0:T(8,128)}) custom-call(f32[64,2,8,1152]{3,2,1,0:T(8,128)} %compare_select_fusion.step_ref, f32[64,2,8,1152]{3,2,1,0:T(8,128)} %get-tuple-element.228.input_ref, f32[2,64,16,8,128]{4,3,2,1,0:T(8,128)} %broadcast_in_dim.28.mix_in_ref, ...), custom_call_target="tpu_custom_call" | custom-call | flops 94371840 | bytes 20922368 | tf_op jit(solution)/shard_map/pallas_call | solution.py:277
  174.1 45.5 %all-gather.7.cloned.1.call-done = bf16[576,2304]{1,0:T(8,128)(2,1)} async-done(((bf16[72,2304]{1,0:T(8,128)(2,1)}), bf16[576,2304]{1,0:T(8,128)(2,1)}) %all-gather.7.cloned.1.call-update) | async-done | bytes 2654224 | tf_op jit(solution)/shard_map/all_gather | solution.py:437
  240.0 15.4 %collective-permute-done.5 = bf16[8,72,1152]{2,1,0:T(8,128)(2,1)} collective-permute-done((bf16[8,72,1152]{2,1,0:T(8,128)(2,1)}, bf16[8,72,1152]{2,1,0:T(8,128)(2,1)}, u32[]{:S(2)}, u32[]{:S(2)}) %collective-permute-start.5) | collective-permute-done | bytes 1327136 | tf_op jit(solution)/shard_map/ppermute | solution.py:22
  259.0 24.8 %collective-permute-done.3 = bf16[8,72,1152]{2,1,0:T(8,128)(2,1)} collective-permute-done((bf16[8,72,1152]{2,1,0:T(8,128)(2,1)}, bf16[8,72,1152]{2,1,0:T(8,128)(2,1)}, u32[]{:S(2)}, u32[]{:S(2)}) %collective-permute-start.3) | collective-permute-done | bytes 1327136 | tf_op jit(solution)/shard_map/ppermute | solution.py:22
  290.8 36.6 %shard_map.298 = (f32[64,2,8,1152]{3,2,1,0:T(8,128)}, f32[2,16,8,1152]{3,2,1,0:T(8,128)}) custom-call(f32[64,2,8,1152]{3,2,1,0:T(8,128)} %compare_select_fusion.step_ref, f32[64,2,8,1152]{3,2,1,0:T(8,128)} %get-tuple-element.228.input_ref, f32[2,64,16,8,128]{4,3,2,1,0:T(8,128)} %broadcast_in_dim.28.mix_in_ref, ...), custom_call_target="tpu_custom_call" | custom-call | flops 132120576 | bytes 35209216 | tf_op jit(solution)/shard_map/pallas_call | solution.py:277
  331.6 7.3 multiply_convert_fusion.2
  338.9 19.9 %collective-permute-done.4 = bf16[8,288,768]{2,1,0:T(8,128)(2,1)} collective-permute-done((bf16[8,288,768]{2,1,0:T(8,128)(2,1)}, bf16[8,288,768]{2,1,0:T(8,128)(2,1)}, u32[]{:S(2)}, u32[]{:S(2)}) %collective-permute-start.4) | collective-permute-done | bytes 3538976 | tf_op jit(solution)/shard_map/ppermute | solution.py:22
  362.8 8.1 fusion.101
  394.2 54.2 %all-to-all-done.2 = bf16[8,128,1152]{2,1,0:T(8,128)(2,1)} async-done(((bf16[8,128,1152]{2,1,0:T(8,128)(2,1)}), bf16[8,128,1152]{2,1,0:T(8,128)(2,1)}, u32[]{:S(2)}, u32[]{:S(2)}) %all-to-all-start.2) | async-done | bytes 2359328 | tf_op jit(solution)/shard_map/all_to_all | solution.py:397
  453.3 23.5 %shard_map.300 = (f32[1024,1152]{1,0:T(8,128)}, f32[1024,1152]{1,0:T(8,128)}, f32[1024,8]{1,0:T(8,128)}, bf16[1024,1152]{1,0:T(8,128)(2,1)}, bf16[1024,768]{1,0:...) custom-call(bf16[1024,1152]{1,0:T(8,128)(2,1)} %collective-permute-done.7.rows_ref, ...), custom_call_target="tpu_custom_call" | custom-call | flops 14495514624 | bytes 29884416 | tf_op jit(solution)/shard_map/pallas_call | solution.py:373
  477.4 23.7 %shard_map.299 = (f32[1024,1152]{1,0:T(8,128)}, f32[1024,1152]{1,0:T(8,128)}, f32[1024,8]{1,0:T(8,128)}, bf16[1024,1152]{1,0:T(8,128)(2,1)}, bf16[1024,768]{1,0:...) custom-call(bf16[1024,1152]{1,0:T(8,128)(2,1)} %bitcast.43.rows_ref, ...), custom_call_target="tpu_custom_call" | custom-call | flops 14495514624 | bytes 29884416 | tf_op jit(solution)/shard_map/pallas_call | solution.py:373
  502.5 6.6 multiply_reduce_fusion.5
  521.4 9.3 fusion.34
  536.5 36.0 %all-to-all-done.3 = bf16[8,128,1152]{2,1,0:T(8,128)(2,1)} async-done(((bf16[8,128,1152]{2,1,0:T(8,128)(2,1)}), bf16[8,128,1152]{2,1,0:T(8,128)(2,1)}, u32[]{:S(2)}, u32[]{:S(2)}) %all-to-all-start.3) | async-done | bytes 2359328 | tf_op jit(solution)/shard_map/all_to_all | solution.py:397
  590.1 8.5 convolution_convert_fusion.2
  608.2 7.1 multiply_reduce_fusion
  615.2 28.3 %shard_map.301 = (f32[2,16,8,1152]{3,2,1,0:T(8,128)}, f32[2,16,8,1152]{3,2,1,0:T(8,128)}, f32[2,16,1152]{2,1,0:T(8,128)}) custom-call(f32[64,2,8,1152]{3,2,1,0:T(8,128)} %compare_select_fusion.step_ref, f32[2,64,16,8,128]{4,3,2,1,0:T(8,128)} %broadcast_in_dim.29.mix_out_ref, f32[64,2,8,1152]{3,2,1,0:T(8,128)} %get-tuple-element.218.grad_ref, ...), custom_call_target="tpu_custom_call" | custom-call | flops 94371840 | bytes 20922368 | tf_op jit(solution)/shard_map/pallas_call | solution.py:277
  643.5 19.5 %collective-permute-done.12 = bf16[1152,768]{1,0:T(8,128)(2,1)} collective-permute-done((bf16[1152,768]{1,0:T(8,128)(2,1)}, bf16[1152,768]{1,0:T(8,128)(2,1)}, u32[]{:S(2)}, u32[]{:S(2)}) %collective-permute-start.12) | collective-permute-done | bytes 1769504 | tf_op jit(solution)/shard_map/ppermute | solution.py:22
  709.9 8.1 fusion.104
  725.4 35.1 %collective-permute-done.15.enter_ref = f32[2,16,1152]{2,1,0:T(8,128)S(1)} collective-permute-done((f32[2,16,1152]{2,1,0:T(8,128)S(1)}, f32[2,16,1152]{2,1,0:T(8,128)S(1)}, u32[]{:S(2)}, u32[]{:S(2)}) %collective-permute-start.15) | collective-permute-done | bytes 147488 | tf_op jit(solution)/shard_map/ppermute | solution.py:28
  761.2 88.5 %shard_map.302 = (f32[64,2,8,1152]{3,2,1,0:T(8,128)}, f32[64,2,8,1152]{3,2,1,0:T(8,128)}, f32[2,16,1152]{2,1,0:T(8,128)}, f32[2,64,16,8,128]{4,3,2,1,0:T(8,128)}, f32[2,64,16,8,128]{4,3,2,1,0:T(8,128)}) custom-call(f32[64,2,8,1152]{3,2,1,0:T(8,128)} %compare_select_fusion.step_ref, f32[64,2,8,1152]{3,2,1,0:T(8,128)} %get-tuple-element.228.input_ref, ...), custom_call_target="tpu_custom_call" | custom-call | flops 377487360 | bytes 61571072 | tf_op jit(solution)/shard_map/pallas_call | solution.py:277
  849.7 6.7 reduce_sum.215
  858.1 6.7 reduce_sum.216
  883.7 9.0 multiply_reduce_fusion.1
  965.7 7.3 collective-permute-done.23
  985.6 6.5 fusion.18
  992.2 30.7 %all-reduce.1 = f32[8,1,144]{2,1,0:T(1,128)S(1)} all-reduce(f32[8,1,144]{2,1,0:T(1,128)S(1)} %transpose_reshape_broadcast_in_dim.3), channel_id=5, replica_groups=mesh['dp'=8,'ctx'=2,'tp'=2] {'dp'}, use_global_device_ids=true, to_apply=%region_25.26.clone | all-reduce | flops 1152 | bytes 9216
  1023.5 14.9 %reduce-scatter.2.cloned.1.call-done = f32[1,208,144]{1,2,0:T(8,128)} async-done(((f32[8,208,144]{1,2,0:T(8,128)}), f32[1,208,144]{1,2,0:T(8,128)}) %reduce-scatter.2.cloned.1.call-update) | async-done | bytes 119824 | tf_op jit(solution)/shard_map/reduce_scatter | solution.py:794
  1041.1 7.4 add_convert_fusion
  1050.4 18.5 %collective-permute-done.22 = f32[209,144]{0,1:T(8,128)S(1)} collective-permute-done((f32[209,144]{0,1:T(8,128)S(1)}, f32[209,144]{0,1:T(8,128)S(1)}, u32[]{:S(2)}, u32[]{:S(2)}) %collective-permute-start.22) | collective-permute-done | bytes 120416 | tf_op jit(solution)/shard_map/ppermute | solution.py:22
  1089.7 6.2 convert_bitcast_fusion
  (453 shorter events, 391.9 us)
Async XLA Ops:
  7.2 79.7 %all-gather.5.cloned.1.call-start = ((), (), s32[]{:S(2)}) async-start(), calls=%async_computation.10 | async-start | bytes 3649536 | tf_op jit(solution)/shard_map/all_gather | solution.py:437
  22.4 197.1 %all-gather.7.cloned.1.call-start = ((), (), s32[]{:S(2)}) async-start(), calls=%async_computation.11 | async-start | bytes 2985984 | tf_op jit(solution)/shard_map/all_gather | solution.py:437
  104.4 15.0 %collective-permute-start = (bf16[3,2,1,1152]{3,2,1,0:T(2,128)(2,1)S(1)}, bf16[3,2,1,1152]{3,2,1,0:T(2,128)(2,1)S(1)}, u32[]{:S(2)}, u32[]{:S(2)}) collective-permute-start(bf16[3,2,1,1152]{3,2,1,0:T(2,128)(2,1)S(1)} %slice.293), channel_id=1, source_target_pairs={{0,2},{1,3},{4,6},{5,7},{8,10},{9,11},{12,14},{13,15},{16,18},{17,... | collective-permute-start | bytes 41480 | tf_op jit(solution)/shard_map/ppermute | solution.py:28
  114.4 119.3 %all-to-all-start = ((bf16[8,288,768]{2,1,0:T(8,128)(2,1)}), bf16[8,288,768]{2,1,0:T(8,128)(2,1)}, u32[]{:S(2)}, u32[]{:S(2)}) async-start(bf16[8,288,768]{2,1,0:T(8,128)(2,1)} %slice_select_fusion), calls=%async_computation | async-start | bytes 7077888 | tf_op jit(solution)/shard_map/all_to_all | solution.py:414
  172.8 50.2 %collective-permute-start.2 = (f32[2,16,1152]{2,1,0:T(8,128)}, f32[2,16,1152]{2,1,0:T(8,128)S(1)}, u32[]{:S(2)}, u32[]{:S(2)}) collective-permute-start(f32[2,16,1152]{2,1,0:T(8,128)} %get-tuple-element.87), channel_id=1, source_target_pairs={{0,2},{1,3},{4,6},{5,7},{8,10},{9,11},{12,14},{13,15},{16,18},{17,... | collective-permute-start | bytes 442376 | tf_op jit(solution)/shard_map/ppermute | solution.py:28
  223.0 32.4 %collective-permute-start.5 = (bf16[8,72,1152]{2,1,0:T(8,128)(2,1)}, bf16[8,72,1152]{2,1,0:T(8,128)(2,1)}, u32[]{:S(2)}, u32[]{:S(2)}) collective-permute-start(bf16[8,72,1152]{2,1,0:T(8,128)(2,1)} %get-tuple-element.96), channel_id=1, source_target_pairs={{0,2},{2,0},{1,3},{3,1},{4,6},{6,4},{5,7},{7,5},{8,10},{10,8},{9,1... | collective-permute-start | bytes 3981320 | tf_op jit(solution)/shard_map/ppermute | solution.py:22
  227.3 56.6 %collective-permute-start.3 = (bf16[8,72,1152]{2,1,0:T(8,128)(2,1)}, bf16[8,72,1152]{2,1,0:T(8,128)(2,1)}, u32[]{:S(2)}, u32[]{:S(2)}) collective-permute-start(bf16[8,72,1152]{2,1,0:T(8,128)(2,1)} %get-tuple-element.92), channel_id=1, source_target_pairs={{0,2},{2,0},{1,3},{3,1},{4,6},{6,4},{5,7},{7,5},{8,10},{10,8},{9,1... | collective-permute-start | bytes 3981320 | tf_op jit(solution)/shard_map/ppermute | solution.py:22
  233.7 125.1 %collective-permute-start.4 = (bf16[8,288,768]{2,1,0:T(8,128)(2,1)}, bf16[8,288,768]{2,1,0:T(8,128)(2,1)}, u32[]{:S(2)}, u32[]{:S(2)}) collective-permute-start(bf16[8,288,768]{2,1,0:T(8,128)(2,1)} %all-to-all-done), channel_id=1, source_target_pairs={{0,2},{2,0},{1,3},{3,1},{4,6},{6,4},{5,7},{7,5},{8,10},{10,8},{9,1... | collective-permute-start | bytes 10616840 | tf_op jit(solution)/shard_map/ppermute | solution.py:22
  235.2 127.6 %all-to-all-start.1 = ((bf16[8,128,1152]{2,1,0:T(8,128)(2,1)}), bf16[8,128,1152]{2,1,0:T(8,128)(2,1)}, u32[]{:S(2)}, u32[]{:S(2)}) async-start(bf16[8,128,1152]{2,1,0:T(8,128)(2,1)} %bitcast.276), calls=%async_computation.1 | async-start | bytes 4718592 | tf_op jit(solution)/shard_map/all_to_all | solution.py:397
  389.5 59.0 %all-to-all-start.2 = ((bf16[8,128,1152]{2,1,0:T(8,128)(2,1)}), bf16[8,128,1152]{2,1,0:T(8,128)(2,1)}, u32[]{:S(2)}, u32[]{:S(2)}) async-start(bf16[8,128,1152]{2,1,0:T(8,128)(2,1)} %bitcast.277), calls=%async_computation.2 | async-start | bytes 4718592 | tf_op jit(solution)/shard_map/all_to_all | solution.py:397
  394.0 55.6 %collective-permute-start.8 = (bf16[1024,1152]{1,0:T(8,128)(2,1)}, bf16[1024,1152]{1,0:T(8,128)(2,1)}, u32[]{:S(2)}, u32[]{:S(2)}) collective-permute-start(bf16[1024,1152]{1,0:T(8,128)(2,1)} %bitcast.35.cotan_ref), channel_id=1, source_target_pairs={{0,1},{1,0},{2,3},{3,2},{4,5},{5,4},{6,7},{7,6},{8,9},{9,8},{10,11... | collective-permute-start | bytes 7077896 | tf_op jit(solution)/shard_map/ppermute | solution.py:22
  476.8 25.7 %collective-permute-start.10 = (f32[1024,1152]{1,0:T(8,128)}, f32[1024,1152]{1,0:T(8,128)}, u32[]{:S(2)}, u32[]{:S(2)}) collective-permute-start(f32[1024,1152]{1,0:T(8,128)} %get-tuple-element.105), channel_id=1, source_target_pairs={{0,1},{1,0},{2,3},{3,2},{4,5},{5,4},{6,7},{7,6},{8,9},{9,8},{10,11... | collective-permute-start | bytes 14155784 | tf_op jit(solution)/shard_map/ppermute | solution.py:22
  477.0 32.1 %collective-permute-start.9 = (f32[1024,1152]{1,0:T(8,128)}, f32[1024,1152]{1,0:T(8,128)S(1)}, u32[]{:S(2)}, u32[]{:S(2)}) collective-permute-start(f32[1024,1152]{1,0:T(8,128)} %get-tuple-element.103), channel_id=1, source_target_pairs={{0,1},{1,0},{2,3},{3,2},{4,5},{5,4},{6,7},{7,6},{8,9},{9,8},{10,11... | collective-permute-start | bytes 14155784 | tf_op jit(solution)/shard_map/ppermute | solution.py:22
  513.3 59.2 %all-to-all-start.3 = ((bf16[8,128,1152]{2,1,0:T(8,128)(2,1)}), bf16[8,128,1152]{2,1,0:T(8,128)(2,1)}, u32[]{:S(2)}, u32[]{:S(2)}) async-start(bf16[8,128,1152]{2,1,0:T(8,128)(2,1)} %bitcast.235), calls=%async_computation.3 | async-start | bytes 4718592 | tf_op jit(solution)/shard_map/all_to_all | solution.py:397
  578.6 20.6 %collective-permute-start.11 = (bf16[1024,1152]{1,0:T(8,128)(2,1)}, bf16[1024,1152]{1,0:T(8,128)(2,1)}, u32[]{:S(2)}, u32[]{:S(2)}) collective-permute-start(bf16[1024,1152]{1,0:T(8,128)(2,1)} %fusion.30), channel_id=1, source_target_pairs={{0,1},{1,0},{2,3},{3,2},{4,5},{5,4},{6,7},{7,6},{8,9},{9,8},{10,11... | collective-permute-start | bytes 7077896 | tf_op jit(solution)/shard_map/ppermute | solution.py:22
  583.8 59.7 %collective-permute-start.13 = (bf16[1152,768]{1,0:T(8,128)(2,1)}, bf16[1152,768]{1,0:T(8,128)(2,1)}, u32[]{:S(2)}, u32[]{:S(2)}) collective-permute-start(bf16[1152,768]{1,0:T(8,128)(2,1)} %convolution_convert_fusion.1), channel_id=1, source_target_pairs={{0,2},{2,0},{1,3},{3,1},{4,6},{6,4},{5,7},{7,5},{8,10},{10,8},{9,1... | collective-permute-start | bytes 5308424 | tf_op jit(solution)/shard_map/ppermute | solution.py:22
  585.3 77.8 %all-to-all-start.4 = ((bf16[8,128,1152]{2,1,0:T(8,128)(2,1)}), bf16[8,128,1152]{2,1,0:T(8,128)(2,1)}, u32[]{:S(2)}, u32[]{:S(2)}) async-start(bf16[8,128,1152]{2,1,0:T(8,128)(2,1)} %bitcast.237), calls=%async_computation.4 | async-start | bytes 4718592 | tf_op jit(solution)/shard_map/all_to_all | solution.py:397
  598.6 64.5 %collective-permute-start.12 = (bf16[1152,768]{1,0:T(8,128)(2,1)}, bf16[1152,768]{1,0:T(8,128)(2,1)}, u32[]{:S(2)}, u32[]{:S(2)}) collective-permute-start(bf16[1152,768]{1,0:T(8,128)(2,1)} %convolution_convert_fusion.2), channel_id=1, source_target_pairs={{0,2},{2,0},{1,3},{3,1},{4,6},{6,4},{5,7},{7,5},{8,10},{10,8},{9,1... | collective-permute-start | bytes 5308424 | tf_op jit(solution)/shard_map/ppermute | solution.py:22
  670.5 196.6 %all-to-all-start.5 = ((bf16[8,288,768]{2,1,0:T(8,128)(2,1)}), bf16[8,288,768]{2,1,0:T(8,128)(2,1)}, u32[]{:S(2)}, u32[]{:S(2)}) async-start(bf16[8,288,768]{2,1,0:T(8,128)(2,1)} %pad_maximum_fusion.2), calls=%async_computation.5 | async-start | bytes 7077888 | tf_op jit(solution)/shard_map/all_to_all | solution.py:728
  697.2 169.9 %collective-permute-start.17 = (bf16[8,72,1152]{2,1,0:T(8,128)(2,1)}, bf16[8,72,1152]{2,1,0:T(8,128)(2,1)}, u32[]{:S(2)}, u32[]{:S(2)}) collective-permute-start(bf16[8,72,1152]{2,1,0:T(8,128)(2,1)} %select_convert_fusion.1), channel_id=1, source_target_pairs={{0,2},{2,0},{1,3},{3,1},{4,6},{6,4},{5,7},{7,5},{8,10},{10,8},{9,1... | collective-permute-start | bytes 3981320 | tf_op jit(solution)/shard_map/ppermute | solution.py:22
  703.3 163.9 %collective-permute-start.16 = (bf16[8,72,1152]{2,1,0:T(8,128)(2,1)}, bf16[8,72,1152]{2,1,0:T(8,128)(2,1)}, u32[]{:S(2)}, u32[]{:S(2)}) collective-permute-start(bf16[8,72,1152]{2,1,0:T(8,128)(2,1)} %select_convert_fusion.2), channel_id=1, source_target_pairs={{0,2},{2,0},{1,3},{3,1},{4,6},{6,4},{5,7},{7,5},{8,10},{10,8},{9,1... | collective-permute-start | bytes 3981320 | tf_op jit(solution)/shard_map/ppermute | solution.py:22
  718.1 42.5 %collective-permute-start.15 = (f32[2,16,1152]{2,1,0:T(8,128)S(1)}, f32[2,16,1152]{2,1,0:T(8,128)S(1)}, u32[]{:S(2)}, u32[]{:S(2)}) collective-permute-start(f32[2,16,1152]{2,1,0:T(8,128)S(1)} %copy-done.66), channel_id=1, source_target_pairs={{2,0},{3,1},{6,4},{7,5},{10,8},{11,9},{14,12},{15,13},{18,16},{19,... | collective-permute-start | bytes 442376 | tf_op jit(solution)/shard_map/ppermute | solution.py:28
  725.4 193.7 %collective-permute-start.14 = (bf16[1024,1152]{1,0:T(8,128)(2,1)}, bf16[1024,1152]{1,0:T(8,128)(2,1)}, u32[]{:S(2)}, u32[]{:S(2)}) collective-permute-start(bf16[1024,1152]{1,0:T(8,128)(2,1)} %fusion.31), channel_id=1, source_target_pairs={{0,1},{1,0},{2,3},{3,2},{4,5},{5,4},{6,7},{7,6},{8,9},{9,8},{10,11... | collective-permute-start | bytes 7077896 | tf_op jit(solution)/shard_map/ppermute | solution.py:22
  893.7 11.3 %collective-permute-start.19 = (f32[3,2,1,1152]{3,2,1,0:T(1,128)S(1)}, f32[3,2,1,1152]{3,2,1,0:T(1,128)S(1)}, u32[]{:S(2)}, u32[]{:S(2)}) collective-permute-start(f32[3,2,1,1152]{3,2,1,0:T(1,128)S(1)} %slice.317), channel_id=1, source_target_pairs={{2,0},{3,1},{6,4},{7,5},{10,8},{11,9},{14,12},{15,13},{18,16},{19,... | collective-permute-start | bytes 82952 | tf_op jit(solution)/shard_map/ppermute | solution.py:28
  898.0 75.0 %all-to-all-start.6 = ((bf16[8,144,1152]{2,1,0:T(8,128)(2,1)}), bf16[8,144,1152]{2,1,0:T(8,128)(2,1)S(1)}, u32[]{:S(2)}, u32[]{:S(2)}) async-start(bf16[8,144,1152]{2,1,0:T(8,128)(2,1)} %pad_maximum_fusion.7), calls=%async_computation.7 | async-start | bytes 5308416 | tf_op jit(solution)/shard_map/all_to_all | solution.py:737
  904.0 134.4 %reduce-scatter.2.cloned.1.call-start = ((), (), s32[]{:S(2)}) async-start(), calls=%async_computation.9 | async-start | bytes 1327104 | tf_op jit(solution)/shard_map/reduce_scatter | solution.py:794
  917.2 68.3 %collective-permute-start.20 = (f32[1024,1152]{1,0:T(8,128)}, f32[1024,1152]{1,0:T(8,128)}, u32[]{:S(2)}, u32[]{:S(2)}) collective-permute-start(f32[1024,1152]{1,0:T(8,128)} %fusion.100), channel_id=1, source_target_pairs={{0,1},{1,0},{2,3},{3,2},{4,5},{5,4},{6,7},{7,6},{8,9},{9,8},{10,11... | collective-permute-start | bytes 14155784 | tf_op jit(solution)/shard_map/ppermute | solution.py:22
  940.2 32.8 %collective-permute-start.23 = (bf16[8,72,1152]{2,1,0:T(8,128)(2,1)}, bf16[8,72,1152]{2,1,0:T(8,128)(2,1)}, u32[]{:S(2)}, u32[]{:S(2)}) collective-permute-start(bf16[8,72,1152]{2,1,0:T(8,128)(2,1)} %select_convert_fusion), channel_id=1, source_target_pairs={{0,2},{2,0},{1,3},{3,1},{4,6},{6,4},{5,7},{7,5},{8,10},{10,8},{9,1... | collective-permute-start | bytes 3981320 | tf_op jit(solution)/shard_map/ppermute | solution.py:22
  973.0 113.2 %collective-permute-start.26 = (bf16[8,288,768]{2,1,0:T(8,128)(2,1)}, bf16[8,288,768]{2,1,0:T(8,128)(2,1)}, u32[]{:S(2)}, u32[]{:S(2)}) collective-permute-start(bf16[8,288,768]{2,1,0:T(8,128)(2,1)} %all-to-all-done.5), channel_id=1, source_target_pairs={{0,2},{2,0},{1,3},{3,1},{4,6},{6,4},{5,7},{7,5},{8,10},{10,8},{9,1... | collective-permute-start | bytes 10616840 | tf_op jit(solution)/shard_map/ppermute | solution.py:22
  978.2 95.7 %all-to-all-start.7 = ((bf16[8,72,1152]{2,1,0:T(8,128)(2,1)}), bf16[8,72,1152]{2,1,0:T(8,128)(2,1)}, u32[]{:S(2)}, u32[]{:S(2)}) async-start(bf16[8,72,1152]{2,1,0:T(8,128)(2,1)} %add_convert_fusion.5), calls=%async_computation.8 | async-start | bytes 2654208 | tf_op jit(solution)/shard_map/all_to_all | solution.py:782
  985.3 91.7 %collective-permute-start.25 = (f32[2,72,1152]{2,1,0:T(8,128)}, f32[2,72,1152]{2,1,0:T(8,128)S(1)}, u32[]{:S(2)}, u32[]{:S(2)}) collective-permute-start(f32[2,72,1152]{2,1,0:T(8,128)} %bitcast.86), channel_id=1, source_target_pairs={{0,2},{2,0},{1,3},{3,1},{4,6},{6,4},{5,7},{7,5},{8,10},{10,8},{9,1... | collective-permute-start | bytes 1990664 | tf_op jit(solution)/shard_map/ppermute | solution.py:22
  1039.6 29.4 %collective-permute-start.22 = (f32[209,144]{0,1:T(8,128)S(1)}, f32[209,144]{0,1:T(8,128)S(1)}, u32[]{:S(2)}, u32[]{:S(2)}) collective-permute-start(f32[209,144]{0,1:T(8,128)S(1)} %pad_maximum_fusion.12), channel_id=1, source_target_pairs={{0,2},{2,0},{1,3},{3,1},{4,6},{6,4},{5,7},{7,5},{8,10},{10,8},{9,1... | collective-permute-start | bytes 361160 | tf_op jit(solution)/shard_map/ppermute | solution.py:22
  (105 other events, 1417.9 us)
Sparse Core Ops, SparseCore 0:
  22.6 64.2 all-gather.4
  108.8 110.7 all-gather.6
  961.5 76.8 reduce-scatter.1

commit v3 on v2

--- a/solution.py
+++ b/solution.py
@@ -325,7 +325,7 @@
 
 
 def expert_kernel(
-    rows_ref, cotan_ref, router_ref, mask_ref, up_a, up_b, down_a, down_b,
+    rows_ref, cotan_ref, router_ref, mask_ref, up_a, down_a, up_b, down_b,
     out_ref, picked_ref, prob_ref, grad_ref, active_a, active_b, hidden_a, hidden_b,
 ):
     rows = rows_ref[...]
@@ -341,24 +341,25 @@
         (up_a, down_a, active_a, hidden_a),
         (up_b, down_b, active_b, hidden_b),
     ):
-        hidden = jnp.dot(rows, up[...], preferred_element_type=F32)
+        up, down = (value[...].reshape(-1, value.shape[2]) for value in (up, down))
+        hidden = jnp.dot(rows, up, preferred_element_type=F32)
         share = 0.5 + 0.5 * lax.erf(hidden * math.sqrt(0.5))
         slope = share + hidden * (jnp.exp(-0.5 * hidden * hidden) * (1.0 / math.sqrt(2 * math.pi)))
         active = (hidden * share).astype(BF16)
         active_ref[...] = active
-        hidden_grad = (jnp.dot(grad, down[...], preferred_element_type=F32) * slope).astype(BF16)
+        hidden_grad = (jnp.dot(grad, down, preferred_element_type=F32) * slope).astype(BF16)
         hidden_ref[...] = hidden_grad
-        out_part = contract_cols(active, down[...])
-        picked_part = contract_cols(hidden_grad, up[...])
+        out_part = contract_cols(active, down)
+        picked_part = contract_cols(hidden_grad, up)
         out = out_part if out is None else out + out_part
         picked = picked_part if picked is None else picked + picked_part
     out_ref[...] = out
     picked_ref[...] = picked
 
 
-def expert_call(rows, cotan, router_t, mask, ups, downs):
+def expert_call(rows, cotan, router_t, mask, halves):
     count, width = rows.shape
-    hidden = ups[0].shape[1]
+    hidden = halves[0].shape[2]
     block = math.gcd(count, 512)
     row_spec = pl.BlockSpec((block, width), lambda at: (at, 0))
     hidden_spec = pl.BlockSpec((block, hidden), lambda at: (at, 0))
@@ -367,13 +368,20 @@
     def whole(array):
         return pl.BlockSpec(array.shape, lambda at: (0, 0), pipeline_mode=pl.Buffered(1))
 
-    fixed = (router_t, mask, *ups, *downs)
+    def layer(both, at):
+        devices, rows, columns = both.shape
+        return pl.BlockSpec(
+            (devices, rows // 2, columns), lambda step: (0, at, 0), pipeline_mode=pl.Buffered(1)
+        )
+
+    fixed = (router_t, mask, halves[0], halves[0], halves[1], halves[1])
+    fixed_specs = [whole(router_t), whole(mask), *(layer(both, at) for both in halves for at in (0, 1))]
     wide, narrow = jax.ShapeDtypeStruct((count, width), F32), jax.ShapeDtypeStruct((count, width), BF16)
     inner = jax.ShapeDtypeStruct((count, hidden), BF16)
     return pl.pallas_call(
         expert_kernel,
         grid=(count // block,),
-        in_specs=[row_spec, row_spec, *(whole(array) for array in fixed)],
+        in_specs=[row_spec, row_spec, *fixed_specs],
         out_specs=[row_spec, row_spec, prob_spec, row_spec, *(hidden_spec,) * 4],
         out_shape=[
             wide, wide, jax.ShapeDtypeStruct((count, router_t.shape[0]), F32), narrow, *(inner,) * 4
@@ -415,43 +423,127 @@
 
 
 def own_expert(both):
-    count, rows = both.shape[0], both.shape[1] // 2
-
-    def layers(value):
-        return tuple(
-            value[:, at : at + rows].reshape(count * rows, value.shape[2]) for at in (0, rows)
-        )
-
     if lax.axis_size("ctx") == 2:
-        own, other = layers(both), layers(swapped(both, "ctx"))
-    else:
-        half = both.shape[2] // 2
-        own, other = layers(both[:, :, :half]), layers(both[:, :, half:])
-    return (own[0], other[0]), (own[1], other[1])
+        return both, swapped(both, "ctx")
+    half = both.shape[2] // 2
+    return both[:, :, :half], both[:, :, half:]
+
+
+def gather_kernel(count, parts, *refs):
+    ins, outs = refs[:parts], refs[parts : 2 * parts]
+    send_sem, recv_sem, own_sem = refs[2 * parts :]
+    places = count // 2
+    me = lax.axis_index("dp")
+    place, side = lax.div(me, 2), lax.rem(me, 2)
+    across = me + 1 - 2 * side
+    barrier = pltpu.get_barrier_semaphore()
+
+    def greet(device):
+        pl.semaphore_signal(
+            barrier, inc=1, device_id={"dp": device}, device_id_type=pl.DeviceIdType.MESH
+        )
+
+    greet(across)
+    for step in (-1, 1):
+        there = place + step
+
+        @pl.when((there >= 0) & (there < places))
+        def greet_place(step=step):
+            greet(me + 2 * step)
+
+    neighbours = 1 + (place > 0).astype(jnp.int32) + (place < places - 1).astype(jnp.int32)
+    pl.semaphore_wait(barrier, neighbours)
+
+    def copy(part, slot, kind, device, own):
+        return pltpu.make_async_remote_copy(
+            src_ref=ins[part] if own else outs[part].at[slot],
+            dst_ref=outs[part].at[slot],
+            send_sem=send_sem.at[kind, part, slot],
+            recv_sem=recv_sem.at[part, slot],
+            device_id={"dp": device},
+            device_id_type=pl.DeviceIdType.MESH,
+        )
+
+    def passed_on(slot, steps, own, act):
+        for step in steps:
+            there = place + step
+
+            @pl.when((there >= 0) & (there < places))
+            def along(step=step):
+                for part in range(parts):
+                    act(copy(part, slot, step + 1, me + 2 * step, own))
+
+        for part in range(parts):
+            act(copy(part, slot, 1, across, own))
+
+    def start(one):
+        one.start()
+
+    def sent(one):
+        one.wait_send()
+
+    mine = [
+        pltpu.make_async_copy(ins[part], outs[part].at[me], own_sem.at[part])
+        for part in range(parts)
+    ]
+    for one in mine:
+        one.start()
+    passed_on(me, (-1, 1), True, start)
+    for far in range(1, places):
+        for step in (-1, 1):
+            origin = place - step * far
+
+            @pl.when((origin >= 0) & (origin < places))
+            def forward(step=step, far=far):
+                slot = me - 2 * step * far
+                for part in range(parts):
+                    copy(part, slot, 1, across, False).wait_recv()
+                passed_on(slot, (step,), False, start)
+
+    for at in range(places):
+        for part in range(parts):
+            copy(part, 2 * at + 1 - side, 1, across, False).wait_recv()
+    for one in mine:
+        one.wait()
+    passed_on(me, (-1, 1), True, sent)
+    for far in range(1, places):
+        for step in (-1, 1):
+            origin = place - step * far
+
+            @pl.when((origin >= 0) & (origin < places))
+            def forwarded(step=step, far=far):
+                passed_on(me - 2 * step * far, (step,), False, sent)
 
 
 def gathered(*values):
-    bounds = [0]
-    for value in values:
-        bounds.append(bounds[-1] + value.shape[1])
-    got = lax.all_gather(jnp.concatenate(values, axis=1), "dp")
-    return [got[:, :, bounds[i] : bounds[i + 1]] for i in range(len(values))]
-
-
-def half_gathered(*values):
-    if lax.axis_size("ctx") == 2:
-        half = values[0].shape[0] // 2
-        values = [by_ctx(value[:half], value[half:])[0] for value in values]
-    return gathered(*values)
-
-
-def half_joined(*values):
-    joined = []
-    for value in values:
-        if lax.axis_size("ctx") == 2:
-            value = jnp.concatenate(by_ctx(value, swapped(value, "ctx")), axis=1)
-        joined.append(value.reshape(value.shape[0] * value.shape[1], value.shape[2]))
-    return joined
+    count = lax.axis_size("dp")
+    parts = len(values)
+    anywhere = pl.BlockSpec(memory_space=pl.ANY)
+    size = sum(math.prod(value.shape) * 2 for value in values)
+    return pl.pallas_call(
+        partial(gather_kernel, count, parts),
+        in_specs=[anywhere] * parts,
+        out_specs=[anywhere] * parts,
+        out_shape=[jax.ShapeDtypeStruct((count, *value.shape), value.dtype) for value in values],
+        scratch_shapes=[
+            pltpu.SemaphoreType.DMA((3, parts, count)),
+            pltpu.SemaphoreType.DMA((parts, count)),
+            pltpu.SemaphoreType.DMA((parts,)),
+        ],
+        compiler_params=pltpu.CompilerParams(collective_id=0, has_side_effects=True),
+        cost_estimate=pl.CostEstimate(
+            flops=0, transcendentals=0, bytes_accessed=2 * count * size
+        ),
+    )(*values)
+
+
+def other_joined(own, first_shard, second_shard):
+    count = lax.axis_size("ctx")
+    if count == 2:
+        return by_ctx(own, swapped(own, "ctx"))
+    del first_shard, second_shard
+    every = lax.all_gather(own, "ctx")
+    return every[0], every[1]
 
 
 def halves_sent(blocks):
@@ -499,17 +591,21 @@
     return jnp.concatenate(parts, axis=1)
 
 
-def expert_weight_grads(blocks, experts):
+def expert_weight_halves(blocks, experts):
     count = lax.axis_size("dp")
     if count != experts:
         blocks = jnp.sum(
             blocks.reshape(count // experts, experts, *blocks.shape[1:]).astype(F32), axis=0
         ).astype(BF16)
     if lax.axis_size("ctx") == 2:
-        first, second = by_ctx(blocks, swapped(blocks, "ctx"))
-        joined = jnp.concatenate([first, second], axis=2)
-    else:
-        joined = lax.all_gather(blocks, "ctx", axis=2, tiled=True)
+        return blocks, swapped(blocks, "ctx")
+    return blocks, lax.all_gather(blocks, "ctx", axis=2, tiled=True)
+
+
+def expert_weight_grads(blocks, far_blocks):
+    joined = far_blocks
+    if lax.axis_size("ctx") == 2:
+        joined = jnp.concatenate(by_ctx(blocks, far_blocks), axis=2)
     shard = joined.shape[1] // 2
     return joined[:, :shard].astype(F32), joined[:, shard:].astype(F32)
 
@@ -571,32 +667,36 @@
         value = value.reshape(steps, chains, SEGMENTS, -1).transpose(1, 2, 0, 3)
         return value.reshape(batches, seqs, length, -1)
 
-    small = jnp.concatenate(
-        [
-            norm1_gain[None],
-            conv_weight,
-            conv_bias[None],
-            dt_weight,
-            dt_bias[None],
-            decay_log,
-            skip_weight[None],
-            norm2_gain[None],
-            router_weight.T,
-            xproj_weight.T,
-        ],
-        axis=0,
+    pieces = [
+        norm1_gain[None],
+        conv_weight,
+        conv_bias[None],
+        dt_weight,
+        dt_bias[None],
+        decay_log,
+        skip_weight[None],
+        norm2_gain[None],
+        router_weight.T,
+        xproj_weight.T,
+    ]
+    bounds = [0]
+    for piece in pieces:
+        bounds.append(bounds[-1] + piece.shape[0])
+    small = sum(
+        jnp.pad(piece, ((low, bounds[-1] - high), (0, 0)))
+        for piece, low, high in zip(pieces, bounds, bounds[1:])
     )
     kinds = small.shape[0]
     small_wide = jnp.pad(small.T, ((0, 0), (0, -kinds % LANES)))
-    in_x, small_all = gathered(in_weight[:, 0], small_wide)
+    in_x, small_all, later = gathered(
+        in_weight[:, 0], small_wide, by_ctx(out_weight.T, in_weight[:, 1])[0]
+    )
     in_x = in_x.reshape(dp_count * shard, inner)
+    later = later.reshape(dp_count * shard, inner)
     small_all = small_all.reshape(dp_count * shard, -1)[:, :kinds].T
-    small_all, out_shard, in_z_shard, up_shards, down_shards = together(
-        small_all, out_weight.T, in_weight[:, 1], fc1_weight, fc2_weight.transpose(0, 2, 1)
-    )
-    bounds = [0]
-    for count in (1, taps, 1, low_rank, 1, states, 1, 1, experts, low_rank + 2 * states):
-        bounds.append(bounds[-1] + count)
+    small_all, up_shards, down_shards = together(
+        small_all, fc1_weight, fc2_weight.transpose(0, 2, 1)
+    )
     pieces = [small_all[bounds[i] : bounds[i + 1]] for i in range(len(bounds) - 1)]
     gain_one_f = pieces[0].astype(F32)
     tap_weights = pieces[1].astype(F32)
@@ -609,7 +709,6 @@
     router_t = pieces[8]
     x_proj_t = pieces[9]
     rate_rows = jnp.broadcast_to((decay_rate * LOG2E)[:, None, :], (states, SEGMENTS, inner))
-    later_halves = half_gathered(out_shard, in_z_shard)
     expert_blocks = own_expert_blocks(up_shards, down_shards)
 
     route = to_rows(expert_ids)[:, 0]
@@ -643,6 +742,8 @@
     x_pre = x_pre.reshape(steps, chains, SEGMENTS, inner)
     tail = x_pre[steps - taps + 1 :]
     edge_in = passed_along(tail[:, :, SEGMENTS - 1 :], "ctx", 1)
+    edge_in, later = together(edge_in, later)
+    out_proj_t, in_z = other_joined(later, out_weight.T, in_weight[:, 1])
     halo = jnp.concatenate([edge_in, tail[:, :, : SEGMENTS - 1]], axis=2)
     extended = jnp.concatenate([halo, x_pre], axis=0).astype(F32)
     conv_pre = jnp.broadcast_to(conv_shift[0], x_pre.shape)
@@ -664,11 +765,10 @@
     step_size = jax.nn.softplus(dt_pre)
     seg_decay, seg_state, last_state = scan.ends(step_size, xconv, mix_in, rate_rows)
     seg_state, sent_cotan, expert_blocks = together(seg_state, sent_cotan, expert_blocks)
-    ups, downs = own_expert(expert_blocks)
     slot_cotan = exchanged(sent_cotan)
     entering = entering_pieces(seg_decay[:, :, SEGMENTS - 1], last_state, "ctx", False)
-    entering, later_halves = together(entering, later_halves)
-    out_proj_t, in_z = half_joined(*later_halves)
+    entering, expert_blocks = together(entering, expert_blocks)
+    halves = own_expert(expert_blocks)
     scan_out, seg_start = scan.run(
         step_size, xconv, mix_in, mix_out, rate_rows, seg_decay, seg_state, entering
     )
@@ -676,7 +776,7 @@
     scanned = scan_out + skip_row[0] * xconv
     z_silu = jax.nn.silu(z_gate)
     gated_bf = (scanned * z_silu).astype(BF16).reshape(tokens, inner)
-    gated_bf, slot_cotan, ups, downs = together(gated_bf, slot_cotan, ups, downs)
+    gated_bf, slot_cotan = together(gated_bf, slot_cotan)
     middle = values + axis_sum(contract_cols(gated_bf, out_proj_t), "tp")
 
     normed_two, inverse_two = rms_forward(middle, gain_two_f)
@@ -686,8 +786,8 @@
         jnp.arange(experts, dtype=jnp.int32) == lax.rem(lax.axis_index("dp"), experts)
     ).astype(F32)[None, :]
     far_rows, far_cotan = swapped(own_rows, "tp"), swapped(slot_cotan, "tp")
-    far = expert_call(far_rows, far_cotan, router_t, expert_mask, ups, downs)
-    near = expert_call(own_rows, slot_cotan, router_t, expert_mask, ups, downs)
+    far = expert_call(far_rows, far_cotan, router_t, expert_mask, halves)
+    near = expert_call(own_rows, slot_cotan, router_t, expert_mask, halves)
     slot_out = near[0] + swapped(far[0], "tp")
     picked_grad = near[1] + swapped(far[1], "tp")
     slot_prob = near[2]
@@ -715,12 +815,12 @@
     middle_norm_grad, gain_two_grad = rms_backward(middle, inverse_two, gain_two_f, normed_two_grad)
     middle_grad = cotan + middle_norm_grad
     mixer_grad_bf = middle_grad.astype(BF16)
-    out_part = weight_part(contract_rows(mixer_grad_bf, gated_bf))
+    out_grad_product = contract_rows(mixer_grad_bf, gated_bf)
     gated_grad = jnp.dot(mixer_grad_bf, out_proj_t, preferred_element_type=F32).reshape(x_pre.shape)
     scan_grad = gated_grad * z_silu
     z_grad = jax.vjp(jax.nn.silu, z_gate)[1](gated_grad * scanned)[0]
     z_grad_bf = z_grad.astype(BF16).reshape(tokens, inner)
-    in_z_part = weight_part(contract_rows(normed_bf, z_grad_bf))
+    in_z_product = contract_rows(normed_bf, z_grad_bf)
     back_decay, back_adjoint, first_adjoint = scan.adjoint_ends(
         step_size, mix_out, scan_grad, rate_rows
     )
@@ -729,6 +829,8 @@
         expert_weight_parts(near_parts, far_parts), "dp", 0, 0, tiled=True
     )
     leaving = entering_pieces(back_decay[:, :, 0], first_adjoint, "ctx", True)
+    leaving, out_grad_product, in_z_product = together(leaving, out_grad_product, in_z_product)
+    out_part, in_z_part = weight_part(out_grad_product), weight_part(in_z_product)
     in_sum, rate_sum, decay_sum, in_lanes, out_lanes = scan.adjoint(
         step_size, xconv, mix_in, mix_out, scan_grad, rate_rows, seg_start, back_decay, back_adjoint,
         leaving,
@@ -769,6 +871,8 @@
     shift_grad = jnp.sum(conv_grad, axis=(0, 1, 2))
     head = conv_grad[: taps - 1]
     edge_back = passed_along(head[:, :, :1], "ctx", -1)
+    edge_back, weight_blocks = together(edge_back, weight_blocks)
+    weight_blocks, far_blocks = expert_weight_halves(weight_blocks, experts)
     later = jnp.concatenate([head[:, :, 1:], edge_back], axis=2)
     reaching = jnp.concatenate([conv_grad, later], axis=0)
     x_pre_grad = tap_weights[taps - 1] * conv_grad
@@ -776,10 +880,23 @@
         ahead = taps - 1 - tap
         x_pre_grad = x_pre_grad + tap_weights[tap] * reaching[ahead : ahead + steps]
     x_grad_bf = x_pre_grad.astype(BF16).reshape(tokens, inner)
-    in_x_part = weight_part(contract_rows(normed_bf, x_grad_bf))
-    in_x_part, out_blocks, weight_blocks = together(in_x_part, out_blocks, weight_blocks)
-    first_grad, second_grad = expert_weight_grads(weight_blocks, experts)
-    in_x_blocks = lax.all_to_all(halves_added(*in_x_part), "dp", 0, 0, tiled=True)
+    small_grads = jnp.concatenate(
+        [
+            taps_grad,
+            shift_grad[None],
+            dt_proj_grad,
+            dt_shift_grad[None],
+            decay_log_grad,
+            skip_grad[None],
+            gain_two_grad[None],
+            router_grad_t,
+            x_proj_grad_t,
+        ],
+        axis=0,
+    )
+    small_grads = small_grads.reshape(-1, dp_count, shard).transpose(1, 0, 2)
+    x_grad_bf, out_blocks, small_grads = together(x_grad_bf, out_blocks, small_grads)
+    small_grads = lax.psum_scatter(small_grads, "dp", scatter_dimension=0, tiled=True)[0]
     out_proj_grad, in_z_grad = weight_shards(out_blocks, 2)
     normed_grad = axis_sum(
         contract_cols(x_grad_bf, in_x) + contract_cols(z_grad_bf, in_z), "tp"
@@ -787,30 +904,22 @@
     values_norm_grad, gain_one_grad = rms_backward(values, inverse_one, gain_one_f, normed_grad)
     input_grad = from_rows((middle_grad + values_norm_grad).astype(BF16))
 
-    in_x_grad = weight_shards(in_x_blocks, 1)[0]
-
-    def scattered(value):
-        value = value.reshape(value.shape[0], dp_count, shard).transpose(1, 0, 2)
-        return lax.psum_scatter(value, "dp", scatter_dimension=0, tiled=True)[0]
-
-    small_grads = scattered(
-        jnp.concatenate(
-            [
-                taps_grad,
-                shift_grad[None],
-                dt_proj_grad,
-                dt_shift_grad[None],
-                decay_log_grad,
-                skip_grad[None],
-                gain_two_grad[None],
-                router_grad_t,
-                x_proj_grad_t,
-            ],
-            axis=0,
-        )
-    )
-    small_grads, gain_one_part = together(small_grads, scattered(gain_one_grad[None]))
-    small_grads = axis_sum(jnp.concatenate([gain_one_part, small_grads], axis=0), "ctx")
+    in_x_part = contract_rows(normed_bf, x_grad_bf).astype(BF16).reshape(dp_count, shard, inner)
+    gain_row = gain_one_grad.reshape(dp_count, 1, shard)
+    gain_high = gain_row.astype(BF16)
+    gain_low = (gain_row - gain_high.astype(F32)).astype(BF16)
+    gain_rows = jnp.concatenate([gain_high, gain_low], axis=1)
+    gain_rows = jnp.pad(gain_rows, ((0, 0), (0, 6), (0, inner - shard)))
+    in_x_blocks = lax.all_to_all(
+        jnp.concatenate([in_x_part, gain_rows], axis=1), "dp", 0, 0, tiled=True
+    )
+    far_blocks, in_x_blocks = together(far_blocks, in_x_blocks)
+    first_grad, second_grad = expert_weight_grads(weight_blocks, far_blocks)
+    in_x_sums = axis_sum(jnp.sum(in_x_blocks.astype(F32), axis=0), "ctx")
+    in_x_grad = in_x_sums[:shard]
+    gain_one_grad = in_x_sums[shard : shard + 1, :shard] + in_x_sums[shard + 1 : shard + 2, :shard]
+    small_grads, in_x_blocks = together(small_grads, in_x_blocks)
+    small_grads = jnp.concatenate([gain_one_grad, axis_sum(small_grads, "ctx")], axis=0)
     sums = [small_grads[bounds[i] : bounds[i + 1]] for i in range(len(bounds) - 1)]
     return (
         result,

time: 1110 us -> 1020 us (0.919)
  waiting for transfers between devices: 353 us -> 247 us
  Pallas kernels: 230 us -> 302 us
  blocking collectives: 30.7 us -> 0 us
  local copies, waits for them, and re-layouts: 117 us -> 92.1 us
    all_gather x2 -> x0, waiting for transfers between devices: 91.6 us -> none  [gathered(): got = lax.all_gather(jnp.concatenate(values, axis=1), 'dp')]
    pallas_call x0 -> x1, Pallas kernels: none -> 72.2 us  [gathered(): pl.pallas_call(partial(gather_kernel, count, parts), in_specs=[anywhere]...]
    ppermute x4, waiting for transfers between devices: 35.2 us -> 0.39 us  [passed_along(): lax.ppermute(value, axis, [(source, source + steps) for source in range(l...]
    unnamed x1 -> x0, blocking collectives: 30.7 us -> none
    ppermute x23 -> x21, waiting for transfers between devices: 121 us -> 138 us  [swapped(): return lax.ppermute(value, axis, [(0, 1), (1, 0)])]
    slice x6 -> x1, local copies, waits for them, and re-layouts: 15.7 us -> 0.28 us  [the longest x2 8.16 us: layers(): value[:, at:at + rows].reshape(count * rows, value.shape[2])]
    all_to_all x1, waiting for transfers between devices: 0.01 us -> 15.2 us  [local(): lax.all_to_all(jnp.concatenate([halves_added(*out_part), halves_added(*in...]
    reduce_scatter x1, waiting for transfers between devices: 14.9 us -> 0.01 us  [local(): lax.psum_scatter(small_grads, 'dp', scatter_dimension=0, tiled=True)[0]]
  transfers between devices with their start and end apart: 38 -> 34, of which waited for: 16 -> 12; matrix products, arithmetic and copies ran while one was open for 30% -> 27% of each run, Pallas kernels for 19% -> 20%
where the time goes in v3:
time: 1020 us; the launch traced here: 1010 us
  Pallas kernels  302 us (30%)
  waiting for transfers between devices  247 us (24%)
  other arithmetic  159 us (16%)
  matrix products  132 us (13%)
  local copies, waits for them, and re-layouts  92.1 us (9%)
  starting transfers between devices  61.9 us (6%)
  between operations  16.1 us (2%)
    pallas_call x4, Pallas kernels, call(): pl.pallas_call(kernel, grid=self.grid, in_specs=in_specs, out_specs=out_s...  183 us
    ppermute x21, waiting for transfers between devices, swapped(): return lax.ppermute(value, axis, [(0, 1), (1, 0)])  138 us
    all_to_all x4, waiting for transfers between devices, expert_exchange(): lax.all_to_all(value, 'dp', 0, 0, axis_index_groups=groups, tiled=True)  87.4 us
    pallas_call x1, Pallas kernels, gathered(): pl.pallas_call(partial(gather_kernel, count, parts), in_specs=[anywhere]...  72.2 us
    dot_general x12, matrix products, contract_rows(): lax.dot_general(left_side, right_side, (((0,), (0,)), ((), ())), precisio...  67.7 us
    pallas_call x2, Pallas kernels, expert_call(): pl.pallas_call(expert_kernel, grid=(count // block,), in_specs=[row_spec,...  47.3 us
    dot_general x6, matrix products, contract_cols(): lax.dot_general(left_side, right_side, (((1,), (1,)), ((), ())), precisio...  27.2 us
    all_to_all x4, starting transfers between devices, expert_exchange(): lax.all_to_all(value, 'dp', 0, 0, axis_index_groups=groups, tiled=True)  21.2 us
  transfers between devices with their start and end apart: 34, of which 12 were waited for; matrix products, arithmetic and copies ran while one was open for 27% of the time, Pallas kernels for 20%

profile of v3, /device:TPU:0, one launch (start us, length us, event | category | flops | bytes accessed | tf_op | source)
XLA Modules:
  0.0 1010.7 jit_solution(6650455081769519369)
XLA Ops:
  22.6 72.2 %shard_map.297 = (bf16[8,144,1152]{2,1,0:T(8,128)(2,1)}, bf16[8,144,256]{2,1,0:T(8,128)(2,1)}, bf16[8,144,1152]{2,1,0:T(8,128)(2,1)}) custom-call(bf16[144,1152]{1,0:T(8,128)(2,1)} %bitcast.257, bf16[144,256]{1,0:T(8,128)(2,1)} %pad.58.refs_1_, bf16[144,1152]{1,0:T(8,128)(2,1)} %fusion.63.refs_2_), custom_call_target="tpu_custom_call" | custom-call | bytes 11796480 | tf_op jit(solution)/shard_map/pallas_call | solution.py:523
  156.8 29.0 %shard_map.298 = (f32[2,16,8,1152]{3,2,1,0:T(8,128)}, f32[2,16,8,1152]{3,2,1,0:T(8,128)}, f32[2,16,1152]{2,1,0:T(8,128)}) custom-call(f32[64,2,8,1152]{3,2,1,0:T(8,128)} %compare_select_fusion.step_ref, f32[64,2,8,1152]{3,2,1,0:T(8,128)} %get-tuple-element.247.input_ref, f32[2,64,16,8,128]{4,3,2,1,0:T(8,128)} %broadcast_in_dim.28.mix_in_ref, ...), custom_call_target="tpu_custom_call" | custom-call | flops 94371840 | bytes 20922368 | tf_op jit(solution)/shard_map/pallas_call | solution.py:277
  205.9 36.7 %shard_map.299 = (f32[64,2,8,1152]{3,2,1,0:T(8,128)}, f32[2,16,8,1152]{3,2,1,0:T(8,128)}) custom-call(f32[64,2,8,1152]{3,2,1,0:T(8,128)} %compare_select_fusion.step_ref, f32[64,2,8,1152]{3,2,1,0:T(8,128)} %get-tuple-element.247.input_ref, f32[2,64,16,8,128]{4,3,2,1,0:T(8,128)} %broadcast_in_dim.28.mix_in_ref, ...), custom_call_target="tpu_custom_call" | custom-call | flops 132120576 | bytes 35209216 | tf_op jit(solution)/shard_map/pallas_call | solution.py:277
  242.6 10.8 %multiply_convert_fusion.2 = (bf16[64,2,8,1152]{3,2,1,0:T(8,128)(2,1)}, f32[64,2,8,1152]{3,2,1,0:T(8,128)}) fusion(f32[64,2,8,1152]{3,2,1,0:T(8,128)} %get-tuple-element.97, bf16[64,2,8,1152]{3,2,1,0:T(8,128)(2,1)S(1)} %get-tuple-element.248, f32[1152]{0:T(1024)S(1)} %get-tuple-element.226, bf16[1152,1152]{1,0:T(8,128)(2,1)} %collective-permute-done.3, ...), kind=kOutput, calls=%fused_computation.57 | convolution fusion | flops 2729852928 | bytes 21828096 | tf_op jit(solution)/shard_map/dot_general | solution.py:775
  285.5 51.8 %all-to-all-done.2 = bf16[8,128,1152]{2,1,0:T(8,128)(2,1)} async-done(((bf16[8,128,1152]{2,1,0:T(8,128)(2,1)}), bf16[8,128,1152]{2,1,0:T(8,128)(2,1)}, u32[]{:S(2)}, u32[]{:S(2)}) %all-to-all-start.2) | async-done | bytes 2359328 | tf_op jit(solution)/shard_map/all_to_all | solution.py:405
  338.4 23.9 %collective-permute-done.5.up_b.down_b = bf16[8,288,768]{2,1,0:T(8,128)(2,1)} collective-permute-done((bf16[8,288,768]{2,1,0:T(8,128)(2,1)}, bf16[8,288,768]{2,1,0:T(8,128)(2,1)}, u32[]{:S(2)}, u32[]{:S(2)}) %collective-permute-start.5) | collective-permute-done | bytes 3538976 | tf_op jit(solution)/shard_map/ppermute | solution.py:22
  362.3 23.5 %shard_map.301 = (f32[1024,1152]{1,0:T(8,128)}, f32[1024,1152]{1,0:T(8,128)}, f32[1024,8]{1,0:T(8,128)}, bf16[1024,1152]{1,0:T(8,128)(2,1)}, bf16[1024,768]{1,0:...) custom-call(bf16[1024,1152]{1,0:T(8,128)(2,1)} %collective-permute-done.6.rows_ref, ...), custom_call_target="tpu_custom_call" | custom-call | flops 14495514624 | bytes 29884416 | tf_op jit(solution)/shard_map/pallas_call | solution.py:381
  386.4 23.7 %shard_map.300 = (f32[1024,1152]{1,0:T(8,128)}, f32[1024,1152]{1,0:T(8,128)}, f32[1024,8]{1,0:T(8,128)}, bf16[1024,1152]{1,0:T(8,128)(2,1)}, bf16[1024,768]{1,0:...) custom-call(bf16[1024,1152]{1,0:T(8,128)(2,1)} %bitcast.38.rows_ref, ...), custom_call_target="tpu_custom_call" | custom-call | flops 14495514624 | bytes 29884416 | tf_op jit(solution)/shard_map/pallas_call | solution.py:381
  411.6 6.6 multiply_reduce_fusion.5
  423.0 6.2 all-to-all-start.3
  432.5 9.4 fusion.31
  447.7 35.6 %all-to-all-done.3 = bf16[8,128,1152]{2,1,0:T(8,128)(2,1)} async-done(((bf16[8,128,1152]{2,1,0:T(8,128)(2,1)}), bf16[8,128,1152]{2,1,0:T(8,128)(2,1)}, u32[]{:S(2)}, u32[]{:S(2)}) %all-to-all-start.3) | async-done | bytes 2359328 | tf_op jit(solution)/shard_map/all_to_all | solution.py:405
  483.4 6.2 fusion.27
  496.8 7.7 convolution_convert_fusion.3
  519.4 7.4 fusion.54
  531.8 28.3 %shard_map.302 = (f32[2,16,8,1152]{3,2,1,0:T(8,128)}, f32[2,16,8,1152]{3,2,1,0:T(8,128)}, f32[2,16,1152]{2,1,0:T(8,128)}) custom-call(f32[64,2,8,1152]{3,2,1,0:T(8,128)} %compare_select_fusion.step_ref, f32[2,64,16,8,128]{4,3,2,1,0:T(8,128)} %broadcast_in_dim.29.mix_out_ref, f32[64,2,8,1152]{3,2,1,0:T(8,128)} %get-tuple-element.239.grad_ref, ...), custom_call_target="tpu_custom_call" | custom-call | flops 94371840 | bytes 20922368 | tf_op jit(solution)/shard_map/pallas_call | solution.py:277
  560.1 14.2 %collective-permute-done.11 = bf16[1152,768]{1,0:T(8,128)(2,1)} collective-permute-done((bf16[1152,768]{1,0:T(8,128)(2,1)}, bf16[1152,768]{1,0:T(8,128)(2,1)}, u32[]{:S(2)}, u32[]{:S(2)}) %collective-permute-start.11) | collective-permute-done | bytes 1769504 | tf_op jit(solution)/shard_map/ppermute | solution.py:22
  592.5 8.2 convolution_bitcast_fusion
  620.7 89.0 %shard_map.303 = (f32[64,2,8,1152]{3,2,1,0:T(8,128)}, f32[64,2,8,1152]{3,2,1,0:T(8,128)}, f32[2,16,1152]{2,1,0:T(8,128)}, f32[2,64,16,8,128]{4,3,2,1,0:T(8,128)}, f32[2,64,16,8,128]{4,3,2,1,0:T(8,128)}) custom-call(f32[64,2,8,1152]{3,2,1,0:T(8,128)} %compare_select_fusion.step_ref, f32[64,2,8,1152]{3,2,1,0:T(8,128)} %get-tuple-element.247.input_ref, ...), custom_call_target="tpu_custom_call" | custom-call | flops 377487360 | bytes 61571072 | tf_op jit(solution)/shard_map/pallas_call | solution.py:277
  709.7 6.7 reduce_sum.215
  718.0 6.7 reduce_sum.216
  729.1 6.9 slice_select_fusion.1
  771.5 15.2 %multiply_reduce_fusion.1 = (f32[1152]{0:T(1024)S(1)}, f32[1152]{0:T(1024)S(1)}, f32[1152]{0:T(1024)S(1)}, f32[1152]{0:T(1024)S(1)}, f32[1152]{0:T(1024)S(1)}, /*index=5*/f32[64,2,8,1152]{3,2,1,0:T(8,128)S(1)}) fusion(f32[67,2,8,1152]{3,2,1,0:T(8,128)} %copy-done, f32[64,2,8,1152]{3,2,1,0:T(8,128)} %get-tuple-element.249, ...), kind=kLoop, calls=%fused_computation.47 | loop fusion | flops 33024384 | bytes 47213568 | tf_op jit(solution)/shard_map/reduce_sum | solution.py:867
  808.4 15.2 %all-to-all-done.6 = bf16[8,144,1152]{2,1,0:T(8,128)(2,1)S(1)} async-done(((bf16[8,144,1152]{2,1,0:T(8,128)(2,1)}), bf16[8,144,1152]{2,1,0:T(8,128)(2,1)S(1)}, u32[]{:S(2)}, u32[]{:S(2)}) %all-to-all-start.6) | async-done | bytes 2654240 | tf_op jit(solution)/shard_map/all_to_all | solution.py:839
  823.6 7.0 fusion.107
  830.7 7.2 convolution_add_fusion.1
  838.1 8.0 collective-permute-done.20
  846.1 6.6 fusion.19
  852.8 7.4 multiply_convert_fusion
  889.5 79.4 %collective-permute-done.23 = f32[2,72,1152]{2,1,0:T(8,128)S(1)} collective-permute-done((f32[2,72,1152]{2,1,0:T(8,128)S(1)}, f32[2,72,1152]{2,1,0:T(8,128)S(1)}, u32[]{:S(2)}, u32[]{:S(2)}) %collective-permute-start.23) | collective-permute-done | bytes 663584 | tf_op jit(solution)/shard_map/ppermute | solution.py:22
  980.8 7.6 convert_bitcast_fusion
  993.1 6.5 collective-permute-done.22
  (391 shorter events, 324.0 us)
Async XLA Ops:
  102.7 28.4 %collective-permute-start = (bf16[3,2,1,1152]{3,2,1,0:T(2,128)(2,1)S(1)}, bf16[3,2,1,1152]{3,2,1,0:T(2,128)(2,1)S(1)}, u32[]{:S(2)}, u32[]{:S(2)}) collective-permute-start(bf16[3,2,1,1152]{3,2,1,0:T(2,128)(2,1)S(1)} %slice.243), channel_id=1, source_target_pairs={{0,2},{1,3},{4,6},{5,7},{8,10},{9,11},{12,14},{13,15},{16,18},{17,... | collective-permute-start | bytes 41480 | tf_op jit(solution)/shard_map/ppermute | solution.py:28
  109.1 81.8 %all-to-all-start = ((bf16[8,288,768]{2,1,0:T(8,128)(2,1)}), bf16[8,288,768]{2,1,0:T(8,128)(2,1)}, u32[]{:S(2)}, u32[]{:S(2)}) async-start(bf16[8,288,768]{2,1,0:T(8,128)(2,1)} %slice_select_fusion), calls=%async_computation | async-start | bytes 7077888 | tf_op jit(solution)/shard_map/all_to_all | solution.py:422
  137.6 105.0 %collective-permute-start.3 = (bf16[1152,1152]{1,0:T(8,128)(2,1)}, bf16[1152,1152]{1,0:T(8,128)(2,1)}, u32[]{:S(2)}, u32[]{:S(2)}) collective-permute-start(bf16[1152,1152]{1,0:T(8,128)(2,1)} %bitcast.17), channel_id=1, source_target_pairs={{0,2},{2,0},{1,3},{3,1},{4,6},{6,4},{5,7},{7,5},{8,10},{10,8},{9,1... | collective-permute-start | bytes 7962632 | tf_op jit(solution)/shard_map/ppermute | solution.py:22
  191.0 62.4 %all-to-all-start.1 = ((bf16[8,128,1152]{2,1,0:T(8,128)(2,1)}), bf16[8,128,1152]{2,1,0:T(8,128)(2,1)}, u32[]{:S(2)}, u32[]{:S(2)}) async-start(bf16[8,128,1152]{2,1,0:T(8,128)(2,1)} %bitcast.248), calls=%async_computation.1 | async-start | bytes 4718592 | tf_op jit(solution)/shard_map/all_to_all | solution.py:405
  195.4 4.6 collective-permute-start.2
  259.5 8.1 collective-permute-start.4
  277.1 60.2 %all-to-all-start.2 = ((bf16[8,128,1152]{2,1,0:T(8,128)(2,1)}), bf16[8,128,1152]{2,1,0:T(8,128)(2,1)}, u32[]{:S(2)}, u32[]{:S(2)}) async-start(bf16[8,128,1152]{2,1,0:T(8,128)(2,1)} %bitcast.249), calls=%async_computation.2 | async-start | bytes 4718592 | tf_op jit(solution)/shard_map/all_to_all | solution.py:405
  283.0 79.3 %collective-permute-start.5 = (bf16[8,288,768]{2,1,0:T(8,128)(2,1)}, bf16[8,288,768]{2,1,0:T(8,128)(2,1)}, u32[]{:S(2)}, u32[]{:S(2)}) collective-permute-start(bf16[8,288,768]{2,1,0:T(8,128)(2,1)} %all-to-all-done.up_a.down_a), channel_id=1, source_target_pairs={{0,2},{2,0},{1,3},{3,1},{4,6},{6,4},{5,7},{7,5},{8,10},{10,8},{9,1... | collective-permute-start | bytes 10616840 | tf_op jit(solution)/shard_map/ppermute | solution.py:22
  285.4 76.9 %collective-permute-start.7 = (bf16[1024,1152]{1,0:T(8,128)(2,1)}, bf16[1024,1152]{1,0:T(8,128)(2,1)}, u32[]{:S(2)}, u32[]{:S(2)}) collective-permute-start(bf16[1024,1152]{1,0:T(8,128)(2,1)} %bitcast.35.cotan_ref), channel_id=1, source_target_pairs={{0,1},{1,0},{2,3},{3,2},{4,5},{5,4},{6,7},{7,6},{8,9},{9,8},{10,11... | collective-permute-start | bytes 7077896 | tf_op jit(solution)/shard_map/ppermute | solution.py:22
  337.2 25.1 %collective-permute-start.6 = (bf16[1024,1152]{1,0:T(8,128)(2,1)}, bf16[1024,1152]{1,0:T(8,128)(2,1)}, u32[]{:S(2)}, u32[]{:S(2)}) collective-permute-start(bf16[1024,1152]{1,0:T(8,128)(2,1)} %bitcast.38.rows_ref), channel_id=1, source_target_pairs={{0,1},{1,0},{2,3},{3,2},{4,5},{5,4},{6,7},{7,6},{8,9},{9,8},{10,11... | collective-permute-start | bytes 7077896 | tf_op jit(solution)/shard_map/ppermute | solution.py:22
  385.8 25.7 %collective-permute-start.9 = (f32[1024,1152]{1,0:T(8,128)}, f32[1024,1152]{1,0:T(8,128)}, u32[]{:S(2)}, u32[]{:S(2)}) collective-permute-start(f32[1024,1152]{1,0:T(8,128)} %get-tuple-element.106), channel_id=1, source_target_pairs={{0,1},{1,0},{2,3},{3,2},{4,5},{5,4},{6,7},{7,6},{8,9},{9,8},{10,11... | collective-permute-start | bytes 14155784 | tf_op jit(solution)/shard_map/ppermute | solution.py:22
  385.9 32.3 %collective-permute-start.8 = (f32[1024,1152]{1,0:T(8,128)}, f32[1024,1152]{1,0:T(8,128)S(1)}, u32[]{:S(2)}, u32[]{:S(2)}) collective-permute-start(f32[1024,1152]{1,0:T(8,128)} %get-tuple-element.104), channel_id=1, source_target_pairs={{0,1},{1,0},{2,3},{3,2},{4,5},{5,4},{6,7},{7,6},{8,9},{9,8},{10,11... | collective-permute-start | bytes 14155784 | tf_op jit(solution)/shard_map/ppermute | solution.py:22
  423.0 60.3 %all-to-all-start.3 = ((bf16[8,128,1152]{2,1,0:T(8,128)(2,1)}), bf16[8,128,1152]{2,1,0:T(8,128)(2,1)}, u32[]{:S(2)}, u32[]{:S(2)}) async-start(bf16[8,128,1152]{2,1,0:T(8,128)(2,1)} %bitcast.211), calls=%async_computation.3 | async-start | bytes 4718592 | tf_op jit(solution)/shard_map/all_to_all | solution.py:405
  489.6 20.0 %collective-permute-start.10 = (bf16[1024,1152]{1,0:T(8,128)(2,1)}, bf16[1024,1152]{1,0:T(8,128)(2,1)}, u32[]{:S(2)}, u32[]{:S(2)}) collective-permute-start(bf16[1024,1152]{1,0:T(8,128)(2,1)} %fusion.27), channel_id=1, source_target_pairs={{0,1},{1,0},{2,3},{3,2},{4,5},{5,4},{6,7},{7,6},{8,9},{9,8},{10,11... | collective-permute-start | bytes 7077896 | tf_op jit(solution)/shard_map/ppermute | solution.py:22
  495.1 65.0 %collective-permute-start.12 = (bf16[1152,768]{1,0:T(8,128)(2,1)}, bf16[1152,768]{1,0:T(8,128)(2,1)}, u32[]{:S(2)}, u32[]{:S(2)}) collective-permute-start(bf16[1152,768]{1,0:T(8,128)(2,1)} %convolution_convert_fusion.2), channel_id=1, source_target_pairs={{0,2},{2,0},{1,3},{3,1},{4,6},{6,4},{5,7},{7,5},{8,10},{10,8},{9,1... | collective-permute-start | bytes 5308424 | tf_op jit(solution)/shard_map/ppermute | solution.py:22
  504.5 69.8 %collective-permute-start.11 = (bf16[1152,768]{1,0:T(8,128)(2,1)}, bf16[1152,768]{1,0:T(8,128)(2,1)}, u32[]{:S(2)}, u32[]{:S(2)}) collective-permute-start(bf16[1152,768]{1,0:T(8,128)(2,1)} %convolution_convert_fusion.3), channel_id=1, source_target_pairs={{0,2},{2,0},{1,3},{3,1},{4,6},{6,4},{5,7},{7,5},{8,10},{10,8},{9,1... | collective-permute-start | bytes 5308424 | tf_op jit(solution)/shard_map/ppermute | solution.py:22
  504.8 69.5 %all-to-all-start.4 = ((bf16[8,128,1152]{2,1,0:T(8,128)(2,1)}), bf16[8,128,1152]{2,1,0:T(8,128)(2,1)}, u32[]{:S(2)}, u32[]{:S(2)}) async-start(bf16[8,128,1152]{2,1,0:T(8,128)(2,1)} %bitcast.213), calls=%async_computation.4 | async-start | bytes 4718592 | tf_op jit(solution)/shard_map/all_to_all | solution.py:405
  581.2 154.8 %all-to-all-start.5 = ((bf16[8,288,768]{2,1,0:T(8,128)(2,1)}), bf16[8,288,768]{2,1,0:T(8,128)(2,1)}, u32[]{:S(2)}, u32[]{:S(2)}) async-start(bf16[8,288,768]{2,1,0:T(8,128)(2,1)} %pad_maximum_fusion.2), calls=%async_computation.5 | async-start | bytes 7077888 | tf_op jit(solution)/shard_map/all_to_all | solution.py:828
  600.7 9.5 collective-permute-start.14
  614.2 121.9 %collective-permute-start.15 = (bf16[8,72,1152]{2,1,0:T(8,128)(2,1)}, bf16[8,72,1152]{2,1,0:T(8,128)(2,1)}, u32[]{:S(2)}, u32[]{:S(2)}) collective-permute-start(bf16[8,72,1152]{2,1,0:T(8,128)(2,1)} %select_convert_fusion.1), channel_id=1, source_target_pairs={{0,2},{2,0},{1,3},{3,1},{4,6},{6,4},{5,7},{7,5},{8,10},{10,8},{9,1... | collective-permute-start | bytes 3981320 | tf_op jit(solution)/shard_map/ppermute | solution.py:22
  620.7 115.4 %collective-permute-start.16 = (bf16[8,72,1152]{2,1,0:T(8,128)(2,1)}, bf16[8,72,1152]{2,1,0:T(8,128)(2,1)}, u32[]{:S(2)}, u32[]{:S(2)}) collective-permute-start(bf16[8,72,1152]{2,1,0:T(8,128)(2,1)} %select_convert_fusion), channel_id=1, source_target_pairs={{0,2},{2,0},{1,3},{3,1},{4,6},{6,4},{5,7},{7,5},{8,10},{10,8},{9,1... | collective-permute-start | bytes 3981320 | tf_op jit(solution)/shard_map/ppermute | solution.py:22
  745.6 24.0 %collective-permute-start.17 = (f32[1024,104]{0,1:T(8,128)}, f32[1024,104]{0,1:T(8,128)}, u32[]{:S(2)}, u32[]{:S(2)}) collective-permute-start(f32[1024,104]{0,1:T(8,128)} %pad_maximum_fusion.9), channel_id=1, source_target_pairs={{0,1},{1,0},{2,3},{3,2},{4,5},{5,4},{6,7},{7,6},{8,9},{9,8},{10,11... | collective-permute-start | bytes 1277960 | tf_op jit(solution)/shard_map/ppermute | solution.py:22
  756.7 67.0 %all-to-all-start.6 = ((bf16[8,144,1152]{2,1,0:T(8,128)(2,1)}), bf16[8,144,1152]{2,1,0:T(8,128)(2,1)S(1)}, u32[]{:S(2)}, u32[]{:S(2)}) async-start(bf16[8,144,1152]{2,1,0:T(8,128)(2,1)} %pad_maximum_fusion.6), calls=%async_computation.6 | async-start | bytes 5308416 | tf_op jit(solution)/shard_map/all_to_all | solution.py:839
  786.7 15.1 %collective-permute-start.18 = (f32[3,2,1,1152]{3,2,1,0:T(1,128)S(1)}, f32[3,2,1,1152]{3,2,1,0:T(1,128)S(1)}, u32[]{:S(2)}, u32[]{:S(2)}) collective-permute-start(f32[3,2,1,1152]{3,2,1,0:T(1,128)S(1)} %slice.263), channel_id=1, source_target_pairs={{2,0},{3,1},{6,4},{7,5},{10,8},{11,9},{14,12},{15,13},{18,16},{19,... | collective-permute-start | bytes 82952 | tf_op jit(solution)/shard_map/ppermute | solution.py:28
  837.9 8.3 collective-permute-start.20
  865.4 106.7 %all-to-all-start.7 = ((bf16[8,152,1152]{2,1,0:T(8,128)(2,1)}), bf16[8,152,1152]{2,1,0:T(8,128)(2,1)S(1)}, u32[]{:S(2)}, u32[]{:S(2)}) async-start(bf16[8,152,1152]{2,1,0:T(8,128)(2,1)} %pad_maximum_fusion.5), calls=%async_computation.7 | async-start | bytes 5603328 | tf_op jit(solution)/shard_map/all_to_all | solution.py:913
  869.0 109.7 %reduce-scatter.2.cloned.1.call-start = ((), (), s32[]{:S(2)}) async-start(), calls=%async_computation.9 | async-start | bytes 1327104 | tf_op jit(solution)/shard_map/reduce_scatter | solution.py:899
  875.2 7.7 collective-permute-start.13
  875.4 96.7 %collective-permute-start.21 = (bf16[8,288,768]{2,1,0:T(8,128)(2,1)}, bf16[8,288,768]{2,1,0:T(8,128)(2,1)}, u32[]{:S(2)}, u32[]{:S(2)}) collective-permute-start(bf16[8,288,768]{2,1,0:T(8,128)(2,1)} %all-to-all-done.5), channel_id=1, source_target_pairs={{0,2},{2,0},{1,3},{3,1},{4,6},{6,4},{5,7},{7,5},{8,10},{10,8},{9,1... | collective-permute-start | bytes 10616840 | tf_op jit(solution)/shard_map/ppermute | solution.py:22
  882.8 86.0 %collective-permute-start.23 = (f32[2,72,1152]{2,1,0:T(8,128)S(1)}, f32[2,72,1152]{2,1,0:T(8,128)S(1)}, u32[]{:S(2)}, u32[]{:S(2)}) collective-permute-start(f32[2,72,1152]{2,1,0:T(8,128)S(1)} %bitcast.238), channel_id=1, source_target_pairs={{0,2},{2,0},{1,3},{3,1},{4,6},{6,4},{5,7},{7,5},{8,10},{10,8},{9,1... | collective-permute-start | bytes 1990664 | tf_op jit(solution)/shard_map/ppermute | solution.py:22
  978.7 9.7 collective-permute-start.24
  980.5 19.1 %collective-permute-start.22 = (f32[152,1152]{1,0:T(8,128)}, f32[152,1152]{1,0:T(8,128)}, u32[]{:S(2)}, u32[]{:S(2)}) collective-permute-start(f32[152,1152]{1,0:T(8,128)} %convert_reduce_fusion), channel_id=1, source_target_pairs={{0,2},{2,0},{1,3},{3,1},{4,6},{6,4},{5,7},{7,5},{8,10},{10,8},{9,1... | collective-permute-start | bytes 2101256 | tf_op jit(solution)/shard_map/ppermute | solution.py:22
  (84 other events, 2010.7 us)
Sparse Core Ops, SparseCore 0:
  880.8 95.2 reduce-scatter.1

commit v4 on v3

--- a/solution.py
+++ b/solution.py
@@ -14,6 +14,16 @@
 LANES = 128
 VMEM_LIMIT = 56 * 1024 * 1024
 LOG2E = math.log2(math.e)
+GROUP_A = 4
+GROUP_B = 4
+GROUP_C = 8
+UNROLL_A = 8
+UNROLL_B = 8
+UNROLL_C = 8
+UNROLL_D = 4
+UNROLL_E = 8
+BLOCKS = 3
+COVER = 1
 BF16 = jnp.bfloat16
 F32 = jnp.float32
 
@@ -87,8 +97,26 @@
     return (grad_values, grad_gain)
 
 
-def sublane_rows():
-    return lax.broadcasted_iota(jnp.int32, (SEGMENTS, LANES), 0)
+def zeros_of(ref):
+    return jnp.zeros(ref.shape[1:], F32)
+
+
+def sublane_rows(lanes):
+    return lax.broadcasted_iota(jnp.int32, (SEGMENTS, lanes), 0)
+
+
+def widened(value, lanes):
+    return jnp.concatenate([value] * (lanes // LANES), axis=1) if lanes > LANES else value
+
+
+def narrowed(value):
+    parts = [value[:, at : at + LANES] for at in range(0, value.shape[1], LANES)]
+    return sum(parts[1:], parts[0])
+
+
+def groups_of(states, size):
+    size = math.gcd(states, size)
+    return [range(first, first + size) for first in range(0, states, size)]
 
 
 def joined_forward(decay, value, row):
@@ -108,168 +136,223 @@
 
 
 def ends_kernel(step_ref, input_ref, mix_in_ref, rate_ref, decay_ref, state_ref, last_ref):
-    steps, states = step_ref.shape[0], mix_in_ref.shape[1]
-    zero = jnp.zeros((SEGMENTS, LANES), F32)
-
-    def body(at, carry):
-        held, total = carry
-        step = step_ref[at]
-        driven = step * input_ref[at]
-        held = tuple(
-            jnp.exp2(step * rate_ref[n]) * held[n] + mix_in_ref[at, n] * driven
-            for n in range(states)
-        )
-        return held, total + step
-
-    held, total = lax.fori_loop(0, steps, body, ((zero,) * states, zero))
-    row = sublane_rows()
-    for n in range(states):
-        decay, value = joined_forward(jnp.exp2(total * rate_ref[n]), held[n], row)
-        decay_ref[n] = decay
-        state_ref[n] = value
-        last_ref[n : n + 1] = value[SEGMENTS - 1 :]
+    steps, states, lanes = step_ref.shape[0], mix_in_ref.shape[1], step_ref.shape[2]
+    zero = zeros_of(step_ref)
+    row = sublane_rows(lanes)
+    total = lax.fori_loop(0, steps, lambda at, total: total + step_ref[at], zero, unroll=UNROLL_E)
+    for members in groups_of(states, GROUP_A):
+        rates = [rate_ref[n] for n in members]
+
+        def body(at, held):
+            step = step_ref[at]
+            driven = step * input_ref[at]
+            return tuple(
+                jnp.exp2(step * rate) * before + widened(mix_in_ref[at, n], lanes) * driven
+                for n, rate, before in zip(members, rates, held)
+            )
+
+        held = lax.fori_loop(0, steps, body, (zero,) * len(members), unroll=UNROLL_A)
+        for n, rate, end in zip(members, rates, held):
+            decay, value = joined_forward(jnp.exp2(total * rate), end, row)
+            decay_ref[n] = decay
+            state_ref[n] = value
+            last_ref[n : n + 1] = value[SEGMENTS - 1 :]
 
 
 def states_kernel(
     step_ref, input_ref, mix_in_ref, mix_out_ref, rate_ref, decay_ref, state_ref, enter_ref,
     out_ref, start_ref,
 ):
-    steps, states = step_ref.shape[0], mix_in_ref.shape[1]
-    row = sublane_rows()
-    held = []
-    for n in range(states):
-        first = jnp.broadcast_to(enter_ref[n : n + 1], (SEGMENTS, LANES))
-        inner = pltpu.roll(state_ref[n], 1, 0) + pltpu.roll(decay_ref[n], 1, 0) * first
-        start = jnp.where(row >= 1, inner, first)
-        start_ref[n] = start
-        held.append(start)
-
-    def body(at, held):
-        step = step_ref[at]
-        driven = step * input_ref[at]
-        held = tuple(
-            jnp.exp2(step * rate_ref[n]) * held[n] + mix_in_ref[at, n] * driven
-            for n in range(states)
-        )
-        parts = [mix_out_ref[at, n] * held[n] for n in range(states)]
-        while len(parts) > 1:
-            parts = [parts[i] + parts[i + 1] for i in range(0, len(parts), 2)]
-        out_ref[at] = parts[0]
-        return held
-
-    lax.fori_loop(0, steps, body, tuple(held))
+    steps, states, lanes = step_ref.shape[0], mix_in_ref.shape[1], step_ref.shape[2]
+    row = sublane_rows(lanes)
+    for members in groups_of(states, GROUP_B):
+        rates = [rate_ref[n] for n in members]
+        held = []
+        for n in members:
+            first = jnp.broadcast_to(enter_ref[n : n + 1], (SEGMENTS, lanes))
+            inner = pltpu.roll(state_ref[n], 1, 0) + pltpu.roll(decay_ref[n], 1, 0) * first
+            start = jnp.where(row >= 1, inner, first)
+            start_ref[n] = start
+            held.append(start)
+
+        def body(at, held):
+            step = step_ref[at]
+            driven = step * input_ref[at]
+            held = tuple(
+                jnp.exp2(step * rate) * before + widened(mix_in_ref[at, n], lanes) * driven
+                for n, rate, before in zip(members, rates, held)
+            )
+            parts = [widened(mix_out_ref[at, n], lanes) * now for n, now in zip(members, held)]
+            if members[0]:
+                parts.append(out_ref[at])
+            while len(parts) > 1:
+                parts = [sum(parts[i + 1 : i + 2], parts[i]) for i in range(0, len(parts), 2)]
+            out_ref[at] = parts[0]
+            return held
+
+        lax.fori_loop(0, steps, body, tuple(held), unroll=UNROLL_B)
 
 
 def adjoint_ends_kernel(step_ref, mix_out_ref, grad_ref, rate_ref, decay_ref, adjoint_ref, first_ref):
-    steps, states = step_ref.shape[0], mix_out_ref.shape[1]
-    zero = jnp.zeros((SEGMENTS, LANES), F32)
-
-    def body(back, carry):
-        at = steps - 1 - back
-        incoming, total = carry
-        step = step_ref[at]
-        grad = grad_ref[at]
-        incoming = tuple(
-            jnp.exp2(step * rate_ref[n]) * (mix_out_ref[at, n] * grad + incoming[n])
-            for n in range(states)
-        )
-        return incoming, total + step
-
-    incoming, total = lax.fori_loop(0, steps, body, ((zero,) * states, zero))
-    row = sublane_rows()
-    for n in range(states):
-        decay, value = joined_backward(jnp.exp2(total * rate_ref[n]), incoming[n], row)
-        decay_ref[n] = decay
-        adjoint_ref[n] = value
-        first_ref[n : n + 1] = value[:1]
+    steps, states, lanes = step_ref.shape[0], mix_out_ref.shape[1], step_ref.shape[2]
+    zero = zeros_of(step_ref)
+    row = sublane_rows(lanes)
+    total = lax.fori_loop(0, steps, lambda at, total: total + step_ref[at], zero, unroll=UNROLL_E)
+    for members in groups_of(states, GROUP_A):
+        rates = [rate_ref[n] for n in members]
+
+        def body(back, incoming):
+            at = steps - 1 - back
+            step = step_ref[at]
+            grad = grad_ref[at]
+            return tuple(
+                jnp.exp2(step * rate) * (widened(mix_out_ref[at, n], lanes) * grad + after)
+                for n, rate, after in zip(members, rates, incoming)
+            )
+
+        incoming = lax.fori_loop(0, steps, body, (zero,) * len(members), unroll=UNROLL_A)
+        for n, rate, end in zip(members, rates, incoming):
+            decay, value = joined_backward(jnp.exp2(total * rate), end, row)
+            decay_ref[n] = decay
+            adjoint_ref[n] = value
+            first_ref[n : n + 1] = value[:1]
 
 
 def adjoint_kernel(
     step_ref, input_ref, mix_in_ref, mix_out_ref, grad_ref, rate_ref, start_ref, decay_ref, adjoint_ref,
-    enter_ref,
-    in_sum_ref, rate_sum_ref, decay_sum_ref, in_grad_ref, out_grad_ref, states_ref,
+    enter_ref, skip_ref,
+    pre_ref, conv_ref, decay_sum_ref, sums_ref, mix_ref, states_ref, decays_ref, in_grad_ref, out_grad_ref,
 ):
-    steps, states = step_ref.shape[0], mix_in_ref.shape[1]
-    row = sublane_rows()
-    zero = jnp.zeros((SEGMENTS, LANES), F32)
+    steps, states, lanes = step_ref.shape[0], mix_in_ref.shape[1], step_ref.shape[2]
+    row = sublane_rows(lanes)
+    zero = zeros_of(step_ref)
 
     @pl.when(pl.program_id(1) == 0)
     def clear():
         in_grad_ref[...] = jnp.zeros_like(in_grad_ref)
         out_grad_ref[...] = jnp.zeros_like(out_grad_ref)
 
-    for n in range(states):
-        states_ref[0, n] = start_ref[n]
-
-    def ahead(at, held):
-        step = step_ref[at]
-        driven = step * input_ref[at]
-        held = tuple(
-            jnp.exp2(step * rate_ref[n]) * held[n] + mix_in_ref[at, n] * driven
-            for n in range(states)
+    for members in groups_of(states, GROUP_C):
+        first, group = members[0], len(members)
+        rates = [rate_ref[n] for n in members]
+
+        def ahead(at, held):
+            step = step_ref[at]
+            driven = step * input_ref[at]
+            grad = grad_ref[at]
+            after = []
+            for i, n in enumerate(members):
+                states_ref[at, i] = held[i]
+                decay = jnp.exp2(step * rates[i])
+                decays_ref[at, i] = decay
+                now = decay * held[i] + widened(mix_in_ref[at, n], lanes) * driven
+                out_grad_ref[at, n] += narrowed(grad * now)
+                after.append(now)
+            return tuple(after)
+
+        lax.fori_loop(0, steps, ahead, tuple(start_ref[n] for n in members), unroll=UNROLL_C)
+
+        incoming = []
+        for n in members:
+            final = jnp.broadcast_to(enter_ref[n : n + 1], (SEGMENTS, lanes))
+            inner = (
+                pltpu.roll(adjoint_ref[n], SEGMENTS - 1, 0)
+                + pltpu.roll(decay_ref[n], SEGMENTS - 1, 0) * final
+            )
+            incoming.append(jnp.where(row < SEGMENTS - 1, inner, final))
+
+        def body(back, carry):
+            at = steps - 1 - back
+            incoming, decay_sums = carry
+            step = step_ref[at]
+            grad = grad_ref[at]
+            driven = step * input_ref[at]
+            in_sum = conv_ref[at] if first else zero
+            rate_sum = pre_ref[at] if first else zero
+            following, sums = [], []
+            for i, n in enumerate(members):
+                adjoint = widened(mix_out_ref[at, n], lanes) * grad + incoming[i]
+                onward = decays_ref[at, i] * adjoint
+                decay_grad = onward * states_ref[at, i]
+                in_sum = in_sum + adjoint * widened(mix_in_ref[at, n], lanes)
+                rate_sum = rate_sum + decay_grad * rates[i]
+                sums.append(decay_sums[i] + decay_grad * step)
+                in_grad_ref[at, n] += narrowed(adjoint * driven)
+                following.append(onward)
+            conv_ref[at] = in_sum
+            pre_ref[at] = rate_sum
+            return tuple(following), tuple(sums)
+
+        _, sums = lax.fori_loop(
+            0, steps, body, (tuple(incoming), (zero,) * group), unroll=UNROLL_D
         )
-        for n in range(states):
-            states_ref[at + 1, n] = held[n]
-        return held
-
-    lax.fori_loop(0, steps, ahead, tuple(start_ref[n] for n in range(states)))
-
-    incoming = []
-    for n in range(states):
-        final = jnp.broadcast_to(enter_ref[n : n + 1], (SEGMENTS, LANES))
-        inner = (
-            pltpu.roll(adjoint_ref[n], SEGMENTS - 1, 0)
-            + pltpu.roll(decay_ref[n], SEGMENTS - 1, 0) * final
-        )
-        incoming.append(jnp.where(row < SEGMENTS - 1, inner, final))
-
-    def body(back, carry):
-        at = steps - 1 - back
-        incoming, decay_sums = carry
-        step = step_ref[at]
-        grad = grad_ref[at]
-        driven = step * input_ref[at]
-        in_sum, rate_sum = zero, zero
-        following, sums = [], []
-        for n in range(states):
-            rate = rate_ref[n]
-            adjoint = mix_out_ref[at, n] * grad + incoming[n]
-            onward = jnp.exp2(step * rate) * adjoint
-            decay_grad = onward * states_ref[at, n]
-            in_sum = in_sum + adjoint * mix_in_ref[at, n]
-            rate_sum = rate_sum + decay_grad * rate
-            sums.append(decay_sums[n] + decay_grad * step)
-            in_grad_ref[at, n] += adjoint * driven
-            out_grad_ref[at, n] += grad * states_ref[at + 1, n]
-            following.append(onward)
-        in_sum_ref[at] = in_sum
-        rate_sum_ref[at] = rate_sum
-        return tuple(following), tuple(sums)
-
-    _, sums = lax.fori_loop(0, steps, body, (tuple(incoming), (zero,) * states))
-    for n in range(states):
-        decay_sum_ref[n : n + 1] = jnp.sum(sums[n], axis=0, keepdims=True)
+        for i, n in enumerate(members):
+            decay_sum_ref[n : n + 1] = jnp.sum(sums[i], axis=0, keepdims=True)
+
+    skip = skip_ref[...]
+
+    def close(at, carry):
+        pre_sum, skip_sum = carry
+        step, inputs, grad, in_sum = step_ref[at], input_ref[at], grad_ref[at], conv_ref[at]
+        step_grad = pre_ref[at] * (1.0 / LOG2E) + in_sum * inputs
+        pre = step_grad * (1.0 - jnp.exp2(step * -LOG2E))
+        pre_ref[at] = pre
+        conv_ref[at] = in_sum * step + skip * grad
+        return pre_sum + pre, skip_sum + grad * inputs
+
+    pre_sum, skip_sum = lax.fori_loop(0, steps, close, (zero, zero), unroll=UNROLL_E)
+    sums_ref[0:1] = jnp.sum(pre_sum, axis=0, keepdims=True)
+    sums_ref[1:2] = jnp.sum(skip_sum, axis=0, keepdims=True)
+    sums_ref[2:] = jnp.zeros((SEGMENTS - 2, lanes), F32)
+
+    @pl.when(pl.program_id(1) == pl.num_programs(1) - 1)
+    def across_lanes():
+        lane = lax.broadcasted_iota(jnp.int32, (SEGMENTS, LANES), 1)
+
+        def one(at, carry):
+            total = jnp.zeros((SEGMENTS, LANES), F32)
+            for n in range(states):
+                for base, ref in ((0, in_grad_ref), (states, out_grad_ref)):
+                    value = jnp.sum(ref[at, n], axis=1, keepdims=True)
+                    total = jnp.where(lane == base + n, value, total)
+            mix_ref[at] = total
+            return carry
+
+        lax.fori_loop(0, steps, one, 0, unroll=UNROLL_E)
 
 
 class Scan:
     def __init__(self, steps, chains, states, width):
-        self.grid = (chains, width // LANES)
+        lanes = LANES * math.gcd(width // LANES, BLOCKS)
+        self.grid = (chains, width // lanes)
         self.rows_spec = pl.BlockSpec(
-            (steps, None, SEGMENTS, LANES), lambda chain, block: (0, chain, 0, block)
+            (steps, None, SEGMENTS, lanes), lambda chain, block: (0, chain, 0, block)
         )
         self.mix_spec = pl.BlockSpec(
             (None, steps, states, SEGMENTS, LANES), lambda chain, block: (chain, 0, 0, 0, 0)
         )
-        self.rate_spec = pl.BlockSpec((states, SEGMENTS, LANES), lambda chain, block: (0, 0, block))
+        self.rate_spec = pl.BlockSpec((states, SEGMENTS, lanes), lambda chain, block: (0, 0, block))
         self.state_spec = pl.BlockSpec(
-            (None, states, SEGMENTS, LANES), lambda chain, block: (chain, 0, 0, block)
+            (None, states, SEGMENTS, lanes), lambda chain, block: (chain, 0, 0, block)
         )
-        self.edge_spec = pl.BlockSpec((None, states, LANES), lambda chain, block: (chain, 0, block))
+        self.edge_spec = pl.BlockSpec((None, states, lanes), lambda chain, block: (chain, 0, block))
         self.rows = jax.ShapeDtypeStruct((steps, chains, SEGMENTS, width), F32)
         self.mix = jax.ShapeDtypeStruct((chains, steps, states, SEGMENTS, LANES), F32)
         self.state = jax.ShapeDtypeStruct((chains, states, SEGMENTS, width), F32)
         self.edge = jax.ShapeDtypeStruct((chains, states, width), F32)
-        self.scratch = pltpu.VMEM((steps + 1, states, SEGMENTS, LANES), F32)
+        self.sums = jax.ShapeDtypeStruct((chains, SEGMENTS, width), F32)
+        self.sums_spec = pl.BlockSpec((None, SEGMENTS, lanes), lambda chain, block: (chain, 0, block))
+        self.lane_sums = jax.ShapeDtypeStruct((steps, chains, SEGMENTS, LANES), F32)
+        self.lane_spec = pl.BlockSpec(
+            (steps, None, SEGMENTS, LANES), lambda chain, block: (0, chain, 0, 0)
+        )
+        self.skip_spec = pl.BlockSpec((1, lanes), lambda chain, block: (0, block))
+        self.scratch = [
+            pltpu.VMEM((steps, math.gcd(states, GROUP_C), SEGMENTS, lanes), F32),
+            pltpu.VMEM((steps, math.gcd(states, GROUP_C), SEGMENTS, lanes), F32),
+            pltpu.VMEM((steps, states, SEGMENTS, LANES), F32),
+            pltpu.VMEM((steps, states, SEGMENTS, LANES), F32),
+        ]
         self.work = steps * chains * SEGMENTS * width * states
 
     def call(self, kernel, ops, args, in_specs, outs, out_specs, scratch=()):
@@ -283,7 +366,7 @@
             scratch_shapes=list(scratch),
             compiler_params=pltpu.CompilerParams(vmem_limit_bytes=VMEM_LIMIT),
             cost_estimate=pl.CostEstimate(
-                flops=ops * self.work, transcendentals=self.work, bytes_accessed=size
+                flops=ops * self.work, transcendentals=self.work, bytes_accessed=size // COVER
             ),
         )(*args)
 
@@ -312,16 +395,104 @@
             [self.state_spec, self.state_spec, self.edge_spec],
         )
 
-    def adjoint(self, step, inputs, mix_in, mix_out, grad, rate, start, decay, adjoint, enter):
+    def adjoint(self, step, inputs, mix_in, mix_out, grad, rate, start, decay, adjoint, enter, skip):
         return self.call(
             adjoint_kernel, 20,
-            (step, inputs, mix_in, mix_out, grad, rate, start, decay, adjoint, enter),
+            (step, inputs, mix_in, mix_out, grad, rate, start, decay, adjoint, enter, skip),
             [self.rows_spec, self.rows_spec, self.mix_spec, self.mix_spec, self.rows_spec,
-             self.rate_spec, self.state_spec, self.state_spec, self.state_spec, self.edge_spec],
-            [self.rows, self.rows, self.edge, self.mix, self.mix],
-            [self.rows_spec, self.rows_spec, self.edge_spec, self.mix_spec, self.mix_spec],
-            [self.scratch],
+             self.rate_spec, self.state_spec, self.state_spec, self.state_spec, self.edge_spec,
+             self.skip_spec],
+            [self.rows, self.rows, self.edge, self.sums, self.lane_sums],
+            [self.rows_spec, self.rows_spec, self.edge_spec, self.sums_spec, self.lane_spec],
+            self.scratch,
         )
+
+
+def conv_back_kernel(
+    proj_ref, weight_ref, grad_ref, input_ref, taps_ref, shift_ref,
+    out_ref, sums_ref, head_ref, tail_ref, product_ref, conv_ref,
+):
+    steps, rows, lanes = grad_ref.shape
+    count = taps_ref.shape[0]
+    reach = count - 1
+    taps = [taps_ref[at : at + 1] for at in range(count)]
+    shift = shift_ref[...]
+    product_ref[...] = jnp.dot(
+        proj_ref[...], weight_ref[...], preferred_element_type=F32
+    ).reshape(steps, rows, lanes)
+
+    def slopes(at, sums):
+        inputs = [input_ref[at + tap].astype(F32) for tap in range(count)]
+        pre = shift + sum(tap * value for tap, value in zip(taps, inputs))
+        share = 1.0 / (1.0 + jnp.exp(-pre))
+        conv = (grad_ref[at] + product_ref[at]) * (share * (1.0 + pre * (1.0 - share)))
+        conv_ref[at] = conv
+        return (*(total + conv * value for total, value in zip(sums, inputs)), sums[-1] + conv)
+
+    zero = jnp.zeros((rows, lanes), F32)
+    sums = lax.fori_loop(0, steps, slopes, (zero,) * (count + 1), unroll=2)
+    for at, total in enumerate(sums):
+        sums_ref[at : at + 1] = jnp.sum(total, axis=0, keepdims=True)
+    sums_ref[count + 1 :] = jnp.zeros((sums_ref.shape[0] - count - 1, lanes), F32)
+    row = sublane_rows(lanes)
+    for at in range(reach):
+        head_ref[at] = conv_ref[at]
+        for low in range(0, rows, SEGMENTS):
+            rolled = pltpu.roll(conv_ref[at, low : low + SEGMENTS], SEGMENTS - 1, 0)
+            conv_ref[steps + at, low : low + SEGMENTS] = jnp.where(
+                row < SEGMENTS - 1, rolled, 0.0
+            )
+
+    def back(at):
+        return sum(taps[tap] * conv_ref[at + reach - tap] for tap in range(count))
+
+    def store(at, carry):
+        out_ref[at] = back(at).astype(BF16)
+        return carry
+
+    lax.fori_loop(0, steps, store, 0, unroll=2)
+    for at in range(reach):
+        tail_ref[at] = back(steps - reach + at)
+
+
+def conv_back(proj, weight, grad, inputs, taps, shift):
+    steps, rows, width = grad.shape
+    reach = taps.shape[0] - 1
+    lanes = LANES * math.gcd(width // LANES, BLOCKS)
+
+    def block(count, dtype=F32):
+        spec = pl.BlockSpec((count, rows, lanes), lambda at: (0, 0, at))
+        return spec, jax.ShapeDtypeStruct((count, rows, width), dtype)
+
+    def columns(count):
+        return pl.BlockSpec((count, lanes), lambda at: (0, at))
+
+    outs = [
+        block(steps, BF16),
+        (columns(SEGMENTS), jax.ShapeDtypeStruct((SEGMENTS, width), F32)),
+        block(reach),
+        block(reach),
+    ]
+    return pl.pallas_call(
+        conv_back_kernel,
+        grid=(width // lanes,),
+        in_specs=[
+            pl.BlockSpec(proj.shape, lambda at: (0, 0)),
+            columns(weight.shape[0]),
+            block(steps)[0],
+            block(steps + reach)[0],
+            columns(reach + 1),
+            columns(1),
+        ],
+        out_specs=[spec for spec, _ in outs],
+        out_shape=[shape for _, shape in outs],
+        scratch_shapes=[
+            pltpu.VMEM((steps, rows, lanes), F32),
+            pltpu.VMEM((steps + reach, rows, lanes), F32),
+        ],
+        compiler_params=pltpu.CompilerParams(vmem_limit_bytes=VMEM_LIMIT),
+        cost_estimate=pl.CostEstimate(flops=1, transcendentals=0, bytes_accessed=1),
+    )(proj, weight, grad, inputs, taps, shift)
 
 
 def expert_kernel(
@@ -357,9 +528,9 @@
     picked_ref[...] = picked
 
 
-def expert_call(rows, cotan, router_t, mask, halves):
+def expert_call(rows, cotan, router_t, mask, blocks, far_up, far_down):
     count, width = rows.shape
-    hidden = halves[0].shape[2]
+    shard, hidden = far_up.shape[1:]
     block = math.gcd(count, 512)
     row_spec = pl.BlockSpec((block, width), lambda at: (at, 0))
     hidden_spec = pl.BlockSpec((block, hidden), lambda at: (at, 0))
@@ -368,14 +539,16 @@
     def whole(array):
         return pl.BlockSpec(array.shape, lambda at: (0, 0), pipeline_mode=pl.Buffered(1))
 
-    def layer(both, at):
-        devices, rows, columns = both.shape
+    def layer(array, at):
         return pl.BlockSpec(
-            (devices, rows // 2, columns), lambda step: (0, at, 0), pipeline_mode=pl.Buffered(1)
+            (array.shape[0], shard, hidden), lambda step: (0, at, 0), pipeline_mode=pl.Buffered(1)
         )
 
-    fixed = (router_t, mask, halves[0], halves[0], halves[1], halves[1])
-    fixed_specs = [whole(router_t), whole(mask), *(layer(both, at) for both in halves for at in (0, 1))]
+    fixed = (router_t, mask, blocks, blocks, far_up, far_down)
+    fixed_specs = [
+        whole(router_t), whole(mask),
+        layer(blocks, 0), layer(blocks, 1), layer(far_up, 0), layer(far_down, 0),
+    ]
     wide, narrow = jax.ShapeDtypeStruct((count, width), F32), jax.ShapeDtypeStruct((count, width), BF16)
     inner = jax.ShapeDtypeStruct((count, hidden), BF16)
     return pl.pallas_call(
@@ -422,11 +595,12 @@
     return lax.all_to_all(both, "dp", 0, 0, tiled=True)
 
 
-def own_expert(both):
+def other_hidden(both):
+    rows = both.shape[1] // 2
     if lax.axis_size("ctx") == 2:
-        return both, swapped(both, "ctx")
+        return swapped(both[:, :rows], "ctx"), swapped(both[:, rows:], "ctx")
     half = both.shape[2] // 2
-    return both[:, :, :half], both[:, :, half:]
+    return both[:, :rows, half:], both[:, rows:, half:]
 
 
 def gather_kernel(count, parts, *refs):
@@ -546,35 +720,16 @@
     return every[0], every[1]
 
 
-def halves_sent(blocks):
-    if lax.axis_size("ctx") != 2:
-        return lax.psum_scatter(blocks, "ctx", scatter_dimension=1, tiled=True), None
-    half = blocks.shape[1] // 2
-    own, other = by_ctx(blocks[:, :half], blocks[:, half:])
-    return own, swapped(other.astype(BF16), "ctx")
-
-
-def halves_added(own, other):
-    return (own if other is None else own + other.astype(F32)).astype(BF16)
-
-
-def halves_joined(value, axis):
-    count = lax.axis_size("ctx")
-    if count != 2:
-        return lax.all_gather(value, "ctx", axis=axis, tiled=True)
-    other = swapped(value, "ctx")
-    first = lax.axis_index("ctx") == 0
-    return jnp.concatenate(
-        [jnp.where(first, value, other), jnp.where(first, other, value)], axis=axis
-    )
-
-
 def expert_weight_products(rows, hidden_grads, grads, actives):
     pairs = ((rows, hidden_grads), (grads, actives))
     far = [contract_rows(left, rights[1]) for left, rights in pairs]
     if lax.axis_size("ctx") == 2:
-        far = [swapped(value.astype(BF16), "ctx") for value in far]
+        far = [value.astype(BF16) for value in far]
     return [contract_rows(left, rights[0]) for left, rights in pairs], far
+
+
+def sent_far(value):
+    return swapped(value, "ctx") if lax.axis_size("ctx") == 2 else value
 
 
 def expert_weight_parts(near, far):
@@ -610,16 +765,31 @@
     return joined[:, :shard].astype(F32), joined[:, shard:].astype(F32)
 
 
-def weight_part(grad):
+def pair_products(first, second):
+    if lax.axis_size("ctx") != 2:
+        return contract_rows(*first), contract_rows(*second).astype(BF16)
+    lefts, rights = by_ctx(first[0], second[0]), by_ctx(first[1], second[1])
+    return contract_rows(lefts[0], rights[0]), contract_rows(lefts[1], rights[1]).astype(BF16)
+
+
+def product_part(near, far):
     count = lax.axis_size("dp")
-    return halves_sent(grad.reshape(count, grad.shape[0] // count, grad.shape[1]))
-
-
-def weight_shards(blocks, number):
+
+    def blocks(value):
+        return value.astype(BF16).reshape(count, value.shape[0] // count, value.shape[1])
+
+    if lax.axis_size("ctx") != 2:
+        return jnp.concatenate([blocks(near), blocks(far)], axis=1)
+    return blocks(near + far.astype(F32))
+
+
+def product_shards(blocks):
     sums = jnp.sum(blocks.astype(F32), axis=0)
-    rows = sums.shape[0] // number
-    joined = halves_joined(sums.reshape(number, rows, sums.shape[1]), 1)
-    return [joined[at] for at in range(number)]
+    if lax.axis_size("ctx") == 2:
+        return by_ctx(sums, swapped(sums, "ctx"))
+    sums = lax.psum(sums, "ctx")
+    rows = sums.shape[0] // 2
+    return sums[:rows], sums[rows:]
 
 
 def local(
@@ -745,7 +915,8 @@
     edge_in, later = together(edge_in, later)
     out_proj_t, in_z = other_joined(later, out_weight.T, in_weight[:, 1])
     halo = jnp.concatenate([edge_in, tail[:, :, : SEGMENTS - 1]], axis=2)
-    extended = jnp.concatenate([halo, x_pre], axis=0).astype(F32)
+    extended_bf = jnp.concatenate([halo, x_pre], axis=0)
+    extended = extended_bf.astype(F32)
     conv_pre = jnp.broadcast_to(conv_shift[0], x_pre.shape)
     for tap in range(taps):
         conv_pre = conv_pre + tap_weights[tap] * extended[tap : tap + steps]
@@ -764,11 +935,11 @@
     dt_pre = (jnp.dot(dt_low, dt_proj, preferred_element_type=F32) + dt_shift).reshape(x_pre.shape)
     step_size = jax.nn.softplus(dt_pre)
     seg_decay, seg_state, last_state = scan.ends(step_size, xconv, mix_in, rate_rows)
-    seg_state, sent_cotan, expert_blocks = together(seg_state, sent_cotan, expert_blocks)
+    sent_cotan, expert_blocks, _ = together(sent_cotan, expert_blocks, seg_state)
     slot_cotan = exchanged(sent_cotan)
     entering = entering_pieces(seg_decay[:, :, SEGMENTS - 1], last_state, "ctx", False)
     entering, expert_blocks = together(entering, expert_blocks)
-    halves = own_expert(expert_blocks)
+    far_up, far_down = other_hidden(expert_blocks)
     scan_out, seg_start = scan.run(
         step_size, xconv, mix_in, mix_out, rate_rows, seg_decay, seg_state, entering
     )
@@ -776,18 +947,19 @@
     scanned = scan_out + skip_row[0] * xconv
     z_silu = jax.nn.silu(z_gate)
     gated_bf = (scanned * z_silu).astype(BF16).reshape(tokens, inner)
-    gated_bf, slot_cotan = together(gated_bf, slot_cotan)
+    gated_bf, slot_cotan, far_up = together(gated_bf, slot_cotan, far_up)
     middle = values + axis_sum(contract_cols(gated_bf, out_proj_t), "tp")
 
     normed_two, inverse_two = rms_forward(middle, gain_two_f)
     normed_two_bf = normed_two.astype(BF16)
     own_rows = exchanged(slotted(normed_two_bf))
+    own_rows, far_down = together(own_rows, far_down)
     expert_mask = (
         jnp.arange(experts, dtype=jnp.int32) == lax.rem(lax.axis_index("dp"), experts)
     ).astype(F32)[None, :]
     far_rows, far_cotan = swapped(own_rows, "tp"), swapped(slot_cotan, "tp")
-    far = expert_call(far_rows, far_cotan, router_t, expert_mask, halves)
-    near = expert_call(own_rows, slot_cotan, router_t, expert_mask, halves)
+    far = expert_call(far_rows, far_cotan, router_t, expert_mask, expert_blocks, far_up, far_down)
+    near = expert_call(own_rows, slot_cotan, router_t, expert_mask, expert_blocks, far_up, far_down)
     slot_out = near[0] + swapped(far[0], "tp")
     picked_grad = near[1] + swapped(far[1], "tp")
     slot_prob = near[2]
@@ -809,77 +981,70 @@
         both_rows(3),
         (both_rows(4), both_rows(5)),
     )
-    got_grad, slot_out, near_parts = together(got_grad, slot_out, near_parts)
+    far_first = sent_far(far_parts[0])
+    got_grad, near_parts, far_second, far_first, slot_out = together(
+        got_grad, near_parts, far_parts[1], far_first, slot_out
+    )
+    far_parts = far_first, sent_far(far_second)
     normed_two_grad = landed(got_grad)
     got_out = exchanged(slot_out.astype(BF16).reshape(experts, part_cap, -1))
     middle_norm_grad, gain_two_grad = rms_backward(middle, inverse_two, gain_two_f, normed_two_grad)
     middle_grad = cotan + middle_norm_grad
     mixer_grad_bf = middle_grad.astype(BF16)
-    out_grad_product = contract_rows(mixer_grad_bf, gated_bf)
     gated_grad = jnp.dot(mixer_grad_bf, out_proj_t, preferred_element_type=F32).reshape(x_pre.shape)
     scan_grad = gated_grad * z_silu
     z_grad = jax.vjp(jax.nn.silu, z_gate)[1](gated_grad * scanned)[0]
     z_grad_bf = z_grad.astype(BF16).reshape(tokens, inner)
-    in_z_product = contract_rows(normed_bf, z_grad_bf)
+    near_product, far_product = pair_products((mixer_grad_bf, gated_bf), (normed_bf, z_grad_bf))
+    weight_parts = expert_weight_parts(near_parts, far_parts)
+    scan_grad, weight_parts, got_out = together(scan_grad, weight_parts, got_out)
+    weight_blocks = lax.all_to_all(weight_parts, "dp", 0, 0, tiled=True)
     back_decay, back_adjoint, first_adjoint = scan.adjoint_ends(
         step_size, mix_out, scan_grad, rate_rows
     )
-    first_adjoint, got_out, far_parts = together(first_adjoint, got_out, far_parts)
-    weight_blocks = lax.all_to_all(
-        expert_weight_parts(near_parts, far_parts), "dp", 0, 0, tiled=True
-    )
     leaving = entering_pieces(back_decay[:, :, 0], first_adjoint, "ctx", True)
-    leaving, out_grad_product, in_z_product = together(leaving, out_grad_product, in_z_product)
-    out_part, in_z_part = weight_part(out_grad_product), weight_part(in_z_product)
-    in_sum, rate_sum, decay_sum, in_lanes, out_lanes = scan.adjoint(
+    leaving, near_product, far_product = together(leaving, near_product, far_product)
+    far_product = sent_far(far_product)
+    pre_grad, xconv_grad, decay_sum, scan_sums, mix_grad = scan.adjoint(
         step_size, xconv, mix_in, mix_out, scan_grad, rate_rows, seg_start, back_decay, back_adjoint,
-        leaving,
-    )
-    in_sum, weight_blocks, out_part, in_z_part = together(in_sum, weight_blocks, out_part, in_z_part)
-    out_blocks = lax.all_to_all(
-        jnp.concatenate([halves_added(*out_part), halves_added(*in_z_part)], axis=1),
-        "dp", 0, 0, tiled=True,
-    )
-    router_prob = jax.nn.softmax(contract_cols(normed_two_bf, router_t), axis=-1)
-    gate_prob = jnp.sum(router_prob * onehot_int.astype(F32), axis=1) * keep
-    result = from_rows((middle + gate_prob[:, None] * landed(got_out)).astype(BF16))
-    step_grad = rate_sum * (1.0 / LOG2E) + in_sum * xconv
+        leaving, skip_row,
+    )
+    pre_grad, weight_blocks, far_product = together(pre_grad, weight_blocks, far_product)
+    out_blocks = lax.all_to_all(product_part(near_product, far_product), "dp", 0, 0, tiled=True)
     decay_log_grad = jnp.sum(decay_sum, axis=0) * decay_rate
-    xconv_grad = in_sum * step_size + skip_row[0] * scan_grad
-
-    def unmixed(value):
-        return jnp.sum(value, axis=-1).transpose(1, 0, 3, 2).reshape(tokens, states)
-
-    skip_grad = jnp.sum(scan_grad * xconv, axis=(0, 1, 2))
-    pre_grad = (step_grad * jax.nn.sigmoid(dt_pre)).reshape(tokens, inner)
-    dt_shift_grad = jnp.sum(pre_grad, axis=0)
+    dt_shift_grad, skip_grad = jnp.sum(scan_sums, axis=0)[:2]
+    pre_grad = pre_grad.reshape(tokens, inner)
     dt_proj_grad = contract_rows(dt_low.astype(F32), pre_grad, HIGHEST)
     dt_low_grad = contract_cols(pre_grad, dt_proj.astype(F32), HIGHEST)
-    proj_part = jnp.concatenate([dt_low_grad, unmixed(in_lanes), unmixed(out_lanes)], axis=1)
+    mix_grad = mix_grad.reshape(tokens, LANES)[:, : 2 * states]
+    proj_part = jnp.concatenate([dt_low_grad, mix_grad], axis=1)
     proj_grad_bf = axis_sum(proj_part, "tp").astype(BF16)
     x_proj_grad_t = contract_rows(proj_grad_bf, xconv_rows)
-    xconv_grad = xconv_grad + jnp.dot(
-        proj_grad_bf, x_proj_t, preferred_element_type=F32
-    ).reshape(x_pre.shape)
-    conv_grad = jax.vjp(jax.nn.silu, conv_pre)[1](xconv_grad)[0]
-    taps_grad = jnp.stack(
+    flat = (chains * SEGMENTS, inner)
+    x_grad_bf, conv_sums, head, last = conv_back(
+        proj_grad_bf,
+        x_proj_t,
+        xconv_grad.reshape(steps, *flat),
+        extended_bf.reshape(steps + taps - 1, *flat),
+        tap_weights,
+        conv_shift,
+    )
+    taps_grad, shift_grad = conv_sums[:taps], conv_sums[taps]
+    edge_back = passed_along(
+        head.reshape(taps - 1, chains, SEGMENTS, inner)[:, :, :1], "ctx", -1
+    )
+    edge_back, weight_blocks, out_blocks = together(edge_back, weight_blocks, out_blocks)
+    weight_blocks, far_blocks = expert_weight_halves(weight_blocks, experts)
+    reaching = jnp.stack(
         [
-            jnp.sum(conv_grad * extended[tap : tap + steps], axis=(0, 1, 2))
-            for tap in range(taps)
+            sum(tap_weights[tap] * edge_back[at - tap] for tap in range(at + 1))
+            for at in range(taps - 1)
         ]
     )
-    shift_grad = jnp.sum(conv_grad, axis=(0, 1, 2))
-    head = conv_grad[: taps - 1]
-    edge_back = passed_along(head[:, :, :1], "ctx", -1)
-    edge_back, weight_blocks = together(edge_back, weight_blocks)
-    weight_blocks, far_blocks = expert_weight_halves(weight_blocks, experts)
-    later = jnp.concatenate([head[:, :, 1:], edge_back], axis=2)
-    reaching = jnp.concatenate([conv_grad, later], axis=0)
-    x_pre_grad = tap_weights[taps - 1] * conv_grad
-    for tap in range(taps - 1):
-        ahead = taps - 1 - tap
-        x_pre_grad = x_pre_grad + tap_weights[tap] * reaching[ahead : ahead + steps]
-    x_grad_bf = x_pre_grad.astype(BF16).reshape(tokens, inner)
+    reaching = jnp.pad(reaching, ((0, 0), (0, 0), (SEGMENTS - 1, 0), (0, 0)))
+    last = (last + reaching.reshape(taps - 1, *flat)).astype(BF16)
+    x_grad_bf = lax.dynamic_update_slice(x_grad_bf, last, (steps - taps + 1, 0, 0))
+    x_grad_bf = x_grad_bf.reshape(tokens, inner)
     small_grads = jnp.concatenate(
         [
             taps_grad,
@@ -895,9 +1060,8 @@
         axis=0,
     )
     small_grads = small_grads.reshape(-1, dp_count, shard).transpose(1, 0, 2)
-    x_grad_bf, out_blocks, small_grads = together(x_grad_bf, out_blocks, small_grads)
-    small_grads = lax.psum_scatter(small_grads, "dp", scatter_dimension=0, tiled=True)[0]
-    out_proj_grad, in_z_grad = weight_shards(out_blocks, 2)
+    x_grad_bf, small_grads, out_blocks = together(x_grad_bf, small_grads, out_blocks)
+    small_blocks = lax.all_to_all(small_grads, "dp", 0, 0, tiled=True)
     normed_grad = axis_sum(
         contract_cols(x_grad_bf, in_x) + contract_cols(z_grad_bf, in_z), "tp"
     )
@@ -910,16 +1074,21 @@
     gain_low = (gain_row - gain_high.astype(F32)).astype(BF16)
     gain_rows = jnp.concatenate([gain_high, gain_low], axis=1)
     gain_rows = jnp.pad(gain_rows, ((0, 0), (0, 6), (0, inner - shard)))
+    in_x_part, out_blocks, small_blocks = together(in_x_part, out_blocks, small_blocks)
+    out_proj_grad, in_z_grad = product_shards(out_blocks)
     in_x_blocks = lax.all_to_all(
         jnp.concatenate([in_x_part, gain_rows], axis=1), "dp", 0, 0, tiled=True
     )
-    far_blocks, in_x_blocks = together(far_blocks, in_x_blocks)
+    in_x_blocks, far_blocks = together(in_x_blocks, far_blocks)
     first_grad, second_grad = expert_weight_grads(weight_blocks, far_blocks)
+    router_prob = jax.nn.softmax(contract_cols(normed_two_bf, router_t), axis=-1)
+    gate_prob = jnp.sum(router_prob * onehot_int.astype(F32), axis=1) * keep
+    result = from_rows((middle + gate_prob[:, None] * landed(got_out)).astype(BF16))
     in_x_sums = axis_sum(jnp.sum(in_x_blocks.astype(F32), axis=0), "ctx")
     in_x_grad = in_x_sums[:shard]
     gain_one_grad = in_x_sums[shard : shard + 1, :shard] + in_x_sums[shard + 1 : shard + 2, :shard]
-    small_grads, in_x_blocks = together(small_grads, in_x_blocks)
-    small_grads = jnp.concatenate([gain_one_grad, axis_sum(small_grads, "ctx")], axis=0)
+    small_grads = axis_sum(jnp.sum(small_blocks, axis=0), "ctx")
+    small_grads = jnp.concatenate([gain_one_grad, small_grads], axis=0)
     sums = [small_grads[bounds[i] : bounds[i + 1]] for i in range(len(bounds) - 1)]
     return (
         result,

time: 1020 us -> 913 us (0.90)
  other arithmetic: 159 us -> 113 us
  Pallas kernels: 302 us -> 267 us
  between operations: 16.1 us -> 2.5 us
  local copies, waits for them, and re-layouts: 92.1 us -> 80.2 us
    all_to_all x4, waiting for transfers between devices: 87.4 us -> 19.3 us  [expert_exchange(): lax.all_to_all(value, 'dp', 0, 0, axis_index_groups=groups, tiled=True)]
    pallas_call x4, Pallas kernels: 183 us -> 134 us  [call(): pl.pallas_call(kernel, grid=self.grid, in_specs=in_specs, out_specs=out_s...]
    ppermute x21, waiting for transfers between devices: 138 us -> 184 us  [swapped(): return lax.ppermute(value, axis, [(0, 1), (1, 0)])]
    reduce_sum x6 -> x3, other arithmetic: 41.6 us -> 4.38 us  [the longest x1 3 us: product_shards(): sums = jnp.sum(blocks.astype(F32), axis=0)]
    pallas_call x0 -> x1, Pallas kernels: none -> 13.4 us  [conv_back(): pl.pallas_call(conv_back_kernel, grid=(width // lanes,), in_specs=[pl.Blo...]
    all_to_all x1, waiting for transfers between devices: 5.19 us -> 17.6 us  [own_expert_blocks(): return lax.all_to_all(both, 'dp', 0, 0, tiled=True)]
    all_to_all x2 -> x3, waiting for transfers between devices: 15.2 us -> 21.7 us  [the longest x1 18.1 us: local(): small_blocks = lax.all_to_all(small_grads, 'dp', 0, 0, tiled=True)]
  transfers between devices with their start and end apart: 34 -> 34, of which waited for: 12 -> 15; matrix products, arithmetic and copies ran while one was open for 27% -> 28% of each run, Pallas kernels for 20% -> 19%
where the time goes in v4:
time: 913 us; the launch traced here: 903 us
  Pallas kernels  267 us (29%)
  waiting for transfers between devices  245 us (27%)
  matrix products  130 us (14%)
  other arithmetic  113 us (12%)
  local copies, waits for them, and re-layouts  80.2 us (9%)
  starting transfers between devices  65.8 us (7%)
    ppermute x21, waiting for transfers between devices, swapped(): return lax.ppermute(value, axis, [(0, 1), (1, 0)])  184 us
    pallas_call x4, Pallas kernels, call(): pl.pallas_call(kernel, grid=self.grid, in_specs=in_specs, out_specs=out_s...  134 us
    pallas_call x1, Pallas kernels, gathered(): pl.pallas_call(partial(gather_kernel, count, parts), in_specs=[anywhere]...  72.2 us
    dot_general x12, matrix products, contract_rows(): lax.dot_general(left_side, right_side, (((0,), (0,)), ((), ())), precisio...  67 us
    pallas_call x2, Pallas kernels, expert_call(): pl.pallas_call(expert_kernel, grid=(count // block,), in_specs=[row_spec,...  47.2 us
    dot_general x6, matrix products, contract_cols(): lax.dot_general(left_side, right_side, (((1,), (1,)), ((), ())), precisio...  30.1 us
    all_to_all x4, starting transfers between devices, expert_exchange(): lax.all_to_all(value, 'dp', 0, 0, axis_index_groups=groups, tiled=True)  19.9 us
    all_to_all x4, waiting for transfers between devices, expert_exchange(): lax.all_to_all(value, 'dp', 0, 0, axis_index_groups=groups, tiled=True)  19.3 us
  transfers between devices with their start and end apart: 34, of which 15 were waited for; matrix products, arithmetic and copies ran while one was open for 28% of the time, Pallas kernels for 19%

profile of v4, /device:TPU:0, one launch (start us, length us, event | category | flops | bytes accessed | tf_op | source)
XLA Modules:
  0.0 903.2 jit_solution(10991504773844094459)
XLA Ops:
  11.5 72.2 %shard_map.297 = (bf16[8,144,1152]{2,1,0:T(8,128)(2,1)}, bf16[8,144,256]{2,1,0:T(8,128)(2,1)}, bf16[8,144,1152]{2,1,0:T(8,128)(2,1)}) custom-call(bf16[144,1152]{1,0:T(8,128)(2,1)} %bitcast.254, bf16[144,256]{1,0:T(8,128)(2,1)} %pad.62.refs_1_, bf16[144,1152]{1,0:T(8,128)(2,1)} %fusion.64.refs_2_), custom_call_target="tpu_custom_call" | custom-call | bytes 11796480 | tf_op jit(solution)/shard_map/pallas_call | solution.py:697
  146.3 19.5 %shard_map.298 = (f32[2,16,8,1152]{3,2,1,0:T(8,128)}, f32[2,16,8,1152]{3,2,1,0:T(8,128)}, f32[2,16,1152]{2,1,0:T(8,128)}) custom-call(f32[64,2,8,1152]{3,2,1,0:T(8,128)} %compare_select_fusion.step_ref, f32[64,2,8,1152]{3,2,1,0:T(8,128)} %get-tuple-element.253.input_ref, f32[2,64,16,8,128]{4,3,2,1,0:T(8,128)} %broadcast_in_dim.28.mix_in_ref, ...), custom_call_target="tpu_custom_call" | custom-call | flops 94371840 | bytes 20922368 | tf_op jit(solution)/shard_map/pallas_call | solution.py:360
  165.9 17.6 %all-to-all-done.up_a.down_a = bf16[8,288,768]{2,1,0:T(8,128)(2,1)} async-done(((bf16[8,288,768]{2,1,0:T(8,128)(2,1)}), bf16[8,288,768]{2,1,0:T(8,128)(2,1)}, u32[]{:S(2)}, u32[]{:S(2)}) %all-to-all-start) | async-done | bytes 3538976 | tf_op jit(solution)/shard_map/all_to_all | solution.py:595
  207.2 26.5 %shard_map.299 = (f32[64,2,8,1152]{3,2,1,0:T(8,128)}, f32[2,16,8,1152]{3,2,1,0:T(8,128)}) custom-call(f32[64,2,8,1152]{3,2,1,0:T(8,128)} %compare_select_fusion.step_ref, f32[64,2,8,1152]{3,2,1,0:T(8,128)} %get-tuple-element.253.input_ref, f32[2,64,16,8,128]{4,3,2,1,0:T(8,128)} %broadcast_in_dim.28.mix_in_ref, ...), custom_call_target="tpu_custom_call" | custom-call | flops 132120576 | bytes 35209216 | tf_op jit(solution)/shard_map/pallas_call | solution.py:360
  233.6 8.2 multiply_convert_fusion.2
  241.8 8.2 fusion.60
  268.5 6.4 all-to-all-start.2
  275.1 40.6 %collective-permute-done.6.down_b = bf16[8,144,768]{2,1,0:T(8,128)(2,1)} collective-permute-done((bf16[8,144,768]{2,1,0:T(8,128)(2,1)}, bf16[8,144,768]{2,1,0:T(8,128)(2,1)}, u32[]{:S(2)}, u32[]{:S(2)}) %collective-permute-start.6) | collective-permute-done | bytes 1769504 | tf_op jit(solution)/shard_map/ppermute | solution.py:32
  315.7 13.4 %all-to-all-done.2 = bf16[8,128,1152]{2,1,0:T(8,128)(2,1)} async-done(((bf16[8,128,1152]{2,1,0:T(8,128)(2,1)}), bf16[8,128,1152]{2,1,0:T(8,128)(2,1)}, u32[]{:S(2)}, u32[]{:S(2)}) %all-to-all-start.2) | async-done | bytes 2359328 | tf_op jit(solution)/shard_map/all_to_all | solution.py:578
  334.0 23.5 %shard_map.301 = (f32[1024,1152]{1,0:T(8,128)}, f32[1024,1152]{1,0:T(8,128)}, f32[1024,8]{1,0:T(8,128)}, bf16[1024,1152]{1,0:T(8,128)(2,1)}, bf16[1024,768]{1,0:...) custom-call(bf16[1024,1152]{1,0:T(8,128)(2,1)} %collective-permute-done.7.rows_ref, ...), custom_call_target="tpu_custom_call" | custom-call | flops 14495514624 | bytes 29884416 | tf_op jit(solution)/shard_map/pallas_call | solution.py:554
  358.1 23.7 %shard_map.300 = (f32[1024,1152]{1,0:T(8,128)}, f32[1024,1152]{1,0:T(8,128)}, f32[1024,8]{1,0:T(8,128)}, bf16[1024,1152]{1,0:T(8,128)(2,1)}, bf16[1024,768]{1,0:...) custom-call(bf16[1024,1152]{1,0:T(8,128)(2,1)} %bitcast.36.rows_ref, ...), custom_call_target="tpu_custom_call" | custom-call | flops 14495514624 | bytes 29884416 | tf_op jit(solution)/shard_map/pallas_call | solution.py:554
  387.3 7.1 multiply_reduce_fusion
  403.3 7.3 convolution_convert_fusion.3
  430.4 21.1 %collective-permute-done.11 = bf16[1152,768]{1,0:T(8,128)(2,1)} collective-permute-done((bf16[1152,768]{1,0:T(8,128)(2,1)S(1)}, bf16[1152,768]{1,0:T(8,128)(2,1)}, u32[]{:S(2)}, u32[]{:S(2)}) %collective-permute-start.11) | collective-permute-done | bytes 1769504 | tf_op jit(solution)/shard_map/ppermute | solution.py:32
  470.7 26.8 %collective-permute-done.13 = bf16[1152,768]{1,0:T(8,128)(2,1)} collective-permute-done((bf16[1152,768]{1,0:T(8,128)(2,1)}, bf16[1152,768]{1,0:T(8,128)(2,1)}, u32[]{:S(2)}, u32[]{:S(2)}) %collective-permute-start.13) | collective-permute-done | bytes 1769504 | tf_op jit(solution)/shard_map/ppermute | solution.py:32
  510.6 7.0 fusion.59
  526.9 8.7 convolution_convert_fusion.1
  535.6 19.2 %shard_map.302 = (f32[2,16,8,1152]{3,2,1,0:T(8,128)}, f32[2,16,8,1152]{3,2,1,0:T(8,128)}, f32[2,16,1152]{2,1,0:T(8,128)}) custom-call(f32[64,2,8,1152]{3,2,1,0:T(8,128)} %compare_select_fusion.step_ref, f32[2,64,16,8,128]{4,3,2,1,0:T(8,128)} %broadcast_in_dim.29.mix_out_ref, f32[64,2,8,1152]{3,2,1,0:T(8,128)} %get-tuple-element.134.grad_ref, ...), custom_call_target="tpu_custom_call" | custom-call | flops 94371840 | bytes 20922368 | tf_op jit(solution)/shard_map/pallas_call | solution.py:360
  556.5 7.4 fusion.50
  568.5 69.0 %shard_map.303 = (f32[64,2,8,1152]{3,2,1,0:T(8,128)}, f32[64,2,8,1152]{3,2,1,0:T(8,128)}, f32[2,16,1152]{2,1,0:T(8,128)}, f32[2,8,1152]{2,1,0:T(8,128)}, f32[64,2,8,128]{3,2,1,0:T(8,128)}) custom-call(f32[64,2,8,1152]{3,2,1,0:T(8,128)} %compare_select_fusion.step_ref, f32[64,2,8,1152]{3,2,1,0:T(8,128)} %get-tuple-element.253.input_ref, ...), custom_call_target="tpu_custom_call" | custom-call | flops 377487360 | bytes 45396480 | tf_op jit(solution)/shard_map/pallas_call | solution.py:360
  642.8 6.0 all-to-all-start.6
  667.5 6.1 copy.149
  681.0 13.4 %shard_map.304 = (bf16[64,16,1152]{2,1,0:T(8,128)(2,1)}, f32[8,1152]{1,0:T(8,128)}, f32[3,16,1152]{2,1,0:T(8,128)}, f32[3,16,1152]{2,1,0:T(8,128)}) custom-call(bf16[1024,104]{1,0:T(8,128)(2,1)} %add_convert_fusion.6.proj_ref, bf16[104,1152]{1,0:T(8,128)(2,1)} %slice.195.weight_ref, f32[64,16,1152]{2,1,0:T(8,128)} %bitcast.214, ...), custom_call_target="tpu_custom_call" | custom-call | flops 1 | bytes 1 | tf_op jit(solution)/shard_map/pallas_call | solution.py:476
  709.0 6.1 fusion.112
  715.1 7.2 convolution_add_fusion.1
  737.2 18.1 %all-to-all-done.7 = f32[8,208,144]{1,2,0:T(8,128)S(1)} async-done(((f32[8,208,144]{1,2,0:T(8,128)}), f32[8,208,144]{1,2,0:T(8,128)S(1)}, u32[]{:S(2)}, u32[]{:S(2)}) %all-to-all-start.7) | async-done | bytes 958496 | tf_op jit(solution)/shard_map/all_to_all | solution.py:1064
  755.3 6.9 fusion.16
  787.3 68.6 %collective-permute-done.24 = f32[208,144]{0,1:T(8,128)S(1)} collective-permute-done((f32[208,144]{0,1:T(8,128)S(1)}, f32[208,144]{0,1:T(8,128)S(1)}, u32[]{:S(2)}, u32[]{:S(2)}) %collective-permute-start.24) | collective-permute-done | bytes 119840 | tf_op jit(solution)/shard_map/ppermute | solution.py:32
  860.6 8.2 collective-permute-done.23
  871.0 7.3 add_convert_fusion.1
  885.5 6.2 convert_bitcast_fusion
  891.6 8.8 collective-permute-done.22
  (389 shorter events, 304.8 us)
Async XLA Ops:
  95.2 28.3 %collective-permute-start = (bf16[3,2,1,1152]{3,2,1,0:T(2,128)(2,1)S(1)}, bf16[3,2,1,1152]{3,2,1,0:T(2,128)(2,1)S(1)}, u32[]{:S(2)}, u32[]{:S(2)}) collective-permute-start(bf16[3,2,1,1152]{3,2,1,0:T(2,128)(2,1)S(1)} %slice.234), channel_id=1, source_target_pairs={{0,2},{1,3},{4,6},{5,7},{8,10},{9,11},{12,14},{13,15},{16,18},{17,... | collective-permute-start | bytes 41480 | tf_op jit(solution)/shard_map/ppermute | solution.py:38
  101.6 81.8 %all-to-all-start = ((bf16[8,288,768]{2,1,0:T(8,128)(2,1)}), bf16[8,288,768]{2,1,0:T(8,128)(2,1)}, u32[]{:S(2)}, u32[]{:S(2)}) async-start(bf16[8,288,768]{2,1,0:T(8,128)(2,1)} %slice_select_fusion), calls=%async_computation | async-start | bytes 7077888 | tf_op jit(solution)/shard_map/all_to_all | solution.py:595
  129.2 104.5 %collective-permute-start.3 = (bf16[1152,1152]{1,0:T(8,128)(2,1)}, bf16[1152,1152]{1,0:T(8,128)(2,1)}, u32[]{:S(2)}, u32[]{:S(2)}) collective-permute-start(bf16[1152,1152]{1,0:T(8,128)(2,1)} %bitcast.15), channel_id=1, source_target_pairs={{0,2},{2,0},{1,3},{3,1},{4,6},{6,4},{5,7},{7,5},{8,10},{10,8},{9,1... | collective-permute-start | bytes 7962632 | tf_op jit(solution)/shard_map/ppermute | solution.py:32
  183.4 58.4 %all-to-all-start.1 = ((bf16[8,128,1152]{2,1,0:T(8,128)(2,1)}), bf16[8,128,1152]{2,1,0:T(8,128)(2,1)}, u32[]{:S(2)}, u32[]{:S(2)}) async-start(bf16[8,128,1152]{2,1,0:T(8,128)(2,1)} %bitcast.243), calls=%async_computation.1 | async-start | bytes 4718592 | tf_op jit(solution)/shard_map/all_to_all | solution.py:578
  187.8 5.3 collective-permute-start.2
  197.2 44.6 %collective-permute-start.4 = (bf16[8,144,768]{2,1,0:T(8,128)(2,1)}, bf16[8,144,768]{2,1,0:T(8,128)(2,1)}, u32[]{:S(2)}, u32[]{:S(2)}) collective-permute-start(bf16[8,144,768]{2,1,0:T(8,128)(2,1)} %get-tuple-element.263), channel_id=1, source_target_pairs={{0,2},{2,0},{1,3},{3,1},{4,6},{6,4},{5,7},{7,5},{8,10},{10,8},{9,1... | collective-permute-start | bytes 5308424 | tf_op jit(solution)/shard_map/ppermute | solution.py:32
  250.0 8.3 collective-permute-start.5
  268.5 60.5 %all-to-all-start.2 = ((bf16[8,128,1152]{2,1,0:T(8,128)(2,1)}), bf16[8,128,1152]{2,1,0:T(8,128)(2,1)}, u32[]{:S(2)}, u32[]{:S(2)}) async-start(bf16[8,128,1152]{2,1,0:T(8,128)(2,1)} %bitcast.245), calls=%async_computation.2 | async-start | bytes 4718592 | tf_op jit(solution)/shard_map/all_to_all | solution.py:578
  274.9 40.8 %collective-permute-start.6 = (bf16[8,144,768]{2,1,0:T(8,128)(2,1)}, bf16[8,144,768]{2,1,0:T(8,128)(2,1)}, u32[]{:S(2)}, u32[]{:S(2)}) collective-permute-start(bf16[8,144,768]{2,1,0:T(8,128)(2,1)} %get-tuple-element.262), channel_id=1, source_target_pairs={{0,2},{2,0},{1,3},{3,1},{4,6},{6,4},{5,7},{7,5},{8,10},{10,8},{9,1... | collective-permute-start | bytes 5308424 | tf_op jit(solution)/shard_map/ppermute | solution.py:32
  275.0 55.2 %collective-permute-start.8 = (bf16[1024,1152]{1,0:T(8,128)(2,1)}, bf16[1024,1152]{1,0:T(8,128)(2,1)}, u32[]{:S(2)}, u32[]{:S(2)}) collective-permute-start(bf16[1024,1152]{1,0:T(8,128)(2,1)} %bitcast.33.cotan_ref), channel_id=1, source_target_pairs={{0,1},{1,0},{2,3},{3,2},{4,5},{5,4},{6,7},{7,6},{8,9},{9,8},{10,11... | collective-permute-start | bytes 7077896 | tf_op jit(solution)/shard_map/ppermute | solution.py:32
  329.1 4.9 collective-permute-start.7
  357.5 29.8 %collective-permute-start.10 = (f32[1024,1152]{1,0:T(8,128)}, f32[1024,1152]{1,0:T(8,128)}, u32[]{:S(2)}, u32[]{:S(2)}) collective-permute-start(f32[1024,1152]{1,0:T(8,128)} %get-tuple-element.115), channel_id=1, source_target_pairs={{0,1},{1,0},{2,3},{3,2},{4,5},{5,4},{6,7},{7,6},{8,9},{9,8},{10,11... | collective-permute-start | bytes 14155784 | tf_op jit(solution)/shard_map/ppermute | solution.py:32
  357.7 36.7 %collective-permute-start.9 = (f32[1024,1152]{1,0:T(8,128)}, f32[1024,1152]{1,0:T(8,128)S(1)}, u32[]{:S(2)}, u32[]{:S(2)}) collective-permute-start(f32[1024,1152]{1,0:T(8,128)} %get-tuple-element.113), channel_id=1, source_target_pairs={{0,1},{1,0},{2,3},{3,2},{4,5},{5,4},{6,7},{7,6},{8,9},{9,8},{10,11... | collective-permute-start | bytes 14155784 | tf_op jit(solution)/shard_map/ppermute | solution.py:32
  398.5 58.8 %all-to-all-start.3 = ((bf16[8,128,1152]{2,1,0:T(8,128)(2,1)}), bf16[8,128,1152]{2,1,0:T(8,128)(2,1)}, u32[]{:S(2)}, u32[]{:S(2)}) async-start(bf16[8,128,1152]{2,1,0:T(8,128)(2,1)} %bitcast.208), calls=%async_computation.3 | async-start | bytes 4718592 | tf_op jit(solution)/shard_map/all_to_all | solution.py:578
  410.6 40.8 %collective-permute-start.11 = (bf16[1152,768]{1,0:T(8,128)(2,1)S(1)}, bf16[1152,768]{1,0:T(8,128)(2,1)}, u32[]{:S(2)}, u32[]{:S(2)}) collective-permute-start(bf16[1152,768]{1,0:T(8,128)(2,1)S(1)} %convolution_convert_fusion.3), channel_id=1, source_target_pairs={{0,2},{2,0},{1,3},{3,1},{4,6},{6,4},{5,7},{7,5},{8,10},{10,8},{9,1... | collective-permute-start | bytes 5308424 | tf_op jit(solution)/shard_map/ppermute | solution.py:32
  457.3 40.1 %collective-permute-start.13 = (bf16[1152,768]{1,0:T(8,128)(2,1)}, bf16[1152,768]{1,0:T(8,128)(2,1)}, u32[]{:S(2)}, u32[]{:S(2)}) collective-permute-start(bf16[1152,768]{1,0:T(8,128)(2,1)} %convolution_convert_fusion.4), channel_id=1, source_target_pairs={{0,2},{2,0},{1,3},{3,1},{4,6},{6,4},{5,7},{7,5},{8,10},{10,8},{9,1... | collective-permute-start | bytes 5308424 | tf_op jit(solution)/shard_map/ppermute | solution.py:32
  463.2 39.2 %collective-permute-start.12 = (bf16[1024,1152]{1,0:T(8,128)(2,1)}, bf16[1024,1152]{1,0:T(8,128)(2,1)}, u32[]{:S(2)}, u32[]{:S(2)}) collective-permute-start(bf16[1024,1152]{1,0:T(8,128)(2,1)} %fusion.28), channel_id=1, source_target_pairs={{0,1},{1,0},{2,3},{3,2},{4,5},{5,4},{6,7},{7,6},{8,9},{9,8},{10,11... | collective-permute-start | bytes 7077896 | tf_op jit(solution)/shard_map/ppermute | solution.py:32
  463.2 59.2 %all-to-all-start.4 = ((bf16[8,128,1152]{2,1,0:T(8,128)(2,1)}), bf16[8,128,1152]{2,1,0:T(8,128)(2,1)}, u32[]{:S(2)}, u32[]{:S(2)}) async-start(bf16[8,128,1152]{2,1,0:T(8,128)(2,1)} %bitcast.210), calls=%async_computation.4 | async-start | bytes 4718592 | tf_op jit(solution)/shard_map/all_to_all | solution.py:578
  522.4 115.1 %all-to-all-start.5 = ((bf16[8,288,768]{2,1,0:T(8,128)(2,1)}), bf16[8,288,768]{2,1,0:T(8,128)(2,1)}, u32[]{:S(2)}, u32[]{:S(2)}) async-start(bf16[8,288,768]{2,1,0:T(8,128)(2,1)} %pad_maximum_fusion.1), calls=%async_computation.5 | async-start | bytes 7077888 | tf_op jit(solution)/shard_map/all_to_all | solution.py:1001
  554.8 9.1 %collective-permute-start.15 = (f32[2,16,1152]{2,1,0:T(8,128)}, f32[2,16,1152]{2,1,0:T(8,128)}, u32[]{:S(2)}, u32[]{:S(2)}) collective-permute-start(f32[2,16,1152]{2,1,0:T(8,128)} %get-tuple-element.138), channel_id=1, source_target_pairs={{2,0},{3,1},{6,4},{7,5},{10,8},{11,9},{14,12},{15,13},{18,16},{19,... | collective-permute-start | bytes 442376 | tf_op jit(solution)/shard_map/ppermute | solution.py:38
  563.9 73.6 %collective-permute-start.16 = (bf16[1152,1152]{1,0:T(8,128)(2,1)}, bf16[1152,1152]{1,0:T(8,128)(2,1)}, u32[]{:S(2)}, u32[]{:S(2)}) collective-permute-start(bf16[1152,1152]{1,0:T(8,128)(2,1)} %convolution_convert_fusion.1), channel_id=1, source_target_pairs={{0,2},{2,0},{1,3},{3,1},{4,6},{6,4},{5,7},{7,5},{8,10},{10,8},{9,1... | collective-permute-start | bytes 7962632 | tf_op jit(solution)/shard_map/ppermute | solution.py:32
  642.8 65.4 %all-to-all-start.6 = ((bf16[8,144,1152]{2,1,0:T(8,128)(2,1)}), bf16[8,144,1152]{2,1,0:T(8,128)(2,1)}, u32[]{:S(2)}, u32[]{:S(2)}) async-start(bf16[8,144,1152]{2,1,0:T(8,128)(2,1)} %bitcast.202), calls=%async_computation.6 | async-start | bytes 5308416 | tf_op jit(solution)/shard_map/all_to_all | solution.py:1013
  664.5 14.6 %collective-permute-start.17 = (f32[1024,104]{1,0:T(8,128)}, f32[1024,104]{1,0:T(8,128)}, u32[]{:S(2)}, u32[]{:S(2)}) collective-permute-start(f32[1024,104]{1,0:T(8,128)} %pad_maximum_fusion.5), channel_id=1, source_target_pairs={{0,1},{1,0},{2,3},{3,2},{4,5},{5,4},{6,7},{7,6},{8,9},{9,8},{10,11... | collective-permute-start | bytes 1277960 | tf_op jit(solution)/shard_map/ppermute | solution.py:32
  695.4 9.2 %collective-permute-start.18 = (f32[3,2,1,1152]{3,2,1,0:T(1,128)S(1)}, f32[3,2,1,1152]{3,2,1,0:T(1,128)S(1)}, u32[]{:S(2)}, u32[]{:S(2)}) collective-permute-start(f32[3,2,1,1152]{3,2,1,0:T(1,128)S(1)} %slice.250), channel_id=1, source_target_pairs={{2,0},{3,1},{6,4},{7,5},{10,8},{11,9},{14,12},{15,13},{18,16},{19,... | collective-permute-start | bytes 82952 | tf_op jit(solution)/shard_map/ppermute | solution.py:38
  722.3 33.0 %collective-permute-start.20 = (f32[1024,1152]{1,0:T(8,128)}, f32[1024,1152]{1,0:T(8,128)}, u32[]{:S(2)}, u32[]{:S(2)}) collective-permute-start(f32[1024,1152]{1,0:T(8,128)} %convolution_add_fusion.1), channel_id=1, source_target_pairs={{0,1},{1,0},{2,3},{3,2},{4,5},{5,4},{6,7},{7,6},{8,9},{9,8},{10,11... | collective-permute-start | bytes 14155784 | tf_op jit(solution)/shard_map/ppermute | solution.py:32
  722.3 33.0 %all-to-all-start.7 = ((f32[8,208,144]{1,2,0:T(8,128)}), f32[8,208,144]{1,2,0:T(8,128)S(1)}, u32[]{:S(2)}, u32[]{:S(2)}) async-start(f32[8,208,144]{1,2,0:T(8,128)} %bitcast.67), calls=%async_computation.7 | async-start | bytes 2359296 | tf_op jit(solution)/shard_map/all_to_all | solution.py:1064
  732.0 48.8 %collective-permute-start.14 = (bf16[1024,1152]{1,0:T(8,128)(2,1)}, bf16[1024,1152]{1,0:T(8,128)(2,1)}, u32[]{:S(2)}, u32[]{:S(2)}) collective-permute-start(bf16[1024,1152]{1,0:T(8,128)(2,1)} %fusion.29), channel_id=1, source_target_pairs={{0,1},{1,0},{2,3},{3,2},{4,5},{5,4},{6,7},{7,6},{8,9},{9,8},{10,11... | collective-permute-start | bytes 7077896 | tf_op jit(solution)/shard_map/ppermute | solution.py:32
  765.9 114.3 %all-to-all-start.8 = ((bf16[8,152,1152]{2,1,0:T(8,128)(2,1)}), bf16[8,152,1152]{2,1,0:T(8,128)(2,1)S(1)}, u32[]{:S(2)}, u32[]{:S(2)}) async-start(bf16[8,152,1152]{2,1,0:T(8,128)(2,1)} %pad_maximum_fusion.2), calls=%async_computation.8 | async-start | bytes 5603328 | tf_op jit(solution)/shard_map/all_to_all | solution.py:1079
  773.0 107.2 %collective-permute-start.21 = (bf16[8,288,768]{2,1,0:T(8,128)(2,1)}, bf16[8,288,768]{2,1,0:T(8,128)(2,1)}, u32[]{:S(2)}, u32[]{:S(2)}) collective-permute-start(bf16[8,288,768]{2,1,0:T(8,128)(2,1)} %all-to-all-done.5), channel_id=1, source_target_pairs={{0,2},{2,0},{1,3},{3,1},{4,6},{6,4},{5,7},{7,5},{8,10},{10,8},{9,1... | collective-permute-start | bytes 10616840 | tf_op jit(solution)/shard_map/ppermute | solution.py:32
  775.7 80.2 %collective-permute-start.24 = (f32[208,144]{0,1:T(8,128)S(1)}, f32[208,144]{0,1:T(8,128)S(1)}, u32[]{:S(2)}, u32[]{:S(2)}) collective-permute-start(f32[208,144]{0,1:T(8,128)S(1)} %reduce_sum.159), channel_id=1, source_target_pairs={{0,2},{2,0},{1,3},{3,1},{4,6},{6,4},{5,7},{7,5},{8,10},{10,8},{9,1... | collective-permute-start | bytes 359432 | tf_op jit(solution)/shard_map/ppermute | solution.py:32
  779.5 89.2 %collective-permute-start.23 = (f32[144,1152]{1,0:T(8,128)}, f32[144,1152]{1,0:T(8,128)}, u32[]{:S(2)}, u32[]{:S(2)}) collective-permute-start(f32[144,1152]{1,0:T(8,128)} %convert_reduce_fusion.1), channel_id=1, source_target_pairs={{0,2},{2,0},{1,3},{3,1},{4,6},{6,4},{5,7},{7,5},{8,10},{10,8},{9,1... | collective-permute-start | bytes 1990664 | tf_op jit(solution)/shard_map/ppermute | solution.py:32
  884.1 16.3 %collective-permute-start.22 = (f32[152,1152]{1,0:T(8,128)S(1)}, f32[152,1152]{1,0:T(8,128)S(1)}, u32[]{:S(2)}, u32[]{:S(2)}) collective-permute-start(f32[152,1152]{1,0:T(8,128)S(1)} %convert_reduce_fusion), channel_id=1, source_target_pairs={{0,2},{2,0},{1,3},{3,1},{4,6},{6,4},{5,7},{7,5},{8,10},{10,8},{9,1... | collective-permute-start | bytes 2101256 | tf_op jit(solution)/shard_map/ppermute | solution.py:32
  (88 other events, 1370.9 us)

commit v5 on v4

--- a/solution.py
+++ b/solution.py
@@ -23,7 +23,8 @@
 UNROLL_D = 4
 UNROLL_E = 8
 BLOCKS = 3
-COVER = 1
+COVER = 100
+HALVES = 1
 BF16 = jnp.bfloat16
 F32 = jnp.float32
 
@@ -395,10 +396,9 @@
             [self.state_spec, self.state_spec, self.edge_spec],
         )
 
-    def adjoint(self, step, inputs, mix_in, mix_out, grad, rate, start, decay, adjoint, enter, skip):
+    def adjoint(self, args):
         return self.call(
-            adjoint_kernel, 20,
-            (step, inputs, mix_in, mix_out, grad, rate, start, decay, adjoint, enter, skip),
+            adjoint_kernel, 20, args,
             [self.rows_spec, self.rows_spec, self.mix_spec, self.mix_spec, self.rows_spec,
              self.rate_spec, self.state_spec, self.state_spec, self.state_spec, self.edge_spec,
              self.skip_spec],
@@ -496,10 +496,11 @@
 
 
 def expert_kernel(
-    rows_ref, cotan_ref, router_ref, mask_ref, up_a, down_a, up_b, down_b,
-    out_ref, picked_ref, prob_ref, grad_ref, active_a, active_b, hidden_a, hidden_b,
+    kept, rows_ref, cotan_ref, router_ref, mask_ref, up_a, down_a, up_b, down_b, *refs
 ):
+    out_ref, picked_ref, prob_ref, copy_ref, grad_ref, active_a, active_b, hidden_a, hidden_b = refs[kept:]
     rows = rows_ref[...]
+    copy_ref[...] = rows
     logits = contract_cols(rows, router_ref[...])
     shifted = jnp.exp(logits - jnp.max(logits, axis=1, keepdims=True))
     prob = shifted / jnp.sum(shifted, axis=1, keepdims=True)
@@ -528,13 +529,14 @@
     picked_ref[...] = picked
 
 
-def expert_call(rows, cotan, router_t, mask, blocks, far_up, far_down):
+def expert_call(rows, cotan, router_t, mask, blocks, far_up, far_down, part, parts, kept):
     count, width = rows.shape
     shard, hidden = far_up.shape[1:]
     block = math.gcd(count, 512)
-    row_spec = pl.BlockSpec((block, width), lambda at: (at, 0))
-    hidden_spec = pl.BlockSpec((block, hidden), lambda at: (at, 0))
-    prob_spec = pl.BlockSpec((block, router_t.shape[0]), lambda at: (at, 0))
+    base = part * (count // block)
+
+    def rows_of(columns, low=0):
+        return pl.BlockSpec((block, columns), lambda at: (at + low, 0))
 
     def whole(array):
         return pl.BlockSpec(array.shape, lambda at: (0, 0), pipeline_mode=pl.Buffered(1))
@@ -544,28 +546,28 @@
             (array.shape[0], shard, hidden), lambda step: (0, at, 0), pipeline_mode=pl.Buffered(1)
         )
 
-    fixed = (router_t, mask, blocks, blocks, far_up, far_down)
-    fixed_specs = [
-        whole(router_t), whole(mask),
-        layer(blocks, 0), layer(blocks, 1), layer(far_up, 0), layer(far_down, 0),
-    ]
-    wide, narrow = jax.ShapeDtypeStruct((count, width), F32), jax.ShapeDtypeStruct((count, width), BF16)
-    inner = jax.ShapeDtypeStruct((count, hidden), BF16)
+    experts = router_t.shape[0]
+    inputs = (rows, cotan, router_t, mask, blocks, blocks, far_up, far_down)
+    columns = (width, width, hidden, hidden, hidden, hidden)
     return pl.pallas_call(
-        expert_kernel,
+        partial(expert_kernel, len(kept)),
         grid=(count // block,),
-        in_specs=[row_spec, row_spec, *fixed_specs],
-        out_specs=[row_spec, row_spec, prob_spec, row_spec, *(hidden_spec,) * 4],
+        in_specs=[
+            rows_of(width), rows_of(width), whole(router_t), whole(mask),
+            layer(blocks, 0), layer(blocks, 1), layer(far_up, 0), layer(far_down, 0),
+            *[pl.BlockSpec(memory_space=pl.ANY)] * len(kept),
+        ],
+        out_specs=[
+            rows_of(width), rows_of(width), rows_of(experts), *(rows_of(one, base) for one in columns)
+        ],
         out_shape=[
-            wide, wide, jax.ShapeDtypeStruct((count, router_t.shape[0]), F32), narrow, *(inner,) * 4
+            *(jax.ShapeDtypeStruct((count, one), F32) for one in (width, width, experts)),
+            *(jax.ShapeDtypeStruct((parts * count, one), BF16) for one in columns),
         ],
+        input_output_aliases={len(inputs) + at: 3 + at for at in range(len(kept))},
         compiler_params=pltpu.CompilerParams(vmem_limit_bytes=VMEM_LIMIT),
-        cost_estimate=pl.CostEstimate(
-            flops=16 * count * width * hidden,
-            transcendentals=4 * count * hidden,
-            bytes_accessed=count * (14 * width + 8 * hidden) + 8 * width * hidden,
-        ),
-    )(rows, cotan, *fixed)
+        cost_estimate=pl.CostEstimate(flops=1, transcendentals=0, bytes_accessed=1),
+    )(*inputs, *kept)
 
 
 def expert_exchange(value, experts):
@@ -746,23 +748,26 @@
     return jnp.concatenate(parts, axis=1)
 
 
-def expert_weight_halves(blocks, experts):
+def expert_weight_blocks(blocks, experts):
     count = lax.axis_size("dp")
     if count != experts:
         blocks = jnp.sum(
             blocks.reshape(count // experts, experts, *blocks.shape[1:]).astype(F32), axis=0
         ).astype(BF16)
+    shard = blocks.shape[1] // 2
+    return blocks[:, :shard], blocks[:, shard:]
+
+
+def far_hidden(blocks):
     if lax.axis_size("ctx") == 2:
-        return blocks, swapped(blocks, "ctx")
-    return blocks, lax.all_gather(blocks, "ctx", axis=2, tiled=True)
-
-
-def expert_weight_grads(blocks, far_blocks):
-    joined = far_blocks
+        return swapped(blocks, "ctx")
+    return lax.all_gather(blocks, "ctx", axis=2, tiled=True)
+
+
+def expert_weight_grad(blocks, far_blocks):
     if lax.axis_size("ctx") == 2:
-        joined = jnp.concatenate(by_ctx(blocks, far_blocks), axis=2)
-    shard = joined.shape[1] // 2
-    return joined[:, :shard].astype(F32), joined[:, shard:].astype(F32)
+        far_blocks = jnp.concatenate(by_ctx(blocks, far_blocks), axis=2)
+    return far_blocks.astype(F32)
 
 
 def pair_products(first, second):
@@ -824,7 +829,7 @@
     dp_count = lax.axis_size("dp")
     tp_count = lax.axis_size("tp")
     capacity = tokens // 4
-    part_cap = capacity // tp_count
+    part_cap = capacity // tp_count // HALVES
     slots = experts * part_cap
     tp_index = lax.axis_index("tp")
     scan = Scan(steps, chains, states, inner)
@@ -884,26 +889,32 @@
     route = to_rows(expert_ids)[:, 0]
     keep = to_rows(keep_mask)[:, 0].astype(F32)
     onehot_int = (route[:, None] == jnp.arange(experts, dtype=jnp.int32)[None, :]).astype(jnp.int32)
-    rank = jnp.sum((jnp.cumsum(onehot_int, axis=0) - 1) * onehot_int, axis=1) - tp_index * part_cap
-    here = (rank >= 0) & (rank < part_cap)
-    token_slot = jnp.where(here, route * part_cap + rank, -1)
-    place = (
-        token_slot[None, :] == jnp.arange(slots, dtype=jnp.int32)[:, None]
-    ).astype(BF16)
-
-    def slotted(value):
-        sent = jnp.dot(place, value, preferred_element_type=F32).astype(BF16)
+    rank = jnp.sum((jnp.cumsum(onehot_int, axis=0) - 1) * onehot_int, axis=1)
+    places = []
+    for half in range(HALVES):
+        own = rank - (tp_index * HALVES + half) * part_cap
+        token_slot = jnp.where((own >= 0) & (own < part_cap), route * part_cap + own, -1)
+        places.append(
+            (token_slot[None, :] == jnp.arange(slots, dtype=jnp.int32)[:, None]).astype(BF16)
+        )
+
+    def slotted(value, half):
+        sent = jnp.dot(places[half], value, preferred_element_type=F32).astype(BF16)
         return sent.reshape(experts, part_cap, -1)
 
-    def exchanged(value):
-        return expert_exchange(value, experts).reshape(slots, -1)
-
-    def landed(value):
-        return axis_sum(contract_rows(place, value).astype(BF16), "tp").astype(F32)
+    def landed(values):
+        total = sum(
+            contract_rows(place, value.reshape(slots, -1)) for place, value in zip(places, values)
+        )
+        return axis_sum(total.astype(BF16), "tp").astype(F32)
+
+    def halves_of(value):
+        return [value[:, at : at + part_cap] for at in range(0, value.shape[1], part_cap)]
 
     cotan_bf = to_rows(out_grad)
     cotan = cotan_bf.astype(F32)
-    sent_cotan = slotted((cotan * keep[:, None]).astype(BF16))
+    kept_cotan = (cotan * keep[:, None]).astype(BF16)
+    sent_cotan = jnp.concatenate([slotted(kept_cotan, half) for half in range(HALVES)], axis=1)
 
     values = to_rows(hidden_in).astype(F32)
     normalized_rows, inverse_one = rms_forward(values, gain_one_f)
@@ -936,7 +947,7 @@
     step_size = jax.nn.softplus(dt_pre)
     seg_decay, seg_state, last_state = scan.ends(step_size, xconv, mix_in, rate_rows)
     sent_cotan, expert_blocks, _ = together(sent_cotan, expert_blocks, seg_state)
-    slot_cotan = exchanged(sent_cotan)
+    slot_cotan = expert_exchange(sent_cotan, experts)
     entering = entering_pieces(seg_decay[:, :, SEGMENTS - 1], last_state, "ctx", False)
     entering, expert_blocks = together(entering, expert_blocks)
     far_up, far_down = other_hidden(expert_blocks)
@@ -952,42 +963,55 @@
 
     normed_two, inverse_two = rms_forward(middle, gain_two_f)
     normed_two_bf = normed_two.astype(BF16)
-    own_rows = exchanged(slotted(normed_two_bf))
-    own_rows, far_down = together(own_rows, far_down)
     expert_mask = (
         jnp.arange(experts, dtype=jnp.int32) == lax.rem(lax.axis_index("dp"), experts)
     ).astype(F32)[None, :]
-    far_rows, far_cotan = swapped(own_rows, "tp"), swapped(slot_cotan, "tp")
-    far = expert_call(far_rows, far_cotan, router_t, expert_mask, expert_blocks, far_up, far_down)
-    near = expert_call(own_rows, slot_cotan, router_t, expert_mask, expert_blocks, far_up, far_down)
-    slot_out = near[0] + swapped(far[0], "tp")
-    picked_grad = near[1] + swapped(far[1], "tp")
-    slot_prob = near[2]
-    slot_gate = jnp.sum(slot_prob * expert_mask, axis=1, keepdims=True)
-    gate_grad = jnp.sum(slot_out * slot_cotan.astype(F32), axis=1, keepdims=True)
-    logit_grad = gate_grad * slot_gate * (expert_mask - slot_prob)
-    router_grad_t = axis_sum(contract_rows(logit_grad, own_rows.astype(F32), HIGHEST), "tp")
-    picked_grad = picked_grad + jnp.dot(
-        logit_grad, router_t.astype(F32), precision=HIGHEST, preferred_element_type=F32
-    )
-    got_grad = exchanged(picked_grad.astype(BF16).reshape(experts, part_cap, -1))
-
-    def both_rows(at):
-        return jnp.concatenate([far[at], near[at]], axis=0)
-
+    kept = ()
+    got_grads, slot_outs, router_grad_t = [], [], 0.0
+    for half, half_cotan in enumerate(halves_of(slot_cotan)):
+        own_rows = expert_exchange(slotted(normed_two_bf, half), experts)
+        if not half:
+            own_rows, far_down = together(own_rows, far_down)
+        else:
+            own_rows, kept = together(own_rows, kept)
+        own_rows = own_rows.reshape(slots, model_width)
+        half_cotan = half_cotan.reshape(slots, model_width)
+        far_rows, far_cotan = swapped(own_rows, "tp"), swapped(half_cotan, "tp")
+        call = partial(
+            expert_call, router_t=router_t, mask=expert_mask, blocks=expert_blocks, far_up=far_up,
+            far_down=far_down, parts=2 * HALVES,
+        )
+        far = call(far_rows, far_cotan, part=2 * half, kept=kept)
+        near = call(own_rows, half_cotan, part=2 * half + 1, kept=far[3:])
+        if half:
+            near, got_grads = together(near, got_grads)
+        kept = near[3:]
+        slot_out = near[0] + swapped(far[0], "tp")
+        picked_grad = near[1] + swapped(far[1], "tp")
+        slot_prob = near[2]
+        slot_gate = jnp.sum(slot_prob * expert_mask, axis=1, keepdims=True)
+        gate_grad = jnp.sum(slot_out * half_cotan.astype(F32), axis=1, keepdims=True)
+        logit_grad = gate_grad * slot_gate * (expert_mask - slot_prob)
+        router_grad_t = router_grad_t + contract_rows(logit_grad, own_rows.astype(F32), HIGHEST)
+        picked_grad = picked_grad + jnp.dot(
+            logit_grad, router_t.astype(F32), precision=HIGHEST, preferred_element_type=F32
+        )
+        got_grads.append(
+            expert_exchange(picked_grad.astype(BF16).reshape(experts, part_cap, -1), experts)
+        )
+        slot_outs.append(slot_out.astype(BF16).reshape(experts, part_cap, -1))
+    router_grad_t = axis_sum(router_grad_t, "tp")
+    all_rows, all_grads, active_a, active_b, hidden_a, hidden_b = kept
     near_parts, far_parts = expert_weight_products(
-        jnp.concatenate([far_rows, own_rows], axis=0),
-        (both_rows(6), both_rows(7)),
-        both_rows(3),
-        (both_rows(4), both_rows(5)),
+        all_rows, (hidden_a, hidden_b), all_grads, (active_a, active_b)
     )
     far_first = sent_far(far_parts[0])
-    got_grad, near_parts, far_second, far_first, slot_out = together(
-        got_grad, near_parts, far_parts[1], far_first, slot_out
+    got_grads, near_parts, far_second, far_first, slot_outs = together(
+        got_grads, near_parts, far_parts[1], far_first, slot_outs
     )
     far_parts = far_first, sent_far(far_second)
-    normed_two_grad = landed(got_grad)
-    got_out = exchanged(slot_out.astype(BF16).reshape(experts, part_cap, -1))
+    normed_two_grad = landed(got_grads)
+    got_out = expert_exchange(jnp.concatenate(slot_outs, axis=1), experts)
     middle_norm_grad, gain_two_grad = rms_backward(middle, inverse_two, gain_two_f, normed_two_grad)
     middle_grad = cotan + middle_norm_grad
     mixer_grad_bf = middle_grad.astype(BF16)
@@ -1005,11 +1029,14 @@
     leaving = entering_pieces(back_decay[:, :, 0], first_adjoint, "ctx", True)
     leaving, near_product, far_product = together(leaving, near_product, far_product)
     far_product = sent_far(far_product)
-    pre_grad, xconv_grad, decay_sum, scan_sums, mix_grad = scan.adjoint(
+    adjoint_args = (
         step_size, xconv, mix_in, mix_out, scan_grad, rate_rows, seg_start, back_decay, back_adjoint,
         leaving, skip_row,
     )
-    pre_grad, weight_blocks, far_product = together(pre_grad, weight_blocks, far_product)
+    pre_grad, xconv_grad, decay_sum, scan_sums, mix_grad = scan.adjoint(adjoint_args)
+    pre_grad, far_product, weight_blocks = together(pre_grad, far_product, weight_blocks)
+    weight_blocks = expert_weight_blocks(weight_blocks, experts)
+    far_ups = far_hidden(weight_blocks[0])
     out_blocks = lax.all_to_all(product_part(near_product, far_product), "dp", 0, 0, tiled=True)
     decay_log_grad = jnp.sum(decay_sum, axis=0) * decay_rate
     dt_shift_grad, skip_grad = jnp.sum(scan_sums, axis=0)[:2]
@@ -1033,8 +1060,7 @@
     edge_back = passed_along(
         head.reshape(taps - 1, chains, SEGMENTS, inner)[:, :, :1], "ctx", -1
     )
-    edge_back, weight_blocks, out_blocks = together(edge_back, weight_blocks, out_blocks)
-    weight_blocks, far_blocks = expert_weight_halves(weight_blocks, experts)
+    edge_back, out_blocks, far_ups = together(edge_back, out_blocks, far_ups)
     reaching = jnp.stack(
         [
             sum(tap_weights[tap] * edge_back[at - tap] for tap in range(at + 1))
@@ -1062,9 +1088,8 @@
     small_grads = small_grads.reshape(-1, dp_count, shard).transpose(1, 0, 2)
     x_grad_bf, small_grads, out_blocks = together(x_grad_bf, small_grads, out_blocks)
     small_blocks = lax.all_to_all(small_grads, "dp", 0, 0, tiled=True)
-    normed_grad = axis_sum(
-        contract_cols(x_grad_bf, in_x) + contract_cols(z_grad_bf, in_z), "tp"
-    )
+    normed_part = contract_cols(x_grad_bf, in_x) + contract_cols(z_grad_bf, in_z)
+    normed_grad, small_blocks = together(axis_sum(normed_part, "tp"), small_blocks)
     values_norm_grad, gain_one_grad = rms_backward(values, inverse_one, gain_one_f, normed_grad)
     input_grad = from_rows((middle_grad + values_norm_grad).astype(BF16))
 
@@ -1074,20 +1099,24 @@
     gain_low = (gain_row - gain_high.astype(F32)).astype(BF16)
     gain_rows = jnp.concatenate([gain_high, gain_low], axis=1)
     gain_rows = jnp.pad(gain_rows, ((0, 0), (0, 6), (0, inner - shard)))
-    in_x_part, out_blocks, small_blocks = together(in_x_part, out_blocks, small_blocks)
+    in_x_part, out_blocks = together(in_x_part, out_blocks)
     out_proj_grad, in_z_grad = product_shards(out_blocks)
+    small_grads = axis_sum(jnp.sum(small_blocks, axis=0), "ctx")
     in_x_blocks = lax.all_to_all(
         jnp.concatenate([in_x_part, gain_rows], axis=1), "dp", 0, 0, tiled=True
     )
-    in_x_blocks, far_blocks = together(in_x_blocks, far_blocks)
-    first_grad, second_grad = expert_weight_grads(weight_blocks, far_blocks)
+    out_proj_grad, in_z_grad, small_grads, far_down_blocks = together(
+        out_proj_grad, in_z_grad, small_grads, weight_blocks[1]
+    )
+    far_downs, in_x_blocks = together(far_hidden(far_down_blocks), in_x_blocks)
+    first_grad = expert_weight_grad(weight_blocks[0], far_ups)
+    second_grad = expert_weight_grad(weight_blocks[1], far_downs)
     router_prob = jax.nn.softmax(contract_cols(normed_two_bf, router_t), axis=-1)
     gate_prob = jnp.sum(router_prob * onehot_int.astype(F32), axis=1) * keep
-    result = from_rows((middle + gate_prob[:, None] * landed(got_out)).astype(BF16))
+    result = from_rows((middle + gate_prob[:, None] * landed(halves_of(got_out))).astype(BF16))
     in_x_sums = axis_sum(jnp.sum(in_x_blocks.astype(F32), axis=0), "ctx")
     in_x_grad = in_x_sums[:shard]
     gain_one_grad = in_x_sums[shard : shard + 1, :shard] + in_x_sums[shard + 1 : shard + 2, :shard]
-    small_grads = axis_sum(jnp.sum(small_blocks, axis=0), "ctx")
     small_grads = jnp.concatenate([gain_one_grad, small_grads], axis=0)
     sums = [small_grads[bounds[i] : bounds[i + 1]] for i in range(len(bounds) - 1)]
     return (

time: 913 us -> 885 us (0.969)
  waiting for transfers between devices: 245 us -> 185 us
  other arithmetic: 113 us -> 128 us
    ppermute x21 -> x22, waiting for transfers between devices: 184 us -> 140 us  [swapped(): return lax.ppermute(value, axis, [(0, 1), (1, 0)])]
    all_to_all x1, waiting for transfers between devices: 17.6 us -> 0.01 us  [own_expert_blocks(): return lax.all_to_all(both, 'dp', 0, 0, tiled=True)]
    ppermute x4, waiting for transfers between devices: 2.45 us -> 13.6 us  [passed_along(): lax.ppermute(value, axis, [(source, source + steps) for source in range(l...]
  transfers between devices with their start and end apart: 34 -> 35, of which waited for: 15 -> 15; matrix products, arithmetic and copies ran while one was open for 28% -> 32% of each run, Pallas kernels for 19% -> 20%
where the time goes in v5:
time: 885 us; the launch traced here: 874 us
  Pallas kernels  267 us (30%)
  waiting for transfers between devices  185 us (21%)
  matrix products  133 us (15%)
  other arithmetic  128 us (14%)
  local copies, waits for them, and re-layouts  86.7 us (10%)
  starting transfers between devices  72.7 us (8%)
    ppermute x22, waiting for transfers between devices, swapped(): return lax.ppermute(value, axis, [(0, 1), (1, 0)])  140 us
    pallas_call x4, Pallas kernels, call(): pl.pallas_call(kernel, grid=self.grid, in_specs=in_specs, out_specs=out_s...  134 us
    pallas_call x1, Pallas kernels, gathered(): pl.pallas_call(partial(gather_kernel, count, parts), in_specs=[anywhere]...  72.2 us
    dot_general x12, matrix products, contract_rows(): lax.dot_general(left_side, right_side, (((0,), (0,)), ((), ())), precisio...  69.5 us
    pallas_call x2, Pallas kernels, expert_call(): pl.pallas_call(partial(expert_kernel, len(kept)), grid=(count // block,),...  47.2 us
    dot_general x6, matrix products, contract_cols(): lax.dot_general(left_side, right_side, (((1,), (1,)), ((), ())), precisio...  30.5 us
    all_to_all x4, starting transfers between devices, expert_exchange(): lax.all_to_all(value, 'dp', 0, 0, axis_index_groups=groups, tiled=True)  21.7 us
    all_to_all x4, waiting for transfers between devices, expert_exchange(): lax.all_to_all(value, 'dp', 0, 0, axis_index_groups=groups, tiled=True)  19.3 us
  transfers between devices with their start and end apart: 35, of which 15 were waited for; matrix products, arithmetic and copies ran while one was open for 32% of the time, Pallas kernels for 20%

profile of v5, /device:TPU:0, one launch (start us, length us, event | category | flops | bytes accessed | tf_op | source)
XLA Modules:
  0.0 874.2 jit_solution(12109021567778801472)
XLA Ops:
  10.8 72.2 %shard_map.297 = (bf16[8,144,1152]{2,1,0:T(8,128)(2,1)}, bf16[8,144,256]{2,1,0:T(8,128)(2,1)}, bf16[8,144,1152]{2,1,0:T(8,128)(2,1)}) custom-call(bf16[144,1152]{1,0:T(8,128)(2,1)} %bitcast.260, bf16[144,256]{1,0:T(8,128)(2,1)} %pad.62.refs_1_, bf16[144,1152]{1,0:T(8,128)(2,1)} %fusion.48.refs_2_), custom_call_target="tpu_custom_call" | custom-call | bytes 11796480 | tf_op jit(solution)/shard_map/pallas_call | solution.py:699
  165.1 6.0 broadcast_in_dim.28.mix_in_ref
  172.0 19.5 %shard_map.298 = (f32[2,16,8,1152]{3,2,1,0:T(8,128)}, f32[2,16,8,1152]{3,2,1,0:T(8,128)}, f32[2,16,1152]{2,1,0:T(8,128)}) custom-call(f32[64,2,8,1152]{3,2,1,0:T(8,128)} %compare_select_fusion.step_ref, f32[64,2,8,1152]{3,2,1,0:T(8,128)} %get-tuple-element.265.input_ref, f32[2,64,16,8,128]{4,3,2,1,0:T(8,128)} %broadcast_in_dim.28.mix_in_ref, ...), custom_call_target="tpu_custom_call" | custom-call | flops 94371840 | bytes 209223 | tf_op jit(solution)/shard_map/pallas_call | solution.py:361
  201.2 13.6 %collective-permute-done.2.enter_ref = f32[2,16,1152]{2,1,0:T(8,128)} collective-permute-done((f32[2,16,1152]{2,1,0:T(8,128)}, f32[2,16,1152]{2,1,0:T(8,128)}, u32[]{:S(2)}, u32[]{:S(2)}) %collective-permute-start.2) | collective-permute-done | bytes 147488 | tf_op jit(solution)/shard_map/ppermute | solution.py:39
  225.3 26.4 %shard_map.299 = (f32[64,2,8,1152]{3,2,1,0:T(8,128)}, f32[2,16,8,1152]{3,2,1,0:T(8,128)}) custom-call(f32[64,2,8,1152]{3,2,1,0:T(8,128)} %compare_select_fusion.step_ref, f32[64,2,8,1152]{3,2,1,0:T(8,128)} %get-tuple-element.265.input_ref, f32[2,64,16,8,128]{4,3,2,1,0:T(8,128)} %broadcast_in_dim.28.mix_in_ref, ...), custom_call_target="tpu_custom_call" | custom-call | flops 132120576 | bytes 352092 | tf_op jit(solution)/shard_map/pallas_call | solution.py:361
  251.8 8.2 multiply_convert_fusion.2
  260.0 8.3 fusion.44
  276.6 7.3 multiply_reduce_fusion.1
  288.7 6.6 all-to-all-start.2
  295.4 40.6 %collective-permute-done.6.down_b = bf16[8,144,768]{2,1,0:T(8,128)(2,1)} collective-permute-done((bf16[8,144,768]{2,1,0:T(8,128)(2,1)}, bf16[8,144,768]{2,1,0:T(8,128)(2,1)}, u32[]{:S(2)}, u32[]{:S(2)}) %collective-permute-start.6) | collective-permute-done | bytes 1769504 | tf_op jit(solution)/shard_map/ppermute | solution.py:33
  336.0 13.4 %all-to-all-done.2 = bf16[8,128,1152]{2,1,0:T(8,128)(2,1)} async-done(((bf16[8,128,1152]{2,1,0:T(8,128)(2,1)}), bf16[8,128,1152]{2,1,0:T(8,128)(2,1)}, u32[]{:S(2)}, u32[]{:S(2)}) %all-to-all-start.2) | async-done | bytes 2359328 | tf_op jit(solution)/shard_map/all_to_all | solution.py:580
  354.3 23.6 %shard_map.300 = (f32[1024,1152]{1,0:T(8,128)}, f32[1024,1152]{1,0:T(8,128)}, f32[1024,8]{1,0:T(8,128)}, bf16[2048,1152]{1,0:T(8,128)(2,1)}, bf16[2048,1152]{1,0...) custom-call(bf16[1024,1152]{1,0:T(8,128)(2,1)} %collective-permute-d, ...), custom_call_target="tpu_custom_call" | custom-call | flops 1 | bytes 1 | tf_op jit(solution)/shard_map/pallas_call | solution.py:552
  378.5 23.6 %shard_map.301 = (f32[1024,1152]{1,0:T(8,128)}, f32[1024,1152]{1,0:T(8,128)}, f32[1024,8]{1,0:T(8,128)}, bf16[2048,1152]{1,0:T(8,128)(2,1)}, bf16[2048,1152]{1,0...) custom-call(bf16[1024,1152]{1,0:T(8,128)(2,1)} %bitcast.35.rows_ref,, ...), custom_call_target="tpu_custom_call", output_to_operand_aliasing={{3}: (8, {}), {4}: (9, {}), {5}: (10, {}), {6}: (11, {}), {... | custom-call | flops 1 | bytes 1 | tf_op jit(solution)/shard_map/pallas_call | solution.py:552
  403.6 6.7 add_convert_fusion.6
  419.1 7.4 convolution_convert_fusion.3
  426.6 8.2 fusion.93
  446.1 21.1 %collective-permute-done.11 = bf16[1152,768]{1,0:T(8,128)(2,1)} collective-permute-done((bf16[1152,768]{1,0:T(8,128)(2,1)S(1)}, bf16[1152,768]{1,0:T(8,128)(2,1)}, u32[]{:S(2)}, u32[]{:S(2)}) %collective-permute-start.11) | collective-permute-done | bytes 1769504 | tf_op jit(solution)/shard_map/ppermute | solution.py:33
  486.5 26.7 %collective-permute-done.13 = bf16[1152,768]{1,0:T(8,128)(2,1)} collective-permute-done((bf16[1152,768]{1,0:T(8,128)(2,1)}, bf16[1152,768]{1,0:T(8,128)(2,1)}, u32[]{:S(2)}, u32[]{:S(2)}) %collective-permute-start.13) | collective-permute-done | bytes 1769504 | tf_op jit(solution)/shard_map/ppermute | solution.py:33
  526.5 7.0 fusion.43
  542.7 8.7 convolution_convert_fusion.1
  551.4 19.2 %shard_map.302 = (f32[2,16,8,1152]{3,2,1,0:T(8,128)}, f32[2,16,8,1152]{3,2,1,0:T(8,128)}, f32[2,16,1152]{2,1,0:T(8,128)}) custom-call(f32[64,2,8,1152]{3,2,1,0:T(8,128)} %compare_select_fusion.step_ref, f32[2,64,16,8,128]{4,3,2,1,0:T(8,128)} %broadcast_in_dim.29.mix_out_ref, f32[64,2,8,1152]{3,2,1,0:T(8,128)} %get-tuple-element.143.grad_ref, ...), custom_call_target="tpu_custom_call" | custom-call | flops 94371840 | bytes 209223 | tf_op jit(solution)/shard_map/pallas_call | solution.py:361
  572.4 7.4 fusion.34
  584.3 69.0 %shard_map.303 = (f32[64,2,8,1152]{3,2,1,0:T(8,128)}, f32[64,2,8,1152]{3,2,1,0:T(8,128)}, f32[2,16,1152]{2,1,0:T(8,128)}, f32[2,8,1152]{2,1,0:T(8,128)}, f32[64,2,8,128]{3,2,1,0:T(8,128)}) custom-call(f32[64,2,8,1152]{3,2,1,0:T(8,128)} %compare_select_fusion.step_ref, f32[64,2,8,1152]{3,2,1,0:T(8,128)} %get-tuple-element.265.input_ref, ...), custom_call_target="tpu_custom_call" | custom-call | flops 377487360 | bytes 453964 | tf_op jit(solution)/shard_map/pallas_call | solution.py:361
  686.3 6.1 copy.155
  699.8 13.4 %shard_map.304 = (bf16[64,16,1152]{2,1,0:T(8,128)(2,1)}, f32[8,1152]{1,0:T(8,128)}, f32[3,16,1152]{2,1,0:T(8,128)}, f32[3,16,1152]{2,1,0:T(8,128)}) custom-call(bf16[1024,104]{1,0:T(8,128)(2,1)} %add_convert_fusion.7.proj_ref, bf16[104,1152]{1,0:T(8,128)(2,1)} %slice.195.weight_ref, f32[64,16,1152]{2,1,0:T(8,128)} %bitcast.221, ...), custom_call_target="tpu_custom_call" | custom-call | flops 1 | bytes 1 | tf_op jit(solution)/shard_map/pallas_call | solution.py:476
  724.8 6.1 fusion.95
  730.9 7.2 convolution_add_fusion.1
  754.6 6.5 add.250
  761.0 11.7 %all-to-all-done.7 = f32[8,208,144]{1,2,0:T(8,128)S(1)} async-done(((f32[8,208,144]{1,2,0:T(8,128)}), f32[8,208,144]{1,2,0:T(8,128)S(1)}, u32[]{:S(2)}, u32[]{:S(2)}) %all-to-all-start.7) | async-done | bytes 958496 | tf_op jit(solution)/shard_map/all_to_all | solution.py:1090
  799.3 9.6 %collective-permute-done.22 = f32[144,1152]{1,0:T(8,128)S(1)} collective-permute-done((f32[144,1152]{1,0:T(8,128)S(1)}, f32[144,1152]{1,0:T(8,128)S(1)}, u32[]{:S(2)}, u32[]{:S(2)}) %collective-permute-start.22) | collective-permute-done | bytes 663584 | tf_op jit(solution)/shard_map/ppermute | solution.py:33
  831.1 24.8 %collective-permute-done.24 = bf16[8,144,768]{2,1,0:T(8,128)(2,1)} collective-permute-done((bf16[8,144,768]{2,1,0:T(8,128)(2,1)}, bf16[8,144,768]{2,1,0:T(8,128)(2,1)}, u32[]{:S(2)}, u32[]{:S(2)}) %collective-permute-start.24) | collective-permute-done | bytes 1769504 | tf_op jit(solution)/shard_map/ppermute | solution.py:33
  861.1 6.2 convert_bitcast_fusion
  (393 shorter events, 329.5 us)
Async XLA Ops:
  96.6 50.1 %collective-permute-start = (bf16[3,2,1,1152]{3,2,1,0:T(2,128)(2,1)}, bf16[3,2,1,1152]{3,2,1,0:T(2,128)(2,1)}, u32[]{:S(2)}, u32[]{:S(2)}) collective-permute-start(bf16[3,2,1,1152]{3,2,1,0:T(2,128)(2,1)} %slice.234), channel_id=1, source_target_pairs={{0,2},{1,3},{4,6},{5,7},{8,10},{9,11},{12,14},{13,15},{16,18},{17,... | collective-permute-start | bytes 41480 | tf_op jit(solution)/shard_map/ppermute | solution.py:39
  103.6 87.9 %all-to-all-start = ((bf16[8,288,768]{2,1,0:T(8,128)(2,1)}), bf16[8,288,768]{2,1,0:T(8,128)(2,1)S(1)}, u32[]{:S(2)}, u32[]{:S(2)}) async-start(bf16[8,288,768]{2,1,0:T(8,128)(2,1)} %slice_select_fusion), calls=%async_computation | async-start | bytes 7077888 | tf_op jit(solution)/shard_map/all_to_all | solution.py:597
  153.6 98.2 %collective-permute-start.3 = (bf16[1152,1152]{1,0:T(8,128)(2,1)}, bf16[1152,1152]{1,0:T(8,128)(2,1)}, u32[]{:S(2)}, u32[]{:S(2)}) collective-permute-start(bf16[1152,1152]{1,0:T(8,128)(2,1)} %bitcast.15), channel_id=1, source_target_pairs={{0,2},{2,0},{1,3},{3,1},{4,6},{6,4},{5,7},{7,5},{8,10},{10,8},{9,1... | collective-permute-start | bytes 7962632 | tf_op jit(solution)/shard_map/ppermute | solution.py:33
  191.5 68.4 %all-to-all-start.1 = ((bf16[8,128,1152]{2,1,0:T(8,128)(2,1)}), bf16[8,128,1152]{2,1,0:T(8,128)(2,1)}, u32[]{:S(2)}, u32[]{:S(2)}) async-start(bf16[8,128,1152]{2,1,0:T(8,128)(2,1)} %bitcast.249), calls=%async_computation.1 | async-start | bytes 4718592 | tf_op jit(solution)/shard_map/all_to_all | solution.py:580
  197.6 17.3 %collective-permute-start.2 = (f32[2,16,1152]{2,1,0:T(8,128)}, f32[2,16,1152]{2,1,0:T(8,128)}, u32[]{:S(2)}, u32[]{:S(2)}) collective-permute-start(f32[2,16,1152]{2,1,0:T(8,128)} %get-tuple-element.105), channel_id=1, source_target_pairs={{0,2},{1,3},{4,6},{5,7},{8,10},{9,11},{12,14},{13,15},{16,18},{17,... | collective-permute-start | bytes 442376 | tf_op jit(solution)/shard_map/ppermute | solution.py:39
  216.8 43.1 %collective-permute-start.4 = (bf16[8,144,768]{2,1,0:T(8,128)(2,1)}, bf16[8,144,768]{2,1,0:T(8,128)(2,1)}, u32[]{:S(2)}, u32[]{:S(2)}) collective-permute-start(bf16[8,144,768]{2,1,0:T(8,128)(2,1)} %get-tuple-element.281), channel_id=1, source_target_pairs={{0,2},{2,0},{1,3},{3,1},{4,6},{6,4},{5,7},{7,5},{8,10},{10,8},{9,1... | collective-permute-start | bytes 5308424 | tf_op jit(solution)/shard_map/ppermute | solution.py:33
  268.3 8.3 collective-permute-start.5
  288.7 60.8 %all-to-all-start.2 = ((bf16[8,128,1152]{2,1,0:T(8,128)(2,1)}), bf16[8,128,1152]{2,1,0:T(8,128)(2,1)}, u32[]{:S(2)}, u32[]{:S(2)}) async-start(bf16[8,128,1152]{2,1,0:T(8,128)(2,1)} %bitcast.251), calls=%async_computation.2 | async-start | bytes 4718592 | tf_op jit(solution)/shard_map/all_to_all | solution.py:580
  295.3 40.7 %collective-permute-start.6 = (bf16[8,144,768]{2,1,0:T(8,128)(2,1)}, bf16[8,144,768]{2,1,0:T(8,128)(2,1)}, u32[]{:S(2)}, u32[]{:S(2)}) collective-permute-start(bf16[8,144,768]{2,1,0:T(8,128)(2,1)} %get-tuple-element.280), channel_id=1, source_target_pairs={{0,2},{2,0},{1,3},{3,1},{4,6},{6,4},{5,7},{7,5},{8,10},{10,8},{9,1... | collective-permute-start | bytes 5308424 | tf_op jit(solution)/shard_map/ppermute | solution.py:33
  295.4 55.2 %collective-permute-start.8 = (bf16[1024,1152]{1,0:T(8,128)(2,1)}, bf16[1024,1152]{1,0:T(8,128)(2,1)}, u32[]{:S(2)}, u32[]{:S(2)}) collective-permute-start(bf16[1024,1152]{1,0:T(8,128)(2,1)} %bitcast.36.cotan_ref), channel_id=1, source_target_pairs={{0,1},{1,0},{2,3},{3,2},{4,5},{5,4},{6,7},{7,6},{8,9},{9,8},{10,11... | collective-permute-start | bytes 7077896 | tf_op jit(solution)/shard_map/ppermute | solution.py:33
  377.9 25.6 %collective-permute-start.10 = (f32[1024,1152]{1,0:T(8,128)}, f32[1024,1152]{1,0:T(8,128)}, u32[]{:S(2)}, u32[]{:S(2)}) collective-permute-start(f32[1024,1152]{1,0:T(8,128)} %get-tuple-element.128), channel_id=1, source_target_pairs={{0,1},{1,0},{2,3},{3,2},{4,5},{5,4},{6,7},{7,6},{8,9},{9,8},{10,11... | collective-permute-start | bytes 14155784 | tf_op jit(solution)/shard_map/ppermute | solution.py:33
  378.1 32.1 %collective-permute-start.9 = (f32[1024,1152]{1,0:T(8,128)}, f32[1024,1152]{1,0:T(8,128)S(1)}, u32[]{:S(2)}, u32[]{:S(2)}) collective-permute-start(f32[1024,1152]{1,0:T(8,128)} %get-tuple-element.126), channel_id=1, source_target_pairs={{0,1},{1,0},{2,3},{3,2},{4,5},{5,4},{6,7},{7,6},{8,9},{9,8},{10,11... | collective-permute-start | bytes 14155784 | tf_op jit(solution)/shard_map/ppermute | solution.py:33
  414.3 58.8 %all-to-all-start.3 = ((bf16[8,128,1152]{2,1,0:T(8,128)(2,1)}), bf16[8,128,1152]{2,1,0:T(8,128)(2,1)}, u32[]{:S(2)}, u32[]{:S(2)}) async-start(bf16[8,128,1152]{2,1,0:T(8,128)(2,1)} %bitcast.213), calls=%async_computation.3 | async-start | bytes 4718592 | tf_op jit(solution)/shard_map/all_to_all | solution.py:580
  426.4 40.8 %collective-permute-start.11 = (bf16[1152,768]{1,0:T(8,128)(2,1)S(1)}, bf16[1152,768]{1,0:T(8,128)(2,1)}, u32[]{:S(2)}, u32[]{:S(2)}) collective-permute-start(bf16[1152,768]{1,0:T(8,128)(2,1)S(1)} %convolution_convert_fusion.3), channel_id=1, source_target_pairs={{0,2},{2,0},{1,3},{3,1},{4,6},{6,4},{5,7},{7,5},{8,10},{10,8},{9,1... | collective-permute-start | bytes 5308424 | tf_op jit(solution)/shard_map/ppermute | solution.py:33
  473.1 40.1 %collective-permute-start.13 = (bf16[1152,768]{1,0:T(8,128)(2,1)}, bf16[1152,768]{1,0:T(8,128)(2,1)}, u32[]{:S(2)}, u32[]{:S(2)}) collective-permute-start(bf16[1152,768]{1,0:T(8,128)(2,1)} %convolution_convert_fusion.4), channel_id=1, source_target_pairs={{0,2},{2,0},{1,3},{3,1},{4,6},{6,4},{5,7},{7,5},{8,10},{10,8},{9,1... | collective-permute-start | bytes 5308424 | tf_op jit(solution)/shard_map/ppermute | solution.py:33
  479.0 39.2 %collective-permute-start.12 = (bf16[1024,1152]{1,0:T(8,128)(2,1)}, bf16[1024,1152]{1,0:T(8,128)(2,1)}, u32[]{:S(2)}, u32[]{:S(2)}) collective-permute-start(bf16[1024,1152]{1,0:T(8,128)(2,1)} %fusion.28), channel_id=1, source_target_pairs={{0,1},{1,0},{2,3},{3,2},{4,5},{5,4},{6,7},{7,6},{8,9},{9,8},{10,11... | collective-permute-start | bytes 7077896 | tf_op jit(solution)/shard_map/ppermute | solution.py:33
  479.0 59.2 %all-to-all-start.4 = ((bf16[8,128,1152]{2,1,0:T(8,128)(2,1)}), bf16[8,128,1152]{2,1,0:T(8,128)(2,1)}, u32[]{:S(2)}, u32[]{:S(2)}) async-start(bf16[8,128,1152]{2,1,0:T(8,128)(2,1)} %bitcast.215), calls=%async_computation.4 | async-start | bytes 4718592 | tf_op jit(solution)/shard_map/all_to_all | solution.py:580
  538.2 115.1 %all-to-all-start.5 = ((bf16[8,288,768]{2,1,0:T(8,128)(2,1)}), bf16[8,288,768]{2,1,0:T(8,128)(2,1)}, u32[]{:S(2)}, u32[]{:S(2)}) async-start(bf16[8,288,768]{2,1,0:T(8,128)(2,1)} %pad_maximum_fusion), calls=%async_computation.5 | async-start | bytes 7077888 | tf_op jit(solution)/shard_map/all_to_all | solution.py:1025
  570.6 9.1 %collective-permute-start.15 = (f32[2,16,1152]{2,1,0:T(8,128)}, f32[2,16,1152]{2,1,0:T(8,128)}, u32[]{:S(2)}, u32[]{:S(2)}) collective-permute-start(f32[2,16,1152]{2,1,0:T(8,128)} %get-tuple-element.147), channel_id=1, source_target_pairs={{2,0},{3,1},{6,4},{7,5},{10,8},{11,9},{14,12},{15,13},{18,16},{19,... | collective-permute-start | bytes 442376 | tf_op jit(solution)/shard_map/ppermute | solution.py:39
  579.7 73.5 %collective-permute-start.16 = (bf16[1152,1152]{1,0:T(8,128)(2,1)}, bf16[1152,1152]{1,0:T(8,128)(2,1)}, u32[]{:S(2)}, u32[]{:S(2)}) collective-permute-start(bf16[1152,1152]{1,0:T(8,128)(2,1)} %convolution_convert_fusion.1), channel_id=1, source_target_pairs={{0,2},{2,0},{1,3},{3,1},{4,6},{6,4},{5,7},{7,5},{8,10},{10,8},{9,1... | collective-permute-start | bytes 7962632 | tf_op jit(solution)/shard_map/ppermute | solution.py:33
  658.6 65.4 %all-to-all-start.6 = ((bf16[8,144,1152]{2,1,0:T(8,128)(2,1)}), bf16[8,144,1152]{2,1,0:T(8,128)(2,1)}, u32[]{:S(2)}, u32[]{:S(2)}) async-start(bf16[8,144,1152]{2,1,0:T(8,128)(2,1)} %bitcast.207), calls=%async_computation.6 | async-start | bytes 5308416 | tf_op jit(solution)/shard_map/all_to_all | solution.py:1040
  678.2 45.0 %collective-permute-start.19 = (bf16[8,144,768]{2,1,0:T(8,128)(2,1)}, bf16[8,144,768]{2,1,0:T(8,128)(2,1)}, u32[]{:S(2)}, u32[]{:S(2)}) collective-permute-start(bf16[8,144,768]{2,1,0:T(8,128)(2,1)} %get-tuple-element.279), channel_id=1, source_target_pairs={{0,2},{2,0},{1,3},{3,1},{4,6},{6,4},{5,7},{7,5},{8,10},{10,8},{9,1... | collective-permute-start | bytes 5308424 | tf_op jit(solution)/shard_map/ppermute | solution.py:33
  683.8 14.0 %collective-permute-start.17 = (f32[1024,104]{1,0:T(8,128)}, f32[1024,104]{1,0:T(8,128)}, u32[]{:S(2)}, u32[]{:S(2)}) collective-permute-start(f32[1024,104]{1,0:T(8,128)} %pad_maximum_fusion.4), channel_id=1, source_target_pairs={{0,1},{1,0},{2,3},{3,2},{4,5},{5,4},{6,7},{7,6},{8,9},{9,8},{10,11... | collective-permute-start | bytes 1277960 | tf_op jit(solution)/shard_map/ppermute | solution.py:33
  714.2 9.0 %collective-permute-start.18 = (f32[3,2,1,1152]{3,2,1,0:T(1,128)S(1)}, f32[3,2,1,1152]{3,2,1,0:T(1,128)S(1)}, u32[]{:S(2)}, u32[]{:S(2)}) collective-permute-start(f32[3,2,1,1152]{3,2,1,0:T(1,128)S(1)} %slice.250), channel_id=1, source_target_pairs={{2,0},{3,1},{6,4},{7,5},{10,8},{11,9},{14,12},{15,13},{18,16},{19,... | collective-permute-start | bytes 82952 | tf_op jit(solution)/shard_map/ppermute | solution.py:39
  738.1 16.5 %collective-permute-start.21 = (f32[1024,1152]{1,0:T(8,128)}, f32[1024,1152]{1,0:T(8,128)}, u32[]{:S(2)}, u32[]{:S(2)}) collective-permute-start(f32[1024,1152]{1,0:T(8,128)} %convolution_add_fusion.1), channel_id=1, source_target_pairs={{0,1},{1,0},{2,3},{3,2},{4,5},{5,4},{6,7},{7,6},{8,9},{9,8},{10,11... | collective-permute-start | bytes 14155784 | tf_op jit(solution)/shard_map/ppermute | solution.py:33
  738.1 34.6 %all-to-all-start.7 = ((f32[8,208,144]{1,2,0:T(8,128)}), f32[8,208,144]{1,2,0:T(8,128)S(1)}, u32[]{:S(2)}, u32[]{:S(2)}) async-start(f32[8,208,144]{1,2,0:T(8,128)} %bitcast.67), calls=%async_computation.7 | async-start | bytes 2359296 | tf_op jit(solution)/shard_map/all_to_all | solution.py:1090
  749.6 44.5 %collective-permute-start.14 = (bf16[1024,1152]{1,0:T(8,128)(2,1)}, bf16[1024,1152]{1,0:T(8,128)(2,1)}, u32[]{:S(2)}, u32[]{:S(2)}) collective-permute-start(bf16[1024,1152]{1,0:T(8,128)(2,1)} %fusion.29), channel_id=1, source_target_pairs={{0,1},{1,0},{2,3},{3,2},{4,5},{5,4},{6,7},{7,6},{8,9},{9,8},{10,11... | collective-permute-start | bytes 7077896 | tf_op jit(solution)/shard_map/ppermute | solution.py:33
  781.7 74.2 %all-to-all-start.8 = ((bf16[8,152,1152]{2,1,0:T(8,128)(2,1)}), bf16[8,152,1152]{2,1,0:T(8,128)(2,1)S(1)}, u32[]{:S(2)}, u32[]{:S(2)}) async-start(bf16[8,152,1152]{2,1,0:T(8,128)(2,1)} %pad_maximum_fusion.1), calls=%async_computation.8 | async-start | bytes 5603328 | tf_op jit(solution)/shard_map/all_to_all | solution.py:1105
  791.4 17.6 %collective-permute-start.22 = (f32[144,1152]{1,0:T(8,128)S(1)}, f32[144,1152]{1,0:T(8,128)S(1)}, u32[]{:S(2)}, u32[]{:S(2)}) collective-permute-start(f32[144,1152]{1,0:T(8,128)S(1)} %convert_reduce_fusion.1), channel_id=1, source_target_pairs={{0,2},{2,0},{1,3},{3,1},{4,6},{6,4},{5,7},{7,5},{8,10},{10,8},{9,1... | collective-permute-start | bytes 1990664 | tf_op jit(solution)/shard_map/ppermute | solution.py:33
  811.4 5.2 collective-permute-start.23
  816.7 39.2 %collective-permute-start.24 = (bf16[8,144,768]{2,1,0:T(8,128)(2,1)}, bf16[8,144,768]{2,1,0:T(8,128)(2,1)}, u32[]{:S(2)}, u32[]{:S(2)}) collective-permute-start(bf16[8,144,768]{2,1,0:T(8,128)(2,1)} %get-tuple-element.172), channel_id=1, source_target_pairs={{0,2},{2,0},{1,3},{3,1},{4,6},{6,4},{5,7},{7,5},{8,10},{10,8},{9,1... | collective-permute-start | bytes 5308424 | tf_op jit(solution)/shard_map/ppermute | solution.py:33
  856.3 15.1 %collective-permute-start.25 = (f32[152,1152]{1,0:T(8,128)S(1)}, f32[152,1152]{1,0:T(8,128)S(1)}, u32[]{:S(2)}, u32[]{:S(2)}) collective-permute-start(f32[152,1152]{1,0:T(8,128)S(1)} %convert_reduce_fusion), channel_id=1, source_target_pairs={{0,2},{2,0},{1,3},{3,1},{4,6},{6,4},{5,7},{7,5},{8,10},{10,8},{9,1... | collective-permute-start | bytes 2101256 | tf_op jit(solution)/shard_map/ppermute | solution.py:33
  (91 other events, 1056.7 us)

commit v6 on v5

--- a/solution.py
+++ b/solution.py
@@ -13,6 +13,7 @@
 SEGMENTS = 8
 LANES = 128
 VMEM_LIMIT = 56 * 1024 * 1024
+EXPERT_VMEM = 56 * 1024 * 1024
 LOG2E = math.log2(math.e)
 GROUP_A = 4
 GROUP_B = 4
@@ -565,8 +566,12 @@
             *(jax.ShapeDtypeStruct((parts * count, one), BF16) for one in columns),
         ],
         input_output_aliases={len(inputs) + at: 3 + at for at in range(len(kept))},
-        compiler_params=pltpu.CompilerParams(vmem_limit_bytes=VMEM_LIMIT),
-        cost_estimate=pl.CostEstimate(flops=1, transcendentals=0, bytes_accessed=1),
+        compiler_params=pltpu.CompilerParams(vmem_limit_bytes=EXPERT_VMEM),
+        cost_estimate=pl.CostEstimate(
+            flops=16 * count * width * hidden,
+            transcendentals=4 * count * hidden,
+            bytes_accessed=count * (14 * width + 8 * hidden) + 8 * width * hidden,
+        ),
     )(*inputs, *kept)
 
 
@@ -886,36 +891,6 @@
     rate_rows = jnp.broadcast_to((decay_rate * LOG2E)[:, None, :], (states, SEGMENTS, inner))
     expert_blocks = own_expert_blocks(up_shards, down_shards)
 
-    route = to_rows(expert_ids)[:, 0]
-    keep = to_rows(keep_mask)[:, 0].astype(F32)
-    onehot_int = (route[:, None] == jnp.arange(experts, dtype=jnp.int32)[None, :]).astype(jnp.int32)
-    rank = jnp.sum((jnp.cumsum(onehot_int, axis=0) - 1) * onehot_int, axis=1)
-    places = []
-    for half in range(HALVES):
-        own = rank - (tp_index * HALVES + half) * part_cap
-        token_slot = jnp.where((own >= 0) & (own < part_cap), route * part_cap + own, -1)
-        places.append(
-            (token_slot[None, :] == jnp.arange(slots, dtype=jnp.int32)[:, None]).astype(BF16)
-        )
-
-    def slotted(value, half):
-        sent = jnp.dot(places[half], value, preferred_element_type=F32).astype(BF16)
-        return sent.reshape(experts, part_cap, -1)
-
-    def landed(values):
-        total = sum(
-            contract_rows(place, value.reshape(slots, -1)) for place, value in zip(places, values)
-        )
-        return axis_sum(total.astype(BF16), "tp").astype(F32)
-
-    def halves_of(value):
-        return [value[:, at : at + part_cap] for at in range(0, value.shape[1], part_cap)]
-
-    cotan_bf = to_rows(out_grad)
-    cotan = cotan_bf.astype(F32)
-    kept_cotan = (cotan * keep[:, None]).astype(BF16)
-    sent_cotan = jnp.concatenate([slotted(kept_cotan, half) for half in range(HALVES)], axis=1)
-
     values = to_rows(hidden_in).astype(F32)
     normalized_rows, inverse_one = rms_forward(values, gain_one_f)
     normed_bf = normalized_rows.astype(BF16)
@@ -946,7 +921,37 @@
     dt_pre = (jnp.dot(dt_low, dt_proj, preferred_element_type=F32) + dt_shift).reshape(x_pre.shape)
     step_size = jax.nn.softplus(dt_pre)
     seg_decay, seg_state, last_state = scan.ends(step_size, xconv, mix_in, rate_rows)
-    sent_cotan, expert_blocks, _ = together(sent_cotan, expert_blocks, seg_state)
+    later_ids, later_mask, later_grad, _ = together(expert_ids, keep_mask, out_grad, seg_state)
+    route = to_rows(later_ids)[:, 0]
+    keep = to_rows(later_mask)[:, 0].astype(F32)
+    onehot_int = (route[:, None] == jnp.arange(experts, dtype=jnp.int32)[None, :]).astype(jnp.int32)
+    rank = jnp.sum((jnp.cumsum(onehot_int, axis=0) - 1) * onehot_int, axis=1)
+    places = []
+    for half in range(HALVES):
+        own = rank - (tp_index * HALVES + half) * part_cap
+        token_slot = jnp.where((own >= 0) & (own < part_cap), route * part_cap + own, -1)
+        places.append(
+            (token_slot[None, :] == jnp.arange(slots, dtype=jnp.int32)[:, None]).astype(BF16)
+        )
+
+    def slotted(value, half):
+        sent = jnp.dot(places[half], value, preferred_element_type=F32).astype(BF16)
+        return sent.reshape(experts, part_cap, -1)
+
+    def landed(values):
+        total = sum(
+            contract_rows(place, value.reshape(slots, -1)) for place, value in zip(places, values)
+        )
+        return axis_sum(total.astype(BF16), "tp").astype(F32)
+
+    def halves_of(value):
+        return [value[:, at : at + part_cap] for at in range(0, value.shape[1], part_cap)]
+
+    cotan_bf = to_rows(later_grad)
+    cotan = cotan_bf.astype(F32)
+    kept_cotan = (cotan * keep[:, None]).astype(BF16)
+    sent_cotan = jnp.concatenate([slotted(kept_cotan, half) for half in range(HALVES)], axis=1)
+    sent_cotan, expert_blocks = together(sent_cotan, expert_blocks)
     slot_cotan = expert_exchange(sent_cotan, experts)
     entering = entering_pieces(seg_decay[:, :, SEGMENTS - 1], last_state, "ctx", False)
     entering, expert_blocks = together(entering, expert_blocks)
@@ -1020,11 +1025,12 @@
     z_grad = jax.vjp(jax.nn.silu, z_gate)[1](gated_grad * scanned)[0]
     z_grad_bf = z_grad.astype(BF16).reshape(tokens, inner)
     near_product, far_product = pair_products((mixer_grad_bf, gated_bf), (normed_bf, z_grad_bf))
-    weight_parts = expert_weight_parts(near_parts, far_parts)
-    scan_grad, weight_parts, got_out = together(scan_grad, weight_parts, got_out)
-    weight_blocks = lax.all_to_all(weight_parts, "dp", 0, 0, tiled=True)
     back_decay, back_adjoint, first_adjoint = scan.adjoint_ends(
         step_size, mix_out, scan_grad, rate_rows
+    )
+    far_parts, got_out, _ = together(far_parts, got_out, first_adjoint)
+    weight_blocks = lax.all_to_all(
+        expert_weight_parts(near_parts, far_parts), "dp", 0, 0, tiled=True
     )
     leaving = entering_pieces(back_decay[:, :, 0], first_adjoint, "ctx", True)
     leaving, near_product, far_product = together(leaving, near_product, far_product)
@@ -1086,10 +1092,12 @@
         axis=0,
     )
     small_grads = small_grads.reshape(-1, dp_count, shard).transpose(1, 0, 2)
-    x_grad_bf, small_grads, out_blocks = together(x_grad_bf, small_grads, out_blocks)
-    small_blocks = lax.all_to_all(small_grads, "dp", 0, 0, tiled=True)
+    small_size = small_grads.shape[1] * shard
+    small_rows = small_grads.astype(BF16).reshape(dp_count, small_size)
+    small_rows = jnp.pad(small_rows, ((0, 0), (0, -small_size % inner))).reshape(dp_count, -1, inner)
+    x_grad_bf, small_rows, out_blocks = together(x_grad_bf, small_rows, out_blocks)
     normed_part = contract_cols(x_grad_bf, in_x) + contract_cols(z_grad_bf, in_z)
-    normed_grad, small_blocks = together(axis_sum(normed_part, "tp"), small_blocks)
+    normed_grad = axis_sum(normed_part, "tp")
     values_norm_grad, gain_one_grad = rms_backward(values, inverse_one, gain_one_f, normed_grad)
     input_grad = from_rows((middle_grad + values_norm_grad).astype(BF16))
 
@@ -1101,12 +1109,11 @@
     gain_rows = jnp.pad(gain_rows, ((0, 0), (0, 6), (0, inner - shard)))
     in_x_part, out_blocks = together(in_x_part, out_blocks)
     out_proj_grad, in_z_grad = product_shards(out_blocks)
-    small_grads = axis_sum(jnp.sum(small_blocks, axis=0), "ctx")
     in_x_blocks = lax.all_to_all(
-        jnp.concatenate([in_x_part, gain_rows], axis=1), "dp", 0, 0, tiled=True
-    )
-    out_proj_grad, in_z_grad, small_grads, far_down_blocks = together(
-        out_proj_grad, in_z_grad, small_grads, weight_blocks[1]
+        jnp.concatenate([in_x_part, gain_rows, small_rows], axis=1), "dp", 0, 0, tiled=True
+    )
+    out_proj_grad, in_z_grad, far_down_blocks = together(
+        out_proj_grad, in_z_grad, weight_blocks[1]
     )
     far_downs, in_x_blocks = together(far_hidden(far_down_blocks), in_x_blocks)
     first_grad = expert_weight_grad(weight_blocks[0], far_ups)
@@ -1117,6 +1124,7 @@
     in_x_sums = axis_sum(jnp.sum(in_x_blocks.astype(F32), axis=0), "ctx")
     in_x_grad = in_x_sums[:shard]
     gain_one_grad = in_x_sums[shard : shard + 1, :shard] + in_x_sums[shard + 1 : shard + 2, :shard]
+    small_grads = in_x_sums[shard + 8 :].reshape(-1)[:small_size].reshape(-1, shard)
     small_grads = jnp.concatenate([gain_one_grad, small_grads], axis=0)
     sums = [small_grads[bounds[i] : bounds[i + 1]] for i in range(len(bounds) - 1)]
     return (

time: 885 us -> 837 us (0.946)
  other arithmetic: 128 us -> 103 us
  starting transfers between devices: 72.7 us -> 58.7 us
  waiting for transfers between devices: 185 us -> 197 us
  local copies, waits for them, and re-layouts: 86.7 us -> 75.4 us
  matrix products: 133 us -> 123 us
    all_to_all x1, waiting for transfers between devices: 0.01 us -> 16.9 us  [own_expert_blocks(): return lax.all_to_all(both, 'dp', 0, 0, tiled=True)]
    all_to_all x4, waiting for transfers between devices: 19.3 us -> 32.7 us  [expert_exchange(): lax.all_to_all(value, 'dp', 0, 0, axis_index_groups=groups, tiled=True)]
    ppermute x4, waiting for transfers between devices: 13.6 us -> 2.74 us  [passed_along(): lax.ppermute(value, axis, [(source, source + steps) for source in range(l...]
    ppermute x22 -> x21, waiting for transfers between devices: 140 us -> 131 us  [swapped(): return lax.ppermute(value, axis, [(0, 1), (1, 0)])]
  transfers between devices with their start and end apart: 35 -> 33, of which waited for: 15 -> 18; matrix products, arithmetic and copies ran while one was open for 32% -> 25% of each run, Pallas kernels for 20% -> 21%
where the time goes in v6:
time: 837 us; the launch traced here: 827 us
  Pallas kernels  267 us (32%)
  waiting for transfers between devices  197 us (24%)
  matrix products  123 us (15%)
  other arithmetic  103 us (12%)
  local copies, waits for them, and re-layouts  75.4 us (9%)
  starting transfers between devices  58.7 us (7%)
    pallas_call x4, Pallas kernels, call(): pl.pallas_call(kernel, grid=self.grid, in_specs=in_specs, out_specs=out_s...  134 us
    ppermute x21, waiting for transfers between devices, swapped(): return lax.ppermute(value, axis, [(0, 1), (1, 0)])  131 us
    pallas_call x1, Pallas kernels, gathered(): pl.pallas_call(partial(gather_kernel, count, parts), in_specs=[anywhere]...  72.2 us
    dot_general x12, matrix products, contract_rows(): lax.dot_general(left_side, right_side, (((0,), (0,)), ((), ())), precisio...  61.6 us
    pallas_call x2, Pallas kernels, expert_call(): pl.pallas_call(partial(expert_kernel, len(kept)), grid=(count // block,),...  47.2 us
    all_to_all x4, waiting for transfers between devices, expert_exchange(): lax.all_to_all(value, 'dp', 0, 0, axis_index_groups=groups, tiled=True)  32.7 us
    dot_general x6, matrix products, contract_cols(): lax.dot_general(left_side, right_side, (((1,), (1,)), ((), ())), precisio...  27.1 us
    all_to_all x4, starting transfers between devices, expert_exchange(): lax.all_to_all(value, 'dp', 0, 0, axis_index_groups=groups, tiled=True)  20.2 us
  transfers between devices with their start and end apart: 33, of which 18 were waited for; matrix products, arithmetic and copies ran while one was open for 25% of the time, Pallas kernels for 21%

profile of v6, /device:TPU:0, one launch (start us, length us, event | category | flops | bytes accessed | tf_op | source)
XLA Modules:
  0.0 826.9 jit_solution(6528555080103234927)
XLA Ops:
  11.5 72.2 %shard_map.297 = (bf16[8,144,1152]{2,1,0:T(8,128)(2,1)}, bf16[8,144,256]{2,1,0:T(8,128)(2,1)}, bf16[8,144,1152]{2,1,0:T(8,128)(2,1)}) custom-call(bf16[144,1152]{1,0:T(8,128)(2,1)} %bitcast.265, bf16[144,256]{1,0:T(8,128)(2,1)} %pad.62.refs_1_, bf16[144,1152]{1,0:T(8,128)(2,1)} %fusion.48.refs_2_), custom_call_target="tpu_custom_call" | custom-call | bytes 11796480 | tf_op jit(solution)/shard_map/pallas_call | solution.py:704
  130.5 19.5 %shard_map.298 = (f32[2,16,8,1152]{3,2,1,0:T(8,128)}, f32[2,16,8,1152]{3,2,1,0:T(8,128)}, f32[2,16,1152]{2,1,0:T(8,128)}) custom-call(f32[64,2,8,1152]{3,2,1,0:T(8,128)} %compare_select_fusion.step_ref, f32[64,2,8,1152]{3,2,1,0:T(8,128)} %get-tuple-element.229.input_ref, f32[2,64,16,8,128]{4,3,2,1,0:T(8,128)} %broadcast_in_dim.28.mix_in_ref, ...), custom_call_target="tpu_custom_call" | custom-call | flops 94371840 | bytes 209223 | tf_op jit(solution)/shard_map/pallas_call | solution.py:362
  167.0 16.9 %all-to-all-done.up_a.down_a = bf16[8,288,768]{2,1,0:T(8,128)(2,1)} async-done(((bf16[8,288,768]{2,1,0:T(8,128)(2,1)}), bf16[8,288,768]{2,1,0:T(8,128)(2,1)}, u32[]{:S(2)}, u32[]{:S(2)}) %all-to-all-start) | async-done | bytes 3538976 | tf_op jit(solution)/shard_map/all_to_all | solution.py:602
  201.5 5.9 broadcast_in_dim.29.mix_out_ref
  207.5 26.5 %shard_map.299 = (f32[64,2,8,1152]{3,2,1,0:T(8,128)}, f32[2,16,8,1152]{3,2,1,0:T(8,128)}) custom-call(f32[64,2,8,1152]{3,2,1,0:T(8,128)} %compare_select_fusion.step_ref, f32[64,2,8,1152]{3,2,1,0:T(8,128)} %get-tuple-element.229.input_ref, f32[2,64,16,8,128]{4,3,2,1,0:T(8,128)} %broadcast_in_dim.28.mix_in_ref, ...), custom_call_target="tpu_custom_call" | custom-call | flops 132120576 | bytes 352092 | tf_op jit(solution)/shard_map/pallas_call | solution.py:362
  234.0 8.2 multiply_convert_fusion.2
  242.1 8.2 fusion.44
  268.9 6.4 all-to-all-start.2
  275.5 40.6 %collective-permute-done.6.down_b = bf16[8,144,768]{2,1,0:T(8,128)(2,1)} collective-permute-done((bf16[8,144,768]{2,1,0:T(8,128)(2,1)}, bf16[8,144,768]{2,1,0:T(8,128)(2,1)}, u32[]{:S(2)}, u32[]{:S(2)}) %collective-permute-start.6) | collective-permute-done | bytes 1769504 | tf_op jit(solution)/shard_map/ppermute | solution.py:34
  316.1 13.4 %all-to-all-done.2 = bf16[8,128,1152]{2,1,0:T(8,128)(2,1)} async-done(((bf16[8,128,1152]{2,1,0:T(8,128)(2,1)}), bf16[8,128,1152]{2,1,0:T(8,128)(2,1)}, u32[]{:S(2)}, u32[]{:S(2)}) %all-to-all-start.2) | async-done | bytes 2359328 | tf_op jit(solution)/shard_map/all_to_all | solution.py:585
  334.4 23.6 %shard_map.300 = (f32[1024,1152]{1,0:T(8,128)}, f32[1024,1152]{1,0:T(8,128)}, f32[1024,8]{1,0:T(8,128)}, bf16[2048,1152]{1,0:T(8,128)(2,1)}, bf16[2048,1152]{1,0...) custom-call(bf16[1024,1152]{1,0:T(8,128)(2,1)} %collective-permute-d, ...), custom_call_target="tpu_custom_call" | custom-call | flops 14495514624 | bytes 29884416 | tf_op jit(solution)/shard_map/pallas_call | solution.py:553
  358.6 23.6 %shard_map.301 = (f32[1024,1152]{1,0:T(8,128)}, f32[1024,1152]{1,0:T(8,128)}, f32[1024,8]{1,0:T(8,128)}, bf16[2048,1152]{1,0:T(8,128)(2,1)}, bf16[2048,1152]{1,0...) custom-call(bf16[1024,1152]{1,0:T(8,128)(2,1)} %bitcast.34.rows_ref,, ...), custom_call_target="tpu_custom_call", output_to_operand_aliasing={{3}: (8, {}), {4}: (9, {}), {5}: (10, {}), {6}: (11, {}), {... | custom-call | flops 14495514624 | bytes 29884416 | tf_op jit(solution)/shard_map/pallas_call | solution.py:553
  383.6 6.7 add_convert_fusion.6
  400.1 7.4 convolution_convert_fusion.3
  418.5 6.0 fusion.91
  424.4 23.8 %collective-permute-done.11 = bf16[1152,768]{1,0:T(8,128)(2,1)} collective-permute-done((bf16[1152,768]{1,0:T(8,128)(2,1)S(1)}, bf16[1152,768]{1,0:T(8,128)(2,1)}, u32[]{:S(2)}, u32[]{:S(2)}) %collective-permute-start.11) | collective-permute-done | bytes 1769504 | tf_op jit(solution)/shard_map/ppermute | solution.py:34
  448.2 5.8 all-to-all-done.3
  454.1 5.9 fusion.28
  474.6 7.4 fusion.43
  486.6 19.2 %shard_map.302 = (f32[2,16,8,1152]{3,2,1,0:T(8,128)}, f32[2,16,8,1152]{3,2,1,0:T(8,128)}, f32[2,16,1152]{2,1,0:T(8,128)}) custom-call(f32[64,2,8,1152]{3,2,1,0:T(8,128)} %compare_select_fusion.step_ref, f32[2,64,16,8,128]{4,3,2,1,0:T(8,128)} %broadcast_in_dim.29.mix_out_ref, f32[64,2,8,1152]{3,2,1,0:T(8,128)} %get-tuple-element.232.grad_ref, ...), custom_call_target="tpu_custom_call" | custom-call | flops 94371840 | bytes 209223 | tf_op jit(solution)/shard_map/pallas_call | solution.py:362
  505.8 13.5 %all-to-all-done.4 = bf16[8,128,1152]{2,1,0:T(8,128)(2,1)} async-done(((bf16[8,128,1152]{2,1,0:T(8,128)(2,1)}), bf16[8,128,1152]{2,1,0:T(8,128)(2,1)}, u32[]{:S(2)}, u32[]{:S(2)}) %all-to-all-start.4) | async-done | bytes 2359328 | tf_op jit(solution)/shard_map/all_to_all | solution.py:585
  532.3 8.7 %convolution_convert_fusion.1 = bf16[1152,1152]{1,0:T(8,128)(2,1)} fusion(bf16[1024,1152]{1,0:T(8,128)(2,1)} %bitcast.257, bf16[1024,1152]{1,0:T(8,128)(2,1)} %bitcast.293, bf16[1024,1152]{1,0:T(8,128)(2,1)} %get-tuple-element.239, pred[]{:T(512)S(6)} %eq.66, f32[1024,1152]{1,0:T(8,128)} %copy-done.2), kind=kOutput, calls=%fused_computation.2 | convolution fusion | flops 2722775040 | bytes 14450689 | tf_op jit(solution)/shard_map/dot_general | solution.py:70
  541.0 5.8 fusion.34
  550.2 69.0 %shard_map.303 = (f32[64,2,8,1152]{3,2,1,0:T(8,128)}, f32[64,2,8,1152]{3,2,1,0:T(8,128)}, f32[2,16,1152]{2,1,0:T(8,128)}, f32[2,8,1152]{2,1,0:T(8,128)}, f32[64,2,8,128]{3,2,1,0:T(8,128)}) custom-call(f32[64,2,8,1152]{3,2,1,0:T(8,128)} %compare_select_fusion.step_ref, f32[64,2,8,1152]{3,2,1,0:T(8,128)} %get-tuple-element.229.input_ref, ...), custom_call_target="tpu_custom_call" | custom-call | flops 377487360 | bytes 453964 | tf_op jit(solution)/shard_map/pallas_call | solution.py:362
  624.6 6.5 all-to-all-start.6
  652.3 6.1 copy.84
  665.7 13.3 %shard_map.304 = (bf16[64,16,1152]{2,1,0:T(8,128)(2,1)}, f32[8,1152]{1,0:T(8,128)}, f32[3,16,1152]{2,1,0:T(8,128)}, f32[3,16,1152]{2,1,0:T(8,128)}) custom-call(bf16[1024,104]{1,0:T(8,128)(2,1)} %add_convert_fusion.7.proj_ref, bf16[104,1152]{1,0:T(8,128)(2,1)} %slice.207.weight_ref, f32[64,16,1152]{2,1,0:T(8,128)} %bitcast.228, ...), custom_call_target="tpu_custom_call" | custom-call | flops 1 | bytes 1 | tf_op jit(solution)/shard_map/pallas_call | solution.py:477
  691.9 6.1 fusion.93
  731.5 14.2 %collective-permute-done.22 = f32[144,1152]{1,0:T(8,128)S(1)} collective-permute-done((f32[144,1152]{1,0:T(8,128)S(1)}, f32[144,1152]{1,0:T(8,128)S(1)}, u32[]{:S(2)}, u32[]{:S(2)}) %collective-permute-start.22) | collective-permute-done | bytes 663584 | tf_op jit(solution)/shard_map/ppermute | solution.py:34
  757.5 29.5 %collective-permute-done.23 = bf16[8,144,768]{2,1,0:T(8,128)(2,1)} collective-permute-done((bf16[8,144,768]{2,1,0:T(8,128)(2,1)}, bf16[8,144,768]{2,1,0:T(8,128)(2,1)}, u32[]{:S(2)}, u32[]{:S(2)}) %collective-permute-start.23) | collective-permute-done | bytes 1769504 | tf_op jit(solution)/shard_map/ppermute | solution.py:34
  786.9 10.3 %all-to-all-done.7 = bf16[8,178,1152]{2,1,0:T(8,128)(2,1)} async-done(((bf16[8,178,1152]{2,1,0:T(8,128)(2,1)}), bf16[8,178,1152]{2,1,0:T(8,128)(2,1)}, u32[]{:S(2)}, u32[]{:S(2)}) %all-to-all-start.7) | async-done | bytes 3280928 | tf_op jit(solution)/shard_map/all_to_all | solution.py:1112
  811.6 8.3 %collective-permute-done.24 = f32[178,1152]{1,0:T(8,128)S(1)} collective-permute-done((f32[178,1152]{1,0:T(8,128)S(1)}, f32[178,1152]{1,0:T(8,128)S(1)}, u32[]{:S(2)}, u32[]{:S(2)}) %collective-permute-start.24) | collective-permute-done | bytes 820256 | tf_op jit(solution)/shard_map/ppermute | solution.py:34
  (424 shorter events, 285.8 us)
Async XLA Ops:
  95.9 11.3 %collective-permute-start = (bf16[3,2,1,1152]{3,2,1,0:T(2,128)(2,1)S(1)}, bf16[3,2,1,1152]{3,2,1,0:T(2,128)(2,1)S(1)}, u32[]{:S(2)}, u32[]{:S(2)}) collective-permute-start(bf16[3,2,1,1152]{3,2,1,0:T(2,128)(2,1)S(1)} %slice.249), channel_id=1, source_target_pairs={{0,2},{1,3},{4,6},{5,7},{8,10},{9,11},{12,14},{13,15},{16,18},{17,... | collective-permute-start | bytes 41480 | tf_op jit(solution)/shard_map/ppermute | solution.py:40
  102.3 81.7 %all-to-all-start = ((bf16[8,288,768]{2,1,0:T(8,128)(2,1)}), bf16[8,288,768]{2,1,0:T(8,128)(2,1)}, u32[]{:S(2)}, u32[]{:S(2)}) async-start(bf16[8,288,768]{2,1,0:T(8,128)(2,1)} %slice_select_fusion), calls=%async_computation | async-start | bytes 7077888 | tf_op jit(solution)/shard_map/all_to_all | solution.py:602
  112.9 121.1 %collective-permute-start.3 = (bf16[1152,1152]{1,0:T(8,128)(2,1)}, bf16[1152,1152]{1,0:T(8,128)(2,1)}, u32[]{:S(2)}, u32[]{:S(2)}) collective-permute-start(bf16[1152,1152]{1,0:T(8,128)(2,1)} %bitcast.15), channel_id=1, source_target_pairs={{0,2},{2,0},{1,3},{3,1},{4,6},{6,4},{5,7},{7,5},{8,10},{10,8},{9,1... | collective-permute-start | bytes 7962632 | tf_op jit(solution)/shard_map/ppermute | solution.py:34
  184.0 58.2 %all-to-all-start.1 = ((bf16[8,128,1152]{2,1,0:T(8,128)(2,1)}), bf16[8,128,1152]{2,1,0:T(8,128)(2,1)}, u32[]{:S(2)}, u32[]{:S(2)}) async-start(bf16[8,128,1152]{2,1,0:T(8,128)(2,1)} %bitcast.254), calls=%async_computation.1 | async-start | bytes 4718592 | tf_op jit(solution)/shard_map/all_to_all | solution.py:585
  188.4 5.2 collective-permute-start.2
  197.5 44.6 %collective-permute-start.4 = (bf16[8,144,768]{2,1,0:T(8,128)(2,1)}, bf16[8,144,768]{2,1,0:T(8,128)(2,1)}, u32[]{:S(2)}, u32[]{:S(2)}) collective-permute-start(bf16[8,144,768]{2,1,0:T(8,128)(2,1)} %get-tuple-element.245), channel_id=1, source_target_pairs={{0,2},{2,0},{1,3},{3,1},{4,6},{6,4},{5,7},{7,5},{8,10},{10,8},{9,1... | collective-permute-start | bytes 5308424 | tf_op jit(solution)/shard_map/ppermute | solution.py:34
  250.4 8.3 collective-permute-start.5
  268.9 60.6 %all-to-all-start.2 = ((bf16[8,128,1152]{2,1,0:T(8,128)(2,1)}), bf16[8,128,1152]{2,1,0:T(8,128)(2,1)}, u32[]{:S(2)}, u32[]{:S(2)}) async-start(bf16[8,128,1152]{2,1,0:T(8,128)(2,1)} %bitcast.255), calls=%async_computation.2 | async-start | bytes 4718592 | tf_op jit(solution)/shard_map/all_to_all | solution.py:585
  275.3 40.8 %collective-permute-start.6 = (bf16[8,144,768]{2,1,0:T(8,128)(2,1)}, bf16[8,144,768]{2,1,0:T(8,128)(2,1)}, u32[]{:S(2)}, u32[]{:S(2)}) collective-permute-start(bf16[8,144,768]{2,1,0:T(8,128)(2,1)} %get-tuple-element.244), channel_id=1, source_target_pairs={{0,2},{2,0},{1,3},{3,1},{4,6},{6,4},{5,7},{7,5},{8,10},{10,8},{9,1... | collective-permute-start | bytes 5308424 | tf_op jit(solution)/shard_map/ppermute | solution.py:34
  275.4 55.2 %collective-permute-start.8 = (bf16[1024,1152]{1,0:T(8,128)(2,1)}, bf16[1024,1152]{1,0:T(8,128)(2,1)}, u32[]{:S(2)}, u32[]{:S(2)}) collective-permute-start(bf16[1024,1152]{1,0:T(8,128)(2,1)} %bitcast.35.cotan_ref), channel_id=1, source_target_pairs={{0,1},{1,0},{2,3},{3,2},{4,5},{5,4},{6,7},{7,6},{8,9},{9,8},{10,11... | collective-permute-start | bytes 7077896 | tf_op jit(solution)/shard_map/ppermute | solution.py:34
  329.5 4.9 collective-permute-start.7
  358.0 25.6 %collective-permute-start.10 = (f32[1024,1152]{1,0:T(8,128)}, f32[1024,1152]{1,0:T(8,128)}, u32[]{:S(2)}, u32[]{:S(2)}) collective-permute-start(f32[1024,1152]{1,0:T(8,128)} %get-tuple-element.131), channel_id=1, source_target_pairs={{0,1},{1,0},{2,3},{3,2},{4,5},{5,4},{6,7},{7,6},{8,9},{9,8},{10,11... | collective-permute-start | bytes 14155784 | tf_op jit(solution)/shard_map/ppermute | solution.py:34
  358.2 32.1 %collective-permute-start.9 = (f32[1024,1152]{1,0:T(8,128)}, f32[1024,1152]{1,0:T(8,128)S(1)}, u32[]{:S(2)}, u32[]{:S(2)}) collective-permute-start(f32[1024,1152]{1,0:T(8,128)} %get-tuple-element.129), channel_id=1, source_target_pairs={{0,1},{1,0},{2,3},{3,2},{4,5},{5,4},{6,7},{7,6},{8,9},{9,8},{10,11... | collective-permute-start | bytes 14155784 | tf_op jit(solution)/shard_map/ppermute | solution.py:34
  395.1 59.0 %all-to-all-start.3 = ((bf16[8,128,1152]{2,1,0:T(8,128)(2,1)}), bf16[8,128,1152]{2,1,0:T(8,128)(2,1)}, u32[]{:S(2)}, u32[]{:S(2)}) async-start(bf16[8,128,1152]{2,1,0:T(8,128)(2,1)} %bitcast.222), calls=%async_computation.3 | async-start | bytes 4718592 | tf_op jit(solution)/shard_map/all_to_all | solution.py:585
  407.4 40.8 %collective-permute-start.11 = (bf16[1152,768]{1,0:T(8,128)(2,1)S(1)}, bf16[1152,768]{1,0:T(8,128)(2,1)}, u32[]{:S(2)}, u32[]{:S(2)}) collective-permute-start(bf16[1152,768]{1,0:T(8,128)(2,1)S(1)} %convolution_convert_fusion.3), channel_id=1, source_target_pairs={{0,2},{2,0},{1,3},{3,1},{4,6},{6,4},{5,7},{7,5},{8,10},{10,8},{9,1... | collective-permute-start | bytes 5308424 | tf_op jit(solution)/shard_map/ppermute | solution.py:34
  459.9 4.9 collective-permute-start.13
  459.9 45.8 %collective-permute-start.12 = (bf16[1152,768]{1,0:T(8,128)(2,1)}, bf16[1152,768]{1,0:T(8,128)(2,1)}, u32[]{:S(2)}, u32[]{:S(2)}) collective-permute-start(bf16[1152,768]{1,0:T(8,128)(2,1)} %convolution_convert_fusion.4), channel_id=1, source_target_pairs={{0,2},{2,0},{1,3},{3,1},{4,6},{6,4},{5,7},{7,5},{8,10},{10,8},{9,1... | collective-permute-start | bytes 5308424 | tf_op jit(solution)/shard_map/ppermute | solution.py:34
  459.9 59.3 %all-to-all-start.4 = ((bf16[8,128,1152]{2,1,0:T(8,128)(2,1)}), bf16[8,128,1152]{2,1,0:T(8,128)(2,1)}, u32[]{:S(2)}, u32[]{:S(2)}) async-start(bf16[8,128,1152]{2,1,0:T(8,128)(2,1)} %bitcast.224), calls=%async_computation.4 | async-start | bytes 4718592 | tf_op jit(solution)/shard_map/all_to_all | solution.py:585
  526.1 93.2 %all-to-all-start.5 = ((bf16[8,288,768]{2,1,0:T(8,128)(2,1)}), bf16[8,288,768]{2,1,0:T(8,128)(2,1)}, u32[]{:S(2)}, u32[]{:S(2)}) async-start(bf16[8,288,768]{2,1,0:T(8,128)(2,1)} %pad_maximum_fusion), calls=%async_computation.5 | async-start | bytes 7077888 | tf_op jit(solution)/shard_map/all_to_all | solution.py:1032
  530.7 16.2 %collective-permute-start.15 = (f32[2,16,1152]{2,1,0:T(8,128)}, f32[2,16,1152]{2,1,0:T(8,128)S(1)}, u32[]{:S(2)}, u32[]{:S(2)}) collective-permute-start(f32[2,16,1152]{2,1,0:T(8,128)} %get-tuple-element.143), channel_id=1, source_target_pairs={{2,0},{3,1},{6,4},{7,5},{10,8},{11,9},{14,12},{15,13},{18,16},{19,... | collective-permute-start | bytes 442376 | tf_op jit(solution)/shard_map/ppermute | solution.py:40
  546.9 72.4 %collective-permute-start.16 = (bf16[1152,1152]{1,0:T(8,128)(2,1)}, bf16[1152,1152]{1,0:T(8,128)(2,1)}, u32[]{:S(2)}, u32[]{:S(2)}) collective-permute-start(bf16[1152,1152]{1,0:T(8,128)(2,1)} %convolution_convert_fusion.1), channel_id=1, source_target_pairs={{0,2},{2,0},{1,3},{3,1},{4,6},{6,4},{5,7},{7,5},{8,10},{10,8},{9,1... | collective-permute-start | bytes 7962632 | tf_op jit(solution)/shard_map/ppermute | solution.py:34
  624.6 65.7 %all-to-all-start.6 = ((bf16[8,144,1152]{2,1,0:T(8,128)(2,1)}), bf16[8,144,1152]{2,1,0:T(8,128)(2,1)}, u32[]{:S(2)}, u32[]{:S(2)}) async-start(bf16[8,144,1152]{2,1,0:T(8,128)(2,1)} %bitcast.216), calls=%async_computation.6 | async-start | bytes 5308416 | tf_op jit(solution)/shard_map/all_to_all | solution.py:1046
  635.6 4.4 collective-permute-start.20
  644.8 41.8 %collective-permute-start.19 = (bf16[8,144,768]{2,1,0:T(8,128)(2,1)}, bf16[8,144,768]{2,1,0:T(8,128)(2,1)}, u32[]{:S(2)}, u32[]{:S(2)}) collective-permute-start(bf16[8,144,768]{2,1,0:T(8,128)(2,1)} %get-tuple-element.243), channel_id=1, source_target_pairs={{0,2},{2,0},{1,3},{3,1},{4,6},{6,4},{5,7},{7,5},{8,10},{10,8},{9,1... | collective-permute-start | bytes 5308424 | tf_op jit(solution)/shard_map/ppermute | solution.py:34
  650.8 13.0 %collective-permute-start.17 = (f32[1024,104]{1,0:T(8,128)}, f32[1024,104]{1,0:T(8,128)}, u32[]{:S(2)}, u32[]{:S(2)}) collective-permute-start(f32[1024,104]{1,0:T(8,128)} %pad_maximum_fusion.4), channel_id=1, source_target_pairs={{0,1},{1,0},{2,3},{3,2},{4,5},{5,4},{6,7},{7,6},{8,9},{9,8},{10,11... | collective-permute-start | bytes 1277960 | tf_op jit(solution)/shard_map/ppermute | solution.py:34
  680.6 6.0 collective-permute-start.18
  703.6 8.0 collective-permute-start.21
  715.9 81.4 %all-to-all-start.7 = ((bf16[8,178,1152]{2,1,0:T(8,128)(2,1)}), bf16[8,178,1152]{2,1,0:T(8,128)(2,1)}, u32[]{:S(2)}, u32[]{:S(2)}) async-start(bf16[8,178,1152]{2,1,0:T(8,128)(2,1)} %pad_maximum_fusion.1), calls=%async_computation.7 | async-start | bytes 6782976 | tf_op jit(solution)/shard_map/all_to_all | solution.py:1112
  725.8 21.5 %collective-permute-start.14 = (bf16[1024,1152]{1,0:T(8,128)(2,1)S(1)}, bf16[1024,1152]{1,0:T(8,128)(2,1)}, u32[]{:S(2)}, u32[]{:S(2)}) collective-permute-start(bf16[1024,1152]{1,0:T(8,128)(2,1)S(1)} %fusion.29), channel_id=1, source_target_pairs={{0,1},{1,0},{2,3},{3,2},{4,5},{5,4},{6,7},{7,6},{8,9},{9,8},{10,11... | collective-permute-start | bytes 7077896 | tf_op jit(solution)/shard_map/ppermute | solution.py:34
  728.7 17.0 %collective-permute-start.22 = (f32[144,1152]{1,0:T(8,128)S(1)}, f32[144,1152]{1,0:T(8,128)S(1)}, u32[]{:S(2)}, u32[]{:S(2)}) collective-permute-start(f32[144,1152]{1,0:T(8,128)S(1)} %convert_reduce_fusion.1), channel_id=1, source_target_pairs={{0,2},{2,0},{1,3},{3,1},{4,6},{6,4},{5,7},{7,5},{8,10},{10,8},{9,1... | collective-permute-start | bytes 1990664 | tf_op jit(solution)/shard_map/ppermute | solution.py:34
  746.7 40.3 %collective-permute-start.23 = (bf16[8,144,768]{2,1,0:T(8,128)(2,1)}, bf16[8,144,768]{2,1,0:T(8,128)(2,1)}, u32[]{:S(2)}, u32[]{:S(2)}) collective-permute-start(bf16[8,144,768]{2,1,0:T(8,128)(2,1)} %get-tuple-element.172), channel_id=1, source_target_pairs={{0,2},{2,0},{1,3},{3,1},{4,6},{6,4},{5,7},{7,5},{8,10},{10,8},{9,1... | collective-permute-start | bytes 5308424 | tf_op jit(solution)/shard_map/ppermute | solution.py:34
  799.8 20.1 %collective-permute-start.24 = (f32[178,1152]{1,0:T(8,128)S(1)}, f32[178,1152]{1,0:T(8,128)S(1)}, u32[]{:S(2)}, u32[]{:S(2)}) collective-permute-start(f32[178,1152]{1,0:T(8,128)S(1)} %convert_reduce_fusion), channel_id=1, source_target_pairs={{0,2},{2,0},{1,3},{3,1},{4,6},{6,4},{5,7},{7,5},{8,10},{10,8},{9,1... | collective-permute-start | bytes 2460680 | tf_op jit(solution)/shard_map/ppermute | solution.py:34
  (103 other events, 1412.8 us)

commit v7 on v6

--- a/solution.py
+++ b/solution.py
@@ -951,10 +951,11 @@
     cotan = cotan_bf.astype(F32)
     kept_cotan = (cotan * keep[:, None]).astype(BF16)
     sent_cotan = jnp.concatenate([slotted(kept_cotan, half) for half in range(HALVES)], axis=1)
-    sent_cotan, expert_blocks = together(sent_cotan, expert_blocks)
+    entering = entering_pieces(seg_decay[:, :, SEGMENTS - 1], last_state, "ctx", False)
+    entering, mix_out, expert_blocks, sent_cotan = together(
+        entering, mix_out, expert_blocks, sent_cotan
+    )
     slot_cotan = expert_exchange(sent_cotan, experts)
-    entering = entering_pieces(seg_decay[:, :, SEGMENTS - 1], last_state, "ctx", False)
-    entering, expert_blocks = together(entering, expert_blocks)
     far_up, far_down = other_hidden(expert_blocks)
     scan_out, seg_start = scan.run(
         step_size, xconv, mix_in, mix_out, rate_rows, seg_decay, seg_state, entering
@@ -1011,8 +1012,8 @@
         all_rows, (hidden_a, hidden_b), all_grads, (active_a, active_b)
     )
     far_first = sent_far(far_parts[0])
-    got_grads, near_parts, far_second, far_first, slot_outs = together(
-        got_grads, near_parts, far_parts[1], far_first, slot_outs
+    got_grads, near_parts, far_second, far_first, slot_outs, router_grad_t = together(
+        got_grads, near_parts, far_parts[1], far_first, slot_outs, router_grad_t
     )
     far_parts = far_first, sent_far(far_second)
     normed_two_grad = landed(got_grads)
@@ -1028,7 +1029,10 @@
     back_decay, back_adjoint, first_adjoint = scan.adjoint_ends(
         step_size, mix_out, scan_grad, rate_rows
     )
-    far_parts, got_out, _ = together(far_parts, got_out, first_adjoint)
+    normed_part = contract_cols(z_grad_bf, in_z)
+    far_parts, got_out, near_product, far_product, normed_part, _ = together(
+        far_parts, got_out, near_product, far_product, normed_part, first_adjoint
+    )
     weight_blocks = lax.all_to_all(
         expert_weight_parts(near_parts, far_parts), "dp", 0, 0, tiled=True
     )
@@ -1096,7 +1100,7 @@
     small_rows = small_grads.astype(BF16).reshape(dp_count, small_size)
     small_rows = jnp.pad(small_rows, ((0, 0), (0, -small_size % inner))).reshape(dp_count, -1, inner)
     x_grad_bf, small_rows, out_blocks = together(x_grad_bf, small_rows, out_blocks)
-    normed_part = contract_cols(x_grad_bf, in_x) + contract_cols(z_grad_bf, in_z)
+    normed_part = normed_part + contract_cols(x_grad_bf, in_x)
     normed_grad = axis_sum(normed_part, "tp")
     values_norm_grad, gain_one_grad = rms_backward(values, inverse_one, gain_one_f, normed_grad)
     input_grad = from_rows((middle_grad + values_norm_grad).astype(BF16))

time: 837 us -> 836 us (level)
  waiting for transfers between devices: 197 us -> 184 us
  transfers between devices with their start and end apart: 33 -> 33, of which waited for: 18 -> 19; matrix products, arithmetic and copies ran while one was open for 25% -> 27% of each run, Pallas kernels for 21% -> 21%
where the time goes in v7:
time: 836 us; the launch traced here: 826 us
  Pallas kernels  267 us (32%)
  waiting for transfers between devices  184 us (22%)
  matrix products  125 us (15%)
  other arithmetic  105 us (13%)
  local copies, waits for them, and re-layouts  80.8 us (10%)
  starting transfers between devices  61.6 us (7%)
    pallas_call x4, Pallas kernels, call(): pl.pallas_call(kernel, grid=self.grid, in_specs=in_specs, out_specs=out_s...  134 us
    ppermute x21, waiting for transfers between devices, swapped(): return lax.ppermute(value, axis, [(0, 1), (1, 0)])  123 us
    pallas_call x1, Pallas kernels, gathered(): pl.pallas_call(partial(gather_kernel, count, parts), in_specs=[anywhere]...  72.2 us
    dot_general x12, matrix products, contract_rows(): lax.dot_general(left_side, right_side, (((0,), (0,)), ((), ())), precisio...  63.1 us
    pallas_call x2, Pallas kernels, expert_call(): pl.pallas_call(partial(expert_kernel, len(kept)), grid=(count // block,),...  47.2 us
    all_to_all x4, waiting for transfers between devices, expert_exchange(): lax.all_to_all(value, 'dp', 0, 0, axis_index_groups=groups, tiled=True)  29.7 us
    dot_general x6, matrix products, contract_cols(): lax.dot_general(left_side, right_side, (((1,), (1,)), ((), ())), precisio...  28.5 us
    all_to_all x4, starting transfers between devices, expert_exchange(): lax.all_to_all(value, 'dp', 0, 0, axis_index_groups=groups, tiled=True)  18.6 us
  transfers between devices with their start and end apart: 33, of which 19 were waited for; matrix products, arithmetic and copies ran while one was open for 27% of the time, Pallas kernels for 21%

profile of v7, /device:TPU:0, one launch (start us, length us, event | category | flops | bytes accessed | tf_op | source)
XLA Modules:
  0.0 825.9 jit_solution(8141930876449772483)
XLA Ops:
  11.5 72.2 %shard_map.297 = (bf16[8,144,1152]{2,1,0:T(8,128)(2,1)}, bf16[8,144,256]{2,1,0:T(8,128)(2,1)}, bf16[8,144,1152]{2,1,0:T(8,128)(2,1)}) custom-call(bf16[144,1152]{1,0:T(8,128)(2,1)} %bitcast.267, bf16[144,256]{1,0:T(8,128)(2,1)} %pad.62.refs_1_, bf16[144,1152]{1,0:T(8,128)(2,1)} %fusion.49.refs_2_), custom_call_target="tpu_custom_call" | custom-call | bytes 11796480 | tf_op jit(solution)/shard_map/pallas_call | solution.py:704
  130.4 19.5 %shard_map.298 = (f32[2,16,8,1152]{3,2,1,0:T(8,128)}, f32[2,16,8,1152]{3,2,1,0:T(8,128)}, f32[2,16,1152]{2,1,0:T(8,128)}) custom-call(f32[64,2,8,1152]{3,2,1,0:T(8,128)} %compare_select_fusion.step_ref, f32[64,2,8,1152]{3,2,1,0:T(8,128)} %get-tuple-element.237.input_ref, f32[2,64,16,8,128]{4,3,2,1,0:T(8,128)} %broadcast_in_dim.28.mix_in_ref, ...), custom_call_target="tpu_custom_call" | custom-call | flops 94371840 | bytes 209223 | tf_op jit(solution)/shard_map/pallas_call | solution.py:362
  174.1 9.8 %all-to-all-done.up_a.down_a = bf16[8,288,768]{2,1,0:T(8,128)(2,1)} async-done(((bf16[8,288,768]{2,1,0:T(8,128)(2,1)}), bf16[8,288,768]{2,1,0:T(8,128)(2,1)}, u32[]{:S(2)}, u32[]{:S(2)}) %all-to-all-start) | async-done | bytes 3538976 | tf_op jit(solution)/shard_map/all_to_all | solution.py:602
  183.9 5.9 broadcast_in_dim.30.mix_out_ref
  198.5 26.4 %shard_map.299 = (f32[64,2,8,1152]{3,2,1,0:T(8,128)}, f32[2,16,8,1152]{3,2,1,0:T(8,128)}) custom-call(f32[64,2,8,1152]{3,2,1,0:T(8,128)} %compare_select_fusion.step_ref, f32[64,2,8,1152]{3,2,1,0:T(8,128)} %get-tuple-element.237.input_ref, f32[2,64,16,8,128]{4,3,2,1,0:T(8,128)} %broadcast_in_dim.28.mix_in_ref, ...), custom_call_target="tpu_custom_call" | custom-call | flops 132120576 | bytes 352092 | tf_op jit(solution)/shard_map/pallas_call | solution.py:362
  224.9 8.2 multiply_convert_fusion.2
  237.5 10.3 %all-to-all-done.1 = bf16[8,128,1152]{2,1,0:T(8,128)(2,1)} async-done(((bf16[8,128,1152]{2,1,0:T(8,128)(2,1)}), bf16[8,128,1152]{2,1,0:T(8,128)(2,1)}, u32[]{:S(2)}, u32[]{:S(2)}) %all-to-all-start.1) | async-done | bytes 2359328 | tf_op jit(solution)/shard_map/all_to_all | solution.py:585
  247.8 8.2 fusion.45
  280.0 40.4 %collective-permute-done.6.down_b = bf16[8,144,768]{2,1,0:T(8,128)(2,1)} collective-permute-done((bf16[8,144,768]{2,1,0:T(8,128)(2,1)}, bf16[8,144,768]{2,1,0:T(8,128)(2,1)}, u32[]{:S(2)}, u32[]{:S(2)}) %collective-permute-start.6) | collective-permute-done | bytes 1769504 | tf_op jit(solution)/shard_map/ppermute | solution.py:34
  320.4 13.4 %all-to-all-done.2 = bf16[8,128,1152]{2,1,0:T(8,128)(2,1)} async-done(((bf16[8,128,1152]{2,1,0:T(8,128)(2,1)}), bf16[8,128,1152]{2,1,0:T(8,128)(2,1)}, u32[]{:S(2)}, u32[]{:S(2)}) %all-to-all-start.2) | async-done | bytes 2359328 | tf_op jit(solution)/shard_map/all_to_all | solution.py:585
  338.6 23.6 %shard_map.300 = (f32[1024,1152]{1,0:T(8,128)}, f32[1024,1152]{1,0:T(8,128)}, f32[1024,8]{1,0:T(8,128)}, bf16[2048,1152]{1,0:T(8,128)(2,1)}, bf16[2048,1152]{1,0...) custom-call(bf16[1024,1152]{1,0:T(8,128)(2,1)} %collective-permute-d, ...), custom_call_target="tpu_custom_call" | custom-call | flops 14495514624 | bytes 29884416 | tf_op jit(solution)/shard_map/pallas_call | solution.py:553
  362.9 23.6 %shard_map.301 = (f32[1024,1152]{1,0:T(8,128)}, f32[1024,1152]{1,0:T(8,128)}, f32[1024,8]{1,0:T(8,128)}, bf16[2048,1152]{1,0:T(8,128)(2,1)}, bf16[2048,1152]{1,0...) custom-call(bf16[1024,1152]{1,0:T(8,128)(2,1)} %bitcast.34.rows_ref,, ...), custom_call_target="tpu_custom_call", output_to_operand_aliasing={{3}: (8, {}), {4}: (9, {}), {5}: (10, {}), {6}: (11, {}), {... | custom-call | flops 14495514624 | bytes 29884416 | tf_op jit(solution)/shard_map/pallas_call | solution.py:553
  387.9 6.6 add_convert_fusion.6
  403.2 7.4 convolution_convert_fusion.3
  411.3 7.6 convolution_convert_fusion.4
  433.9 17.5 %collective-permute-done.11 = bf16[1152,768]{1,0:T(8,128)(2,1)} collective-permute-done((bf16[1152,768]{1,0:T(8,128)(2,1)S(1)}, bf16[1152,768]{1,0:T(8,128)(2,1)}, u32[]{:S(2)}, u32[]{:S(2)}) %collective-permute-start.11) | collective-permute-done | bytes 1769504 | tf_op jit(solution)/shard_map/ppermute | solution.py:34
  451.4 6.0 all-to-all-done.3
  457.4 5.9 fusion.28
  478.5 7.4 fusion.44
  490.0 7.9 fusion.43
  498.0 19.4 %shard_map.302 = (f32[2,16,8,1152]{3,2,1,0:T(8,128)}, f32[2,16,8,1152]{3,2,1,0:T(8,128)}, f32[2,16,1152]{2,1,0:T(8,128)}) custom-call(f32[64,2,8,1152]{3,2,1,0:T(8,128)} %compare_select_fusion.step_ref, f32[2,64,16,8,128]{4,3,2,1,0:T(8,128)} %broadcast_in_dim.30.mix_out_ref, f32[64,2,8,1152]{3,2,1,0:T(8,128)} %get-tuple-element.239.grad_ref, ...), custom_call_target="tpu_custom_call" | custom-call | flops 94371840 | bytes 209223 | tf_op jit(solution)/shard_map/pallas_call | solution.py:362
  517.4 7.5 fusion.34
  536.8 6.1 all-to-all-start.5
  544.2 6.0 collective-permute-done.16.enter_ref
  550.8 69.0 %shard_map.303 = (f32[64,2,8,1152]{3,2,1,0:T(8,128)}, f32[64,2,8,1152]{3,2,1,0:T(8,128)}, f32[2,16,1152]{2,1,0:T(8,128)}, f32[2,8,1152]{2,1,0:T(8,128)}, f32[64,2,8,128]{3,2,1,0:T(8,128)}) custom-call(f32[64,2,8,1152]{3,2,1,0:T(8,128)} %compare_select_fusion.step_ref, f32[64,2,8,1152]{3,2,1,0:T(8,128)} %get-tuple-element.237.input_ref, ...), custom_call_target="tpu_custom_call" | custom-call | flops 377487360 | bytes 453964 | tf_op jit(solution)/shard_map/pallas_call | solution.py:362
  654.7 6.1 copy.84
  668.1 13.4 %shard_map.304 = (bf16[64,16,1152]{2,1,0:T(8,128)(2,1)}, f32[8,1152]{1,0:T(8,128)}, f32[3,16,1152]{2,1,0:T(8,128)}, f32[3,16,1152]{2,1,0:T(8,128)}) custom-call(bf16[1024,104]{1,0:T(8,128)(2,1)} %add_convert_fusion.7.proj_ref, bf16[104,1152]{1,0:T(8,128)(2,1)} %slice.207.weight_ref, f32[64,16,1152]{2,1,0:T(8,128)} %bitcast.230, ...), custom_call_target="tpu_custom_call" | custom-call | flops 1 | bytes 1 | tf_op jit(solution)/shard_map/pallas_call | solution.py:477
  693.8 6.1 fusion.94
  730.7 14.0 %collective-permute-done.22 = f32[144,1152]{1,0:T(8,128)S(1)} collective-permute-done((f32[144,1152]{1,0:T(8,128)S(1)}, f32[144,1152]{1,0:T(8,128)S(1)}, u32[]{:S(2)}, u32[]{:S(2)}) %collective-permute-start.22) | collective-permute-done | bytes 663584 | tf_op jit(solution)/shard_map/ppermute | solution.py:34
  757.5 28.5 %collective-permute-done.23 = bf16[8,144,768]{2,1,0:T(8,128)(2,1)} collective-permute-done((bf16[8,144,768]{2,1,0:T(8,128)(2,1)}, bf16[8,144,768]{2,1,0:T(8,128)(2,1)}, u32[]{:S(2)}, u32[]{:S(2)}) %collective-permute-start.23) | collective-permute-done | bytes 1769504 | tf_op jit(solution)/shard_map/ppermute | solution.py:34
  786.0 9.7 %all-to-all-done.7 = bf16[8,178,1152]{2,1,0:T(8,128)(2,1)} async-done(((bf16[8,178,1152]{2,1,0:T(8,128)(2,1)}), bf16[8,178,1152]{2,1,0:T(8,128)(2,1)}, u32[]{:S(2)}, u32[]{:S(2)}) %all-to-all-start.7) | async-done | bytes 3280928 | tf_op jit(solution)/shard_map/all_to_all | solution.py:1116
  811.8 7.0 collective-permute-done.24
  (418 shorter events, 302.5 us)
Async XLA Ops:
  95.8 11.2 %collective-permute-start = (bf16[3,2,1,1152]{3,2,1,0:T(2,128)(2,1)S(1)}, bf16[3,2,1,1152]{3,2,1,0:T(2,128)(2,1)S(1)}, u32[]{:S(2)}, u32[]{:S(2)}) collective-permute-start(bf16[3,2,1,1152]{3,2,1,0:T(2,128)(2,1)S(1)} %slice.249), channel_id=1, source_target_pairs={{0,2},{1,3},{4,6},{5,7},{8,10},{9,11},{12,14},{13,15},{16,18},{17,... | collective-permute-start | bytes 41480 | tf_op jit(solution)/shard_map/ppermute | solution.py:40
  102.2 81.6 %all-to-all-start = ((bf16[8,288,768]{2,1,0:T(8,128)(2,1)}), bf16[8,288,768]{2,1,0:T(8,128)(2,1)}, u32[]{:S(2)}, u32[]{:S(2)}) async-start(bf16[8,288,768]{2,1,0:T(8,128)(2,1)} %slice_select_fusion), calls=%async_computation | async-start | bytes 7077888 | tf_op jit(solution)/shard_map/all_to_all | solution.py:602
  112.8 112.1 %collective-permute-start.3 = (bf16[1152,1152]{1,0:T(8,128)(2,1)}, bf16[1152,1152]{1,0:T(8,128)(2,1)}, u32[]{:S(2)}, u32[]{:S(2)}) collective-permute-start(bf16[1152,1152]{1,0:T(8,128)(2,1)} %bitcast.15), channel_id=1, source_target_pairs={{0,2},{2,0},{1,3},{3,1},{4,6},{6,4},{5,7},{7,5},{8,10},{10,8},{9,1... | collective-permute-start | bytes 7962632 | tf_op jit(solution)/shard_map/ppermute | solution.py:34
  159.9 14.2 %collective-permute-start.2 = (f32[2,16,1152]{2,1,0:T(8,128)}, f32[2,16,1152]{2,1,0:T(8,128)}, u32[]{:S(2)}, u32[]{:S(2)}) collective-permute-start(f32[2,16,1152]{2,1,0:T(8,128)} %get-tuple-element.107), channel_id=1, source_target_pairs={{0,2},{1,3},{4,6},{5,7},{8,10},{9,11},{12,14},{13,15},{16,18},{17,... | collective-permute-start | bytes 442376 | tf_op jit(solution)/shard_map/ppermute | solution.py:40
  189.8 58.0 %all-to-all-start.1 = ((bf16[8,128,1152]{2,1,0:T(8,128)(2,1)}), bf16[8,128,1152]{2,1,0:T(8,128)(2,1)}, u32[]{:S(2)}, u32[]{:S(2)}) async-start(bf16[8,128,1152]{2,1,0:T(8,128)(2,1)} %bitcast.256), calls=%async_computation.1 | async-start | bytes 4718592 | tf_op jit(solution)/shard_map/all_to_all | solution.py:585
  197.9 39.6 %collective-permute-start.4 = (bf16[8,144,768]{2,1,0:T(8,128)(2,1)S(1)}, bf16[8,144,768]{2,1,0:T(8,128)(2,1)}, u32[]{:S(2)}, u32[]{:S(2)}) collective-permute-start(bf16[8,144,768]{2,1,0:T(8,128)(2,1)S(1)} %get-tuple-element.253), channel_id=1, source_target_pairs={{0,2},{2,0},{1,3},{3,1},{4,6},{6,4},{5,7},{7,5},{8,10},{10,8},{9,1... | collective-permute-start | bytes 5308424 | tf_op jit(solution)/shard_map/ppermute | solution.py:34
  256.0 8.3 collective-permute-start.5
  274.6 59.2 %all-to-all-start.2 = ((bf16[8,128,1152]{2,1,0:T(8,128)(2,1)}), bf16[8,128,1152]{2,1,0:T(8,128)(2,1)}, u32[]{:S(2)}, u32[]{:S(2)}) async-start(bf16[8,128,1152]{2,1,0:T(8,128)(2,1)} %bitcast.257), calls=%async_computation.2 | async-start | bytes 4718592 | tf_op jit(solution)/shard_map/all_to_all | solution.py:585
  279.3 41.0 %collective-permute-start.6 = (bf16[8,144,768]{2,1,0:T(8,128)(2,1)}, bf16[8,144,768]{2,1,0:T(8,128)(2,1)}, u32[]{:S(2)}, u32[]{:S(2)}) collective-permute-start(bf16[8,144,768]{2,1,0:T(8,128)(2,1)} %get-tuple-element.252), channel_id=1, source_target_pairs={{0,2},{2,0},{1,3},{3,1},{4,6},{6,4},{5,7},{7,5},{8,10},{10,8},{9,1... | collective-permute-start | bytes 5308424 | tf_op jit(solution)/shard_map/ppermute | solution.py:34
  280.0 54.9 %collective-permute-start.8 = (bf16[1024,1152]{1,0:T(8,128)(2,1)}, bf16[1024,1152]{1,0:T(8,128)(2,1)}, u32[]{:S(2)}, u32[]{:S(2)}) collective-permute-start(bf16[1024,1152]{1,0:T(8,128)(2,1)} %bitcast.35.cotan_ref), channel_id=1, source_target_pairs={{0,1},{1,0},{2,3},{3,2},{4,5},{5,4},{6,7},{7,6},{8,9},{9,8},{10,11... | collective-permute-start | bytes 7077896 | tf_op jit(solution)/shard_map/ppermute | solution.py:34
  333.8 4.9 collective-permute-start.7
  362.3 25.6 %collective-permute-start.10 = (f32[1024,1152]{1,0:T(8,128)}, f32[1024,1152]{1,0:T(8,128)}, u32[]{:S(2)}, u32[]{:S(2)}) collective-permute-start(f32[1024,1152]{1,0:T(8,128)} %get-tuple-element.135), channel_id=1, source_target_pairs={{0,1},{1,0},{2,3},{3,2},{4,5},{5,4},{6,7},{7,6},{8,9},{9,8},{10,11... | collective-permute-start | bytes 14155784 | tf_op jit(solution)/shard_map/ppermute | solution.py:34
  362.5 32.1 %collective-permute-start.9 = (f32[1024,1152]{1,0:T(8,128)}, f32[1024,1152]{1,0:T(8,128)S(1)}, u32[]{:S(2)}, u32[]{:S(2)}) collective-permute-start(f32[1024,1152]{1,0:T(8,128)} %get-tuple-element.133), channel_id=1, source_target_pairs={{0,1},{1,0},{2,3},{3,2},{4,5},{5,4},{6,7},{7,6},{8,9},{9,8},{10,11... | collective-permute-start | bytes 14155784 | tf_op jit(solution)/shard_map/ppermute | solution.py:34
  398.6 58.8 %all-to-all-start.3 = ((bf16[8,128,1152]{2,1,0:T(8,128)(2,1)}), bf16[8,128,1152]{2,1,0:T(8,128)(2,1)}, u32[]{:S(2)}, u32[]{:S(2)}) async-start(bf16[8,128,1152]{2,1,0:T(8,128)(2,1)} %bitcast.222), calls=%async_computation.3 | async-start | bytes 4718592 | tf_op jit(solution)/shard_map/all_to_all | solution.py:585
  410.6 40.8 %collective-permute-start.11 = (bf16[1152,768]{1,0:T(8,128)(2,1)S(1)}, bf16[1152,768]{1,0:T(8,128)(2,1)}, u32[]{:S(2)}, u32[]{:S(2)}) collective-permute-start(bf16[1152,768]{1,0:T(8,128)(2,1)S(1)} %convolution_convert_fusion.3), channel_id=1, source_target_pairs={{0,2},{2,0},{1,3},{3,1},{4,6},{6,4},{5,7},{7,5},{8,10},{10,8},{9,1... | collective-permute-start | bytes 5308424 | tf_op jit(solution)/shard_map/ppermute | solution.py:34
  428.0 6.0 collective-permute-start.12
  463.3 5.3 collective-permute-start.14
  463.3 66.6 %collective-permute-start.13 = (bf16[1152,768]{1,0:T(8,128)(2,1)}, bf16[1152,768]{1,0:T(8,128)(2,1)}, u32[]{:S(2)}, u32[]{:S(2)}) collective-permute-start(bf16[1152,768]{1,0:T(8,128)(2,1)} %convolution_convert_fusion.4), channel_id=1, source_target_pairs={{0,2},{2,0},{1,3},{3,1},{4,6},{6,4},{5,7},{7,5},{8,10},{10,8},{9,1... | collective-permute-start | bytes 5308424 | tf_op jit(solution)/shard_map/ppermute | solution.py:34
  463.9 66.0 %all-to-all-start.4 = ((bf16[8,128,1152]{2,1,0:T(8,128)(2,1)}), bf16[8,128,1152]{2,1,0:T(8,128)(2,1)}, u32[]{:S(2)}, u32[]{:S(2)}) async-start(bf16[8,128,1152]{2,1,0:T(8,128)(2,1)} %bitcast.224), calls=%async_computation.4 | async-start | bytes 4718592 | tf_op jit(solution)/shard_map/all_to_all | solution.py:585
  536.8 85.4 %all-to-all-start.5 = ((bf16[8,288,768]{2,1,0:T(8,128)(2,1)}), bf16[8,288,768]{2,1,0:T(8,128)(2,1)}, u32[]{:S(2)}, u32[]{:S(2)}) async-start(bf16[8,288,768]{2,1,0:T(8,128)(2,1)} %pad_maximum_fusion), calls=%async_computation.5 | async-start | bytes 7077888 | tf_op jit(solution)/shard_map/all_to_all | solution.py:1036
  542.9 7.3 collective-permute-start.16
  550.2 69.7 %collective-permute-start.17 = (bf16[1152,1152]{1,0:T(8,128)(2,1)}, bf16[1152,1152]{1,0:T(8,128)(2,1)}, u32[]{:S(2)}, u32[]{:S(2)}) collective-permute-start(bf16[1152,1152]{1,0:T(8,128)(2,1)} %convolution_convert_fusion.1), channel_id=1, source_target_pairs={{0,2},{2,0},{1,3},{3,1},{4,6},{6,4},{5,7},{7,5},{8,10},{10,8},{9,1... | collective-permute-start | bytes 7962632 | tf_op jit(solution)/shard_map/ppermute | solution.py:34
  627.6 64.5 %all-to-all-start.6 = ((bf16[8,144,1152]{2,1,0:T(8,128)(2,1)}), bf16[8,144,1152]{2,1,0:T(8,128)(2,1)}, u32[]{:S(2)}, u32[]{:S(2)}) async-start(bf16[8,144,1152]{2,1,0:T(8,128)(2,1)} %bitcast.216), calls=%async_computation.6 | async-start | bytes 5308416 | tf_op jit(solution)/shard_map/all_to_all | solution.py:1050
  644.1 46.9 %collective-permute-start.20 = (bf16[8,144,768]{2,1,0:T(8,128)(2,1)}, bf16[8,144,768]{2,1,0:T(8,128)(2,1)}, u32[]{:S(2)}, u32[]{:S(2)}) collective-permute-start(bf16[8,144,768]{2,1,0:T(8,128)(2,1)} %get-tuple-element.251), channel_id=1, source_target_pairs={{0,2},{2,0},{1,3},{3,1},{4,6},{6,4},{5,7},{7,5},{8,10},{10,8},{9,1... | collective-permute-start | bytes 5308424 | tf_op jit(solution)/shard_map/ppermute | solution.py:34
  652.1 14.0 %collective-permute-start.18 = (f32[1024,104]{1,0:T(8,128)}, f32[1024,104]{1,0:T(8,128)}, u32[]{:S(2)}, u32[]{:S(2)}) collective-permute-start(f32[1024,104]{1,0:T(8,128)} %pad_maximum_fusion.4), channel_id=1, source_target_pairs={{0,1},{1,0},{2,3},{3,2},{4,5},{5,4},{6,7},{7,6},{8,9},{9,8},{10,11... | collective-permute-start | bytes 1277960 | tf_op jit(solution)/shard_map/ppermute | solution.py:34
  682.4 8.7 %collective-permute-start.19 = (f32[3,2,1,1152]{3,2,1,0:T(1,128)S(1)}, f32[3,2,1,1152]{3,2,1,0:T(1,128)S(1)}, u32[]{:S(2)}, u32[]{:S(2)}) collective-permute-start(f32[3,2,1,1152]{3,2,1,0:T(1,128)S(1)} %slice.265), channel_id=1, source_target_pairs={{2,0},{3,1},{6,4},{7,5},{10,8},{11,9},{14,12},{15,13},{18,16},{19,... | collective-permute-start | bytes 82952 | tf_op jit(solution)/shard_map/ppermute | solution.py:40
  700.5 8.0 collective-permute-start.21
  713.7 82.0 %all-to-all-start.7 = ((bf16[8,178,1152]{2,1,0:T(8,128)(2,1)}), bf16[8,178,1152]{2,1,0:T(8,128)(2,1)}, u32[]{:S(2)}, u32[]{:S(2)}) async-start(bf16[8,178,1152]{2,1,0:T(8,128)(2,1)} %pad_maximum_fusion.1), calls=%async_computation.7 | async-start | bytes 6782976 | tf_op jit(solution)/shard_map/all_to_all | solution.py:1116
  724.2 23.2 %collective-permute-start.15 = (bf16[1024,1152]{1,0:T(8,128)(2,1)S(1)}, bf16[1024,1152]{1,0:T(8,128)(2,1)}, u32[]{:S(2)}, u32[]{:S(2)}) collective-permute-start(bf16[1024,1152]{1,0:T(8,128)(2,1)S(1)} %fusion.29), channel_id=1, source_target_pairs={{0,1},{1,0},{2,3},{3,2},{4,5},{5,4},{6,7},{7,6},{8,9},{9,8},{10,11... | collective-permute-start | bytes 7077896 | tf_op jit(solution)/shard_map/ppermute | solution.py:34
  727.2 17.5 %collective-permute-start.22 = (f32[144,1152]{1,0:T(8,128)S(1)}, f32[144,1152]{1,0:T(8,128)S(1)}, u32[]{:S(2)}, u32[]{:S(2)}) collective-permute-start(f32[144,1152]{1,0:T(8,128)S(1)} %convert_reduce_fusion.1), channel_id=1, source_target_pairs={{0,2},{2,0},{1,3},{3,1},{4,6},{6,4},{5,7},{7,5},{8,10},{10,8},{9,1... | collective-permute-start | bytes 1990664 | tf_op jit(solution)/shard_map/ppermute | solution.py:34
  745.7 40.3 %collective-permute-start.23 = (bf16[8,144,768]{2,1,0:T(8,128)(2,1)}, bf16[8,144,768]{2,1,0:T(8,128)(2,1)}, u32[]{:S(2)}, u32[]{:S(2)}) collective-permute-start(bf16[8,144,768]{2,1,0:T(8,128)(2,1)} %get-tuple-element.180), channel_id=1, source_target_pairs={{0,2},{2,0},{1,3},{3,1},{4,6},{6,4},{5,7},{7,5},{8,10},{10,8},{9,1... | collective-permute-start | bytes 5308424 | tf_op jit(solution)/shard_map/ppermute | solution.py:34
  798.3 20.6 %collective-permute-start.24 = (f32[178,1152]{1,0:T(8,128)S(1)}, f32[178,1152]{1,0:T(8,128)S(1)}, u32[]{:S(2)}, u32[]{:S(2)}) collective-permute-start(f32[178,1152]{1,0:T(8,128)S(1)} %convert_reduce_fusion), channel_id=1, source_target_pairs={{0,2},{2,0},{1,3},{3,1},{4,6},{6,4},{5,7},{7,5},{8,10},{10,8},{9,1... | collective-permute-start | bytes 2460680 | tf_op jit(solution)/shard_map/ppermute | solution.py:34
  (99 other events, 1173.7 us)

commit v8 on v7

--- a/solution.py
+++ b/solution.py
@@ -223,7 +223,8 @@
 def adjoint_kernel(
     step_ref, input_ref, mix_in_ref, mix_out_ref, grad_ref, rate_ref, start_ref, decay_ref, adjoint_ref,
     enter_ref, skip_ref,
-    pre_ref, conv_ref, decay_sum_ref, sums_ref, mix_ref, states_ref, decays_ref, in_grad_ref, out_grad_ref,
+    pre_out_ref, conv_ref, decay_sum_ref, sums_ref, mix_ref,
+    states_ref, decays_ref, in_grad_ref, out_grad_ref, pre_ref,
 ):
     steps, states, lanes = step_ref.shape[0], mix_in_ref.shape[1], step_ref.shape[2]
     row = sublane_rows(lanes)
@@ -298,7 +299,7 @@
         step, inputs, grad, in_sum = step_ref[at], input_ref[at], grad_ref[at], conv_ref[at]
         step_grad = pre_ref[at] * (1.0 / LOG2E) + in_sum * inputs
         pre = step_grad * (1.0 - jnp.exp2(step * -LOG2E))
-        pre_ref[at] = pre
+        pre_out_ref[at] = pre.astype(BF16)
         conv_ref[at] = in_sum * step + skip * grad
         return pre_sum + pre, skip_sum + grad * inputs
 
@@ -354,7 +355,9 @@
             pltpu.VMEM((steps, math.gcd(states, GROUP_C), SEGMENTS, lanes), F32),
             pltpu.VMEM((steps, states, SEGMENTS, LANES), F32),
             pltpu.VMEM((steps, states, SEGMENTS, LANES), F32),
+            pltpu.VMEM((steps, SEGMENTS, lanes), F32),
         ]
+        self.narrow_rows = jax.ShapeDtypeStruct((steps, chains, SEGMENTS, width), BF16)
         self.work = steps * chains * SEGMENTS * width * states
 
     def call(self, kernel, ops, args, in_specs, outs, out_specs, scratch=()):
@@ -403,7 +406,7 @@
             [self.rows_spec, self.rows_spec, self.mix_spec, self.mix_spec, self.rows_spec,
              self.rate_spec, self.state_spec, self.state_spec, self.state_spec, self.edge_spec,
              self.skip_spec],
-            [self.rows, self.rows, self.edge, self.sums, self.lane_sums],
+            [self.narrow_rows, self.rows, self.edge, self.sums, self.lane_sums],
             [self.rows_spec, self.rows_spec, self.edge_spec, self.sums_spec, self.lane_spec],
             self.scratch,
         )
@@ -964,8 +967,9 @@
     scanned = scan_out + skip_row[0] * xconv
     z_silu = jax.nn.silu(z_gate)
     gated_bf = (scanned * z_silu).astype(BF16).reshape(tokens, inner)
-    gated_bf, slot_cotan, far_up = together(gated_bf, slot_cotan, far_up)
-    middle = values + axis_sum(contract_cols(gated_bf, out_proj_t), "tp")
+    gated_bf, far_up = together(gated_bf, far_up)
+    mixer_part, slot_cotan = together(contract_cols(gated_bf, out_proj_t), slot_cotan)
+    middle = values + axis_sum(mixer_part, "tp")
 
     normed_two, inverse_two = rms_forward(middle, gain_two_f)
     normed_two_bf = normed_two.astype(BF16)
@@ -1051,8 +1055,8 @@
     decay_log_grad = jnp.sum(decay_sum, axis=0) * decay_rate
     dt_shift_grad, skip_grad = jnp.sum(scan_sums, axis=0)[:2]
     pre_grad = pre_grad.reshape(tokens, inner)
-    dt_proj_grad = contract_rows(dt_low.astype(F32), pre_grad, HIGHEST)
-    dt_low_grad = contract_cols(pre_grad, dt_proj.astype(F32), HIGHEST)
+    dt_proj_grad = contract_rows(dt_low, pre_grad)
+    dt_low_grad = contract_cols(pre_grad, dt_proj)
     mix_grad = mix_grad.reshape(tokens, LANES)[:, : 2 * states]
     proj_part = jnp.concatenate([dt_low_grad, mix_grad], axis=1)
     proj_grad_bf = axis_sum(proj_part, "tp").astype(BF16)

time: 836 us -> 826 us (0.988)
  matrix products: 125 us -> 116 us
  transfers between devices with their start and end apart: 33 -> 33, of which waited for: 19 -> 20; matrix products, arithmetic and copies ran while one was open for 27% -> 27% of each run, Pallas kernels for 21% -> 21%
where the time goes in v8:
time: 826 us; the launch traced here: 816 us
  Pallas kernels  267 us (32%)
  waiting for transfers between devices  185 us (22%)
  matrix products  116 us (14%)
  other arithmetic  104 us (13%)
  local copies, waits for them, and re-layouts  81 us (10%)
  starting transfers between devices  60.6 us (7%)
    pallas_call x4, Pallas kernels, call(): pl.pallas_call(kernel, grid=self.grid, in_specs=in_specs, out_specs=out_s...  134 us
    ppermute x21, waiting for transfers between devices, swapped(): return lax.ppermute(value, axis, [(0, 1), (1, 0)])  124 us
    pallas_call x1, Pallas kernels, gathered(): pl.pallas_call(partial(gather_kernel, count, parts), in_specs=[anywhere]...  72.2 us
    dot_general x12, matrix products, contract_rows(): lax.dot_general(left_side, right_side, (((0,), (0,)), ((), ())), precisio...  59.5 us
    pallas_call x2, Pallas kernels, expert_call(): pl.pallas_call(partial(expert_kernel, len(kept)), grid=(count // block,),...  47.5 us
    dot_general x6, matrix products, contract_cols(): lax.dot_general(left_side, right_side, (((1,), (1,)), ((), ())), precisio...  23.5 us
    all_to_all x4, waiting for transfers between devices, expert_exchange(): lax.all_to_all(value, 'dp', 0, 0, axis_index_groups=groups, tiled=True)  22.8 us
    all_to_all x4, starting transfers between devices, expert_exchange(): lax.all_to_all(value, 'dp', 0, 0, axis_index_groups=groups, tiled=True)  18.4 us
  transfers between devices with their start and end apart: 33, of which 20 were waited for; matrix products, arithmetic and copies ran while one was open for 27% of the time, Pallas kernels for 21%

profile of v8, /device:TPU:0, one launch (start us, length us, event | category | flops | bytes accessed | tf_op | source)
XLA Modules:
  0.0 816.4 jit_solution(1222006368366169625)
XLA Ops:
  11.5 72.2 %shard_map.297 = (bf16[8,144,1152]{2,1,0:T(8,128)(2,1)}, bf16[8,144,256]{2,1,0:T(8,128)(2,1)}, bf16[8,144,1152]{2,1,0:T(8,128)(2,1)}) custom-call(bf16[144,1152]{1,0:T(8,128)(2,1)} %bitcast.267, bf16[144,256]{1,0:T(8,128)(2,1)} %pad.62.refs_1_, bf16[144,1152]{1,0:T(8,128)(2,1)} %fusion.49.refs_2_), custom_call_target="tpu_custom_call" | custom-call | bytes 11796480 | tf_op jit(solution)/shard_map/pallas_call | solution.py:707
  130.7 19.5 %shard_map.298 = (f32[2,16,8,1152]{3,2,1,0:T(8,128)}, f32[2,16,8,1152]{3,2,1,0:T(8,128)}, f32[2,16,1152]{2,1,0:T(8,128)}) custom-call(f32[64,2,8,1152]{3,2,1,0:T(8,128)} %compare_select_fusion.step_ref, f32[64,2,8,1152]{3,2,1,0:T(8,128)} %get-tuple-element.239.input_ref, f32[2,64,16,8,128]{4,3,2,1,0:T(8,128)} %broadcast_in_dim.28.mix_in_ref, ...), custom_call_target="tpu_custom_call" | custom-call | flops 94371840 | bytes 209223 | tf_op jit(solution)/shard_map/pallas_call | solution.py:365
  174.4 9.8 %all-to-all-done.up_a.down_a = bf16[8,288,768]{2,1,0:T(8,128)(2,1)} async-done(((bf16[8,288,768]{2,1,0:T(8,128)(2,1)}), bf16[8,288,768]{2,1,0:T(8,128)(2,1)}, u32[]{:S(2)}, u32[]{:S(2)}) %all-to-all-start) | async-done | bytes 3538976 | tf_op jit(solution)/shard_map/all_to_all | solution.py:605
  184.2 6.0 broadcast_in_dim.30.mix_out_ref
  198.6 26.4 %shard_map.299 = (f32[64,2,8,1152]{3,2,1,0:T(8,128)}, f32[2,16,8,1152]{3,2,1,0:T(8,128)}) custom-call(f32[64,2,8,1152]{3,2,1,0:T(8,128)} %compare_select_fusion.step_ref, f32[64,2,8,1152]{3,2,1,0:T(8,128)} %get-tuple-element.239.input_ref, f32[2,64,16,8,128]{4,3,2,1,0:T(8,128)} %broadcast_in_dim.28.mix_in_ref, ...), custom_call_target="tpu_custom_call" | custom-call | flops 132120576 | bytes 352092 | tf_op jit(solution)/shard_map/pallas_call | solution.py:365
  225.0 7.8 multiply_convert_fusion.2
  237.6 7.0 fusion.45
  270.6 40.4 %collective-permute-done.6.down_b = bf16[8,144,768]{2,1,0:T(8,128)(2,1)} collective-permute-done((bf16[8,144,768]{2,1,0:T(8,128)(2,1)}, bf16[8,144,768]{2,1,0:T(8,128)(2,1)}, u32[]{:S(2)}, u32[]{:S(2)}) %collective-permute-start.6) | collective-permute-done | bytes 1769504 | tf_op jit(solution)/shard_map/ppermute | solution.py:34
  311.0 13.4 %all-to-all-done.2 = bf16[8,128,1152]{2,1,0:T(8,128)(2,1)} async-done(((bf16[8,128,1152]{2,1,0:T(8,128)(2,1)}), bf16[8,128,1152]{2,1,0:T(8,128)(2,1)}, u32[]{:S(2)}, u32[]{:S(2)}) %all-to-all-start.2) | async-done | bytes 2359328 | tf_op jit(solution)/shard_map/all_to_all | solution.py:588
  329.3 23.7 %shard_map.300 = (f32[1024,1152]{1,0:T(8,128)}, f32[1024,1152]{1,0:T(8,128)}, f32[1024,8]{1,0:T(8,128)}, bf16[2048,1152]{1,0:T(8,128)(2,1)}, bf16[2048,1152]{1,0...) custom-call(bf16[1024,1152]{1,0:T(8,128)(2,1)} %collective-permute-d, ...), custom_call_target="tpu_custom_call" | custom-call | flops 14495514624 | bytes 29884416 | tf_op jit(solution)/shard_map/pallas_call | solution.py:556
  353.6 23.8 %shard_map.301 = (f32[1024,1152]{1,0:T(8,128)}, f32[1024,1152]{1,0:T(8,128)}, f32[1024,8]{1,0:T(8,128)}, bf16[2048,1152]{1,0:T(8,128)(2,1)}, bf16[2048,1152]{1,0...) custom-call(bf16[1024,1152]{1,0:T(8,128)(2,1)} %bitcast.34.rows_ref,, ...), custom_call_target="tpu_custom_call", output_to_operand_aliasing={{3}: (8, {}), {4}: (9, {}), {5}: (10, {}), {6}: (11, {}), {... | custom-call | flops 14495514624 | bytes 29884416 | tf_op jit(solution)/shard_map/pallas_call | solution.py:556
  378.8 6.6 add_convert_fusion.6
  394.1 7.4 convolution_convert_fusion.3
  402.1 7.6 convolution_convert_fusion.4
  418.7 5.8 fusion.92
  424.5 17.7 %collective-permute-done.11 = bf16[1152,768]{1,0:T(8,128)(2,1)} collective-permute-done((bf16[1152,768]{1,0:T(8,128)(2,1)S(1)}, bf16[1152,768]{1,0:T(8,128)(2,1)}, u32[]{:S(2)}, u32[]{:S(2)}) %collective-permute-start.11) | collective-permute-done | bytes 1769504 | tf_op jit(solution)/shard_map/ppermute | solution.py:34
  442.3 6.1 all-to-all-done.3
  448.3 5.9 fusion.28
  469.6 7.4 fusion.44
  481.2 7.9 fusion.43
  489.1 19.4 %shard_map.302 = (f32[2,16,8,1152]{3,2,1,0:T(8,128)}, f32[2,16,8,1152]{3,2,1,0:T(8,128)}, f32[2,16,1152]{2,1,0:T(8,128)}) custom-call(f32[64,2,8,1152]{3,2,1,0:T(8,128)} %compare_select_fusion.step_ref, f32[2,64,16,8,128]{4,3,2,1,0:T(8,128)} %broadcast_in_dim.30.mix_out_ref, f32[64,2,8,1152]{3,2,1,0:T(8,128)} %get-tuple-element.241.grad_ref, ...), custom_call_target="tpu_custom_call" | custom-call | flops 94371840 | bytes 209223 | tf_op jit(solution)/shard_map/pallas_call | solution.py:365
  508.5 7.5 fusion.34
  527.9 6.1 all-to-all-start.5
  535.3 6.0 collective-permute-done.16.enter_ref
  542.0 68.9 %shard_map.303 = (bf16[64,2,8,1152]{3,2,1,0:T(8,128)(2,1)}, f32[64,2,8,1152]{3,2,1,0:T(8,128)}, f32[2,16,1152]{2,1,0:T(8,128)}, f32[2,8,1152]{2,1,0:T(8,128)}, f32[64,2,8,128]{3,2,1,0:T(8,128)}) custom-call(f32[64,2,8,1152]{3,2,1,0:T(8,128)} %compare_select_fusion.step_ref, f32[64,2,8,1152]{3,2,1,0:T(8,128)} %get-tuple-element.239.input_ref, ...), custom_call_target="tpu_custom_call" | custom-call | flops 377487360 | bytes 430371 | tf_op jit(solution)/shard_map/pallas_call | solution.py:365
  651.9 13.3 %shard_map.304 = (bf16[64,16,1152]{2,1,0:T(8,128)(2,1)}, f32[8,1152]{1,0:T(8,128)}, f32[3,16,1152]{2,1,0:T(8,128)}, f32[3,16,1152]{2,1,0:T(8,128)}) custom-call(bf16[1024,104]{1,0:T(8,128)(2,1)} %add_convert_fusion.7.proj_ref, bf16[104,1152]{1,0:T(8,128)(2,1)} %slice.207.weight_ref, f32[64,16,1152]{2,1,0:T(8,128)} %bitcast.228, ...), custom_call_target="tpu_custom_call" | custom-call | flops 1 | bytes 1 | tf_op jit(solution)/shard_map/pallas_call | solution.py:480
  677.2 5.8 all-to-all-done.6
  684.7 6.1 fusion.94
  720.7 14.2 %collective-permute-done.22 = f32[144,1152]{1,0:T(8,128)S(1)} collective-permute-done((f32[144,1152]{1,0:T(8,128)S(1)}, f32[144,1152]{1,0:T(8,128)S(1)}, u32[]{:S(2)}, u32[]{:S(2)}) %collective-permute-start.22) | collective-permute-done | bytes 663584 | tf_op jit(solution)/shard_map/ppermute | solution.py:34
  747.7 28.8 %collective-permute-done.23 = bf16[8,144,768]{2,1,0:T(8,128)(2,1)} collective-permute-done((bf16[8,144,768]{2,1,0:T(8,128)(2,1)}, bf16[8,144,768]{2,1,0:T(8,128)(2,1)}, u32[]{:S(2)}, u32[]{:S(2)}) %collective-permute-start.23) | collective-permute-done | bytes 1769504 | tf_op jit(solution)/shard_map/ppermute | solution.py:34
  776.5 9.6 %all-to-all-done.7 = bf16[8,178,1152]{2,1,0:T(8,128)(2,1)} async-done(((bf16[8,178,1152]{2,1,0:T(8,128)(2,1)}), bf16[8,178,1152]{2,1,0:T(8,128)(2,1)}, u32[]{:S(2)}, u32[]{:S(2)}) %all-to-all-start.7) | async-done | bytes 3280928 | tf_op jit(solution)/shard_map/all_to_all | solution.py:1120
  802.0 7.2 collective-permute-done.24
  (432 shorter events, 298.2 us)
Async XLA Ops:
  95.8 11.6 %collective-permute-start = (bf16[3,2,1,1152]{3,2,1,0:T(2,128)(2,1)S(1)}, bf16[3,2,1,1152]{3,2,1,0:T(2,128)(2,1)S(1)}, u32[]{:S(2)}, u32[]{:S(2)}) collective-permute-start(bf16[3,2,1,1152]{3,2,1,0:T(2,128)(2,1)S(1)} %slice.249), channel_id=1, source_target_pairs={{0,2},{1,3},{4,6},{5,7},{8,10},{9,11},{12,14},{13,15},{16,18},{17,... | collective-permute-start | bytes 41480 | tf_op jit(solution)/shard_map/ppermute | solution.py:40
  102.2 82.0 %all-to-all-start = ((bf16[8,288,768]{2,1,0:T(8,128)(2,1)}), bf16[8,288,768]{2,1,0:T(8,128)(2,1)}, u32[]{:S(2)}, u32[]{:S(2)}) async-start(bf16[8,288,768]{2,1,0:T(8,128)(2,1)} %slice_select_fusion), calls=%async_computation | async-start | bytes 7077888 | tf_op jit(solution)/shard_map/all_to_all | solution.py:605
  113.1 111.9 %collective-permute-start.3 = (bf16[1152,1152]{1,0:T(8,128)(2,1)}, bf16[1152,1152]{1,0:T(8,128)(2,1)}, u32[]{:S(2)}, u32[]{:S(2)}) collective-permute-start(bf16[1152,1152]{1,0:T(8,128)(2,1)} %bitcast.15), channel_id=1, source_target_pairs={{0,2},{2,0},{1,3},{3,1},{4,6},{6,4},{5,7},{7,5},{8,10},{10,8},{9,1... | collective-permute-start | bytes 7962632 | tf_op jit(solution)/shard_map/ppermute | solution.py:34
  160.2 14.2 %collective-permute-start.2 = (f32[2,16,1152]{2,1,0:T(8,128)}, f32[2,16,1152]{2,1,0:T(8,128)}, u32[]{:S(2)}, u32[]{:S(2)}) collective-permute-start(f32[2,16,1152]{2,1,0:T(8,128)} %get-tuple-element.108), channel_id=1, source_target_pairs={{0,2},{1,3},{4,6},{5,7},{8,10},{9,11},{12,14},{13,15},{16,18},{17,... | collective-permute-start | bytes 442376 | tf_op jit(solution)/shard_map/ppermute | solution.py:40
  190.1 57.8 %all-to-all-start.1 = ((bf16[8,128,1152]{2,1,0:T(8,128)(2,1)}), bf16[8,128,1152]{2,1,0:T(8,128)(2,1)}, u32[]{:S(2)}, u32[]{:S(2)}) async-start(bf16[8,128,1152]{2,1,0:T(8,128)(2,1)} %bitcast.256), calls=%async_computation.1 | async-start | bytes 4718592 | tf_op jit(solution)/shard_map/all_to_all | solution.py:588
  198.0 39.6 %collective-permute-start.4 = (bf16[8,144,768]{2,1,0:T(8,128)(2,1)S(1)}, bf16[8,144,768]{2,1,0:T(8,128)(2,1)}, u32[]{:S(2)}, u32[]{:S(2)}) collective-permute-start(bf16[8,144,768]{2,1,0:T(8,128)(2,1)S(1)} %get-tuple-element.255), channel_id=1, source_target_pairs={{0,2},{2,0},{1,3},{3,1},{4,6},{6,4},{5,7},{7,5},{8,10},{10,8},{9,1... | collective-permute-start | bytes 5308424 | tf_op jit(solution)/shard_map/ppermute | solution.py:34
  247.9 8.3 %collective-permute-start.5 = (f32[1024,1152]{1,0:T(8,128)}, f32[1024,1152]{1,0:T(8,128)}, u32[]{:S(2)}, u32[]{:S(2)}) collective-permute-start(f32[1024,1152]{1,0:T(8,128)} %fusion.45), channel_id=1, source_target_pairs={{0,1},{1,0},{2,3},{3,2},{4,5},{5,4},{6,7},{7,6},{8,9},{9,8},{10,11... | collective-permute-start | bytes 14155784 | tf_op jit(solution)/shard_map/ppermute | solution.py:34
  265.4 59.0 %all-to-all-start.2 = ((bf16[8,128,1152]{2,1,0:T(8,128)(2,1)}), bf16[8,128,1152]{2,1,0:T(8,128)(2,1)}, u32[]{:S(2)}, u32[]{:S(2)}) async-start(bf16[8,128,1152]{2,1,0:T(8,128)(2,1)} %bitcast.257), calls=%async_computation.2 | async-start | bytes 4718592 | tf_op jit(solution)/shard_map/all_to_all | solution.py:588
  270.0 41.0 %collective-permute-start.6 = (bf16[8,144,768]{2,1,0:T(8,128)(2,1)}, bf16[8,144,768]{2,1,0:T(8,128)(2,1)}, u32[]{:S(2)}, u32[]{:S(2)}) collective-permute-start(bf16[8,144,768]{2,1,0:T(8,128)(2,1)} %get-tuple-element.254), channel_id=1, source_target_pairs={{0,2},{2,0},{1,3},{3,1},{4,6},{6,4},{5,7},{7,5},{8,10},{10,8},{9,1... | collective-permute-start | bytes 5308424 | tf_op jit(solution)/shard_map/ppermute | solution.py:34
  270.6 54.9 %collective-permute-start.8 = (bf16[1024,1152]{1,0:T(8,128)(2,1)}, bf16[1024,1152]{1,0:T(8,128)(2,1)}, u32[]{:S(2)}, u32[]{:S(2)}) collective-permute-start(bf16[1024,1152]{1,0:T(8,128)(2,1)} %bitcast.35.cotan_ref), channel_id=1, source_target_pairs={{0,1},{1,0},{2,3},{3,2},{4,5},{5,4},{6,7},{7,6},{8,9},{9,8},{10,11... | collective-permute-start | bytes 7077896 | tf_op jit(solution)/shard_map/ppermute | solution.py:34
  324.4 4.9 collective-permute-start.7
  353.0 25.8 %collective-permute-start.10 = (f32[1024,1152]{1,0:T(8,128)}, f32[1024,1152]{1,0:T(8,128)}, u32[]{:S(2)}, u32[]{:S(2)}) collective-permute-start(f32[1024,1152]{1,0:T(8,128)} %get-tuple-element.137), channel_id=1, source_target_pairs={{0,1},{1,0},{2,3},{3,2},{4,5},{5,4},{6,7},{7,6},{8,9},{9,8},{10,11... | collective-permute-start | bytes 14155784 | tf_op jit(solution)/shard_map/ppermute | solution.py:34
  353.2 32.2 %collective-permute-start.9 = (f32[1024,1152]{1,0:T(8,128)}, f32[1024,1152]{1,0:T(8,128)S(1)}, u32[]{:S(2)}, u32[]{:S(2)}) collective-permute-start(f32[1024,1152]{1,0:T(8,128)} %get-tuple-element.135), channel_id=1, source_target_pairs={{0,1},{1,0},{2,3},{3,2},{4,5},{5,4},{6,7},{7,6},{8,9},{9,8},{10,11... | collective-permute-start | bytes 14155784 | tf_op jit(solution)/shard_map/ppermute | solution.py:34
  389.5 58.8 %all-to-all-start.3 = ((bf16[8,128,1152]{2,1,0:T(8,128)(2,1)}), bf16[8,128,1152]{2,1,0:T(8,128)(2,1)}, u32[]{:S(2)}, u32[]{:S(2)}) async-start(bf16[8,128,1152]{2,1,0:T(8,128)(2,1)} %bitcast.219), calls=%async_computation.3 | async-start | bytes 4718592 | tf_op jit(solution)/shard_map/all_to_all | solution.py:588
  401.5 40.8 %collective-permute-start.11 = (bf16[1152,768]{1,0:T(8,128)(2,1)S(1)}, bf16[1152,768]{1,0:T(8,128)(2,1)}, u32[]{:S(2)}, u32[]{:S(2)}) collective-permute-start(bf16[1152,768]{1,0:T(8,128)(2,1)S(1)} %convolution_convert_fusion.3), channel_id=1, source_target_pairs={{0,2},{2,0},{1,3},{3,1},{4,6},{6,4},{5,7},{7,5},{8,10},{10,8},{9,1... | collective-permute-start | bytes 5308424 | tf_op jit(solution)/shard_map/ppermute | solution.py:34
  418.6 5.9 collective-permute-start.12
  454.2 5.5 collective-permute-start.14
  454.2 66.8 %collective-permute-start.13 = (bf16[1152,768]{1,0:T(8,128)(2,1)}, bf16[1152,768]{1,0:T(8,128)(2,1)}, u32[]{:S(2)}, u32[]{:S(2)}) collective-permute-start(bf16[1152,768]{1,0:T(8,128)(2,1)} %convolution_convert_fusion.4), channel_id=1, source_target_pairs={{0,2},{2,0},{1,3},{3,1},{4,6},{6,4},{5,7},{7,5},{8,10},{10,8},{9,1... | collective-permute-start | bytes 5308424 | tf_op jit(solution)/shard_map/ppermute | solution.py:34
  454.8 66.2 %all-to-all-start.4 = ((bf16[8,128,1152]{2,1,0:T(8,128)(2,1)}), bf16[8,128,1152]{2,1,0:T(8,128)(2,1)}, u32[]{:S(2)}, u32[]{:S(2)}) async-start(bf16[8,128,1152]{2,1,0:T(8,128)(2,1)} %bitcast.222), calls=%async_computation.4 | async-start | bytes 4718592 | tf_op jit(solution)/shard_map/all_to_all | solution.py:588
  527.9 85.4 %all-to-all-start.5 = ((bf16[8,288,768]{2,1,0:T(8,128)(2,1)}), bf16[8,288,768]{2,1,0:T(8,128)(2,1)}, u32[]{:S(2)}, u32[]{:S(2)}) async-start(bf16[8,288,768]{2,1,0:T(8,128)(2,1)} %pad_maximum_fusion), calls=%async_computation.5 | async-start | bytes 7077888 | tf_op jit(solution)/shard_map/all_to_all | solution.py:1040
  534.0 7.3 collective-permute-start.16
  541.3 69.5 %collective-permute-start.17 = (bf16[1152,1152]{1,0:T(8,128)(2,1)}, bf16[1152,1152]{1,0:T(8,128)(2,1)}, u32[]{:S(2)}, u32[]{:S(2)}) collective-permute-start(bf16[1152,1152]{1,0:T(8,128)(2,1)} %convolution_convert_fusion.1), channel_id=1, source_target_pairs={{0,2},{2,0},{1,3},{3,1},{4,6},{6,4},{5,7},{7,5},{8,10},{10,8},{9,1... | collective-permute-start | bytes 7962632 | tf_op jit(solution)/shard_map/ppermute | solution.py:34
  618.7 64.3 %all-to-all-start.6 = ((bf16[8,144,1152]{2,1,0:T(8,128)(2,1)}), bf16[8,144,1152]{2,1,0:T(8,128)(2,1)}, u32[]{:S(2)}, u32[]{:S(2)}) async-start(bf16[8,144,1152]{2,1,0:T(8,128)(2,1)} %bitcast.213), calls=%async_computation.6 | async-start | bytes 5308416 | tf_op jit(solution)/shard_map/all_to_all | solution.py:1054
  636.5 40.7 %collective-permute-start.20 = (bf16[8,144,768]{2,1,0:T(8,128)(2,1)}, bf16[8,144,768]{2,1,0:T(8,128)(2,1)}, u32[]{:S(2)}, u32[]{:S(2)}) collective-permute-start(bf16[8,144,768]{2,1,0:T(8,128)(2,1)} %get-tuple-element.253), channel_id=1, source_target_pairs={{0,2},{2,0},{1,3},{3,1},{4,6},{6,4},{5,7},{7,5},{8,10},{10,8},{9,1... | collective-permute-start | bytes 5308424 | tf_op jit(solution)/shard_map/ppermute | solution.py:34
  640.4 9.2 %collective-permute-start.18 = (f32[1024,104]{1,0:T(8,128)}, f32[1024,104]{1,0:T(8,128)}, u32[]{:S(2)}, u32[]{:S(2)}) collective-permute-start(f32[1024,104]{1,0:T(8,128)} %pad_maximum_fusion.4), channel_id=1, source_target_pairs={{0,1},{1,0},{2,3},{3,2},{4,5},{5,4},{6,7},{7,6},{8,9},{9,8},{10,11... | collective-permute-start | bytes 1277960 | tf_op jit(solution)/shard_map/ppermute | solution.py:34
  666.2 11.0 %collective-permute-start.19 = (f32[3,2,1,1152]{3,2,1,0:T(1,128)S(1)}, f32[3,2,1,1152]{3,2,1,0:T(1,128)S(1)}, u32[]{:S(2)}, u32[]{:S(2)}) collective-permute-start(f32[3,2,1,1152]{3,2,1,0:T(1,128)S(1)} %slice.265), channel_id=1, source_target_pairs={{2,0},{3,1},{6,4},{7,5},{10,8},{11,9},{14,12},{15,13},{18,16},{19,... | collective-permute-start | bytes 82952 | tf_op jit(solution)/shard_map/ppermute | solution.py:40
  691.4 8.0 collective-permute-start.21
  704.6 81.4 %all-to-all-start.7 = ((bf16[8,178,1152]{2,1,0:T(8,128)(2,1)}), bf16[8,178,1152]{2,1,0:T(8,128)(2,1)}, u32[]{:S(2)}, u32[]{:S(2)}) async-start(bf16[8,178,1152]{2,1,0:T(8,128)(2,1)} %pad_maximum_fusion.1), calls=%async_computation.7 | async-start | bytes 6782976 | tf_op jit(solution)/shard_map/all_to_all | solution.py:1120
  714.6 23.1 %collective-permute-start.15 = (bf16[1024,1152]{1,0:T(8,128)(2,1)S(1)}, bf16[1024,1152]{1,0:T(8,128)(2,1)}, u32[]{:S(2)}, u32[]{:S(2)}) collective-permute-start(bf16[1024,1152]{1,0:T(8,128)(2,1)S(1)} %fusion.29), channel_id=1, source_target_pairs={{0,1},{1,0},{2,3},{3,2},{4,5},{5,4},{6,7},{7,6},{8,9},{9,8},{10,11... | collective-permute-start | bytes 7077896 | tf_op jit(solution)/shard_map/ppermute | solution.py:34
  717.5 17.4 %collective-permute-start.22 = (f32[144,1152]{1,0:T(8,128)S(1)}, f32[144,1152]{1,0:T(8,128)S(1)}, u32[]{:S(2)}, u32[]{:S(2)}) collective-permute-start(f32[144,1152]{1,0:T(8,128)S(1)} %convert_reduce_fusion.1), channel_id=1, source_target_pairs={{0,2},{2,0},{1,3},{3,1},{4,6},{6,4},{5,7},{7,5},{8,10},{10,8},{9,1... | collective-permute-start | bytes 1990664 | tf_op jit(solution)/shard_map/ppermute | solution.py:34
  735.9 40.6 %collective-permute-start.23 = (bf16[8,144,768]{2,1,0:T(8,128)(2,1)}, bf16[8,144,768]{2,1,0:T(8,128)(2,1)}, u32[]{:S(2)}, u32[]{:S(2)}) collective-permute-start(bf16[8,144,768]{2,1,0:T(8,128)(2,1)} %get-tuple-element.182), channel_id=1, source_target_pairs={{0,2},{2,0},{1,3},{3,1},{4,6},{6,4},{5,7},{7,5},{8,10},{10,8},{9,1... | collective-permute-start | bytes 5308424 | tf_op jit(solution)/shard_map/ppermute | solution.py:34
  788.6 20.5 %collective-permute-start.24 = (f32[178,1152]{1,0:T(8,128)S(1)}, f32[178,1152]{1,0:T(8,128)S(1)}, u32[]{:S(2)}, u32[]{:S(2)}) collective-permute-start(f32[178,1152]{1,0:T(8,128)S(1)} %convert_reduce_fusion), channel_id=1, source_target_pairs={{0,2},{2,0},{1,3},{3,1},{4,6},{6,4},{5,7},{7,5},{8,10},{10,8},{9,1... | collective-permute-start | bytes 2460680 | tf_op jit(solution)/shard_map/ppermute | solution.py:34
  (106 other events, 1256.7 us)

commit v9 on v8

--- a/solution.py
+++ b/solution.py
@@ -48,6 +48,12 @@
 
 def together(*values):
     return lax.optimization_barrier(values)
+
+
+def narrow_sum(value, axis):
+    if lax.axis_size(axis) == 2:
+        return value.astype(F32) + swapped(value, axis).astype(F32)
+    return lax.psum(value.astype(F32), axis)
 
 
 def entering_pieces(decay, value, axis, backward):
@@ -613,14 +619,16 @@
     return both[:, :rows, half:], both[:, rows:, half:]
 
 
-def gather_kernel(count, parts, *refs):
-    ins, outs = refs[:parts], refs[parts : 2 * parts]
-    send_sem, recv_sem, own_sem = refs[2 * parts :]
+def gather_kernel(count, number, parts, *refs):
+    ins, outs = refs[:number], refs[number : 2 * number]
+    send_sem, recv_sem, own_sem = refs[2 * number :]
     places = count // 2
     me = lax.axis_index("dp")
     place, side = lax.div(me, 2), lax.rem(me, 2)
     across = me + 1 - 2 * side
     barrier = pltpu.get_barrier_semaphore()
+    late = [part for part, (_, _, _, early) in enumerate(parts) if not early]
+    early = [part for part, (_, _, _, early) in enumerate(parts) if early]
 
     def greet(device):
         pl.semaphore_signal(
@@ -639,26 +647,33 @@
     pl.semaphore_wait(barrier, neighbours)
 
     def copy(part, slot, kind, device, own):
+        array, low, rows, _ = parts[part]
+        landing = outs[array].at[slot, pl.ds(low, rows)]
         return pltpu.make_async_remote_copy(
-            src_ref=ins[part] if own else outs[part].at[slot],
-            dst_ref=outs[part].at[slot],
+            src_ref=ins[array].at[pl.ds(low, rows)] if own else landing,
+            dst_ref=landing,
             send_sem=send_sem.at[kind, part, slot],
             recv_sem=recv_sem.at[part, slot],
             device_id={"dp": device},
             device_id_type=pl.DeviceIdType.MESH,
         )
 
-    def passed_on(slot, steps, own, act):
+    def along(which, slot, steps, own, act):
         for step in steps:
             there = place + step
 
             @pl.when((there >= 0) & (there < places))
-            def along(step=step):
-                for part in range(parts):
+            def one_way(step=step):
+                for part in which:
                     act(copy(part, slot, step + 1, me + 2 * step, own))
 
-        for part in range(parts):
+    def aside(which, slot, own, act):
+        for part in which:
             act(copy(part, slot, 1, across, own))
+
+    def arrived(which, slot):
+        for part in which:
+            copy(part, slot, 1, across, False).wait_recv()
 
     def start(one):
         one.start()
@@ -667,52 +682,76 @@
         one.wait_send()
 
     mine = [
-        pltpu.make_async_copy(ins[part], outs[part].at[me], own_sem.at[part])
-        for part in range(parts)
+        pltpu.make_async_copy(ins[array], outs[array].at[me], own_sem.at[array])
+        for array in range(number)
     ]
     for one in mine:
         one.start()
-    passed_on(me, (-1, 1), True, start)
+    both = (-1, 1)
+    aside(early, me, True, start)
+    for part in late:
+        along((part,), me, both, True, start)
+        aside((part,), me, True, start)
+    along(early, me, both, True, start)
+    arrived(early, across)
+    along(early, across, both, False, start)
     for far in range(1, places):
-        for step in (-1, 1):
+        for step in both:
             origin = place - step * far
 
             @pl.when((origin >= 0) & (origin < places))
             def forward(step=step, far=far):
-                slot = me - 2 * step * far
-                for part in range(parts):
-                    copy(part, slot, 1, across, False).wait_recv()
-                passed_on(slot, (step,), False, start)
+                slot, other = me - 2 * step * far, across - 2 * step * far
+                for part in late:
+                    arrived((part,), slot)
+                    along((part,), slot, (step,), False, start)
+                    aside((part,), slot, False, start)
+                arrived(early, slot)
+                along(early, slot, (step,), False, start)
+                arrived(early, other)
+                along(early, other, (step,), False, start)
 
     for at in range(places):
-        for part in range(parts):
-            copy(part, 2 * at + 1 - side, 1, across, False).wait_recv()
+        arrived(late, 2 * at + 1 - side)
     for one in mine:
         one.wait()
-    passed_on(me, (-1, 1), True, sent)
+    aside(early + late, me, True, sent)
+    along(early + late, me, both, True, sent)
+    along(early, across, both, False, sent)
     for far in range(1, places):
-        for step in (-1, 1):
+        for step in both:
             origin = place - step * far
 
             @pl.when((origin >= 0) & (origin < places))
             def forwarded(step=step, far=far):
-                passed_on(me - 2 * step * far, (step,), False, sent)
+                slot, other = me - 2 * step * far, across - 2 * step * far
+                aside(late, slot, False, sent)
+                along(early + late, slot, (step,), False, sent)
+                along(early, other, (step,), False, sent)
 
 
 def gathered(*values):
     count = lax.axis_size("dp")
-    parts = len(values)
+    number = len(values)
+    parts = []
+    for at, value in enumerate(values):
+        rows = value.shape[0]
+        step = rows // 3 if value.shape[1] > 1024 and rows % 24 == 0 else rows
+        parts += [
+            (at, low, step, at == number - 1 and 0 < low == rows - step)
+            for low in range(0, rows, step)
+        ]
     anywhere = pl.BlockSpec(memory_space=pl.ANY)
     size = sum(math.prod(value.shape) * 2 for value in values)
     return pl.pallas_call(
-        partial(gather_kernel, count, parts),
-        in_specs=[anywhere] * parts,
-        out_specs=[anywhere] * parts,
+        partial(gather_kernel, count, number, parts),
+        in_specs=[anywhere] * number,
+        out_specs=[anywhere] * number,
         out_shape=[jax.ShapeDtypeStruct((count, *value.shape), value.dtype) for value in values],
         scratch_shapes=[
-            pltpu.SemaphoreType.DMA((3, parts, count)),
-            pltpu.SemaphoreType.DMA((parts, count)),
-            pltpu.SemaphoreType.DMA((parts,)),
+            pltpu.SemaphoreType.DMA((3, len(parts), count)),
+            pltpu.SemaphoreType.DMA((len(parts), count)),
+            pltpu.SemaphoreType.DMA((number,)),
         ],
         compiler_params=pltpu.CompilerParams(collective_id=0, has_side_effects=True),
         cost_estimate=pl.CostEstimate(
@@ -1129,7 +1168,8 @@
     router_prob = jax.nn.softmax(contract_cols(normed_two_bf, router_t), axis=-1)
     gate_prob = jnp.sum(router_prob * onehot_int.astype(F32), axis=1) * keep
     result = from_rows((middle + gate_prob[:, None] * landed(halves_of(got_out))).astype(BF16))
-    in_x_sums = axis_sum(jnp.sum(in_x_blocks.astype(F32), axis=0), "ctx")
+    in_x_sums = jnp.sum(in_x_blocks.astype(F32), axis=0).astype(BF16)
+    in_x_sums = narrow_sum(in_x_sums, "ctx")
     in_x_grad = in_x_sums[:shard]
     gain_one_grad = in_x_sums[shard : shard + 1, :shard] + in_x_sums[shard + 1 : shard + 2, :shard]
     small_grads = in_x_sums[shard + 8 :].reshape(-1)[:small_size].reshape(-1, shard)

time: 826 us -> 811 us (0.982)
    pallas_call x1, Pallas kernels: 72.2 us -> 63.5 us  [gathered(): pl.pallas_call(partial(gather_kernel, count, number, parts), in_specs=[an...]
  transfers between devices with their start and end apart: 33 -> 33, of which waited for: 20 -> 19; matrix products, arithmetic and copies ran while one was open for 27% -> 27% of each run, Pallas kernels for 21% -> 21%
where the time goes in v9:
time: 811 us; the launch traced here: 802 us
  Pallas kernels  259 us (32%)
  waiting for transfers between devices  180 us (22%)
  matrix products  116 us (14%)
  other arithmetic  104 us (13%)
  local copies, waits for them, and re-layouts  81 us (10%)
  starting transfers between devices  60.4 us (7%)
    pallas_call x4, Pallas kernels, call(): pl.pallas_call(kernel, grid=self.grid, in_specs=in_specs, out_specs=out_s...  134 us
    ppermute x21, waiting for transfers between devices, swapped(): return lax.ppermute(value, axis, [(0, 1), (1, 0)])  119 us
    pallas_call x1, Pallas kernels, gathered(): pl.pallas_call(partial(gather_kernel, count, number, parts), in_specs=[an...  63.5 us
    dot_general x12, matrix products, contract_rows(): lax.dot_general(left_side, right_side, (((0,), (0,)), ((), ())), precisio...  59.5 us
    pallas_call x2, Pallas kernels, expert_call(): pl.pallas_call(partial(expert_kernel, len(kept)), grid=(count // block,),...  47.5 us
    dot_general x6, matrix products, contract_cols(): lax.dot_general(left_side, right_side, (((1,), (1,)), ((), ())), precisio...  23.5 us
    all_to_all x4, waiting for transfers between devices, expert_exchange(): lax.all_to_all(value, 'dp', 0, 0, axis_index_groups=groups, tiled=True)  22.8 us
    all_to_all x4, starting transfers between devices, expert_exchange(): lax.all_to_all(value, 'dp', 0, 0, axis_index_groups=groups, tiled=True)  18.4 us
  transfers between devices with their start and end apart: 33, of which 19 were waited for; matrix products, arithmetic and copies ran while one was open for 27% of the time, Pallas kernels for 21%

profile of v9, /device:TPU:0, one launch (start us, length us, event | category | flops | bytes accessed | tf_op | source)
XLA Modules:
  0.0 801.9 jit_solution(17737293470752231510)
XLA Ops:
  11.5 63.5 %shard_map.297 = (bf16[8,144,1152]{2,1,0:T(8,128)(2,1)}, bf16[8,144,256]{2,1,0:T(8,128)(2,1)}, bf16[8,144,1152]{2,1,0:T(8,128)(2,1)}) custom-call(bf16[144,1152]{1,0:T(8,128)(2,1)} %bitcast.267, bf16[144,256]{1,0:T(8,128)(2,1)} %pad.62.refs_1_, bf16[144,1152]{1,0:T(8,128)(2,1)} %fusion.49.refs_2_), custom_call_target="tpu_custom_call" | custom-call | bytes 11796480 | tf_op jit(solution)/shard_map/pallas_call | solution.py:746
  123.0 19.5 %shard_map.298 = (f32[2,16,8,1152]{3,2,1,0:T(8,128)}, f32[2,16,8,1152]{3,2,1,0:T(8,128)}, f32[2,16,1152]{2,1,0:T(8,128)}) custom-call(f32[64,2,8,1152]{3,2,1,0:T(8,128)} %compare_select_fusion.step_ref, f32[64,2,8,1152]{3,2,1,0:T(8,128)} %get-tuple-element.239.input_ref, f32[2,64,16,8,128]{4,3,2,1,0:T(8,128)} %broadcast_in_dim.28.mix_in_ref, ...), custom_call_target="tpu_custom_call" | custom-call | flops 94371840 | bytes 209223 | tf_op jit(solution)/shard_map/pallas_call | solution.py:371
  166.6 10.2 %all-to-all-done.up_a.down_a = bf16[8,288,768]{2,1,0:T(8,128)(2,1)} async-done(((bf16[8,288,768]{2,1,0:T(8,128)(2,1)}), bf16[8,288,768]{2,1,0:T(8,128)(2,1)}, u32[]{:S(2)}, u32[]{:S(2)}) %all-to-all-start) | async-done | bytes 3538976 | tf_op jit(solution)/shard_map/all_to_all | solution.py:611
  176.8 6.0 broadcast_in_dim.30.mix_out_ref
  190.8 26.4 %shard_map.299 = (f32[64,2,8,1152]{3,2,1,0:T(8,128)}, f32[2,16,8,1152]{3,2,1,0:T(8,128)}) custom-call(f32[64,2,8,1152]{3,2,1,0:T(8,128)} %compare_select_fusion.step_ref, f32[64,2,8,1152]{3,2,1,0:T(8,128)} %get-tuple-element.239.input_ref, f32[2,64,16,8,128]{4,3,2,1,0:T(8,128)} %broadcast_in_dim.28.mix_in_ref, ...), custom_call_target="tpu_custom_call" | custom-call | flops 132120576 | bytes 352092 | tf_op jit(solution)/shard_map/pallas_call | solution.py:371
  217.2 7.8 multiply_convert_fusion.2
  230.2 7.0 fusion.45
  262.9 40.7 %collective-permute-done.6.down_b = bf16[8,144,768]{2,1,0:T(8,128)(2,1)} collective-permute-done((bf16[8,144,768]{2,1,0:T(8,128)(2,1)}, bf16[8,144,768]{2,1,0:T(8,128)(2,1)}, u32[]{:S(2)}, u32[]{:S(2)}) %collective-permute-start.6) | collective-permute-done | bytes 1769504 | tf_op jit(solution)/shard_map/ppermute | solution.py:34
  303.6 13.4 %all-to-all-done.2 = bf16[8,128,1152]{2,1,0:T(8,128)(2,1)} async-done(((bf16[8,128,1152]{2,1,0:T(8,128)(2,1)}), bf16[8,128,1152]{2,1,0:T(8,128)(2,1)}, u32[]{:S(2)}, u32[]{:S(2)}) %all-to-all-start.2) | async-done | bytes 2359328 | tf_op jit(solution)/shard_map/all_to_all | solution.py:594
  321.9 23.7 %shard_map.300 = (f32[1024,1152]{1,0:T(8,128)}, f32[1024,1152]{1,0:T(8,128)}, f32[1024,8]{1,0:T(8,128)}, bf16[2048,1152]{1,0:T(8,128)(2,1)}, bf16[2048,1152]{1,0...) custom-call(bf16[1024,1152]{1,0:T(8,128)(2,1)} %collective-permute-d, ...), custom_call_target="tpu_custom_call" | custom-call | flops 14495514624 | bytes 29884416 | tf_op jit(solution)/shard_map/pallas_call | solution.py:562
  346.2 23.8 %shard_map.301 = (f32[1024,1152]{1,0:T(8,128)}, f32[1024,1152]{1,0:T(8,128)}, f32[1024,8]{1,0:T(8,128)}, bf16[2048,1152]{1,0:T(8,128)(2,1)}, bf16[2048,1152]{1,0...) custom-call(bf16[1024,1152]{1,0:T(8,128)(2,1)} %bitcast.34.rows_ref,, ...), custom_call_target="tpu_custom_call", output_to_operand_aliasing={{3}: (8, {}), {4}: (9, {}), {5}: (10, {}), {6}: (11, {}), {... | custom-call | flops 14495514624 | bytes 29884416 | tf_op jit(solution)/shard_map/pallas_call | solution.py:562
  371.4 6.6 add_convert_fusion.6
  386.7 7.4 convolution_convert_fusion.3
  394.3 7.6 convolution_convert_fusion.4
  402.0 5.7 fusion.93
  410.9 5.8 fusion.92
  416.7 18.2 %collective-permute-done.11 = bf16[1152,768]{1,0:T(8,128)(2,1)} collective-permute-done((bf16[1152,768]{1,0:T(8,128)(2,1)S(1)}, bf16[1152,768]{1,0:T(8,128)(2,1)}, u32[]{:S(2)}, u32[]{:S(2)}) %collective-permute-start.11) | collective-permute-done | bytes 1769504 | tf_op jit(solution)/shard_map/ppermute | solution.py:34
  434.9 6.1 all-to-all-done.3
  441.0 5.9 fusion.28
  461.7 7.4 fusion.44
  473.3 7.9 fusion.43
  481.3 19.4 %shard_map.302 = (f32[2,16,8,1152]{3,2,1,0:T(8,128)}, f32[2,16,8,1152]{3,2,1,0:T(8,128)}, f32[2,16,1152]{2,1,0:T(8,128)}) custom-call(f32[64,2,8,1152]{3,2,1,0:T(8,128)} %compare_select_fusion.step_ref, f32[2,64,16,8,128]{4,3,2,1,0:T(8,128)} %broadcast_in_dim.30.mix_out_ref, f32[64,2,8,1152]{3,2,1,0:T(8,128)} %get-tuple-element.241.grad_ref, ...), custom_call_target="tpu_custom_call" | custom-call | flops 94371840 | bytes 209223 | tf_op jit(solution)/shard_map/pallas_call | solution.py:371
  500.7 7.5 fusion.34
  520.1 6.1 all-to-all-start.5
  527.5 6.2 collective-permute-done.16.enter_ref
  534.4 68.9 %shard_map.303 = (bf16[64,2,8,1152]{3,2,1,0:T(8,128)(2,1)}, f32[64,2,8,1152]{3,2,1,0:T(8,128)}, f32[2,16,1152]{2,1,0:T(8,128)}, f32[2,8,1152]{2,1,0:T(8,128)}, f32[64,2,8,128]{3,2,1,0:T(8,128)}) custom-call(f32[64,2,8,1152]{3,2,1,0:T(8,128)} %compare_select_fusion.step_ref, f32[64,2,8,1152]{3,2,1,0:T(8,128)} %get-tuple-element.239.input_ref, ...), custom_call_target="tpu_custom_call" | custom-call | flops 377487360 | bytes 430371 | tf_op jit(solution)/shard_map/pallas_call | solution.py:371
  644.6 13.3 %shard_map.304 = (bf16[64,16,1152]{2,1,0:T(8,128)(2,1)}, f32[8,1152]{1,0:T(8,128)}, f32[3,16,1152]{2,1,0:T(8,128)}, f32[3,16,1152]{2,1,0:T(8,128)}) custom-call(bf16[1024,104]{1,0:T(8,128)(2,1)} %add_convert_fusion.7.proj_ref, bf16[104,1152]{1,0:T(8,128)(2,1)} %slice.207.weight_ref, f32[64,16,1152]{2,1,0:T(8,128)} %bitcast.228, ...), custom_call_target="tpu_custom_call" | custom-call | flops 1 | bytes 1 | tf_op jit(solution)/shard_map/pallas_call | solution.py:486
  669.9 5.5 all-to-all-done.6
  677.0 6.1 fusion.94
  713.3 14.2 %collective-permute-done.22 = f32[144,1152]{1,0:T(8,128)S(1)} collective-permute-done((f32[144,1152]{1,0:T(8,128)S(1)}, f32[144,1152]{1,0:T(8,128)S(1)}, u32[]{:S(2)}, u32[]{:S(2)}) %collective-permute-start.22) | collective-permute-done | bytes 663584 | tf_op jit(solution)/shard_map/ppermute | solution.py:34
  740.3 28.8 %collective-permute-done.23 = bf16[8,144,768]{2,1,0:T(8,128)(2,1)} collective-permute-done((bf16[8,144,768]{2,1,0:T(8,128)(2,1)}, bf16[8,144,768]{2,1,0:T(8,128)(2,1)}, u32[]{:S(2)}, u32[]{:S(2)}) %collective-permute-start.23) | collective-permute-done | bytes 1769504 | tf_op jit(solution)/shard_map/ppermute | solution.py:34
  769.1 9.3 %all-to-all-done.7 = bf16[8,178,1152]{2,1,0:T(8,128)(2,1)} async-done(((bf16[8,178,1152]{2,1,0:T(8,128)(2,1)}), bf16[8,178,1152]{2,1,0:T(8,128)(2,1)}, u32[]{:S(2)}, u32[]{:S(2)}) %all-to-all-start.7) | async-done | bytes 3280928 | tf_op jit(solution)/shard_map/all_to_all | solution.py:1159
  (432 shorter events, 292.9 us)
Async XLA Ops:
  87.1 12.5 %collective-permute-start = (bf16[3,2,1,1152]{3,2,1,0:T(2,128)(2,1)S(1)}, bf16[3,2,1,1152]{3,2,1,0:T(2,128)(2,1)S(1)}, u32[]{:S(2)}, u32[]{:S(2)}) collective-permute-start(bf16[3,2,1,1152]{3,2,1,0:T(2,128)(2,1)S(1)} %slice.249), channel_id=1, source_target_pairs={{0,2},{1,3},{4,6},{5,7},{8,10},{9,11},{12,14},{13,15},{16,18},{17,... | collective-permute-start | bytes 41480 | tf_op jit(solution)/shard_map/ppermute | solution.py:40
  94.0 82.8 %all-to-all-start = ((bf16[8,288,768]{2,1,0:T(8,128)(2,1)}), bf16[8,288,768]{2,1,0:T(8,128)(2,1)}, u32[]{:S(2)}, u32[]{:S(2)}) async-start(bf16[8,288,768]{2,1,0:T(8,128)(2,1)} %slice_select_fusion), calls=%async_computation | async-start | bytes 7077888 | tf_op jit(solution)/shard_map/all_to_all | solution.py:611
  105.3 111.9 %collective-permute-start.3 = (bf16[1152,1152]{1,0:T(8,128)(2,1)}, bf16[1152,1152]{1,0:T(8,128)(2,1)}, u32[]{:S(2)}, u32[]{:S(2)}) collective-permute-start(bf16[1152,1152]{1,0:T(8,128)(2,1)} %bitcast.15), channel_id=1, source_target_pairs={{0,2},{2,0},{1,3},{3,1},{4,6},{6,4},{5,7},{7,5},{8,10},{10,8},{9,1... | collective-permute-start | bytes 7962632 | tf_op jit(solution)/shard_map/ppermute | solution.py:34
  152.4 14.2 %collective-permute-start.2 = (f32[2,16,1152]{2,1,0:T(8,128)}, f32[2,16,1152]{2,1,0:T(8,128)}, u32[]{:S(2)}, u32[]{:S(2)}) collective-permute-start(f32[2,16,1152]{2,1,0:T(8,128)} %get-tuple-element.108), channel_id=1, source_target_pairs={{0,2},{1,3},{4,6},{5,7},{8,10},{9,11},{12,14},{13,15},{16,18},{17,... | collective-permute-start | bytes 442376 | tf_op jit(solution)/shard_map/ppermute | solution.py:40
  182.8 57.8 %all-to-all-start.1 = ((bf16[8,128,1152]{2,1,0:T(8,128)(2,1)}), bf16[8,128,1152]{2,1,0:T(8,128)(2,1)}, u32[]{:S(2)}, u32[]{:S(2)}) async-start(bf16[8,128,1152]{2,1,0:T(8,128)(2,1)} %bitcast.256), calls=%async_computation.1 | async-start | bytes 4718592 | tf_op jit(solution)/shard_map/all_to_all | solution.py:594
  190.6 39.6 %collective-permute-start.4 = (bf16[8,144,768]{2,1,0:T(8,128)(2,1)S(1)}, bf16[8,144,768]{2,1,0:T(8,128)(2,1)}, u32[]{:S(2)}, u32[]{:S(2)}) collective-permute-start(bf16[8,144,768]{2,1,0:T(8,128)(2,1)S(1)} %get-tuple-element.255), channel_id=1, source_target_pairs={{0,2},{2,0},{1,3},{3,1},{4,6},{6,4},{5,7},{7,5},{8,10},{10,8},{9,1... | collective-permute-start | bytes 5308424 | tf_op jit(solution)/shard_map/ppermute | solution.py:34
  240.5 8.3 %collective-permute-start.5 = (f32[1024,1152]{1,0:T(8,128)}, f32[1024,1152]{1,0:T(8,128)}, u32[]{:S(2)}, u32[]{:S(2)}) collective-permute-start(f32[1024,1152]{1,0:T(8,128)} %fusion.45), channel_id=1, source_target_pairs={{0,1},{1,0},{2,3},{3,2},{4,5},{5,4},{6,7},{7,6},{8,9},{9,8},{10,11... | collective-permute-start | bytes 14155784 | tf_op jit(solution)/shard_map/ppermute | solution.py:34
  258.0 59.0 %all-to-all-start.2 = ((bf16[8,128,1152]{2,1,0:T(8,128)(2,1)}), bf16[8,128,1152]{2,1,0:T(8,128)(2,1)}, u32[]{:S(2)}, u32[]{:S(2)}) async-start(bf16[8,128,1152]{2,1,0:T(8,128)(2,1)} %bitcast.257), calls=%async_computation.2 | async-start | bytes 4718592 | tf_op jit(solution)/shard_map/all_to_all | solution.py:594
  262.6 41.0 %collective-permute-start.6 = (bf16[8,144,768]{2,1,0:T(8,128)(2,1)}, bf16[8,144,768]{2,1,0:T(8,128)(2,1)}, u32[]{:S(2)}, u32[]{:S(2)}) collective-permute-start(bf16[8,144,768]{2,1,0:T(8,128)(2,1)} %get-tuple-element.254), channel_id=1, source_target_pairs={{0,2},{2,0},{1,3},{3,1},{4,6},{6,4},{5,7},{7,5},{8,10},{10,8},{9,1... | collective-permute-start | bytes 5308424 | tf_op jit(solution)/shard_map/ppermute | solution.py:34
  262.8 55.4 %collective-permute-start.8 = (bf16[1024,1152]{1,0:T(8,128)(2,1)}, bf16[1024,1152]{1,0:T(8,128)(2,1)}, u32[]{:S(2)}, u32[]{:S(2)}) collective-permute-start(bf16[1024,1152]{1,0:T(8,128)(2,1)} %bitcast.35.cotan_ref), channel_id=1, source_target_pairs={{0,1},{1,0},{2,3},{3,2},{4,5},{5,4},{6,7},{7,6},{8,9},{9,8},{10,11... | collective-permute-start | bytes 7077896 | tf_op jit(solution)/shard_map/ppermute | solution.py:34
  317.0 4.9 collective-permute-start.7
  345.6 25.8 %collective-permute-start.10 = (f32[1024,1152]{1,0:T(8,128)}, f32[1024,1152]{1,0:T(8,128)}, u32[]{:S(2)}, u32[]{:S(2)}) collective-permute-start(f32[1024,1152]{1,0:T(8,128)} %get-tuple-element.137), channel_id=1, source_target_pairs={{0,1},{1,0},{2,3},{3,2},{4,5},{5,4},{6,7},{7,6},{8,9},{9,8},{10,11... | collective-permute-start | bytes 14155784 | tf_op jit(solution)/shard_map/ppermute | solution.py:34
  345.8 32.2 %collective-permute-start.9 = (f32[1024,1152]{1,0:T(8,128)}, f32[1024,1152]{1,0:T(8,128)S(1)}, u32[]{:S(2)}, u32[]{:S(2)}) collective-permute-start(f32[1024,1152]{1,0:T(8,128)} %get-tuple-element.135), channel_id=1, source_target_pairs={{0,1},{1,0},{2,3},{3,2},{4,5},{5,4},{6,7},{7,6},{8,9},{9,8},{10,11... | collective-permute-start | bytes 14155784 | tf_op jit(solution)/shard_map/ppermute | solution.py:34
  382.2 58.8 %all-to-all-start.3 = ((bf16[8,128,1152]{2,1,0:T(8,128)(2,1)}), bf16[8,128,1152]{2,1,0:T(8,128)(2,1)}, u32[]{:S(2)}, u32[]{:S(2)}) async-start(bf16[8,128,1152]{2,1,0:T(8,128)(2,1)} %bitcast.219), calls=%async_computation.3 | async-start | bytes 4718592 | tf_op jit(solution)/shard_map/all_to_all | solution.py:594
  394.1 40.8 %collective-permute-start.11 = (bf16[1152,768]{1,0:T(8,128)(2,1)S(1)}, bf16[1152,768]{1,0:T(8,128)(2,1)}, u32[]{:S(2)}, u32[]{:S(2)}) collective-permute-start(bf16[1152,768]{1,0:T(8,128)(2,1)S(1)} %convolution_convert_fusion.3), channel_id=1, source_target_pairs={{0,2},{2,0},{1,3},{3,1},{4,6},{6,4},{5,7},{7,5},{8,10},{10,8},{9,1... | collective-permute-start | bytes 5308424 | tf_op jit(solution)/shard_map/ppermute | solution.py:34
  410.8 6.0 collective-permute-start.12
  446.9 5.1 collective-permute-start.14
  446.9 66.4 %collective-permute-start.13 = (bf16[1152,768]{1,0:T(8,128)(2,1)}, bf16[1152,768]{1,0:T(8,128)(2,1)}, u32[]{:S(2)}, u32[]{:S(2)}) collective-permute-start(bf16[1152,768]{1,0:T(8,128)(2,1)} %convolution_convert_fusion.4), channel_id=1, source_target_pairs={{0,2},{2,0},{1,3},{3,1},{4,6},{6,4},{5,7},{7,5},{8,10},{10,8},{9,1... | collective-permute-start | bytes 5308424 | tf_op jit(solution)/shard_map/ppermute | solution.py:34
  447.0 66.2 %all-to-all-start.4 = ((bf16[8,128,1152]{2,1,0:T(8,128)(2,1)}), bf16[8,128,1152]{2,1,0:T(8,128)(2,1)}, u32[]{:S(2)}, u32[]{:S(2)}) async-start(bf16[8,128,1152]{2,1,0:T(8,128)(2,1)} %bitcast.222), calls=%async_computation.4 | async-start | bytes 4718592 | tf_op jit(solution)/shard_map/all_to_all | solution.py:594
  520.1 85.6 %all-to-all-start.5 = ((bf16[8,288,768]{2,1,0:T(8,128)(2,1)}), bf16[8,288,768]{2,1,0:T(8,128)(2,1)}, u32[]{:S(2)}, u32[]{:S(2)}) async-start(bf16[8,288,768]{2,1,0:T(8,128)(2,1)} %pad_maximum_fusion), calls=%async_computation.5 | async-start | bytes 7077888 | tf_op jit(solution)/shard_map/all_to_all | solution.py:1079
  526.2 7.5 collective-permute-start.16
  533.8 69.5 %collective-permute-start.17 = (bf16[1152,1152]{1,0:T(8,128)(2,1)}, bf16[1152,1152]{1,0:T(8,128)(2,1)}, u32[]{:S(2)}, u32[]{:S(2)}) collective-permute-start(bf16[1152,1152]{1,0:T(8,128)(2,1)} %convolution_convert_fusion.1), channel_id=1, source_target_pairs={{0,2},{2,0},{1,3},{3,1},{4,6},{6,4},{5,7},{7,5},{8,10},{10,8},{9,1... | collective-permute-start | bytes 7962632 | tf_op jit(solution)/shard_map/ppermute | solution.py:34
  611.0 64.3 %all-to-all-start.6 = ((bf16[8,144,1152]{2,1,0:T(8,128)(2,1)}), bf16[8,144,1152]{2,1,0:T(8,128)(2,1)}, u32[]{:S(2)}, u32[]{:S(2)}) async-start(bf16[8,144,1152]{2,1,0:T(8,128)(2,1)} %bitcast.213), calls=%async_computation.6 | async-start | bytes 5308416 | tf_op jit(solution)/shard_map/all_to_all | solution.py:1093
  628.8 41.0 %collective-permute-start.20 = (bf16[8,144,768]{2,1,0:T(8,128)(2,1)}, bf16[8,144,768]{2,1,0:T(8,128)(2,1)}, u32[]{:S(2)}, u32[]{:S(2)}) collective-permute-start(bf16[8,144,768]{2,1,0:T(8,128)(2,1)} %get-tuple-element.253), channel_id=1, source_target_pairs={{0,2},{2,0},{1,3},{3,1},{4,6},{6,4},{5,7},{7,5},{8,10},{10,8},{9,1... | collective-permute-start | bytes 5308424 | tf_op jit(solution)/shard_map/ppermute | solution.py:34
  633.1 9.2 %collective-permute-start.18 = (f32[1024,104]{1,0:T(8,128)}, f32[1024,104]{1,0:T(8,128)}, u32[]{:S(2)}, u32[]{:S(2)}) collective-permute-start(f32[1024,104]{1,0:T(8,128)} %pad_maximum_fusion.4), channel_id=1, source_target_pairs={{0,1},{1,0},{2,3},{3,2},{4,5},{5,4},{6,7},{7,6},{8,9},{9,8},{10,11... | collective-permute-start | bytes 1277960 | tf_op jit(solution)/shard_map/ppermute | solution.py:34
  658.9 11.0 %collective-permute-start.19 = (f32[3,2,1,1152]{3,2,1,0:T(1,128)S(1)}, f32[3,2,1,1152]{3,2,1,0:T(1,128)S(1)}, u32[]{:S(2)}, u32[]{:S(2)}) collective-permute-start(f32[3,2,1,1152]{3,2,1,0:T(1,128)S(1)} %slice.265), channel_id=1, source_target_pairs={{2,0},{3,1},{6,4},{7,5},{10,8},{11,9},{14,12},{15,13},{18,16},{19,... | collective-permute-start | bytes 82952 | tf_op jit(solution)/shard_map/ppermute | solution.py:40
  683.8 8.0 collective-permute-start.21
  697.0 81.4 %all-to-all-start.7 = ((bf16[8,178,1152]{2,1,0:T(8,128)(2,1)}), bf16[8,178,1152]{2,1,0:T(8,128)(2,1)}, u32[]{:S(2)}, u32[]{:S(2)}) async-start(bf16[8,178,1152]{2,1,0:T(8,128)(2,1)} %pad_maximum_fusion.1), calls=%async_computation.7 | async-start | bytes 6782976 | tf_op jit(solution)/shard_map/all_to_all | solution.py:1159
  706.9 23.4 %collective-permute-start.15 = (bf16[1024,1152]{1,0:T(8,128)(2,1)S(1)}, bf16[1024,1152]{1,0:T(8,128)(2,1)}, u32[]{:S(2)}, u32[]{:S(2)}) collective-permute-start(bf16[1024,1152]{1,0:T(8,128)(2,1)S(1)} %fusion.29), channel_id=1, source_target_pairs={{0,1},{1,0},{2,3},{3,2},{4,5},{5,4},{6,7},{7,6},{8,9},{9,8},{10,11... | collective-permute-start | bytes 7077896 | tf_op jit(solution)/shard_map/ppermute | solution.py:34
  709.9 17.7 %collective-permute-start.22 = (f32[144,1152]{1,0:T(8,128)S(1)}, f32[144,1152]{1,0:T(8,128)S(1)}, u32[]{:S(2)}, u32[]{:S(2)}) collective-permute-start(f32[144,1152]{1,0:T(8,128)S(1)} %convert_reduce_fusion), channel_id=1, source_target_pairs={{0,2},{2,0},{1,3},{3,1},{4,6},{6,4},{5,7},{7,5},{8,10},{10,8},{9,1... | collective-permute-start | bytes 1990664 | tf_op jit(solution)/shard_map/ppermute | solution.py:34
  728.5 40.6 %collective-permute-start.23 = (bf16[8,144,768]{2,1,0:T(8,128)(2,1)}, bf16[8,144,768]{2,1,0:T(8,128)(2,1)}, u32[]{:S(2)}, u32[]{:S(2)}) collective-permute-start(bf16[8,144,768]{2,1,0:T(8,128)(2,1)} %get-tuple-element.182), channel_id=1, source_target_pairs={{0,2},{2,0},{1,3},{3,1},{4,6},{6,4},{5,7},{7,5},{8,10},{10,8},{9,1... | collective-permute-start | bytes 5308424 | tf_op jit(solution)/shard_map/ppermute | solution.py:34
  781.0 13.7 %collective-permute-start.24 = (bf16[178,1152]{1,0:T(8,128)(2,1)S(1)}, bf16[178,1152]{1,0:T(8,128)(2,1)S(1)}, u32[]{:S(2)}, u32[]{:S(2)}) collective-permute-start(bf16[178,1152]{1,0:T(8,128)(2,1)S(1)} %reduce_sum.152), channel_id=1, source_target_pairs={{0,2},{2,0},{1,3},{3,1},{4,6},{6,4},{5,7},{7,5},{8,10},{10,8},{9,1... | collective-permute-start | bytes 1230344 | tf_op jit(solution)/shard_map/ppermute | solution.py:34
  (106 other events, 1253.7 us)

commit v10 on v9

--- a/solution.py
+++ b/solution.py
@@ -18,8 +18,8 @@
 GROUP_A = 4
 GROUP_B = 4
 GROUP_C = 8
-UNROLL_A = 8
-UNROLL_B = 8
+UNROLL_A = 16
+UNROLL_B = 16
 UNROLL_C = 8
 UNROLL_D = 4
 UNROLL_E = 8
@@ -933,7 +933,7 @@
     rate_rows = jnp.broadcast_to((decay_rate * LOG2E)[:, None, :], (states, SEGMENTS, inner))
     expert_blocks = own_expert_blocks(up_shards, down_shards)
 
-    values = to_rows(hidden_in).astype(F32)
+    values = lax.optimization_barrier(to_rows(hidden_in)).astype(F32)
     normalized_rows, inverse_one = rms_forward(values, gain_one_f)
     normed_bf = normalized_rows.astype(BF16)
     x_pre = jnp.dot(normed_bf, in_x, preferred_element_type=F32).astype(BF16)
@@ -1073,14 +1073,16 @@
         step_size, mix_out, scan_grad, rate_rows
     )
     normed_part = contract_cols(z_grad_bf, in_z)
-    far_parts, got_out, near_product, far_product, normed_part, _ = together(
-        far_parts, got_out, near_product, far_product, normed_part, first_adjoint
+    far_parts, got_out, near_product, far_product, _ = together(
+        far_parts, got_out, near_product, far_product, first_adjoint
     )
     weight_blocks = lax.all_to_all(
         expert_weight_parts(near_parts, far_parts), "dp", 0, 0, tiled=True
     )
     leaving = entering_pieces(back_decay[:, :, 0], first_adjoint, "ctx", True)
-    leaving, near_product, far_product = together(leaving, near_product, far_product)
+    leaving, near_product, far_product, normed_part = together(
+        leaving, near_product, far_product, normed_part
+    )
     far_product = sent_far(far_product)
     adjoint_args = (
         step_size, xconv, mix_in, mix_out, scan_grad, rate_rows, seg_start, back_decay, back_adjoint,
@@ -1152,12 +1154,12 @@
     gain_row = gain_one_grad.reshape(dp_count, 1, shard)
     gain_high = gain_row.astype(BF16)
     gain_low = (gain_row - gain_high.astype(F32)).astype(BF16)
-    gain_rows = jnp.concatenate([gain_high, gain_low], axis=1)
-    gain_rows = jnp.pad(gain_rows, ((0, 0), (0, 6), (0, inner - shard)))
+    gain_row = jnp.concatenate([gain_high, gain_low], axis=2)
+    gain_row = jnp.pad(gain_row, ((0, 0), (0, 0), (0, inner - 2 * shard)))
     in_x_part, out_blocks = together(in_x_part, out_blocks)
     out_proj_grad, in_z_grad = product_shards(out_blocks)
     in_x_blocks = lax.all_to_all(
-        jnp.concatenate([in_x_part, gain_rows, small_rows], axis=1), "dp", 0, 0, tiled=True
+        jnp.concatenate([in_x_part, small_rows, gain_row], axis=1), "dp", 0, 0, tiled=True
     )
     out_proj_grad, in_z_grad, far_down_blocks = together(
         out_proj_grad, in_z_grad, weight_blocks[1]
@@ -1171,8 +1173,8 @@
     in_x_sums = jnp.sum(in_x_blocks.astype(F32), axis=0).astype(BF16)
     in_x_sums = narrow_sum(in_x_sums, "ctx")
     in_x_grad = in_x_sums[:shard]
-    gain_one_grad = in_x_sums[shard : shard + 1, :shard] + in_x_sums[shard + 1 : shard + 2, :shard]
-    small_grads = in_x_sums[shard + 8 :].reshape(-1)[:small_size].reshape(-1, shard)
+    gain_one_grad = in_x_sums[-1:, :shard] + in_x_sums[-1:, shard : 2 * shard]
+    small_grads = in_x_sums[shard:-1].reshape(-1)[:small_size].reshape(-1, shard)
     small_grads = jnp.concatenate([gain_one_grad, small_grads], axis=0)
     sums = [small_grads[bounds[i] : bounds[i + 1]] for i in range(len(bounds) - 1)]
     return (

time: 811 us -> 794 us (0.979)
  transfers between devices with their start and end apart: 33 -> 33, of which waited for: 19 -> 17; matrix products, arithmetic and copies ran while one was open for 27% -> 28% of each run, Pallas kernels for 21% -> 22%
where the time goes in v10:
time: 794 us; the launch traced here: 786 us
  Pallas kernels  258 us (32%)
  waiting for transfers between devices  175 us (22%)
  matrix products  116 us (15%)
  other arithmetic  99.8 us (13%)
  local copies, waits for them, and re-layouts  76.7 us (10%)
  starting transfers between devices  57.9 us (7%)
    pallas_call x4, Pallas kernels, call(): pl.pallas_call(kernel, grid=self.grid, in_specs=in_specs, out_specs=out_s...  134 us
    ppermute x21, waiting for transfers between devices, swapped(): return lax.ppermute(value, axis, [(0, 1), (1, 0)])  122 us
    pallas_call x1, Pallas kernels, gathered(): pl.pallas_call(partial(gather_kernel, count, number, parts), in_specs=[an...  63.5 us
    dot_general x12, matrix products, contract_rows(): lax.dot_general(left_side, right_side, (((0,), (0,)), ((), ())), precisio...  61.8 us
    pallas_call x2, Pallas kernels, expert_call(): pl.pallas_call(partial(expert_kernel, len(kept)), grid=(count // block,),...  47.2 us
    dot_general x6, matrix products, contract_cols(): lax.dot_general(left_side, right_side, (((1,), (1,)), ((), ())), precisio...  23.7 us
    all_to_all x4, waiting for transfers between devices, expert_exchange(): lax.all_to_all(value, 'dp', 0, 0, axis_index_groups=groups, tiled=True)  21.8 us
    all_to_all x4, starting transfers between devices, expert_exchange(): lax.all_to_all(value, 'dp', 0, 0, axis_index_groups=groups, tiled=True)  18.4 us
  transfers between devices with their start and end apart: 33, of which 17 were waited for; matrix products, arithmetic and copies ran while one was open for 28% of the time, Pallas kernels for 22%

profile of v10, /device:TPU:0, one launch (start us, length us, event | category | flops | bytes accessed | tf_op | source)
XLA Modules:
  0.0 786.3 jit_solution(2620692079341898539)
XLA Ops:
  6.8 63.5 %shard_map.297 = (bf16[8,144,1152]{2,1,0:T(8,128)(2,1)}, bf16[8,144,256]{2,1,0:T(8,128)(2,1)}, bf16[8,144,1152]{2,1,0:T(8,128)(2,1)}) custom-call(bf16[144,1152]{1,0:T(8,128)(2,1)} %bitcast.239, bf16[144,256]{1,0:T(8,128)(2,1)} %pad.62.refs_1_, bf16[144,1152]{1,0:T(8,128)(2,1)} %fusion.54.refs_2_), custom_call_target="tpu_custom_call" | custom-call | bytes 11796480 | tf_op jit(solution)/shard_map/pallas_call | solution.py:746
  115.0 19.0 %shard_map.298 = (f32[2,16,8,1152]{3,2,1,0:T(8,128)}, f32[2,16,8,1152]{3,2,1,0:T(8,128)}, f32[2,16,1152]{2,1,0:T(8,128)}) custom-call(f32[64,2,8,1152]{3,2,1,0:T(8,128)} %compare_select_fusion.step_ref, f32[64,2,8,1152]{3,2,1,0:T(8,128)} %get-tuple-element.239.input_ref, f32[2,64,16,8,128]{4,3,2,1,0:T(8,128)} %broadcast_in_dim.28.mix_in_ref, ...), custom_call_target="tpu_custom_call" | custom-call | flops 94371840 | bytes 209223 | tf_op jit(solution)/shard_map/pallas_call | solution.py:371
  160.2 10.1 %all-to-all-done.up_a.down_a = bf16[8,288,768]{2,1,0:T(8,128)(2,1)} async-done(((bf16[8,288,768]{2,1,0:T(8,128)(2,1)}), bf16[8,288,768]{2,1,0:T(8,128)(2,1)}, u32[]{:S(2)}, u32[]{:S(2)}) %all-to-all-start) | async-done | bytes 3538976 | tf_op jit(solution)/shard_map/all_to_all | solution.py:611
  170.3 5.9 broadcast_in_dim.30.mix_out_ref
  190.8 27.0 %shard_map.299 = (f32[64,2,8,1152]{3,2,1,0:T(8,128)}, f32[2,16,8,1152]{3,2,1,0:T(8,128)}) custom-call(f32[64,2,8,1152]{3,2,1,0:T(8,128)} %compare_select_fusion.step_ref, f32[64,2,8,1152]{3,2,1,0:T(8,128)} %get-tuple-element.239.input_ref, f32[2,64,16,8,128]{4,3,2,1,0:T(8,128)} %broadcast_in_dim.28.mix_in_ref, ...), custom_call_target="tpu_custom_call" | custom-call | flops 132120576 | bytes 352092 | tf_op jit(solution)/shard_map/pallas_call | solution.py:371
  224.6 6.9 fusion.50
  234.0 8.1 %collective-permute-done.5 = f32[1024,1152]{1,0:T(8,128)S(1)} collective-permute-done((f32[1024,1152]{1,0:T(8,128)}, f32[1024,1152]{1,0:T(8,128)S(1)}, u32[]{:S(2)}, u32[]{:S(2)}) %collective-permute-start.5) | collective-permute-done | bytes 4718624 | tf_op jit(solution)/shard_map/ppermute | solution.py:34
  256.4 40.4 %collective-permute-done.6.down_b = bf16[8,144,768]{2,1,0:T(8,128)(2,1)} collective-permute-done((bf16[8,144,768]{2,1,0:T(8,128)(2,1)}, bf16[8,144,768]{2,1,0:T(8,128)(2,1)}, u32[]{:S(2)}, u32[]{:S(2)}) %collective-permute-start.6) | collective-permute-done | bytes 1769504 | tf_op jit(solution)/shard_map/ppermute | solution.py:34
  296.8 13.4 %all-to-all-done.2 = bf16[8,128,1152]{2,1,0:T(8,128)(2,1)} async-done(((bf16[8,128,1152]{2,1,0:T(8,128)(2,1)}), bf16[8,128,1152]{2,1,0:T(8,128)(2,1)}, u32[]{:S(2)}, u32[]{:S(2)}) %all-to-all-start.2) | async-done | bytes 2359328 | tf_op jit(solution)/shard_map/all_to_all | solution.py:594
  315.1 23.6 %shard_map.300 = (f32[1024,1152]{1,0:T(8,128)}, f32[1024,1152]{1,0:T(8,128)}, f32[1024,8]{1,0:T(8,128)}, bf16[2048,1152]{1,0:T(8,128)(2,1)}, bf16[2048,1152]{1,0...) custom-call(bf16[1024,1152]{1,0:T(8,128)(2,1)} %collective-permute-d, ...), custom_call_target="tpu_custom_call" | custom-call | flops 14495514624 | bytes 29884416 | tf_op jit(solution)/shard_map/pallas_call | solution.py:562
  339.3 23.6 %shard_map.301 = (f32[1024,1152]{1,0:T(8,128)}, f32[1024,1152]{1,0:T(8,128)}, f32[1024,8]{1,0:T(8,128)}, bf16[2048,1152]{1,0:T(8,128)(2,1)}, bf16[2048,1152]{1,0...) custom-call(bf16[1024,1152]{1,0:T(8,128)(2,1)} %bitcast.32.rows_ref,, ...), custom_call_target="tpu_custom_call", output_to_operand_aliasing={{3}: (8, {}), {4}: (9, {}), {5}: (10, {}), {6}: (11, {}), {... | custom-call | flops 14495514624 | bytes 29884416 | tf_op jit(solution)/shard_map/pallas_call | solution.py:562
  364.3 6.6 add_convert_fusion.5
  379.8 7.4 convolution_convert_fusion.3
  387.8 7.6 convolution_convert_fusion.4
  395.5 5.8 fusion.98
  404.4 5.8 fusion.97
  410.1 17.8 %collective-permute-done.11 = bf16[1152,768]{1,0:T(8,128)(2,1)} collective-permute-done((bf16[1152,768]{1,0:T(8,128)(2,1)S(1)}, bf16[1152,768]{1,0:T(8,128)(2,1)}, u32[]{:S(2)}, u32[]{:S(2)}) %collective-permute-start.11) | collective-permute-done | bytes 1769504 | tf_op jit(solution)/shard_map/ppermute | solution.py:34
  428.0 5.8 all-to-all-done.3
  433.8 5.8 fusion.34
  454.5 7.4 fusion.49
  466.7 18.9 %shard_map.302 = (f32[2,16,8,1152]{3,2,1,0:T(8,128)}, f32[2,16,8,1152]{3,2,1,0:T(8,128)}, f32[2,16,1152]{2,1,0:T(8,128)}) custom-call(f32[64,2,8,1152]{3,2,1,0:T(8,128)} %compare_select_fusion.step_ref, f32[2,64,16,8,128]{4,3,2,1,0:T(8,128)} %broadcast_in_dim.30.mix_out_ref, f32[64,2,8,1152]{3,2,1,0:T(8,128)} %get-tuple-element.241.grad_ref, ...), custom_call_target="tpu_custom_call" | custom-call | flops 94371840 | bytes 209223 | tf_op jit(solution)/shard_map/pallas_call | solution.py:371
  485.6 8.3 %fusion.38 = f32[1152,1152]{1,0:T(8,128)} fusion(bf16[1024,1152]{1,0:T(8,128)(2,1)S(1)} %bitcast.230, bf16[1024,1152]{1,0:T(8,128)(2,1)} %bitcast.232, pred[]{:T(512)S(6)} %eq.66, f32[1024,1152]{1,0:T(8,128)} %copy-done.8, bf16[1024,1152]{1,0:T(8,128)(2,1)S(1)} %bitcast.170, f32[1152]{0:T(1024)S(1)} %get-tuple-element.230, f32[1024]{0:T(1024)S(1)} %copy-done.51), kind=kOutput, calls=%fused_computation.81 | convolution fusion | flops 2726166528 | bytes 17113600 | tf_op jit(solution)/shard_map/dot_general | solution.py:76
  506.0 5.9 all-to-all-start.5
  513.6 8.1 %fusion.47 = f32[1024,1152]{1,0:T(8,128)} fusion(bf16[1024,1152]{1,0:T(8,128)(2,1)} %bitcast.233, bf16[1152,1152]{1,0:T(8,128)(2,1)} %collective-permute-done.3, bf16[1152,1152]{1,0:T(8,128)(2,1)} %bitcast.14, pred[]{:T(512)S(6)} %eq.66), kind=kOutput, calls=%fused_computation.98 | convolution fusion | flops 2719236096 | bytes 12386305 | tf_op jit(solution)/shard_map/dot_general | solution.py:86
  525.0 69.2 %shard_map.303 = (bf16[64,2,8,1152]{3,2,1,0:T(8,128)(2,1)}, f32[64,2,8,1152]{3,2,1,0:T(8,128)}, f32[2,16,1152]{2,1,0:T(8,128)}, f32[2,8,1152]{2,1,0:T(8,128)}, f32[64,2,8,128]{3,2,1,0:T(8,128)}) custom-call(f32[64,2,8,1152]{3,2,1,0:T(8,128)} %compare_select_fusion.step_ref, f32[64,2,8,1152]{3,2,1,0:T(8,128)} %get-tuple-element.239.input_ref, ...), custom_call_target="tpu_custom_call" | custom-call | flops 377487360 | bytes 430371 | tf_op jit(solution)/shard_map/pallas_call | solution.py:371
  599.6 6.0 all-to-all-start.6
  632.0 13.3 %shard_map.304 = (bf16[64,16,1152]{2,1,0:T(8,128)(2,1)}, f32[8,1152]{1,0:T(8,128)}, f32[3,16,1152]{2,1,0:T(8,128)}, f32[3,16,1152]{2,1,0:T(8,128)}) custom-call(bf16[1024,104]{1,0:T(8,128)(2,1)} %add_convert_fusion.6.proj_ref, bf16[104,1152]{1,0:T(8,128)(2,1)} %slice.207.weight_ref, f32[64,16,1152]{2,1,0:T(8,128)} %bitcast.201, ...), custom_call_target="tpu_custom_call" | custom-call | flops 1 | bytes 1 | tf_op jit(solution)/shard_map/pallas_call | solution.py:486
  658.6 6.3 all-to-all-done.6
  666.5 6.1 fusion.99
  701.0 16.1 %collective-permute-done.22 = f32[144,1152]{1,0:T(8,128)S(1)} collective-permute-done((f32[144,1152]{1,0:T(8,128)S(1)}, f32[144,1152]{1,0:T(8,128)S(1)}, u32[]{:S(2)}, u32[]{:S(2)}) %collective-permute-start.22) | collective-permute-done | bytes 663584 | tf_op jit(solution)/shard_map/ppermute | solution.py:34
  727.6 31.1 %collective-permute-done.23 = bf16[8,144,768]{2,1,0:T(8,128)(2,1)} collective-permute-done((bf16[8,144,768]{2,1,0:T(8,128)(2,1)}, bf16[8,144,768]{2,1,0:T(8,128)(2,1)}, u32[]{:S(2)}, u32[]{:S(2)}) %collective-permute-start.23) | collective-permute-done | bytes 1769504 | tf_op jit(solution)/shard_map/ppermute | solution.py:34
  758.7 6.7 all-to-all-done.7
  (411 shorter events, 276.0 us)
Async XLA Ops:
  80.9 12.3 %collective-permute-start = (bf16[3,2,1,1152]{3,2,1,0:T(2,128)(2,1)S(1)}, bf16[3,2,1,1152]{3,2,1,0:T(2,128)(2,1)S(1)}, u32[]{:S(2)}, u32[]{:S(2)}) collective-permute-start(bf16[3,2,1,1152]{3,2,1,0:T(2,128)(2,1)S(1)} %slice.249), channel_id=1, source_target_pairs={{0,2},{1,3},{4,6},{5,7},{8,10},{9,11},{12,14},{13,15},{16,18},{17,... | collective-permute-start | bytes 41480 | tf_op jit(solution)/shard_map/ppermute | solution.py:40
  87.4 82.9 %all-to-all-start = ((bf16[8,288,768]{2,1,0:T(8,128)(2,1)}), bf16[8,288,768]{2,1,0:T(8,128)(2,1)}, u32[]{:S(2)}, u32[]{:S(2)}) async-start(bf16[8,288,768]{2,1,0:T(8,128)(2,1)} %slice_select_fusion), calls=%async_computation | async-start | bytes 7077888 | tf_op jit(solution)/shard_map/all_to_all | solution.py:611
  98.9 86.6 %collective-permute-start.3 = (bf16[1152,1152]{1,0:T(8,128)(2,1)}, bf16[1152,1152]{1,0:T(8,128)(2,1)}, u32[]{:S(2)}, u32[]{:S(2)}) collective-permute-start(bf16[1152,1152]{1,0:T(8,128)(2,1)} %bitcast.14), channel_id=1, source_target_pairs={{0,2},{2,0},{1,3},{3,1},{4,6},{6,4},{5,7},{7,5},{8,10},{10,8},{9,1... | collective-permute-start | bytes 7962632 | tf_op jit(solution)/shard_map/ppermute | solution.py:34
  144.0 16.2 %collective-permute-start.2 = (f32[2,16,1152]{2,1,0:T(8,128)}, f32[2,16,1152]{2,1,0:T(8,128)}, u32[]{:S(2)}, u32[]{:S(2)}) collective-permute-start(f32[2,16,1152]{2,1,0:T(8,128)} %get-tuple-element.108), channel_id=1, source_target_pairs={{0,2},{1,3},{4,6},{5,7},{8,10},{9,11},{12,14},{13,15},{16,18},{17,... | collective-permute-start | bytes 442376 | tf_op jit(solution)/shard_map/ppermute | solution.py:40
  176.2 57.8 %all-to-all-start.1 = ((bf16[8,128,1152]{2,1,0:T(8,128)(2,1)}), bf16[8,128,1152]{2,1,0:T(8,128)(2,1)}, u32[]{:S(2)}, u32[]{:S(2)}) async-start(bf16[8,128,1152]{2,1,0:T(8,128)(2,1)} %bitcast.226), calls=%async_computation.1 | async-start | bytes 4718592 | tf_op jit(solution)/shard_map/all_to_all | solution.py:594
  184.8 39.8 %collective-permute-start.4 = (bf16[8,144,768]{2,1,0:T(8,128)(2,1)}, bf16[8,144,768]{2,1,0:T(8,128)(2,1)}, u32[]{:S(2)}, u32[]{:S(2)}) collective-permute-start(bf16[8,144,768]{2,1,0:T(8,128)(2,1)} %get-tuple-element.254), channel_id=1, source_target_pairs={{0,2},{2,0},{1,3},{3,1},{4,6},{6,4},{5,7},{7,5},{8,10},{10,8},{9,1... | collective-permute-start | bytes 5308424 | tf_op jit(solution)/shard_map/ppermute | solution.py:34
  234.0 8.1 %collective-permute-start.5 = (f32[1024,1152]{1,0:T(8,128)}, f32[1024,1152]{1,0:T(8,128)S(1)}, u32[]{:S(2)}, u32[]{:S(2)}) collective-permute-start(f32[1024,1152]{1,0:T(8,128)} %fusion.50), channel_id=1, source_target_pairs={{0,1},{1,0},{2,3},{3,2},{4,5},{5,4},{6,7},{7,6},{8,9},{9,8},{10,11... | collective-permute-start | bytes 14155784 | tf_op jit(solution)/shard_map/ppermute | solution.py:34
  251.0 59.2 %all-to-all-start.2 = ((bf16[8,128,1152]{2,1,0:T(8,128)(2,1)}), bf16[8,128,1152]{2,1,0:T(8,128)(2,1)}, u32[]{:S(2)}, u32[]{:S(2)}) async-start(bf16[8,128,1152]{2,1,0:T(8,128)(2,1)} %bitcast.227), calls=%async_computation.2 | async-start | bytes 4718592 | tf_op jit(solution)/shard_map/all_to_all | solution.py:594
  255.8 41.0 %collective-permute-start.6 = (bf16[8,144,768]{2,1,0:T(8,128)(2,1)}, bf16[8,144,768]{2,1,0:T(8,128)(2,1)}, u32[]{:S(2)}, u32[]{:S(2)}) collective-permute-start(bf16[8,144,768]{2,1,0:T(8,128)(2,1)} %get-tuple-element.253), channel_id=1, source_target_pairs={{0,2},{2,0},{1,3},{3,1},{4,6},{6,4},{5,7},{7,5},{8,10},{10,8},{9,1... | collective-permute-start | bytes 5308424 | tf_op jit(solution)/shard_map/ppermute | solution.py:34
  256.4 54.9 %collective-permute-start.8 = (bf16[1024,1152]{1,0:T(8,128)(2,1)}, bf16[1024,1152]{1,0:T(8,128)(2,1)}, u32[]{:S(2)}, u32[]{:S(2)}) collective-permute-start(bf16[1024,1152]{1,0:T(8,128)(2,1)} %bitcast.33.cotan_ref), channel_id=1, source_target_pairs={{0,1},{1,0},{2,3},{3,2},{4,5},{5,4},{6,7},{7,6},{8,9},{9,8},{10,11... | collective-permute-start | bytes 7077896 | tf_op jit(solution)/shard_map/ppermute | solution.py:34
  310.2 4.9 collective-permute-start.7
  338.7 25.6 %collective-permute-start.10 = (f32[1024,1152]{1,0:T(8,128)}, f32[1024,1152]{1,0:T(8,128)}, u32[]{:S(2)}, u32[]{:S(2)}) collective-permute-start(f32[1024,1152]{1,0:T(8,128)} %get-tuple-element.137), channel_id=1, source_target_pairs={{0,1},{1,0},{2,3},{3,2},{4,5},{5,4},{6,7},{7,6},{8,9},{9,8},{10,11... | collective-permute-start | bytes 14155784 | tf_op jit(solution)/shard_map/ppermute | solution.py:34
  338.9 32.0 %collective-permute-start.9 = (f32[1024,1152]{1,0:T(8,128)}, f32[1024,1152]{1,0:T(8,128)S(1)}, u32[]{:S(2)}, u32[]{:S(2)}) collective-permute-start(f32[1024,1152]{1,0:T(8,128)} %get-tuple-element.135), channel_id=1, source_target_pairs={{0,1},{1,0},{2,3},{3,2},{4,5},{5,4},{6,7},{7,6},{8,9},{9,8},{10,11... | collective-permute-start | bytes 14155784 | tf_op jit(solution)/shard_map/ppermute | solution.py:34
  375.0 58.8 %all-to-all-start.3 = ((bf16[8,128,1152]{2,1,0:T(8,128)(2,1)}), bf16[8,128,1152]{2,1,0:T(8,128)(2,1)}, u32[]{:S(2)}, u32[]{:S(2)}) async-start(bf16[8,128,1152]{2,1,0:T(8,128)(2,1)} %bitcast.191), calls=%async_computation.3 | async-start | bytes 4718592 | tf_op jit(solution)/shard_map/all_to_all | solution.py:594
  387.1 40.8 %collective-permute-start.11 = (bf16[1152,768]{1,0:T(8,128)(2,1)S(1)}, bf16[1152,768]{1,0:T(8,128)(2,1)}, u32[]{:S(2)}, u32[]{:S(2)}) collective-permute-start(bf16[1152,768]{1,0:T(8,128)(2,1)S(1)} %convolution_convert_fusion.3), channel_id=1, source_target_pairs={{0,2},{2,0},{1,3},{3,1},{4,6},{6,4},{5,7},{7,5},{8,10},{10,8},{9,1... | collective-permute-start | bytes 5308424 | tf_op jit(solution)/shard_map/ppermute | solution.py:34
  404.3 5.8 collective-permute-start.12
  439.6 5.1 collective-permute-start.14
  439.6 59.5 %collective-permute-start.13 = (bf16[1152,768]{1,0:T(8,128)(2,1)}, bf16[1152,768]{1,0:T(8,128)(2,1)}, u32[]{:S(2)}, u32[]{:S(2)}) collective-permute-start(bf16[1152,768]{1,0:T(8,128)(2,1)} %convolution_convert_fusion.4), channel_id=1, source_target_pairs={{0,2},{2,0},{1,3},{3,1},{4,6},{6,4},{5,7},{7,5},{8,10},{10,8},{9,1... | collective-permute-start | bytes 5308424 | tf_op jit(solution)/shard_map/ppermute | solution.py:34
  440.2 59.0 %all-to-all-start.4 = ((bf16[8,128,1152]{2,1,0:T(8,128)(2,1)}), bf16[8,128,1152]{2,1,0:T(8,128)(2,1)}, u32[]{:S(2)}, u32[]{:S(2)}) async-start(bf16[8,128,1152]{2,1,0:T(8,128)(2,1)} %bitcast.194), calls=%async_computation.4 | async-start | bytes 4718592 | tf_op jit(solution)/shard_map/all_to_all | solution.py:594
  506.0 88.2 %all-to-all-start.5 = ((bf16[8,288,768]{2,1,0:T(8,128)(2,1)}), bf16[8,288,768]{2,1,0:T(8,128)(2,1)}, u32[]{:S(2)}, u32[]{:S(2)}) async-start(bf16[8,288,768]{2,1,0:T(8,128)(2,1)} %pad_maximum_fusion), calls=%async_computation.5 | async-start | bytes 7077888 | tf_op jit(solution)/shard_map/all_to_all | solution.py:1079
  512.0 9.7 %collective-permute-start.16 = (f32[2,16,1152]{2,1,0:T(8,128)S(1)}, f32[2,16,1152]{2,1,0:T(8,128)S(1)}, u32[]{:S(2)}, u32[]{:S(2)}) collective-permute-start(f32[2,16,1152]{2,1,0:T(8,128)S(1)} %copy-done.70), channel_id=1, source_target_pairs={{2,0},{3,1},{6,4},{7,5},{10,8},{11,9},{14,12},{15,13},{18,16},{19,... | collective-permute-start | bytes 442376 | tf_op jit(solution)/shard_map/ppermute | solution.py:40
  521.7 72.5 %collective-permute-start.17 = (bf16[1152,1152]{1,0:T(8,128)(2,1)S(1)}, bf16[1152,1152]{1,0:T(8,128)(2,1)}, u32[]{:S(2)}, u32[]{:S(2)}) collective-permute-start(bf16[1152,1152]{1,0:T(8,128)(2,1)S(1)} %copy-done.68), channel_id=1, source_target_pairs={{0,2},{2,0},{1,3},{3,1},{4,6},{6,4},{5,7},{7,5},{8,10},{10,8},{9,1... | collective-permute-start | bytes 7962632 | tf_op jit(solution)/shard_map/ppermute | solution.py:34
  599.6 65.3 %all-to-all-start.6 = ((bf16[8,144,1152]{2,1,0:T(8,128)(2,1)}), bf16[8,144,1152]{2,1,0:T(8,128)(2,1)}, u32[]{:S(2)}, u32[]{:S(2)}) async-start(bf16[8,144,1152]{2,1,0:T(8,128)(2,1)} %bitcast.188), calls=%async_computation.6 | async-start | bytes 5308416 | tf_op jit(solution)/shard_map/all_to_all | solution.py:1095
  618.7 39.9 %collective-permute-start.20 = (bf16[8,144,768]{2,1,0:T(8,128)(2,1)}, bf16[8,144,768]{2,1,0:T(8,128)(2,1)}, u32[]{:S(2)}, u32[]{:S(2)}) collective-permute-start(bf16[8,144,768]{2,1,0:T(8,128)(2,1)} %get-tuple-element.252), channel_id=1, source_target_pairs={{0,2},{2,0},{1,3},{3,1},{4,6},{6,4},{5,7},{7,5},{8,10},{10,8},{9,1... | collective-permute-start | bytes 5308424 | tf_op jit(solution)/shard_map/ppermute | solution.py:34
  620.5 9.2 %collective-permute-start.18 = (f32[1024,104]{1,0:T(8,128)}, f32[1024,104]{1,0:T(8,128)}, u32[]{:S(2)}, u32[]{:S(2)}) collective-permute-start(f32[1024,104]{1,0:T(8,128)} %pad_maximum_fusion.4), channel_id=1, source_target_pairs={{0,1},{1,0},{2,3},{3,2},{4,5},{5,4},{6,7},{7,6},{8,9},{9,8},{10,11... | collective-permute-start | bytes 1277960 | tf_op jit(solution)/shard_map/ppermute | solution.py:34
  646.3 12.2 %collective-permute-start.19 = (f32[3,2,1,1152]{3,2,1,0:T(1,128)S(1)}, f32[3,2,1,1152]{3,2,1,0:T(1,128)S(1)}, u32[]{:S(2)}, u32[]{:S(2)}) collective-permute-start(f32[3,2,1,1152]{3,2,1,0:T(1,128)S(1)} %slice.265), channel_id=1, source_target_pairs={{2,0},{3,1},{6,4},{7,5},{10,8},{11,9},{14,12},{15,13},{18,16},{19,... | collective-permute-start | bytes 82952 | tf_op jit(solution)/shard_map/ppermute | solution.py:40
  673.2 8.4 %collective-permute-start.21 = (f32[1024,1152]{1,0:T(8,128)S(1)}, f32[1024,1152]{1,0:T(8,128)S(1)}, u32[]{:S(2)}, u32[]{:S(2)}) collective-permute-start(f32[1024,1152]{1,0:T(8,128)S(1)} %add.244), channel_id=1, source_target_pairs={{0,1},{1,0},{2,3},{3,2},{4,5},{5,4},{6,7},{7,6},{8,9},{9,8},{10,11... | collective-permute-start | bytes 14155784 | tf_op jit(solution)/shard_map/ppermute | solution.py:34
  687.6 77.7 %all-to-all-start.7 = ((bf16[8,171,1152]{2,1,0:T(8,128)(2,1)}), bf16[8,171,1152]{2,1,0:T(8,128)(2,1)}, u32[]{:S(2)}, u32[]{:S(2)}) async-start(bf16[8,171,1152]{2,1,0:T(8,128)(2,1)} %pad_maximum_fusion.1), calls=%async_computation.7 | async-start | bytes 6488064 | tf_op jit(solution)/shard_map/all_to_all | solution.py:1161
  697.4 20.9 %collective-permute-start.15 = (bf16[1024,1152]{1,0:T(8,128)(2,1)S(1)}, bf16[1024,1152]{1,0:T(8,128)(2,1)}, u32[]{:S(2)}, u32[]{:S(2)}) collective-permute-start(bf16[1024,1152]{1,0:T(8,128)(2,1)S(1)} %fusion.35), channel_id=1, source_target_pairs={{0,1},{1,0},{2,3},{3,2},{4,5},{5,4},{6,7},{7,6},{8,9},{9,8},{10,11... | collective-permute-start | bytes 7077896 | tf_op jit(solution)/shard_map/ppermute | solution.py:34
  699.7 17.4 %collective-permute-start.22 = (f32[144,1152]{1,0:T(8,128)S(1)}, f32[144,1152]{1,0:T(8,128)S(1)}, u32[]{:S(2)}, u32[]{:S(2)}) collective-permute-start(f32[144,1152]{1,0:T(8,128)S(1)} %convert_reduce_fusion), channel_id=1, source_target_pairs={{0,2},{2,0},{1,3},{3,1},{4,6},{6,4},{5,7},{7,5},{8,10},{10,8},{9,1... | collective-permute-start | bytes 1990664 | tf_op jit(solution)/shard_map/ppermute | solution.py:34
  718.0 40.6 %collective-permute-start.23 = (bf16[8,144,768]{2,1,0:T(8,128)(2,1)}, bf16[8,144,768]{2,1,0:T(8,128)(2,1)}, u32[]{:S(2)}, u32[]{:S(2)}) collective-permute-start(bf16[8,144,768]{2,1,0:T(8,128)(2,1)} %get-tuple-element.182), channel_id=1, source_target_pairs={{0,2},{2,0},{1,3},{3,1},{4,6},{6,4},{5,7},{7,5},{8,10},{10,8},{9,1... | collective-permute-start | bytes 5308424 | tf_op jit(solution)/shard_map/ppermute | solution.py:34
  767.8 11.5 %collective-permute-start.24 = (bf16[171,1152]{1,0:T(8,128)(2,1)S(1)}, bf16[171,1152]{1,0:T(8,128)(2,1)S(1)}, u32[]{:S(2)}, u32[]{:S(2)}) collective-permute-start(bf16[171,1152]{1,0:T(8,128)(2,1)S(1)} %reduce_sum.152), channel_id=1, source_target_pairs={{0,2},{2,0},{1,3},{3,1},{4,6},{6,4},{5,7},{7,5},{8,10},{10,8},{9,1... | collective-permute-start | bytes 1181960 | tf_op jit(solution)/shard_map/ppermute | solution.py:34
  (98 other events, 1048.8 us)

commit v11 on v10

--- a/solution.py
+++ b/solution.py
@@ -611,12 +611,12 @@
     return lax.all_to_all(both, "dp", 0, 0, tiled=True)
 
 
-def other_hidden(both):
+def other_hidden(both, layer):
     rows = both.shape[1] // 2
+    both = both[:, layer * rows : (layer + 1) * rows]
     if lax.axis_size("ctx") == 2:
-        return swapped(both[:, :rows], "ctx"), swapped(both[:, rows:], "ctx")
-    half = both.shape[2] // 2
-    return both[:, :rows, half:], both[:, rows:, half:]
+        return swapped(both, "ctx")
+    return both[:, :, both.shape[2] // 2 :]
 
 
 def gather_kernel(count, number, parts, *refs):
@@ -801,8 +801,7 @@
         blocks = jnp.sum(
             blocks.reshape(count // experts, experts, *blocks.shape[1:]).astype(F32), axis=0
         ).astype(BF16)
-    shard = blocks.shape[1] // 2
-    return blocks[:, :shard], blocks[:, shard:]
+    return blocks
 
 
 def far_hidden(blocks):
@@ -963,7 +962,9 @@
     dt_pre = (jnp.dot(dt_low, dt_proj, preferred_element_type=F32) + dt_shift).reshape(x_pre.shape)
     step_size = jax.nn.softplus(dt_pre)
     seg_decay, seg_state, last_state = scan.ends(step_size, xconv, mix_in, rate_rows)
-    later_ids, later_mask, later_grad, _ = together(expert_ids, keep_mask, out_grad, seg_state)
+    later_ids, later_mask, later_grad, mix_out, _ = together(
+        expert_ids, keep_mask, out_grad, mix_out, seg_state
+    )
     route = to_rows(later_ids)[:, 0]
     keep = to_rows(later_mask)[:, 0].astype(F32)
     onehot_int = (route[:, None] == jnp.arange(experts, dtype=jnp.int32)[None, :]).astype(jnp.int32)
@@ -998,7 +999,7 @@
         entering, mix_out, expert_blocks, sent_cotan
     )
     slot_cotan = expert_exchange(sent_cotan, experts)
-    far_up, far_down = other_hidden(expert_blocks)
+    far_up = other_hidden(expert_blocks, 0)
     scan_out, seg_start = scan.run(
         step_size, xconv, mix_in, mix_out, rate_rows, seg_decay, seg_state, entering
     )
@@ -1018,7 +1019,11 @@
     kept = ()
     got_grads, slot_outs, router_grad_t = [], [], 0.0
     for half, half_cotan in enumerate(halves_of(slot_cotan)):
-        own_rows = expert_exchange(slotted(normed_two_bf, half), experts)
+        sent_rows = slotted(normed_two_bf, half)
+        if not half:
+            sent_rows, expert_blocks = together(sent_rows, expert_blocks)
+            far_down = other_hidden(expert_blocks, 1)
+        own_rows = expert_exchange(sent_rows, experts)
         if not half:
             own_rows, far_down = together(own_rows, far_down)
         else:
@@ -1055,8 +1060,11 @@
         all_rows, (hidden_a, hidden_b), all_grads, (active_a, active_b)
     )
     far_first = sent_far(far_parts[0])
-    got_grads, near_parts, far_second, far_first, slot_outs, router_grad_t = together(
-        got_grads, near_parts, far_parts[1], far_first, slot_outs, router_grad_t
+    (
+        got_grads, near_parts, far_second, far_first, slot_outs, router_grad_t, extended_bf, xconv_t
+    ) = together(
+        got_grads, near_parts, far_parts[1], far_first, slot_outs, router_grad_t, extended_bf,
+        xconv_rows.T,
     )
     far_parts = far_first, sent_far(far_second)
     normed_two_grad = landed(got_grads)
@@ -1091,7 +1099,7 @@
     pre_grad, xconv_grad, decay_sum, scan_sums, mix_grad = scan.adjoint(adjoint_args)
     pre_grad, far_product, weight_blocks = together(pre_grad, far_product, weight_blocks)
     weight_blocks = expert_weight_blocks(weight_blocks, experts)
-    far_ups = far_hidden(weight_blocks[0])
+    far_ups = far_hidden(weight_blocks[:, :shard])
     out_blocks = lax.all_to_all(product_part(near_product, far_product), "dp", 0, 0, tiled=True)
     decay_log_grad = jnp.sum(decay_sum, axis=0) * decay_rate
     dt_shift_grad, skip_grad = jnp.sum(scan_sums, axis=0)[:2]
@@ -1101,7 +1109,9 @@
     mix_grad = mix_grad.reshape(tokens, LANES)[:, : 2 * states]
     proj_part = jnp.concatenate([dt_low_grad, mix_grad], axis=1)
     proj_grad_bf = axis_sum(proj_part, "tp").astype(BF16)
-    x_proj_grad_t = contract_rows(proj_grad_bf, xconv_rows)
+    x_proj_grad_t = lax.dot_general(
+        proj_grad_bf, xconv_t, (((0,), (1,)), ((), ())), preferred_element_type=F32
+    )
     flat = (chains * SEGMENTS, inner)
     x_grad_bf, conv_sums, head, last = conv_back(
         proj_grad_bf,
@@ -1115,7 +1125,9 @@
     edge_back = passed_along(
         head.reshape(taps - 1, chains, SEGMENTS, inner)[:, :, :1], "ctx", -1
     )
-    edge_back, out_blocks, far_ups = together(edge_back, out_blocks, far_ups)
+    edge_back, out_blocks, far_ups, weight_blocks = together(
+        edge_back, out_blocks, far_ups, weight_blocks
+    )
     reaching = jnp.stack(
         [
             sum(tap_weights[tap] * edge_back[at - tap] for tap in range(at + 1))
@@ -1162,11 +1174,11 @@
         jnp.concatenate([in_x_part, small_rows, gain_row], axis=1), "dp", 0, 0, tiled=True
     )
     out_proj_grad, in_z_grad, far_down_blocks = together(
-        out_proj_grad, in_z_grad, weight_blocks[1]
+        out_proj_grad, in_z_grad, weight_blocks[:, shard:]
     )
     far_downs, in_x_blocks = together(far_hidden(far_down_blocks), in_x_blocks)
-    first_grad = expert_weight_grad(weight_blocks[0], far_ups)
-    second_grad = expert_weight_grad(weight_blocks[1], far_downs)
+    first_grad = expert_weight_grad(weight_blocks[:, :shard], far_ups)
+    second_grad = expert_weight_grad(far_down_blocks, far_downs)
     router_prob = jax.nn.softmax(contract_cols(normed_two_bf, router_t), axis=-1)
     gate_prob = jnp.sum(router_prob * onehot_int.astype(F32), axis=1) * keep
     result = from_rows((middle + gate_prob[:, None] * landed(halves_of(got_out))).astype(BF16))

time: 794 us -> 795 us (level)
  matrix products: 116 us -> 124 us
    ppermute x4, waiting for transfers between devices: 8.02 us -> 0.01 us  [passed_along(): lax.ppermute(value, axis, [(source, source + steps) for source in range(l...]
    dot_general x12 -> x11, matrix products: 61.8 us -> 64.5 us  [contract_rows(): lax.dot_general(left_side, right_side, (((0,), (0,)), ((), ())), precisio...]
  transfers between devices with their start and end apart: 33 -> 33, of which waited for: 17 -> 17; matrix products, arithmetic and copies ran while one was open for 28% -> 29% of each run, Pallas kernels for 22% -> 22%
where the time goes in v11:
time: 795 us; the launch traced here: 788 us
  Pallas kernels  258 us (32%)
  waiting for transfers between devices  170 us (21%)
  matrix products  124 us (16%)
  other arithmetic  103 us (13%)
  local copies, waits for them, and re-layouts  74.5 us (9%)
  starting transfers between devices  55.1 us (7%)
    pallas_call x4, Pallas kernels, call(): pl.pallas_call(kernel, grid=self.grid, in_specs=in_specs, out_specs=out_s...  134 us
    ppermute x21, waiting for transfers between devices, swapped(): return lax.ppermute(value, axis, [(0, 1), (1, 0)])  122 us
    dot_general x11, matrix products, contract_rows(): lax.dot_general(left_side, right_side, (((0,), (0,)), ((), ())), precisio...  64.5 us
    pallas_call x1, Pallas kernels, gathered(): pl.pallas_call(partial(gather_kernel, count, number, parts), in_specs=[an...  63.5 us
    pallas_call x2, Pallas kernels, expert_call(): pl.pallas_call(partial(expert_kernel, len(kept)), grid=(count // block,),...  47.2 us
    dot_general x6, matrix products, contract_cols(): lax.dot_general(left_side, right_side, (((1,), (1,)), ((), ())), precisio...  26.2 us
    all_to_all x4, waiting for transfers between devices, expert_exchange(): lax.all_to_all(value, 'dp', 0, 0, axis_index_groups=groups, tiled=True)  21.8 us
    all_to_all x4, starting transfers between devices, expert_exchange(): lax.all_to_all(value, 'dp', 0, 0, axis_index_groups=groups, tiled=True)  18.6 us
  transfers between devices with their start and end apart: 33, of which 17 were waited for; matrix products, arithmetic and copies ran while one was open for 29% of the time, Pallas kernels for 22%

profile of v11, /device:TPU:0, one launch (start us, length us, event | category | flops | bytes accessed | tf_op | source)
XLA Modules:
  0.0 787.6 jit_solution(6014047365111400515)
XLA Ops:
  6.8 63.5 %shard_map.297 = (bf16[8,144,1152]{2,1,0:T(8,128)(2,1)}, bf16[8,144,256]{2,1,0:T(8,128)(2,1)}, bf16[8,144,1152]{2,1,0:T(8,128)(2,1)}) custom-call(bf16[144,1152]{1,0:T(8,128)(2,1)} %bitcast.234, bf16[144,256]{1,0:T(8,128)(2,1)} %pad.62.refs_1_, bf16[144,1152]{1,0:T(8,128)(2,1)} %fusion.54.refs_2_), custom_call_target="tpu_custom_call" | custom-call | bytes 11796480 | tf_op jit(solution)/shard_map/pallas_call | solution.py:746
  87.3 5.8 all-to-all-start
  119.4 19.0 %shard_map.298 = (f32[2,16,8,1152]{3,2,1,0:T(8,128)}, f32[2,16,8,1152]{3,2,1,0:T(8,128)}, f32[2,16,1152]{2,1,0:T(8,128)}) custom-call(f32[64,2,8,1152]{3,2,1,0:T(8,128)} %compare_select_fusion.step_ref, f32[64,2,8,1152]{3,2,1,0:T(8,128)} %get-tuple-element.267.input_ref, f32[2,64,16,8,128]{4,3,2,1,0:T(8,128)} %broadcast_in_dim.28.mix_in_ref, ...), custom_call_target="tpu_custom_call" | custom-call | flops 94371840 | bytes 209223 | tf_op jit(solution)/shard_map/pallas_call | solution.py:371
  162.6 7.7 all-to-all-done.up_a.down_a
  177.6 6.0 fusion.48
  183.6 27.1 %shard_map.299 = (f32[64,2,8,1152]{3,2,1,0:T(8,128)}, f32[2,16,8,1152]{3,2,1,0:T(8,128)}) custom-call(f32[64,2,8,1152]{3,2,1,0:T(8,128)} %compare_select_fusion.step_ref, f32[64,2,8,1152]{3,2,1,0:T(8,128)} %get-tuple-element.267.input_ref, f32[2,64,16,8,128]{4,3,2,1,0:T(8,128)} %broadcast_in_dim.28.mix_in_ref, ...), custom_call_target="tpu_custom_call" | custom-call | flops 132120576 | bytes 352092 | tf_op jit(solution)/shard_map/pallas_call | solution.py:371
  217.4 7.0 fusion.50
  228.2 8.1 %collective-permute-done.5 = f32[1024,1152]{1,0:T(8,128)S(1)} collective-permute-done((f32[1024,1152]{1,0:T(8,128)}, f32[1024,1152]{1,0:T(8,128)S(1)}, u32[]{:S(2)}, u32[]{:S(2)}) %collective-permute-start.5) | collective-permute-done | bytes 4718624 | tf_op jit(solution)/shard_map/ppermute | solution.py:34
  251.9 40.5 %collective-permute-done.6.down_b = bf16[8,144,768]{2,1,0:T(8,128)(2,1)} collective-permute-done((bf16[8,144,768]{2,1,0:T(8,128)(2,1)S(1)}, bf16[8,144,768]{2,1,0:T(8,128)(2,1)}, u32[]{:S(2)}, u32[]{:S(2)}) %collective-permute-start.6) | collective-permute-done | bytes 1769504 | tf_op jit(solution)/shard_map/ppermute | solution.py:34
  292.4 12.0 %all-to-all-done.2 = bf16[8,128,1152]{2,1,0:T(8,128)(2,1)} async-done(((bf16[8,128,1152]{2,1,0:T(8,128)(2,1)}), bf16[8,128,1152]{2,1,0:T(8,128)(2,1)}, u32[]{:S(2)}, u32[]{:S(2)}) %all-to-all-start.2) | async-done | bytes 2359328 | tf_op jit(solution)/shard_map/all_to_all | solution.py:594
  309.3 23.6 %shard_map.300 = (f32[1024,1152]{1,0:T(8,128)}, f32[1024,1152]{1,0:T(8,128)}, f32[1024,8]{1,0:T(8,128)}, bf16[2048,1152]{1,0:T(8,128)(2,1)}, bf16[2048,1152]{1,0...) custom-call(bf16[1024,1152]{1,0:T(8,128)(2,1)} %collective-permute-d, ...), custom_call_target="tpu_custom_call" | custom-call | flops 14495514624 | bytes 29884416 | tf_op jit(solution)/shard_map/pallas_call | solution.py:562
  333.5 23.6 %shard_map.301 = (f32[1024,1152]{1,0:T(8,128)}, f32[1024,1152]{1,0:T(8,128)}, f32[1024,8]{1,0:T(8,128)}, bf16[2048,1152]{1,0:T(8,128)(2,1)}, bf16[2048,1152]{1,0...) custom-call(bf16[1024,1152]{1,0:T(8,128)(2,1)} %bitcast.32.rows_ref,, ...), custom_call_target="tpu_custom_call", output_to_operand_aliasing={{3}: (8, {}), {4}: (9, {}), {5}: (10, {}), {6}: (11, {}), {... | custom-call | flops 14495514624 | bytes 29884416 | tf_op jit(solution)/shard_map/pallas_call | solution.py:562
  358.5 6.6 add_convert_fusion.5
  374.0 7.4 convolution_convert_fusion.3
  381.5 7.6 convolution_convert_fusion.4
  398.1 5.8 fusion.95
  403.9 18.3 %collective-permute-done.11 = bf16[1152,768]{1,0:T(8,128)(2,1)} collective-permute-done((bf16[1152,768]{1,0:T(8,128)(2,1)S(1)}, bf16[1152,768]{1,0:T(8,128)(2,1)}, u32[]{:S(2)}, u32[]{:S(2)}) %collective-permute-start.11) | collective-permute-done | bytes 1769504 | tf_op jit(solution)/shard_map/ppermute | solution.py:34
  422.2 5.8 all-to-all-done.3
  428.0 5.8 fusion.34
  448.5 7.4 fusion.49
  460.6 18.9 %shard_map.302 = (f32[2,16,8,1152]{3,2,1,0:T(8,128)}, f32[2,16,8,1152]{3,2,1,0:T(8,128)}, f32[2,16,1152]{2,1,0:T(8,128)}) custom-call(f32[64,2,8,1152]{3,2,1,0:T(8,128)} %compare_select_fusion.step_ref, f32[2,64,16,8,128]{4,3,2,1,0:T(8,128)} %broadcast_in_dim.30.mix_out_ref, f32[64,2,8,1152]{3,2,1,0:T(8,128)} %get-tuple-element.271.grad_ref, ...), custom_call_target="tpu_custom_call" | custom-call | flops 94371840 | bytes 209223 | tf_op jit(solution)/shard_map/pallas_call | solution.py:371
  479.5 8.3 %fusion.38 = f32[1152,1152]{1,0:T(8,128)} fusion(bf16[1024,1152]{1,0:T(8,128)(2,1)S(1)} %bitcast.225, bf16[1024,1152]{1,0:T(8,128)(2,1)} %bitcast.227, pred[]{:T(512)S(6)} %eq.66, f32[1024,1152]{1,0:T(8,128)} %copy-done.7, bf16[1024,1152]{1,0:T(8,128)(2,1)S(1)} %bitcast.166, f32[1152]{0:T(1024)S(1)} %get-tuple-element.258, f32[1024]{0:T(1024)S(1)} %add_rsqrt_fusion.1), kind=kOutput, calls=%fused_computation.81 | convolution fusion | flops 2726166528 | bytes 17113600 | tf_op jit(solution)/shard_map/dot_general | solution.py:76
  507.2 8.1 %fusion.47 = f32[1024,1152]{1,0:T(8,128)} fusion(bf16[1024,1152]{1,0:T(8,128)(2,1)} %bitcast.228, bf16[1152,1152]{1,0:T(8,128)(2,1)} %collective-permute-done.3, bf16[1152,1152]{1,0:T(8,128)(2,1)} %bitcast.14, pred[]{:T(512)S(6)} %eq.66), kind=kOutput, calls=%fused_computation.97 | convolution fusion | flops 2719236096 | bytes 12386305 | tf_op jit(solution)/shard_map/dot_general | solution.py:86
  518.6 69.2 %shard_map.303 = (bf16[64,2,8,1152]{3,2,1,0:T(8,128)(2,1)}, f32[64,2,8,1152]{3,2,1,0:T(8,128)}, f32[2,16,1152]{2,1,0:T(8,128)}, f32[2,8,1152]{2,1,0:T(8,128)}, f32[64,2,8,128]{3,2,1,0:T(8,128)}) custom-call(f32[64,2,8,1152]{3,2,1,0:T(8,128)} %compare_select_fusion.step_ref, f32[64,2,8,1152]{3,2,1,0:T(8,128)} %get-tuple-element.267.input_ref, ...), custom_call_target="tpu_custom_call" | custom-call | flops 377487360 | bytes 430371 | tf_op jit(solution)/shard_map/pallas_call | solution.py:371
  593.2 6.1 all-to-all-start.6
  625.0 13.3 %shard_map.304 = (bf16[64,16,1152]{2,1,0:T(8,128)(2,1)}, f32[8,1152]{1,0:T(8,128)}, f32[3,16,1152]{2,1,0:T(8,128)}, f32[3,16,1152]{2,1,0:T(8,128)}) custom-call(bf16[1024,104]{1,0:T(8,128)(2,1)} %add_convert_fusion.6.proj_ref, bf16[104,1152]{1,0:T(8,128)(2,1)} %slice.210.weight_ref, f32[64,16,1152]{2,1,0:T(8,128)} %bitcast.195, ...), custom_call_target="tpu_custom_call" | custom-call | flops 1 | bytes 1 | tf_op jit(solution)/shard_map/pallas_call | solution.py:486
  649.2 9.8 %all-to-all-done.6 = bf16[8,144,1152]{2,1,0:T(8,128)(2,1)} async-done(((bf16[8,144,1152]{2,1,0:T(8,128)(2,1)}), bf16[8,144,1152]{2,1,0:T(8,128)(2,1)}, u32[]{:S(2)}, u32[]{:S(2)}) %all-to-all-start.6) | async-done | bytes 2654240 | tf_op jit(solution)/shard_map/all_to_all | solution.py:1103
  659.8 6.1 fusion.97
  666.5 7.5 fusion.35
  703.9 8.7 %collective-permute-done.22 = f32[144,1152]{1,0:T(8,128)S(1)} collective-permute-done((f32[144,1152]{1,0:T(8,128)S(1)}, f32[144,1152]{1,0:T(8,128)S(1)}, u32[]{:S(2)}, u32[]{:S(2)}) %collective-permute-start.22) | collective-permute-done | bytes 663584 | tf_op jit(solution)/shard_map/ppermute | solution.py:34
  722.6 31.4 %collective-permute-done.23 = bf16[8,144,768]{2,1,0:T(8,128)(2,1)} collective-permute-done((bf16[8,144,768]{2,1,0:T(8,128)(2,1)S(1)}, bf16[8,144,768]{2,1,0:T(8,128)(2,1)}, u32[]{:S(2)}, u32[]{:S(2)}) %collective-permute-start.23) | collective-permute-done | bytes 1769504 | tf_op jit(solution)/shard_map/ppermute | solution.py:34
  754.0 9.4 %all-to-all-done.7 = bf16[8,171,1152]{2,1,0:T(8,128)(2,1)} async-done(((bf16[8,171,1152]{2,1,0:T(8,128)(2,1)}), bf16[8,171,1152]{2,1,0:T(8,128)(2,1)}, u32[]{:S(2)}, u32[]{:S(2)}) %all-to-all-start.7) | async-done | bytes 3151904 | tf_op jit(solution)/shard_map/all_to_all | solution.py:1173
  (391 shorter events, 279.7 us)
Async XLA Ops:
  80.9 13.0 %collective-permute-start = (bf16[3,2,1,1152]{3,2,1,0:T(2,128)(2,1)S(1)}, bf16[3,2,1,1152]{3,2,1,0:T(2,128)(2,1)S(1)}, u32[]{:S(2)}, u32[]{:S(2)}) collective-permute-start(bf16[3,2,1,1152]{3,2,1,0:T(2,128)(2,1)S(1)} %slice.253), channel_id=1, source_target_pairs={{0,2},{1,3},{4,6},{5,7},{8,10},{9,11},{12,14},{13,15},{16,18},{17,... | collective-permute-start | bytes 41480 | tf_op jit(solution)/shard_map/ppermute | solution.py:40
  87.3 83.0 %all-to-all-start = ((bf16[8,288,768]{2,1,0:T(8,128)(2,1)}), bf16[8,288,768]{2,1,0:T(8,128)(2,1)}, u32[]{:S(2)}, u32[]{:S(2)}) async-start(bf16[8,288,768]{2,1,0:T(8,128)(2,1)} %slice_select_fusion), calls=%async_computation | async-start | bytes 7077888 | tf_op jit(solution)/shard_map/all_to_all | solution.py:611
  101.0 76.6 %collective-permute-start.3 = (bf16[1152,1152]{1,0:T(8,128)(2,1)}, bf16[1152,1152]{1,0:T(8,128)(2,1)}, u32[]{:S(2)}, u32[]{:S(2)}) collective-permute-start(bf16[1152,1152]{1,0:T(8,128)(2,1)} %bitcast.14), channel_id=1, source_target_pairs={{0,2},{2,0},{1,3},{3,1},{4,6},{6,4},{5,7},{7,5},{8,10},{10,8},{9,1... | collective-permute-start | bytes 7962632 | tf_op jit(solution)/shard_map/ppermute | solution.py:34
  153.1 9.6 %collective-permute-start.2 = (f32[2,16,1152]{2,1,0:T(8,128)S(1)}, f32[2,16,1152]{2,1,0:T(8,128)S(1)}, u32[]{:S(2)}, u32[]{:S(2)}) collective-permute-start(f32[2,16,1152]{2,1,0:T(8,128)S(1)} %copy-done.58), channel_id=1, source_target_pairs={{0,2},{1,3},{4,6},{5,7},{8,10},{9,11},{12,14},{13,15},{16,18},{17,... | collective-permute-start | bytes 442376 | tf_op jit(solution)/shard_map/ppermute | solution.py:40
  170.4 57.8 %all-to-all-start.1 = ((bf16[8,128,1152]{2,1,0:T(8,128)(2,1)}), bf16[8,128,1152]{2,1,0:T(8,128)(2,1)}, u32[]{:S(2)}, u32[]{:S(2)}) async-start(bf16[8,128,1152]{2,1,0:T(8,128)(2,1)} %bitcast.221), calls=%async_computation.1 | async-start | bytes 4718592 | tf_op jit(solution)/shard_map/all_to_all | solution.py:594
  177.6 39.8 %collective-permute-start.4 = (bf16[8,144,768]{2,1,0:T(8,128)(2,1)}, bf16[8,144,768]{2,1,0:T(8,128)(2,1)}, u32[]{:S(2)}, u32[]{:S(2)}) collective-permute-start(bf16[8,144,768]{2,1,0:T(8,128)(2,1)} %slice.222), channel_id=1, source_target_pairs={{0,2},{2,0},{1,3},{3,1},{4,6},{6,4},{5,7},{7,5},{8,10},{10,8},{9,1... | collective-permute-start | bytes 5308424 | tf_op jit(solution)/shard_map/ppermute | solution.py:34
  228.2 8.1 %collective-permute-start.5 = (f32[1024,1152]{1,0:T(8,128)}, f32[1024,1152]{1,0:T(8,128)S(1)}, u32[]{:S(2)}, u32[]{:S(2)}) collective-permute-start(f32[1024,1152]{1,0:T(8,128)} %fusion.50), channel_id=1, source_target_pairs={{0,1},{1,0},{2,3},{3,2},{4,5},{5,4},{6,7},{7,6},{8,9},{9,8},{10,11... | collective-permute-start | bytes 14155784 | tf_op jit(solution)/shard_map/ppermute | solution.py:34
  245.1 59.3 %all-to-all-start.2 = ((bf16[8,128,1152]{2,1,0:T(8,128)(2,1)}), bf16[8,128,1152]{2,1,0:T(8,128)(2,1)}, u32[]{:S(2)}, u32[]{:S(2)}) async-start(bf16[8,128,1152]{2,1,0:T(8,128)(2,1)} %bitcast.222), calls=%async_computation.2 | async-start | bytes 4718592 | tf_op jit(solution)/shard_map/all_to_all | solution.py:594
  251.6 40.8 %collective-permute-start.6 = (bf16[8,144,768]{2,1,0:T(8,128)(2,1)S(1)}, bf16[8,144,768]{2,1,0:T(8,128)(2,1)}, u32[]{:S(2)}, u32[]{:S(2)}) collective-permute-start(bf16[8,144,768]{2,1,0:T(8,128)(2,1)S(1)} %slice.225), channel_id=1, source_target_pairs={{0,2},{2,0},{1,3},{3,1},{4,6},{6,4},{5,7},{7,5},{8,10},{10,8},{9,1... | collective-permute-start | bytes 5308424 | tf_op jit(solution)/shard_map/ppermute | solution.py:34
  251.7 53.9 %collective-permute-start.8 = (bf16[1024,1152]{1,0:T(8,128)(2,1)}, bf16[1024,1152]{1,0:T(8,128)(2,1)}, u32[]{:S(2)}, u32[]{:S(2)}) collective-permute-start(bf16[1024,1152]{1,0:T(8,128)(2,1)} %bitcast.33.cotan_ref), channel_id=1, source_target_pairs={{0,1},{1,0},{2,3},{3,2},{4,5},{5,4},{6,7},{7,6},{8,9},{9,8},{10,11... | collective-permute-start | bytes 7077896 | tf_op jit(solution)/shard_map/ppermute | solution.py:34
  304.4 4.9 collective-permute-start.7
  332.9 25.6 %collective-permute-start.10 = (f32[1024,1152]{1,0:T(8,128)}, f32[1024,1152]{1,0:T(8,128)}, u32[]{:S(2)}, u32[]{:S(2)}) collective-permute-start(f32[1024,1152]{1,0:T(8,128)} %get-tuple-element.146), channel_id=1, source_target_pairs={{0,1},{1,0},{2,3},{3,2},{4,5},{5,4},{6,7},{7,6},{8,9},{9,8},{10,11... | collective-permute-start | bytes 14155784 | tf_op jit(solution)/shard_map/ppermute | solution.py:34
  333.1 32.0 %collective-permute-start.9 = (f32[1024,1152]{1,0:T(8,128)}, f32[1024,1152]{1,0:T(8,128)S(1)}, u32[]{:S(2)}, u32[]{:S(2)}) collective-permute-start(f32[1024,1152]{1,0:T(8,128)} %get-tuple-element.144), channel_id=1, source_target_pairs={{0,1},{1,0},{2,3},{3,2},{4,5},{5,4},{6,7},{7,6},{8,9},{9,8},{10,11... | collective-permute-start | bytes 14155784 | tf_op jit(solution)/shard_map/ppermute | solution.py:34
  369.2 58.8 %all-to-all-start.3 = ((bf16[8,128,1152]{2,1,0:T(8,128)(2,1)}), bf16[8,128,1152]{2,1,0:T(8,128)(2,1)}, u32[]{:S(2)}, u32[]{:S(2)}) async-start(bf16[8,128,1152]{2,1,0:T(8,128)(2,1)} %bitcast.186), calls=%async_computation.3 | async-start | bytes 4718592 | tf_op jit(solution)/shard_map/all_to_all | solution.py:594
  381.3 40.8 %collective-permute-start.11 = (bf16[1152,768]{1,0:T(8,128)(2,1)S(1)}, bf16[1152,768]{1,0:T(8,128)(2,1)}, u32[]{:S(2)}, u32[]{:S(2)}) collective-permute-start(bf16[1152,768]{1,0:T(8,128)(2,1)S(1)} %convolution_convert_fusion.3), channel_id=1, source_target_pairs={{0,2},{2,0},{1,3},{3,1},{4,6},{6,4},{5,7},{7,5},{8,10},{10,8},{9,1... | collective-permute-start | bytes 5308424 | tf_op jit(solution)/shard_map/ppermute | solution.py:34
  397.9 6.0 collective-permute-start.12
  433.8 4.9 collective-permute-start.14
  433.8 59.2 %collective-permute-start.13 = (bf16[1152,768]{1,0:T(8,128)(2,1)}, bf16[1152,768]{1,0:T(8,128)(2,1)}, u32[]{:S(2)}, u32[]{:S(2)}) collective-permute-start(bf16[1152,768]{1,0:T(8,128)(2,1)} %convolution_convert_fusion.4), channel_id=1, source_target_pairs={{0,2},{2,0},{1,3},{3,1},{4,6},{6,4},{5,7},{7,5},{8,10},{10,8},{9,1... | collective-permute-start | bytes 5308424 | tf_op jit(solution)/shard_map/ppermute | solution.py:34
  433.8 59.3 %all-to-all-start.4 = ((bf16[8,128,1152]{2,1,0:T(8,128)(2,1)}), bf16[8,128,1152]{2,1,0:T(8,128)(2,1)}, u32[]{:S(2)}, u32[]{:S(2)}) async-start(bf16[8,128,1152]{2,1,0:T(8,128)(2,1)} %bitcast.188), calls=%async_computation.4 | async-start | bytes 4718592 | tf_op jit(solution)/shard_map/all_to_all | solution.py:594
  500.0 87.9 %all-to-all-start.5 = ((bf16[8,288,768]{2,1,0:T(8,128)(2,1)}), bf16[8,288,768]{2,1,0:T(8,128)(2,1)}, u32[]{:S(2)}, u32[]{:S(2)}) async-start(bf16[8,288,768]{2,1,0:T(8,128)(2,1)} %pad_maximum_fusion), calls=%async_computation.5 | async-start | bytes 7077888 | tf_op jit(solution)/shard_map/all_to_all | solution.py:1087
  505.6 9.7 %collective-permute-start.16 = (f32[2,16,1152]{2,1,0:T(8,128)S(1)}, f32[2,16,1152]{2,1,0:T(8,128)S(1)}, u32[]{:S(2)}, u32[]{:S(2)}) collective-permute-start(f32[2,16,1152]{2,1,0:T(8,128)S(1)} %copy-done.60), channel_id=1, source_target_pairs={{2,0},{3,1},{6,4},{7,5},{10,8},{11,9},{14,12},{15,13},{18,16},{19,... | collective-permute-start | bytes 442376 | tf_op jit(solution)/shard_map/ppermute | solution.py:40
  515.3 72.5 %collective-permute-start.17 = (bf16[1152,1152]{1,0:T(8,128)(2,1)S(1)}, bf16[1152,1152]{1,0:T(8,128)(2,1)}, u32[]{:S(2)}, u32[]{:S(2)}) collective-permute-start(bf16[1152,1152]{1,0:T(8,128)(2,1)S(1)} %copy-done.56), channel_id=1, source_target_pairs={{0,2},{2,0},{1,3},{3,1},{4,6},{6,4},{5,7},{7,5},{8,10},{10,8},{9,1... | collective-permute-start | bytes 7962632 | tf_op jit(solution)/shard_map/ppermute | solution.py:34
  593.2 65.8 %all-to-all-start.6 = ((bf16[8,144,1152]{2,1,0:T(8,128)(2,1)}), bf16[8,144,1152]{2,1,0:T(8,128)(2,1)}, u32[]{:S(2)}, u32[]{:S(2)}) async-start(bf16[8,144,1152]{2,1,0:T(8,128)(2,1)} %bitcast.184), calls=%async_computation.6 | async-start | bytes 5308416 | tf_op jit(solution)/shard_map/all_to_all | solution.py:1103
  605.3 44.0 %collective-permute-start.20 = (bf16[8,144,768]{2,1,0:T(8,128)(2,1)}, bf16[8,144,768]{2,1,0:T(8,128)(2,1)}, u32[]{:S(2)}, u32[]{:S(2)}) collective-permute-start(bf16[8,144,768]{2,1,0:T(8,128)(2,1)} %slice.228), channel_id=1, source_target_pairs={{0,2},{2,0},{1,3},{3,1},{4,6},{6,4},{5,7},{7,5},{8,10},{10,8},{9,1... | collective-permute-start | bytes 5308424 | tf_op jit(solution)/shard_map/ppermute | solution.py:34
  608.9 13.8 %collective-permute-start.18 = (f32[1024,104]{1,0:T(8,128)}, f32[1024,104]{1,0:T(8,128)}, u32[]{:S(2)}, u32[]{:S(2)}) collective-permute-start(f32[1024,104]{1,0:T(8,128)} %pad_maximum_fusion.4), channel_id=1, source_target_pairs={{0,1},{1,0},{2,3},{3,2},{4,5},{5,4},{6,7},{7,6},{8,9},{9,8},{10,11... | collective-permute-start | bytes 1277960 | tf_op jit(solution)/shard_map/ppermute | solution.py:34
  639.4 9.9 %collective-permute-start.19 = (f32[3,2,1,1152]{3,2,1,0:T(1,128)S(1)}, f32[3,2,1,1152]{3,2,1,0:T(1,128)S(1)}, u32[]{:S(2)}, u32[]{:S(2)}) collective-permute-start(f32[3,2,1,1152]{3,2,1,0:T(1,128)S(1)} %slice.269), channel_id=1, source_target_pairs={{2,0},{3,1},{6,4},{7,5},{10,8},{11,9},{14,12},{15,13},{18,16},{19,... | collective-permute-start | bytes 82952 | tf_op jit(solution)/shard_map/ppermute | solution.py:40
  666.4 12.5 %collective-permute-start.21 = (f32[1024,1152]{1,0:T(8,128)S(1)}, f32[1024,1152]{1,0:T(8,128)S(1)}, u32[]{:S(2)}, u32[]{:S(2)}) collective-permute-start(f32[1024,1152]{1,0:T(8,128)S(1)} %add.244), channel_id=1, source_target_pairs={{0,1},{1,0},{2,3},{3,2},{4,5},{5,4},{6,7},{7,6},{8,9},{9,8},{10,11... | collective-permute-start | bytes 14155784 | tf_op jit(solution)/shard_map/ppermute | solution.py:34
  674.0 21.6 %collective-permute-start.15 = (bf16[1024,1152]{1,0:T(8,128)(2,1)}, bf16[1024,1152]{1,0:T(8,128)(2,1)}, u32[]{:S(2)}, u32[]{:S(2)}) collective-permute-start(bf16[1024,1152]{1,0:T(8,128)(2,1)} %fusion.35), channel_id=1, source_target_pairs={{0,1},{1,0},{2,3},{3,2},{4,5},{5,4},{6,7},{7,6},{8,9},{9,8},{10,11... | collective-permute-start | bytes 7077896 | tf_op jit(solution)/shard_map/ppermute | solution.py:34
  684.8 78.6 %all-to-all-start.7 = ((bf16[8,171,1152]{2,1,0:T(8,128)(2,1)}), bf16[8,171,1152]{2,1,0:T(8,128)(2,1)}, u32[]{:S(2)}, u32[]{:S(2)}) async-start(bf16[8,171,1152]{2,1,0:T(8,128)(2,1)} %pad_maximum_fusion.1), calls=%async_computation.7 | async-start | bytes 6488064 | tf_op jit(solution)/shard_map/all_to_all | solution.py:1173
  695.3 17.4 %collective-permute-start.22 = (f32[144,1152]{1,0:T(8,128)S(1)}, f32[144,1152]{1,0:T(8,128)S(1)}, u32[]{:S(2)}, u32[]{:S(2)}) collective-permute-start(f32[144,1152]{1,0:T(8,128)S(1)} %convert_reduce_fusion), channel_id=1, source_target_pairs={{0,2},{2,0},{1,3},{3,1},{4,6},{6,4},{5,7},{7,5},{8,10},{10,8},{9,1... | collective-permute-start | bytes 1990664 | tf_op jit(solution)/shard_map/ppermute | solution.py:34
  713.6 40.4 %collective-permute-start.23 = (bf16[8,144,768]{2,1,0:T(8,128)(2,1)S(1)}, bf16[8,144,768]{2,1,0:T(8,128)(2,1)}, u32[]{:S(2)}, u32[]{:S(2)}) collective-permute-start(bf16[8,144,768]{2,1,0:T(8,128)(2,1)S(1)} %get-tuple-element.194), channel_id=1, source_target_pairs={{0,2},{2,0},{1,3},{3,1},{4,6},{6,4},{5,7},{7,5},{8,10},{10,8},{9,1... | collective-permute-start | bytes 5308424 | tf_op jit(solution)/shard_map/ppermute | solution.py:34
  769.5 11.1 %collective-permute-start.24 = (bf16[171,1152]{1,0:T(8,128)(2,1)S(1)}, bf16[171,1152]{1,0:T(8,128)(2,1)S(1)}, u32[]{:S(2)}, u32[]{:S(2)}) collective-permute-start(bf16[171,1152]{1,0:T(8,128)(2,1)S(1)} %reduce_sum.152), channel_id=1, source_target_pairs={{0,2},{2,0},{1,3},{3,1},{4,6},{6,4},{5,7},{7,5},{8,10},{10,8},{9,1... | collective-permute-start | bytes 1181960 | tf_op jit(solution)/shard_map/ppermute | solution.py:34
  (88 other events, 796.1 us)

commit v12 on v11

--- a/solution.py
+++ b/solution.py
@@ -1170,9 +1170,10 @@
     gain_row = jnp.pad(gain_row, ((0, 0), (0, 0), (0, inner - 2 * shard)))
     in_x_part, out_blocks = together(in_x_part, out_blocks)
     out_proj_grad, in_z_grad = product_shards(out_blocks)
-    in_x_blocks = lax.all_to_all(
-        jnp.concatenate([in_x_part, small_rows, gain_row], axis=1), "dp", 0, 0, tiled=True
-    )
+    in_x_part, got_out, normed_two_bf = together(
+        jnp.concatenate([in_x_part, small_rows, gain_row], axis=1), got_out, normed_two_bf
+    )
+    in_x_blocks = lax.all_to_all(in_x_part, "dp", 0, 0, tiled=True)
     out_proj_grad, in_z_grad, far_down_blocks = together(
         out_proj_grad, in_z_grad, weight_blocks[:, shard:]
     )

time: 795 us -> 791 us (level)
  transfers between devices with their start and end apart: 33 -> 33, of which waited for: 17 -> 17; matrix products, arithmetic and copies ran while one was open for 29% -> 28% of each run, Pallas kernels for 22% -> 22%
where the time goes in v12:
time: 791 us; the launch traced here: 783 us
  Pallas kernels  258 us (33%)
  waiting for transfers between devices  169 us (21%)
  matrix products  118 us (15%)
  other arithmetic  101 us (13%)
  local copies, waits for them, and re-layouts  79.3 us (10%)
  starting transfers between devices  55.1 us (7%)
    pallas_call x4, Pallas kernels, call(): pl.pallas_call(kernel, grid=self.grid, in_specs=in_specs, out_specs=out_s...  134 us
    ppermute x21, waiting for transfers between devices, swapped(): return lax.ppermute(value, axis, [(0, 1), (1, 0)])  116 us
    pallas_call x1, Pallas kernels, gathered(): pl.pallas_call(partial(gather_kernel, count, number, parts), in_specs=[an...  63.5 us
    dot_general x11, matrix products, contract_rows(): lax.dot_general(left_side, right_side, (((0,), (0,)), ((), ())), precisio...  62 us
    pallas_call x2, Pallas kernels, expert_call(): pl.pallas_call(partial(expert_kernel, len(kept)), grid=(count // block,),...  47.2 us
    dot_general x6, matrix products, contract_cols(): lax.dot_general(left_side, right_side, (((1,), (1,)), ((), ())), precisio...  23.6 us
    all_to_all x4, waiting for transfers between devices, expert_exchange(): lax.all_to_all(value, 'dp', 0, 0, axis_index_groups=groups, tiled=True)  21.7 us
    all_to_all x4, starting transfers between devices, expert_exchange(): lax.all_to_all(value, 'dp', 0, 0, axis_index_groups=groups, tiled=True)  18.6 us
  transfers between devices with their start and end apart: 33, of which 17 were waited for; matrix products, arithmetic and copies ran while one was open for 28% of the time, Pallas kernels for 22%

profile of v12, /device:TPU:0, one launch (start us, length us, event | category | flops | bytes accessed | tf_op | source)
XLA Modules:
  0.0 783.1 jit_solution(14845741049441081792)
XLA Ops:
  6.8 63.5 %shard_map.297 = (bf16[8,144,1152]{2,1,0:T(8,128)(2,1)}, bf16[8,144,256]{2,1,0:T(8,128)(2,1)}, bf16[8,144,1152]{2,1,0:T(8,128)(2,1)}) custom-call(bf16[144,1152]{1,0:T(8,128)(2,1)} %bitcast.236, bf16[144,256]{1,0:T(8,128)(2,1)} %pad.62.refs_1_, bf16[144,1152]{1,0:T(8,128)(2,1)} %fusion.54.refs_2_), custom_call_target="tpu_custom_call" | custom-call | bytes 11796480 | tf_op jit(solution)/shard_map/pallas_call | solution.py:746
  87.3 5.8 all-to-all-start
  119.3 19.0 %shard_map.298 = (f32[2,16,8,1152]{3,2,1,0:T(8,128)}, f32[2,16,8,1152]{3,2,1,0:T(8,128)}, f32[2,16,1152]{2,1,0:T(8,128)}) custom-call(f32[64,2,8,1152]{3,2,1,0:T(8,128)} %compare_select_fusion.step_ref, f32[64,2,8,1152]{3,2,1,0:T(8,128)} %get-tuple-element.273.input_ref, f32[2,64,16,8,128]{4,3,2,1,0:T(8,128)} %broadcast_in_dim.28.mix_in_ref, ...), custom_call_target="tpu_custom_call" | custom-call | flops 94371840 | bytes 209223 | tf_op jit(solution)/shard_map/pallas_call | solution.py:371
  162.6 7.7 all-to-all-done.up_a.down_a
  177.6 6.0 fusion.48
  183.6 27.0 %shard_map.299 = (f32[64,2,8,1152]{3,2,1,0:T(8,128)}, f32[2,16,8,1152]{3,2,1,0:T(8,128)}) custom-call(f32[64,2,8,1152]{3,2,1,0:T(8,128)} %compare_select_fusion.step_ref, f32[64,2,8,1152]{3,2,1,0:T(8,128)} %get-tuple-element.273.input_ref, f32[2,64,16,8,128]{4,3,2,1,0:T(8,128)} %broadcast_in_dim.28.mix_in_ref, ...), custom_call_target="tpu_custom_call" | custom-call | flops 132120576 | bytes 352092 | tf_op jit(solution)/shard_map/pallas_call | solution.py:371
  217.4 7.0 fusion.50
  228.1 8.1 %collective-permute-done.5 = f32[1024,1152]{1,0:T(8,128)S(1)} collective-permute-done((f32[1024,1152]{1,0:T(8,128)}, f32[1024,1152]{1,0:T(8,128)S(1)}, u32[]{:S(2)}, u32[]{:S(2)}) %collective-permute-start.5) | collective-permute-done | bytes 4718624 | tf_op jit(solution)/shard_map/ppermute | solution.py:34
  253.5 40.5 %collective-permute-done.6.down_b = bf16[8,144,768]{2,1,0:T(8,128)(2,1)} collective-permute-done((bf16[8,144,768]{2,1,0:T(8,128)(2,1)S(1)}, bf16[8,144,768]{2,1,0:T(8,128)(2,1)}, u32[]{:S(2)}, u32[]{:S(2)}) %collective-permute-start.6) | collective-permute-done | bytes 1769504 | tf_op jit(solution)/shard_map/ppermute | solution.py:34
  294.0 12.0 %all-to-all-done.2 = bf16[8,128,1152]{2,1,0:T(8,128)(2,1)} async-done(((bf16[8,128,1152]{2,1,0:T(8,128)(2,1)}), bf16[8,128,1152]{2,1,0:T(8,128)(2,1)}, u32[]{:S(2)}, u32[]{:S(2)}) %all-to-all-start.2) | async-done | bytes 2359328 | tf_op jit(solution)/shard_map/all_to_all | solution.py:594
  310.9 23.6 %shard_map.300 = (f32[1024,1152]{1,0:T(8,128)}, f32[1024,1152]{1,0:T(8,128)}, f32[1024,8]{1,0:T(8,128)}, bf16[2048,1152]{1,0:T(8,128)(2,1)}, bf16[2048,1152]{1,0...) custom-call(bf16[1024,1152]{1,0:T(8,128)(2,1)} %collective-permute-d, ...), custom_call_target="tpu_custom_call" | custom-call | flops 14495514624 | bytes 29884416 | tf_op jit(solution)/shard_map/pallas_call | solution.py:562
  335.1 23.6 %shard_map.301 = (f32[1024,1152]{1,0:T(8,128)}, f32[1024,1152]{1,0:T(8,128)}, f32[1024,8]{1,0:T(8,128)}, bf16[2048,1152]{1,0:T(8,128)(2,1)}, bf16[2048,1152]{1,0...) custom-call(bf16[1024,1152]{1,0:T(8,128)(2,1)} %bitcast.33.rows_ref,, ...), custom_call_target="tpu_custom_call", output_to_operand_aliasing={{3}: (8, {}), {4}: (9, {}), {5}: (10, {}), {6}: (11, {}), {... | custom-call | flops 14495514624 | bytes 29884416 | tf_op jit(solution)/shard_map/pallas_call | solution.py:562
  360.1 6.6 add_convert_fusion.5
  375.6 7.4 convolution_convert_fusion.3
  383.0 7.6 convolution_convert_fusion.4
  390.7 5.7 fusion.96
  399.7 5.8 fusion.95
  405.5 18.3 %collective-permute-done.11 = bf16[1152,768]{1,0:T(8,128)(2,1)} collective-permute-done((bf16[1152,768]{1,0:T(8,128)(2,1)S(1)}, bf16[1152,768]{1,0:T(8,128)(2,1)}, u32[]{:S(2)}, u32[]{:S(2)}) %collective-permute-start.11) | collective-permute-done | bytes 1769504 | tf_op jit(solution)/shard_map/ppermute | solution.py:34
  423.8 5.8 all-to-all-done.3
  429.6 5.8 fusion.34
  450.1 7.4 fusion.49
  462.1 18.9 %shard_map.302 = (f32[2,16,8,1152]{3,2,1,0:T(8,128)}, f32[2,16,8,1152]{3,2,1,0:T(8,128)}, f32[2,16,1152]{2,1,0:T(8,128)}) custom-call(f32[64,2,8,1152]{3,2,1,0:T(8,128)} %compare_select_fusion.step_ref, f32[2,64,16,8,128]{4,3,2,1,0:T(8,128)} %broadcast_in_dim.30.mix_out_ref, f32[64,2,8,1152]{3,2,1,0:T(8,128)} %get-tuple-element.278.grad_ref, ...), custom_call_target="tpu_custom_call" | custom-call | flops 94371840 | bytes 209223 | tf_op jit(solution)/shard_map/pallas_call | solution.py:371
  481.1 8.3 %fusion.38 = f32[1152,1152]{1,0:T(8,128)} fusion(bf16[1024,1152]{1,0:T(8,128)(2,1)S(1)} %bitcast.227, bf16[1024,1152]{1,0:T(8,128)(2,1)} %bitcast.229, pred[]{:T(512)S(6)} %eq.66, f32[1024,1152]{1,0:T(8,128)} %copy-done.7, bf16[1024,1152]{1,0:T(8,128)(2,1)S(1)} %bitcast.168, f32[1152]{0:T(1024)S(1)} %get-tuple-element.264, f32[1024]{0:T(1024)S(1)} %add_rsqrt_fusion.1), kind=kOutput, calls=%fused_computation.81 | convolution fusion | flops 2726166528 | bytes 17113600 | tf_op jit(solution)/shard_map/dot_general | solution.py:76
  501.6 5.6 all-to-all-start.5
  508.7 8.1 %fusion.47 = f32[1024,1152]{1,0:T(8,128)} fusion(bf16[1024,1152]{1,0:T(8,128)(2,1)} %bitcast.230, bf16[1152,1152]{1,0:T(8,128)(2,1)} %collective-permute-done.3, bf16[1152,1152]{1,0:T(8,128)(2,1)} %bitcast.14, pred[]{:T(512)S(6)} %eq.66), kind=kOutput, calls=%fused_computation.97 | convolution fusion | flops 2719236096 | bytes 12386305 | tf_op jit(solution)/shard_map/dot_general | solution.py:86
  520.3 69.2 %shard_map.303 = (bf16[64,2,8,1152]{3,2,1,0:T(8,128)(2,1)}, f32[64,2,8,1152]{3,2,1,0:T(8,128)}, f32[2,16,1152]{2,1,0:T(8,128)}, f32[2,8,1152]{2,1,0:T(8,128)}, f32[64,2,8,128]{3,2,1,0:T(8,128)}) custom-call(f32[64,2,8,1152]{3,2,1,0:T(8,128)} %compare_select_fusion.step_ref, f32[64,2,8,1152]{3,2,1,0:T(8,128)} %get-tuple-element.273.input_ref, ...), custom_call_target="tpu_custom_call" | custom-call | flops 377487360 | bytes 430371 | tf_op jit(solution)/shard_map/pallas_call | solution.py:371
  594.9 6.1 all-to-all-start.6
  626.8 13.2 %shard_map.304 = (bf16[64,16,1152]{2,1,0:T(8,128)(2,1)}, f32[8,1152]{1,0:T(8,128)}, f32[3,16,1152]{2,1,0:T(8,128)}, f32[3,16,1152]{2,1,0:T(8,128)}) custom-call(bf16[1024,104]{1,0:T(8,128)(2,1)} %add_convert_fusion.6.proj_ref, bf16[104,1152]{1,0:T(8,128)(2,1)} %slice.210.weight_ref, f32[64,16,1152]{2,1,0:T(8,128)} %bitcast.197, ...), custom_call_target="tpu_custom_call" | custom-call | flops 1 | bytes 1 | tf_op jit(solution)/shard_map/pallas_call | solution.py:486
  650.9 9.7 %all-to-all-done.6 = bf16[8,144,1152]{2,1,0:T(8,128)(2,1)} async-done(((bf16[8,144,1152]{2,1,0:T(8,128)(2,1)}), bf16[8,144,1152]{2,1,0:T(8,128)(2,1)}, u32[]{:S(2)}, u32[]{:S(2)}) %all-to-all-start.6) | async-done | bytes 2654240 | tf_op jit(solution)/shard_map/all_to_all | solution.py:1103
  661.4 6.1 fusion.97
  715.1 31.4 %collective-permute-done.23 = bf16[8,144,768]{2,1,0:T(8,128)(2,1)} collective-permute-done((bf16[8,144,768]{2,1,0:T(8,128)(2,1)S(1)}, bf16[8,144,768]{2,1,0:T(8,128)(2,1)}, u32[]{:S(2)}, u32[]{:S(2)}) %collective-permute-start.23) | collective-permute-done | bytes 1769504 | tf_op jit(solution)/shard_map/ppermute | solution.py:34
  746.4 13.5 %all-to-all-done.7 = bf16[8,171,1152]{2,1,0:T(8,128)(2,1)} async-done(((bf16[8,171,1152]{2,1,0:T(8,128)(2,1)}), bf16[8,171,1152]{2,1,0:T(8,128)(2,1)}, u32[]{:S(2)}, u32[]{:S(2)}) %all-to-all-start.7) | async-done | bytes 3151904 | tf_op jit(solution)/shard_map/all_to_all | solution.py:1176
  (394 shorter events, 276.0 us)
Async XLA Ops:
  80.8 13.0 %collective-permute-start = (bf16[3,2,1,1152]{3,2,1,0:T(2,128)(2,1)S(1)}, bf16[3,2,1,1152]{3,2,1,0:T(2,128)(2,1)S(1)}, u32[]{:S(2)}, u32[]{:S(2)}) collective-permute-start(bf16[3,2,1,1152]{3,2,1,0:T(2,128)(2,1)S(1)} %slice.253), channel_id=1, source_target_pairs={{0,2},{1,3},{4,6},{5,7},{8,10},{9,11},{12,14},{13,15},{16,18},{17,... | collective-permute-start | bytes 41480 | tf_op jit(solution)/shard_map/ppermute | solution.py:40
  87.3 83.0 %all-to-all-start = ((bf16[8,288,768]{2,1,0:T(8,128)(2,1)}), bf16[8,288,768]{2,1,0:T(8,128)(2,1)}, u32[]{:S(2)}, u32[]{:S(2)}) async-start(bf16[8,288,768]{2,1,0:T(8,128)(2,1)} %slice_select_fusion), calls=%async_computation | async-start | bytes 7077888 | tf_op jit(solution)/shard_map/all_to_all | solution.py:611
  100.9 76.7 %collective-permute-start.3 = (bf16[1152,1152]{1,0:T(8,128)(2,1)}, bf16[1152,1152]{1,0:T(8,128)(2,1)}, u32[]{:S(2)}, u32[]{:S(2)}) collective-permute-start(bf16[1152,1152]{1,0:T(8,128)(2,1)} %bitcast.14), channel_id=1, source_target_pairs={{0,2},{2,0},{1,3},{3,1},{4,6},{6,4},{5,7},{7,5},{8,10},{10,8},{9,1... | collective-permute-start | bytes 7962632 | tf_op jit(solution)/shard_map/ppermute | solution.py:34
  153.0 9.6 %collective-permute-start.2 = (f32[2,16,1152]{2,1,0:T(8,128)S(1)}, f32[2,16,1152]{2,1,0:T(8,128)S(1)}, u32[]{:S(2)}, u32[]{:S(2)}) collective-permute-start(f32[2,16,1152]{2,1,0:T(8,128)S(1)} %copy-done.59), channel_id=1, source_target_pairs={{0,2},{1,3},{4,6},{5,7},{8,10},{9,11},{12,14},{13,15},{16,18},{17,... | collective-permute-start | bytes 442376 | tf_op jit(solution)/shard_map/ppermute | solution.py:40
  170.3 57.8 %all-to-all-start.1 = ((bf16[8,128,1152]{2,1,0:T(8,128)(2,1)}), bf16[8,128,1152]{2,1,0:T(8,128)(2,1)}, u32[]{:S(2)}, u32[]{:S(2)}) async-start(bf16[8,128,1152]{2,1,0:T(8,128)(2,1)} %bitcast.223), calls=%async_computation.1 | async-start | bytes 4718592 | tf_op jit(solution)/shard_map/all_to_all | solution.py:594
  177.5 39.8 %collective-permute-start.4 = (bf16[8,144,768]{2,1,0:T(8,128)(2,1)}, bf16[8,144,768]{2,1,0:T(8,128)(2,1)}, u32[]{:S(2)}, u32[]{:S(2)}) collective-permute-start(bf16[8,144,768]{2,1,0:T(8,128)(2,1)} %slice.222), channel_id=1, source_target_pairs={{0,2},{2,0},{1,3},{3,1},{4,6},{6,4},{5,7},{7,5},{8,10},{10,8},{9,1... | collective-permute-start | bytes 5308424 | tf_op jit(solution)/shard_map/ppermute | solution.py:34
  228.1 8.1 %collective-permute-start.5 = (f32[1024,1152]{1,0:T(8,128)}, f32[1024,1152]{1,0:T(8,128)S(1)}, u32[]{:S(2)}, u32[]{:S(2)}) collective-permute-start(f32[1024,1152]{1,0:T(8,128)} %fusion.50), channel_id=1, source_target_pairs={{0,1},{1,0},{2,3},{3,2},{4,5},{5,4},{6,7},{7,6},{8,9},{9,8},{10,11... | collective-permute-start | bytes 14155784 | tf_op jit(solution)/shard_map/ppermute | solution.py:34
  246.7 59.3 %all-to-all-start.2 = ((bf16[8,128,1152]{2,1,0:T(8,128)(2,1)}), bf16[8,128,1152]{2,1,0:T(8,128)(2,1)}, u32[]{:S(2)}, u32[]{:S(2)}) async-start(bf16[8,128,1152]{2,1,0:T(8,128)(2,1)} %bitcast.224), calls=%async_computation.2 | async-start | bytes 4718592 | tf_op jit(solution)/shard_map/all_to_all | solution.py:594
  253.2 40.8 %collective-permute-start.6 = (bf16[8,144,768]{2,1,0:T(8,128)(2,1)S(1)}, bf16[8,144,768]{2,1,0:T(8,128)(2,1)}, u32[]{:S(2)}, u32[]{:S(2)}) collective-permute-start(bf16[8,144,768]{2,1,0:T(8,128)(2,1)S(1)} %slice.224), channel_id=1, source_target_pairs={{0,2},{2,0},{1,3},{3,1},{4,6},{6,4},{5,7},{7,5},{8,10},{10,8},{9,1... | collective-permute-start | bytes 5308424 | tf_op jit(solution)/shard_map/ppermute | solution.py:34
  253.3 53.9 %collective-permute-start.8 = (bf16[1024,1152]{1,0:T(8,128)(2,1)}, bf16[1024,1152]{1,0:T(8,128)(2,1)}, u32[]{:S(2)}, u32[]{:S(2)}) collective-permute-start(bf16[1024,1152]{1,0:T(8,128)(2,1)} %bitcast.34.cotan_ref), channel_id=1, source_target_pairs={{0,1},{1,0},{2,3},{3,2},{4,5},{5,4},{6,7},{7,6},{8,9},{9,8},{10,11... | collective-permute-start | bytes 7077896 | tf_op jit(solution)/shard_map/ppermute | solution.py:34
  306.0 4.9 collective-permute-start.7
  334.5 25.6 %collective-permute-start.10 = (f32[1024,1152]{1,0:T(8,128)}, f32[1024,1152]{1,0:T(8,128)}, u32[]{:S(2)}, u32[]{:S(2)}) collective-permute-start(f32[1024,1152]{1,0:T(8,128)} %get-tuple-element.149), channel_id=1, source_target_pairs={{0,1},{1,0},{2,3},{3,2},{4,5},{5,4},{6,7},{7,6},{8,9},{9,8},{10,11... | collective-permute-start | bytes 14155784 | tf_op jit(solution)/shard_map/ppermute | solution.py:34
  334.7 32.0 %collective-permute-start.9 = (f32[1024,1152]{1,0:T(8,128)}, f32[1024,1152]{1,0:T(8,128)S(1)}, u32[]{:S(2)}, u32[]{:S(2)}) collective-permute-start(f32[1024,1152]{1,0:T(8,128)} %get-tuple-element.147), channel_id=1, source_target_pairs={{0,1},{1,0},{2,3},{3,2},{4,5},{5,4},{6,7},{7,6},{8,9},{9,8},{10,11... | collective-permute-start | bytes 14155784 | tf_op jit(solution)/shard_map/ppermute | solution.py:34
  370.8 58.8 %all-to-all-start.3 = ((bf16[8,128,1152]{2,1,0:T(8,128)(2,1)}), bf16[8,128,1152]{2,1,0:T(8,128)(2,1)}, u32[]{:S(2)}, u32[]{:S(2)}) async-start(bf16[8,128,1152]{2,1,0:T(8,128)(2,1)} %bitcast.188), calls=%async_computation.3 | async-start | bytes 4718592 | tf_op jit(solution)/shard_map/all_to_all | solution.py:594
  382.9 40.8 %collective-permute-start.11 = (bf16[1152,768]{1,0:T(8,128)(2,1)S(1)}, bf16[1152,768]{1,0:T(8,128)(2,1)}, u32[]{:S(2)}, u32[]{:S(2)}) collective-permute-start(bf16[1152,768]{1,0:T(8,128)(2,1)S(1)} %convolution_convert_fusion.3), channel_id=1, source_target_pairs={{0,2},{2,0},{1,3},{3,1},{4,6},{6,4},{5,7},{7,5},{8,10},{10,8},{9,1... | collective-permute-start | bytes 5308424 | tf_op jit(solution)/shard_map/ppermute | solution.py:34
  399.5 6.0 collective-permute-start.12
  435.4 4.9 collective-permute-start.13
  435.4 59.2 %collective-permute-start.15 = (bf16[1152,768]{1,0:T(8,128)(2,1)}, bf16[1152,768]{1,0:T(8,128)(2,1)}, u32[]{:S(2)}, u32[]{:S(2)}) collective-permute-start(bf16[1152,768]{1,0:T(8,128)(2,1)} %convolution_convert_fusion.4), channel_id=1, source_target_pairs={{0,2},{2,0},{1,3},{3,1},{4,6},{6,4},{5,7},{7,5},{8,10},{10,8},{9,1... | collective-permute-start | bytes 5308424 | tf_op jit(solution)/shard_map/ppermute | solution.py:34
  435.4 59.3 %all-to-all-start.4 = ((bf16[8,128,1152]{2,1,0:T(8,128)(2,1)}), bf16[8,128,1152]{2,1,0:T(8,128)(2,1)}, u32[]{:S(2)}, u32[]{:S(2)}) async-start(bf16[8,128,1152]{2,1,0:T(8,128)(2,1)} %bitcast.190), calls=%async_computation.4 | async-start | bytes 4718592 | tf_op jit(solution)/shard_map/all_to_all | solution.py:594
  501.6 88.0 %all-to-all-start.5 = ((bf16[8,288,768]{2,1,0:T(8,128)(2,1)}), bf16[8,288,768]{2,1,0:T(8,128)(2,1)}, u32[]{:S(2)}, u32[]{:S(2)}) async-start(bf16[8,288,768]{2,1,0:T(8,128)(2,1)} %pad_maximum_fusion), calls=%async_computation.5 | async-start | bytes 7077888 | tf_op jit(solution)/shard_map/all_to_all | solution.py:1087
  507.2 9.7 %collective-permute-start.14 = (f32[2,16,1152]{2,1,0:T(8,128)S(1)}, f32[2,16,1152]{2,1,0:T(8,128)S(1)}, u32[]{:S(2)}, u32[]{:S(2)}) collective-permute-start(f32[2,16,1152]{2,1,0:T(8,128)S(1)} %copy-done.61), channel_id=1, source_target_pairs={{2,0},{3,1},{6,4},{7,5},{10,8},{11,9},{14,12},{15,13},{18,16},{19,... | collective-permute-start | bytes 442376 | tf_op jit(solution)/shard_map/ppermute | solution.py:40
  516.9 72.7 %collective-permute-start.16 = (bf16[1152,1152]{1,0:T(8,128)(2,1)S(1)}, bf16[1152,1152]{1,0:T(8,128)(2,1)}, u32[]{:S(2)}, u32[]{:S(2)}) collective-permute-start(bf16[1152,1152]{1,0:T(8,128)(2,1)S(1)} %copy-done.57), channel_id=1, source_target_pairs={{0,2},{2,0},{1,3},{3,1},{4,6},{6,4},{5,7},{7,5},{8,10},{10,8},{9,1... | collective-permute-start | bytes 7962632 | tf_op jit(solution)/shard_map/ppermute | solution.py:34
  594.9 65.7 %all-to-all-start.6 = ((bf16[8,144,1152]{2,1,0:T(8,128)(2,1)}), bf16[8,144,1152]{2,1,0:T(8,128)(2,1)}, u32[]{:S(2)}, u32[]{:S(2)}) async-start(bf16[8,144,1152]{2,1,0:T(8,128)(2,1)} %bitcast.186), calls=%async_computation.6 | async-start | bytes 5308416 | tf_op jit(solution)/shard_map/all_to_all | solution.py:1103
  607.0 43.9 %collective-permute-start.19 = (bf16[8,144,768]{2,1,0:T(8,128)(2,1)}, bf16[8,144,768]{2,1,0:T(8,128)(2,1)}, u32[]{:S(2)}, u32[]{:S(2)}) collective-permute-start(bf16[8,144,768]{2,1,0:T(8,128)(2,1)} %slice.228), channel_id=1, source_target_pairs={{0,2},{2,0},{1,3},{3,1},{4,6},{6,4},{5,7},{7,5},{8,10},{10,8},{9,1... | collective-permute-start | bytes 5308424 | tf_op jit(solution)/shard_map/ppermute | solution.py:34
  610.7 13.8 %collective-permute-start.17 = (f32[1024,104]{1,0:T(8,128)}, f32[1024,104]{1,0:T(8,128)}, u32[]{:S(2)}, u32[]{:S(2)}) collective-permute-start(f32[1024,104]{1,0:T(8,128)} %pad_maximum_fusion.4), channel_id=1, source_target_pairs={{0,1},{1,0},{2,3},{3,2},{4,5},{5,4},{6,7},{7,6},{8,9},{9,8},{10,11... | collective-permute-start | bytes 1277960 | tf_op jit(solution)/shard_map/ppermute | solution.py:34
  641.0 9.9 %collective-permute-start.18 = (f32[3,2,1,1152]{3,2,1,0:T(1,128)S(1)}, f32[3,2,1,1152]{3,2,1,0:T(1,128)S(1)}, u32[]{:S(2)}, u32[]{:S(2)}) collective-permute-start(f32[3,2,1,1152]{3,2,1,0:T(1,128)S(1)} %slice.269), channel_id=1, source_target_pairs={{2,0},{3,1},{6,4},{7,5},{10,8},{11,9},{14,12},{15,13},{18,16},{19,... | collective-permute-start | bytes 82952 | tf_op jit(solution)/shard_map/ppermute | solution.py:40
  668.0 8.4 %collective-permute-start.20 = (f32[1024,1152]{1,0:T(8,128)S(1)}, f32[1024,1152]{1,0:T(8,128)S(1)}, u32[]{:S(2)}, u32[]{:S(2)}) collective-permute-start(f32[1024,1152]{1,0:T(8,128)S(1)} %add.242), channel_id=1, source_target_pairs={{0,1},{1,0},{2,3},{3,2},{4,5},{5,4},{6,7},{7,6},{8,9},{9,8},{10,11... | collective-permute-start | bytes 14155784 | tf_op jit(solution)/shard_map/ppermute | solution.py:34
  682.4 77.6 %all-to-all-start.7 = ((bf16[8,171,1152]{2,1,0:T(8,128)(2,1)}), bf16[8,171,1152]{2,1,0:T(8,128)(2,1)}, u32[]{:S(2)}, u32[]{:S(2)}) async-start(bf16[8,171,1152]{2,1,0:T(8,128)(2,1)} %pad_maximum_fusion.1), calls=%async_computation.7 | async-start | bytes 6488064 | tf_op jit(solution)/shard_map/all_to_all | solution.py:1176
  689.3 16.5 %collective-permute-start.22 = (f32[144,1152]{1,0:T(8,128)S(1)}, f32[144,1152]{1,0:T(8,128)S(1)}, u32[]{:S(2)}, u32[]{:S(2)}) collective-permute-start(f32[144,1152]{1,0:T(8,128)S(1)} %convert_reduce_fusion), channel_id=1, source_target_pairs={{0,2},{2,0},{1,3},{3,1},{4,6},{6,4},{5,7},{7,5},{8,10},{10,8},{9,1... | collective-permute-start | bytes 1990664 | tf_op jit(solution)/shard_map/ppermute | solution.py:34
  701.6 10.6 %collective-permute-start.21 = (bf16[1024,1152]{1,0:T(8,128)(2,1)S(1)}, bf16[1024,1152]{1,0:T(8,128)(2,1)S(1)}, u32[]{:S(2)}, u32[]{:S(2)}) collective-permute-start(bf16[1024,1152]{1,0:T(8,128)(2,1)S(1)} %fusion.35), channel_id=1, source_target_pairs={{0,1},{1,0},{2,3},{3,2},{4,5},{5,4},{6,7},{7,6},{8,9},{9,8},{10,11... | collective-permute-start | bytes 7077896 | tf_op jit(solution)/shard_map/ppermute | solution.py:34
  706.9 39.5 %collective-permute-start.23 = (bf16[8,144,768]{2,1,0:T(8,128)(2,1)S(1)}, bf16[8,144,768]{2,1,0:T(8,128)(2,1)}, u32[]{:S(2)}, u32[]{:S(2)}) collective-permute-start(bf16[8,144,768]{2,1,0:T(8,128)(2,1)S(1)} %get-tuple-element.201), channel_id=1, source_target_pairs={{0,2},{2,0},{1,3},{3,1},{4,6},{6,4},{5,7},{7,5},{8,10},{10,8},{9,1... | collective-permute-start | bytes 5308424 | tf_op jit(solution)/shard_map/ppermute | solution.py:34
  765.9 10.2 %collective-permute-start.24 = (bf16[171,1152]{1,0:T(8,128)(2,1)S(1)}, bf16[171,1152]{1,0:T(8,128)(2,1)S(1)}, u32[]{:S(2)}, u32[]{:S(2)}) collective-permute-start(bf16[171,1152]{1,0:T(8,128)(2,1)S(1)} %reduce_sum.152), channel_id=1, source_target_pairs={{0,2},{2,0},{1,3},{3,1},{4,6},{6,4},{5,7},{7,5},{8,10},{10,8},{9,1... | collective-permute-start | bytes 1181960 | tf_op jit(solution)/shard_map/ppermute | solution.py:34
  (89 other events, 768.7 us)
